TPU v7x, 32 devices: a whole 2x2x4 slice. The times are simulated.
32 devices in a mesh: dp: 8 (over y, x, core), rep: 4 (over z).
Axes of the slice: x: 2, y: 2, z: 4, core: 2. Of those that a mesh axis runs over, the one named last changes fastest.
Arguments:
- tokens: int32 [8, 1024], P('dp', 'rep'), may hold values from 0 to 31999
- segments: int32 [8, 1024], P('dp'), may hold values from 0 to 3, never falling along the last dimension, each value on 1 to 800 neighbouring positions
- completion: int32 [8, 256], P('dp'), may hold values from 0 to 1023, as said below
- targets: int32 [8, 256], P('dp'), may hold values from 0 to 31999
- owners: int32 [32], replicated, may hold values from 0 to 7, as said below
- step_count: int32 [1], replicated, may hold values from 2 to 20
- tile_weight: float32 [192, 192, 768], P(('dp', 'rep')), may hold values from -0.21875 to 0.21875
- tile_first: float32 [192, 192, 768], P(('dp', 'rep')), may hold values from -9.536743e-06 to 9.536743e-06
- tile_second: float32 [192, 192, 768], P(('dp', 'rep')), may hold values from 3.6748382e-13 to 1.4699353e-12
- table_weight: float32 [32000, 768], P(('dp', 'rep')), may hold values from -5 to 5
- table_first: float32 [32000, 768], P(('dp', 'rep')), may hold values from -9.536743e-06 to 9.536743e-06
- table_second: float32 [32000, 768], P(('dp', 'rep')), may hold values from 3.6748382e-13 to 1.4699353e-12
- head_weight: float32 [32000, 768], P(('dp', 'rep')), may hold values from -0.625 to 0.625
- head_first: float32 [32000, 768], P(('dp', 'rep')), may hold values from -9.536743e-06 to 9.536743e-06
- head_second: float32 [32000, 768], P(('dp', 'rep')), may hold values from 3.6748382e-13 to 1.4699353e-12
- gain_weight: float32 [5, 768], replicated, may hold values from 0.5 to 1.5
- gain_first: float32 [5, 768], replicated, may hold values from -3.8146973e-05 to 3.8146973e-05
- gain_second: float32 [5, 768], replicated, may hold values from 5.879741e-12 to 2.3518965e-11
Outputs:
- loss: float32 [], replicated
- clip_norm: float32 [], replicated
- new_tile_weight: float32 [192, 192, 768], P(('dp', 'rep'))
- new_tile_copy: bfloat16 [192, 192, 768], P(('dp', 'rep'))
- new_tile_first: float32 [192, 192, 768], P(('dp', 'rep'))
- new_tile_second: float32 [192, 192, 768], P(('dp', 'rep'))
- new_table_weight: float32 [32000, 768], P(('dp', 'rep'))
- new_table_copy: bfloat16 [32000, 768], P(('dp', 'rep'))
- new_table_first: float32 [32000, 768], P(('dp', 'rep'))
- new_table_second: float32 [32000, 768], P(('dp', 'rep'))
- new_head_weight: float32 [32000, 768], P(('dp', 'rep'))
- new_head_copy: bfloat16 [32000, 768], P(('dp', 'rep'))
- new_head_first: float32 [32000, 768], P(('dp', 'rep'))
- new_head_second: float32 [32000, 768], P(('dp', 'rep'))
- new_gain_weight: float32 [5, 768], replicated
- new_gain_first: float32 [5, 768], replicated
- new_gain_second: float32 [5, 768], replicated
Inputs may be any that keep to these rules, and one draw needn't show every extreme that they name: `completion`: in every sequence the 256 positions are distinct and ascending; of each aligned block of 256 positions at most 96 are listed, and in every sequence some block holds exactly 96. `owners`: at most 6 matrices share an owner, and some owner holds exactly 6.
All inputs are finite; a program needn't handle non-finite values.
Results may differ from a plain program's by a relative error of at most 0.012.
The roundings to bfloat16 on the way count: a program that leaves them out, or rounds other values in their place, can miss the bound.
Values may be sent and summed in bfloat16 or wider, within the bound.
A program may use at most 640 MiB of HBM per device.

v0:
```python
import math

import jax
import jax.numpy as jnp
from jax import lax
from jax.sharding import PartitionSpec as P

D = 768
HEADS = 12
HD = 64
FF = 3072
LAYERS = 2
COMP = 256


HIGHEST_ACCURACY = lax.Precision.HIGHEST
EPS_NORM = 1e-05
EPS_ADAM = 1e-08
CLIP_NORM = 0.005
BETA_FIRST = 0.5
BETA_SECOND = 0.5
DECAY = 0.1
RATE_TILE = 0.02
RATE_HEAD = 0.05
RATE_TABLE = 0.5
RATE_GAIN = 0.3
MASKED = -1e30


def joined(part, axis, combine):
    gathered = jax.tree.map(lambda a: lax.all_gather(a, axis), part)

    def take(source):
        return jax.tree.map(lambda a: lax.dynamic_index_in_dim(a, source, 0, False), gathered)

    return lax.fori_loop(
        1, lax.axis_size(axis), lambda source, state: combine(state, take(source)), take(0)
    )


def root_norm(training_state, gain):
    return (
        training_state
        * lax.rsqrt(jnp.mean(training_state * training_state, axis=-1, keepdims=True) + EPS_NORM)
        * gain
    )


def norm_back(training_state, gain, grad):
    scale = lax.rsqrt(jnp.mean(training_state * training_state, axis=-1, keepdims=True) + EPS_NORM)
    scaled = grad * gain
    state_grad = scale * scaled - training_state * scale**3 * jnp.mean(
        scaled * training_state, axis=-1, keepdims=True
    )
    gain_grad = jnp.sum(
        (grad * training_state * scale).reshape(-1, training_state.shape[-1]), axis=0
    )
    return (state_grad, gain_grad)


def rope_tables(places, width):
    half = width // 2
    freqs = jnp.power(10000.0, -2.0 * jnp.arange(half).astype(jnp.float32) / width)
    angle = places[:, None] * freqs[None, :]
    return (jnp.cos(angle), jnp.sin(angle))


def rotate(field, cosine, sine):
    half = field.shape[-1] // 2
    first, second = (field[..., :half], field[..., half:])
    cosine, sine = (cosine[:, None, :], sine[:, None, :])
    return jnp.concatenate(
        [first * cosine - second * sine, second * cosine + first * sine], axis=-1
    )


def rotate_back(field, cosine, sine):
    half = field.shape[-1] // 2
    first, second = (field[..., :half], field[..., half:])
    cosine, sine = (cosine[:, None, :], sine[:, None, :])
    return jnp.concatenate(
        [first * cosine + second * sine, second * cosine - first * sine], axis=-1
    )


def tile_slots(owners):
    order = jnp.arange(owners.shape[0], dtype=jnp.int32)
    same = (owners[:, None] == owners[None, :]) & (order[None, :] < order[:, None])
    return jnp.sum(same.astype(jnp.int32), axis=1)


def from_owners(stored, owners, slots, dp_size, rep_size, slots_cap):
    width = stored.shape[-1]
    grid = stored.reshape(dp_size, rep_size, slots_cap, -1, width).transpose(0, 2, 1, 3, 4)
    grid = grid.reshape(dp_size * slots_cap, -1, width)
    return jnp.take(grid, owners * slots_cap + slots, axis=0)


def to_owners(tiles, owners, slots, dp_size, rep_size, slots_cap):
    width = tiles.shape[-1]
    grid = (
        jnp.zeros((dp_size * slots_cap,) + tiles.shape[1:], tiles.dtype)
        .at[owners * slots_cap + slots]
        .set(tiles)
    )
    grid = grid.reshape(dp_size, slots_cap, rep_size, -1, width).transpose(0, 2, 1, 3, 4)
    return grid.reshape(dp_size * rep_size * slots_cap, -1, width)


def layer_weights(tiles):
    units = FF // D
    input_projection_weight = tiles[0:3].transpose(1, 0, 2).reshape(D, 3 * D)
    output_projection_weight = tiles[3]
    gate_projection_weight = tiles[4 : 4 + 2 * units].transpose(1, 0, 2).reshape(D, 2 * FF)
    down_projection_weight = tiles[4 + 2 * units : 4 + 3 * units].reshape(FF, D)
    return (
        input_projection_weight,
        output_projection_weight,
        gate_projection_weight,
        down_projection_weight,
    )


def adam(weight, first, second, grad, factor, rate, decay, steps):
    grad = grad * factor
    first = BETA_FIRST * first + (1.0 - BETA_FIRST) * grad
    second = BETA_SECOND * second + (1.0 - BETA_SECOND) * grad * grad
    first_hat = first / (1.0 - jnp.power(BETA_FIRST, steps))
    second_hat = second / (1.0 - jnp.power(BETA_SECOND, steps))
    weight = weight - rate * (first_hat / (jnp.sqrt(second_hat) + EPS_ADAM) + decay * weight)
    return (weight, first, second)


def layer_forward(training_state, weights, gain_pair, cosine, sine, allowed):
    (
        input_projection_weight,
        output_projection_weight,
        gate_projection_weight,
        down_projection_weight,
    ) = weights
    batch, rows = (training_state.shape[0], training_state.shape[1])
    normalized_input = root_norm(training_state, gain_pair[0]).astype(jnp.bfloat16)
    mixed_heads_output = jnp.einsum(
        "bld,de->ble", normalized_input, input_projection_weight, preferred_element_type=jnp.float32
    )
    parts = mixed_heads_output.reshape(batch, rows, 3, HEADS, HD)
    query = rotate(parts[:, :, 0], cosine, sine).astype(jnp.bfloat16)
    keys = rotate(parts[:, :, 1], cosine, sine).astype(jnp.bfloat16).reshape(batch, rows, D)
    value = parts[:, :, 2].astype(jnp.bfloat16).reshape(batch, rows, D)
    keys_all, value_all = (
        lax.all_gather(keys, "rep", axis=1, tiled=True),
        lax.all_gather(value, "rep", axis=1, tiled=True),
    )
    length = keys_all.shape[1]
    keys_all = keys_all.reshape(batch, length, HEADS, HD)
    value_all = value_all.reshape(batch, length, HEADS, HD)
    scores = jnp.einsum(
        "bqhd,bkhd->bhqk", query, keys_all, preferred_element_type=jnp.float32
    ) * HD ** (-0.5)
    scores = jnp.where(allowed, scores, MASKED)
    top = jnp.max(scores, axis=-1, keepdims=True)
    exponent = jnp.exp(scores - top)
    total = jnp.sum(exponent, axis=-1, keepdims=True)
    prob = (exponent / total).astype(jnp.bfloat16)
    log_total = top + jnp.log(total)
    attention_heads = jnp.einsum(
        "bhqk,bkhd->bqhd", prob, value_all, preferred_element_type=jnp.float32
    )
    attention_heads = attention_heads.reshape(batch, rows, D).astype(jnp.bfloat16)
    middle_activation = training_state + jnp.einsum(
        "bld,de->ble", attention_heads, output_projection_weight, preferred_element_type=jnp.float32
    )
    normed_feed = root_norm(middle_activation, gain_pair[1]).astype(jnp.bfloat16)
    gate_upward_product = jnp.einsum(
        "bld,de->ble", normed_feed, gate_projection_weight, preferred_element_type=jnp.float32
    )
    hidden_state = (
        jax.nn.silu(gate_upward_product[..., :FF]) * gate_upward_product[..., FF:]
    ).astype(jnp.bfloat16)
    output = middle_activation + jnp.einsum(
        "ble,ed->bld", hidden_state, down_projection_weight, preferred_element_type=jnp.float32
    )
    return (
        output,
        (
            training_state,
            middle_activation,
            normalized_input,
            normed_feed,
            query,
            keys_all,
            value_all,
            log_total,
            attention_heads,
            gate_upward_product,
            hidden_state,
        ),
    )


def layer_backward(grad, kept, weights, gain_pair, cosine, sine, allowed):
    (
        training_state,
        middle_activation,
        normalized_input,
        normed_feed,
        query,
        keys_all,
        value_all,
        log_total,
        attention_heads,
        gate_upward_product,
        hidden_state,
    ) = kept
    (
        input_projection_weight,
        output_projection_weight,
        gate_projection_weight,
        down_projection_weight,
    ) = weights
    batch, rows = (training_state.shape[0], training_state.shape[1])
    length = keys_all.shape[1]
    branch = grad.astype(jnp.bfloat16)
    down_grad = jnp.einsum("ble,bld->ed", hidden_state, branch, preferred_element_type=jnp.float32)
    hidden_grad = jnp.einsum(
        "bld,ed->ble", branch, down_projection_weight, preferred_element_type=jnp.float32
    )
    gate, upper = (gate_upward_product[..., :FF], gate_upward_product[..., FF:])
    sigma = jax.nn.sigmoid(gate)
    mixed_grad = jnp.concatenate(
        [hidden_grad * upper * sigma * (1.0 + gate * (1.0 - sigma)), hidden_grad * gate * sigma],
        axis=-1,
    ).astype(jnp.bfloat16)
    gate_tile = jnp.einsum(
        "bld,ble->de", normed_feed, mixed_grad, preferred_element_type=jnp.float32
    )
    back, feed_gain = norm_back(
        middle_activation,
        gain_pair[1],
        jnp.einsum(
            "ble,de->bld", mixed_grad, gate_projection_weight, preferred_element_type=jnp.float32
        ),
    )
    middle_grad = grad + back
    branch = middle_grad.astype(jnp.bfloat16)
    output_tile = jnp.einsum(
        "bld,ble->de", attention_heads, branch, preferred_element_type=jnp.float32
    )
    heads_grad = jnp.einsum(
        "ble,de->bld", branch, output_projection_weight, preferred_element_type=jnp.float32
    )
    heads_grad = heads_grad.astype(jnp.bfloat16).reshape(batch, rows, HEADS, HD)
    scores = jnp.einsum(
        "bqhd,bkhd->bhqk", query, keys_all, preferred_element_type=jnp.float32
    ) * HD ** (-0.5)
    prob = jnp.exp(jnp.where(allowed, scores, MASKED) - log_total)
    value_part = jnp.einsum(
        "bhqk,bqhd->bkhd", prob.astype(jnp.bfloat16), heads_grad, preferred_element_type=jnp.float32
    )
    prob_grad = jnp.einsum(
        "bqhd,bkhd->bhqk", heads_grad, value_all, preferred_element_type=jnp.float32
    )
    score_grad = (
        prob * (prob_grad - jnp.sum(prob * prob_grad, axis=-1, keepdims=True)) * HD ** (-0.5)
    ).astype(jnp.bfloat16)
    query_grad = jnp.einsum(
        "bhqk,bkhd->bqhd", score_grad, keys_all, preferred_element_type=jnp.float32
    )
    keys_part = jnp.einsum("bhqk,bqhd->bkhd", score_grad, query, preferred_element_type=jnp.float32)
    keys_grad, value_grad = (
        lax.psum_scatter(
            keys_part.reshape(batch, length, D).astype(jnp.bfloat16),
            "rep",
            scatter_dimension=1,
            tiled=True,
        ).astype(jnp.float32),
        lax.psum_scatter(
            value_part.reshape(batch, length, D).astype(jnp.bfloat16),
            "rep",
            scatter_dimension=1,
            tiled=True,
        ).astype(jnp.float32),
    )
    input_grad = jnp.concatenate(
        [
            rotate_back(query_grad, cosine, sine).reshape(batch, rows, D),
            rotate_back(keys_grad.reshape(batch, rows, HEADS, HD), cosine, sine).reshape(
                batch, rows, D
            ),
            value_grad,
        ],
        axis=-1,
    ).astype(jnp.bfloat16)
    input_tile = jnp.einsum(
        "bld,ble->de", normalized_input, input_grad, preferred_element_type=jnp.float32
    )
    back, attend_gain = norm_back(
        training_state,
        gain_pair[0],
        jnp.einsum(
            "ble,de->bld", input_grad, input_projection_weight, preferred_element_type=jnp.float32
        ),
    )
    units = FF // D
    tiles_grad = jnp.concatenate(
        [
            input_tile.reshape(D, 3, D).transpose(1, 0, 2),
            output_tile[None],
            gate_tile.reshape(D, 2 * units, D).transpose(1, 0, 2),
            down_grad.reshape(units, D, D),
        ],
        axis=0,
    )
    return (middle_grad + back, tiles_grad, jnp.stack([attend_gain, feed_gain]))


def shards(
    tokens,
    segments,
    completion,
    targets,
    owners,
    step_count,
    tile_weight,
    tile_first,
    tile_second,
    table_weight,
    table_first,
    table_second,
    head_weight,
    head_first,
    head_second,
    gain_weight,
    gain_first,
    gain_second,
):
    dp_size = lax.axis_size("dp")
    rep_size = lax.axis_size("rep")
    dp_index = lax.axis_index("dp")
    rep_index = lax.axis_index("rep")
    device = dp_index * rep_size + rep_index
    batch, rows = tokens.shape
    length = segments.shape[1]
    slots_cap = tile_weight.shape[0]
    vocab_rows = table_weight.shape[0]
    vocab_start = device * vocab_rows
    slots = tile_slots(owners)
    gathered = lax.all_gather(tile_weight.astype(jnp.bfloat16), ("dp", "rep"), axis=0, tiled=True)
    tiles = from_owners(gathered, owners, slots, dp_size, rep_size, slots_cap)
    flat_tokens = tokens.reshape(-1)
    piece = lax.all_gather(table_weight.astype(jnp.bfloat16), ("dp", "rep"), axis=0, tiled=True)
    local = flat_tokens
    inside = (local >= 0) & (local < piece.shape[0])
    picked = jnp.take(piece, jnp.clip(local, 0, piece.shape[0] - 1), axis=0)
    training_state = jnp.where(inside[:, None], picked.astype(jnp.float32), 0.0)
    training_state = training_state.reshape(batch, rows, D)
    first_place = rep_index * rows
    query_places = first_place + jnp.arange(rows)
    cosine, sine = rope_tables(query_places.astype(jnp.float32), HD)
    query_segments = lax.dynamic_slice_in_dim(segments, first_place, rows, 1)
    allowed = (jnp.arange(length)[None, None, :] <= query_places[None, :, None]) & (
        query_segments[:, :, None] == segments[:, None, :]
    )
    allowed = allowed[:, None]
    tiles_per = 4 + 3 * FF // D
    layer_list = [
        layer_weights(tiles[index * tiles_per : (index + 1) * tiles_per]) for index in range(LAYERS)
    ]
    kept_list = []
    for index in range(LAYERS):
        training_state, kept = layer_forward(
            training_state,
            layer_list[index],
            gain_weight[2 * index : 2 * index + 2],
            cosine,
            sine,
            allowed,
        )
        kept_list.append(kept)
    final_gain = gain_weight[2 * LAYERS]
    final = root_norm(training_state, final_gain).astype(jnp.bfloat16)
    capacity = 3 * COMP // (2 * rep_size)
    local = completion - first_place
    inside = (local >= 0) & (local < rows)
    rank = jnp.cumsum(inside.astype(jnp.int32), axis=1) - 1
    slot_pick = (
        inside[:, :, None] & (rank[:, :, None] == jnp.arange(capacity)[None, None, :])
    ).astype(jnp.int32)
    row_pick = (inside[:, :, None] & (local[:, :, None] == jnp.arange(rows)[None, None, :])).astype(
        jnp.bfloat16
    )
    select = jnp.einsum(
        "bpc,bpt->bct", slot_pick.astype(jnp.bfloat16), row_pick, preferred_element_type=jnp.float32
    ).astype(jnp.bfloat16)
    chosen = jnp.einsum("bct,btd->bcd", select, final, preferred_element_type=jnp.float32).astype(
        jnp.bfloat16
    )
    filled = jnp.sum(slot_pick, axis=1)
    wanted = jnp.where(filled > 0, jnp.sum(slot_pick * targets[:, :, None], axis=1), -1)
    all_rows, all_wanted = (
        lax.all_gather(chosen.reshape(batch * capacity, D), ("dp", "rep"), axis=0, tiled=True),
        lax.all_gather(wanted.reshape(-1), ("dp", "rep"), axis=0, tiled=True),
    )
    head_low = head_weight.astype(jnp.bfloat16)
    slot_total = all_rows.shape[0]
    block = math.gcd(slot_total, 2048)
    row_blocks = all_rows.reshape(-1, block, D)
    wanted_blocks = all_wanted.reshape(-1, block)
    vocab_ids = vocab_start + jnp.arange(vocab_rows)

    def block_logits(piece):
        return jnp.einsum("rd,vd->rv", piece, head_low, preferred_element_type=jnp.float32)

    def block_stats(item):
        piece, want = item
        logits = block_logits(piece)
        top = jnp.max(logits, axis=-1)
        total = jnp.sum(jnp.exp(logits - top[:, None]), axis=-1)
        target_hit = jnp.sum(jnp.where(vocab_ids[None, :] == want[:, None], logits, 0.0), axis=-1)
        return (top, total, target_hit)

    tops, totals, target_hits = lax.map(block_stats, (row_blocks, wanted_blocks))

    def combine(first, second):
        top = jnp.maximum(first[0], second[0])
        return (
            top,
            first[1] * jnp.exp(first[0] - top) + second[1] * jnp.exp(second[0] - top),
            first[2] + second[2],
        )

    top, total, target_hit = joined(
        (tops.reshape(-1), totals.reshape(-1), target_hits.reshape(-1)), ("dp", "rep"), combine
    )
    log_total = top + jnp.log(total)
    valid = all_wanted >= 0
    scored = batch * dp_size * COMP
    loss = jnp.sum(jnp.where(valid, log_total - target_hit, 0.0)) / scored

    def head_back(carry, item):
        piece, want, log_part, good = item
        logits = block_logits(piece)
        onehot = jnp.where(vocab_ids[None, :] == want[:, None], 1.0, 0.0)
        logit_grad = jnp.where(
            good[:, None], (jnp.exp(logits - log_part[:, None]) - onehot) / scored, 0.0
        ).astype(jnp.bfloat16)
        carry = carry + jnp.einsum(
            "rv,rd->vd", logit_grad, piece, preferred_element_type=jnp.float32
        )
        return (
            carry,
            jnp.einsum("rv,vd->rd", logit_grad, head_low, preferred_element_type=jnp.float32),
        )

    head_grad, rows_grad = lax.scan(
        head_back,
        jnp.zeros((vocab_rows, D), jnp.float32),
        (row_blocks, wanted_blocks, log_total.reshape(-1, block), valid.reshape(-1, block)),
    )
    own_rows = lax.psum_scatter(
        rows_grad.reshape(slot_total, D), ("dp", "rep"), scatter_dimension=0, tiled=True
    )
    final_grad = jnp.einsum(
        "bct,bcd->btd",
        select.astype(jnp.float32),
        own_rows.reshape(batch, capacity, D),
        precision=HIGHEST_ACCURACY,
        preferred_element_type=jnp.float32,
    )
    state_grad, final_gain_grad = norm_back(training_state, final_gain, final_grad)
    tile_parts = [None] * LAYERS
    gain_parts = [None] * LAYERS
    for index in reversed(range(LAYERS)):
        state_grad, tiles_grad, gains_grad = layer_backward(
            state_grad,
            kept_list[index],
            layer_list[index],
            gain_weight[2 * index : 2 * index + 2],
            cosine,
            sine,
            allowed,
        )
        tile_parts[index] = tiles_grad
        gain_parts[index] = gains_grad
    entry_grad = state_grad.reshape(-1, D).astype(jnp.bfloat16)
    piece_tokens = lax.all_gather(flat_tokens, ("dp", "rep"), axis=0, tiled=True)
    piece_grads = lax.all_gather(entry_grad, ("dp", "rep"), axis=0, tiled=True)
    place = piece_tokens - vocab_start
    within = (place >= 0) & (place < vocab_rows)
    summed = jax.ops.segment_sum(
        piece_grads.astype(jnp.float32),
        jnp.where(within, place, vocab_rows),
        num_segments=vocab_rows + 1,
    )
    table_grad = summed[:vocab_rows]
    tile_grads = jnp.concatenate(tile_parts, axis=0)
    grid = to_owners(tile_grads, owners, slots, dp_size, rep_size, slots_cap)
    own_grad = lax.psum_scatter(grid, ("dp", "rep"), scatter_dimension=0, tiled=True)
    gain_grads = jnp.concatenate(gain_parts + [final_gain_grad[None]], axis=0)
    square = (
        jnp.sum(own_grad * own_grad)
        + jnp.sum(table_grad * table_grad)
        + jnp.sum(head_grad * head_grad)
    )
    square, gain_grads = lax.psum((square, gain_grads), ("dp", "rep"))
    norm = jnp.sqrt(square + jnp.sum(gain_grads * gain_grads))
    factor = jnp.minimum(1.0, CLIP_NORM / norm)
    steps = step_count[0].astype(jnp.float32)
    own_count = jnp.sum((owners == dp_index).astype(jnp.int32))
    slot_valid = (jnp.arange(slots_cap) < own_count)[:, None, None]
    tile_new, tile_first_new, tile_second_new = adam(
        tile_weight, tile_first, tile_second, own_grad, factor, RATE_TILE, DECAY, steps
    )
    tile_new = jnp.where(slot_valid, tile_new, 0.0)
    tile_first_new = jnp.where(slot_valid, tile_first_new, 0.0)
    tile_second_new = jnp.where(slot_valid, tile_second_new, 0.0)
    table_new, table_first_new, table_second_new = adam(
        table_weight, table_first, table_second, table_grad, factor, RATE_TABLE, DECAY, steps
    )
    head_new, head_first_new, head_second_new = adam(
        head_weight, head_first, head_second, head_grad, factor, RATE_HEAD, DECAY, steps
    )
    gain_new, gain_first_new, gain_second_new = adam(
        gain_weight, gain_first, gain_second, gain_grads, factor, RATE_GAIN, 0.0, steps
    )
    return (
        loss,
        norm,
        tile_new,
        tile_new.astype(jnp.bfloat16),
        tile_first_new,
        tile_second_new,
        table_new,
        table_new.astype(jnp.bfloat16),
        table_first_new,
        table_second_new,
        head_new,
        head_new.astype(jnp.bfloat16),
        head_first_new,
        head_second_new,
        gain_new,
        gain_first_new,
        gain_second_new,
    )


def solution(mesh):
    return jax.shard_map(
        shards,
        mesh=mesh,
        in_specs=(
            P("dp", "rep"),
            P("dp", None),
            P("dp", None),
            P("dp", None),
            P(),
            P(),
            P(("dp", "rep"), None, None),
            P(("dp", "rep"), None, None),
            P(("dp", "rep"), None, None),
            P(("dp", "rep"), None),
            P(("dp", "rep"), None),
            P(("dp", "rep"), None),
            P(("dp", "rep"), None),
            P(("dp", "rep"), None),
            P(("dp", "rep"), None),
            P(),
            P(),
            P(),
        ),
        out_specs=(
            P(),
            P(),
            P(("dp", "rep"), None, None),
            P(("dp", "rep"), None, None),
            P(("dp", "rep"), None, None),
            P(("dp", "rep"), None, None),
            P(("dp", "rep"), None),
            P(("dp", "rep"), None),
            P(("dp", "rep"), None),
            P(("dp", "rep"), None),
            P(("dp", "rep"), None),
            P(("dp", "rep"), None),
            P(("dp", "rep"), None),
            P(("dp", "rep"), None),
            P(),
            P(),
            P(),
        ),
        check_vma=False,
    )
```

profile of v0, /device:TPU:0, one launch (start us, length us, event | category | flops | bytes accessed | tf_op | source)
XLA Modules:
  0.0 2946.4 jit_solution(10049333964625083591)
XLA Ops:
  15.4 268.5 %all-gather.13.cloned.1.call-done = bf16[32000,768]{1,0:T(8,128)(2,1)} async-done(((bf16[1000,768]{1,0:T(8,128)(2,1)}), bf16[32000,768]{1,0:T(8,128)(2,1)}) %all-gather.13.cloned.1.call-update) | async-done | bytes 49152016 | tf_op jit(solution)/shard_map/all_gather | solution.py:351
  288.0 303.5 %all-gather.15.cloned.1.call-done = bf16[192,192,768]{2,1,0:T(8,128)(2,1)} async-done(((bf16[6,192,768]{2,1,0:T(8,128)(2,1)}), bf16[192,192,768]{2,1,0:T(8,128)(2,1)}) %all-gather.15.cloned.1.call-update) | async-done | bytes 56623120 | tf_op jit(solution)/shard_map/all_gather | solution.py:348
  591.6 37.7 %copy.98 = bf16[8,6,4,192,768]{4,3,2,1,0:T(8,128)(2,1)} copy(bf16[8,6,4,192,768]{4,3,1,2,0:T(8,128)(2,1)} %bitcast.357) | data formatting | bytes 113246208 | tf_op jit(solution)/shard_map/transpose | solution.py:94
  629.2 25.3 gather_fusion.1
  654.5 25.6 broadcast_select_fusion
  700.5 14.2 slice_bitcast_fusion
  714.7 12.7 copy.100
  731.1 7.9 fusion.211
  751.0 20.3 all-gather.17.cloned.1.call-done
  771.3 7.3 fusion.123
  784.0 6.6 multiply_reduce_fusion.17
  798.3 12.9 copy.102
  811.2 20.0 all-gather.23.cloned.1.call-done
  843.1 26.1 all-gather.21.cloned.1.call-done
  869.2 7.1 fusion.122
  881.1 6.6 multiply_reduce_fusion.15
  889.1 39.3 %all-reduce = s32[3072]{0:T(1024)S(1)} all-reduce(s32[3072]{0:T(1024)S(1)} %fusion.163), channel_id=1, replica_groups=mesh['dp'=8,'rep'=4] {'dp','rep'}, use_global_device_ids=true, to_apply=%add | all-reduce | flops 3072 | bytes 24576
  931.5 19.2 all-gather.25.cloned.1.call-done
  950.7 16.1 while.48
  966.8 69.6 %all-gather.1 = f32[32,1,3072]{2,1,0:T(1,128)S(1)} all-gather(f32[1,1,3072]{2,1,0:T(1,128)S(1)} %reshape.1644), channel_id=1, replica_groups=mesh['dp'=8,'rep'=4] {'dp','rep'}, dimensions={0}, use_global_device_ids=true | all-gather | bytes 405504 | tf_op jit(solution)/shard_map/all_gather | solution.py:31
  1036.5 66.7 %all-gather.2 = f32[32,1,3072]{2,1,0:T(1,128)S(1)} all-gather(f32[1,1,3072]{2,1,0:T(1,128)S(1)} %reshape.1646), channel_id=1, replica_groups=mesh['dp'=8,'rep'=4] {'dp','rep'}, dimensions={0}, use_global_device_ids=true | all-gather | bytes 405504 | tf_op jit(solution)/shard_map/all_gather | solution.py:31
  1103.3 68.5 %all-gather.3 = f32[32,1,3072]{2,1,0:T(1,128)S(1)} all-gather(f32[1,1,3072]{2,1,0:T(1,128)S(1)} %reshape.1648), channel_id=1, replica_groups=mesh['dp'=8,'rep'=4] {'dp','rep'}, dimensions={0}, use_global_device_ids=true | all-gather | bytes 405504 | tf_op jit(solution)/shard_map/all_gather | solution.py:31
  1172.6 31.1 %while.47 = (s32[]{:T(128)}, f32[3072]{0:T(1024)S(1)}, f32[3072]{0:T(1024)S(1)}, f32[3072]{0:T(1024)S(1)}, f32[32,3072]{1,0:T(8,128)S(1)}, /*index=5*/f32[32,307...) while((s32[]{:T(128)}, f32[3072]{0:T(1024)S(1)}, f32[3072]{0:T(1024)S(1)}, ...), condition=%wide.region_20.21_spmd, body=%wide.region_19.20_spmd.sunk | while | flops 21509 | bytes 184471 | solution.py:36
  1204.4 46.3 %while.49 = (s32[]{:T(128)}, f32[1000,768]{1,0:T(8,128)}, f32[3,1024,768]{2,1,0:T(8,128)}, pred[3,1024]{1,0:T(4,128)(4,1)S(1)}, bf16[3,1024,768]{2,1,0:T(8,128)(...) while((s32[]{:T(128)}, f32[1000,768]{1,0:T(8,128)}, ...), condition=%wide.region_23.24_spmd.clone, body=%wide.region_22.23_spmd.clone.sunk | while | flops 4727297024 | bytes 36024832 | solution.py:455
  1228.5 6.4 select_add_fusion.2
  1250.7 133.0 %reduce-scatter.7.cloned.1.call-done = f32[96,768]{1,0:T(8,128)} async-done(((f32[3072,768]{1,0:T(8,128)}), f32[96,768]{1,0:T(8,128)}) %reduce-scatter.7.cloned.1.call-update) | async-done | bytes 294928 | tf_op jit(solution)/shard_map/reduce_scatter | solution.py:460
  1386.2 7.5 fusion.107
  1400.2 7.8 fusion.216
  1408.0 34.7 %fusion.95 = bf16[12,64,1024]{2,1,0:T(8,128)(2,1)} fusion(f32[12,256,1024]{2,1,0:T(8,128)} %fusion.216, f32[12,256,1024]{2,1,0:T(8,128)} %copy-done.1, f32[12,256]{1,0:T(8,128)S(1)} %log_add_fusion, pred[256,1024]{1,0:T(8,128)(4,1)S(1)} %copy-done.32, bf16[256,12,32]{0,2,1:T(8,128)(2,1)S(1)} %get-tuple-element.467, ...), kind=kOutput, calls=%fused_computation.134 | convolution fusion | flops 438833152 | bytes 27406336 | tf_op jit(solution)/shard_map/bhqk,bqhd->bkhd/dot_general | solution.py:269
  1442.8 7.9 fusion.92
  1451.5 29.2 fusion.110
  1484.3 30.2 %reduce-scatter.11.cloned.1.call-done = bf16[1,256,768]{1,2,0:T(8,128)(2,1)} async-done(((bf16[1,1024,768]{1,2,0:T(8,128)(2,1)}), bf16[1,256,768]{1,2,0:T(8,128)(2,1)}) %reduce-scatter.11.cloned.1.call-update) | async-done | bytes 393232 | tf_op jit(solution)/shard_map/reduce_scatter | solution.py:277
  1518.3 7.1 fusion.108
  1531.7 6.4 fusion.217
  1538.1 34.7 %fusion.98 = bf16[12,64,1024]{2,1,0:T(8,128)(2,1)} fusion(f32[12,256,1024]{2,1,0:T(8,128)} %fusion.217, f32[12,256,1024]{2,1,0:T(8,128)} %copy-done, f32[12,256]{1,0:T(8,128)S(1)} %copy-done.88, pred[256,1024]{1,0:T(8,128)(4,1)S(1)} %copy-done.33, bf16[256,12,32]{0,2,1:T(8,128)(2,1)S(1)} %copy-done.64, bf16[256,12,32]{0,2,1:T(8,128)(2,1)S(1)} %copy-done.62), kind=kOutput, calls=%fused_computation.135 | convolution fusion | flops 438833152 | bytes 27406336 | tf_op jit(solution)/shard_map/bhqk,bqhd->bkhd/dot_general | solution.py:269
  1572.9 7.9 fusion.89
  1580.9 28.4 fusion.113
  1611.9 32.5 %reduce-scatter.15.cloned.1.call-done = bf16[1,256,768]{1,2,0:T(8,128)(2,1)} async-done(((bf16[1,1024,768]{1,2,0:T(8,128)(2,1)}), bf16[1,256,768]{1,2,0:T(8,128)(2,1)}) %reduce-scatter.15.cloned.1.call-update) | async-done | bytes 393232 | tf_op jit(solution)/shard_map/reduce_scatter | solution.py:277
  1685.8 8.1 bitcast_dynamic-update-slice_fusion.2
  1705.2 8.0 bitcast_dynamic-update-slice_fusion.1
  1718.3 35.9 %broadcast_in_dim.222 = f32[48,768,768]{2,1,0:T(8,128)} broadcast(f32[]{:T(128)} %constant.193.clone.1), dimensions={} | broadcast | bytes 113246208 | tf_op jit(solution)/shard_map/broadcast_in_dim | solution.py:102
  1754.2 126.6 %scatter_fusion = f32[48,768,768]{2,1,0:T(8,128)} fusion(f32[48,768,768]{2,1,0:T(8,128)} %broadcast_in_dim.222, s32[32]{0:T(128)S(1)} %copy-done.107, f32[32,768,768]{2,1,0:T(8,128)} %convolution_dynamic-update-slice_fusion), kind=kCustom, calls=%fused_computation.2 | custom fusion | bytes 226492544 | tf_op jit(solution)/shard_map/scatter | solution.py:104
  1880.8 73.6 %copy.113 = f32[8,4,6,192,768]{4,3,2,1,0:T(8,128)} copy(f32[8,4,6,192,768]{4,3,1,2,0:T(8,128)} %bitcast.138) | data formatting | bytes 226492416 | tf_op jit(solution)/shard_map/transpose | solution.py:106
  1955.4 66.2 %all-gather = s32[1,8192]{1,0:T(1,128)S(1)} all-gather(s32[1,256]{1,0:T(1,128)S(1)} %copy-done.96), channel_id=2, replica_groups=mesh['dp'=8,'rep'=4] {'dp','rep'}, dimensions={1}, use_global_device_ids=true | all-gather | bytes 33792 | tf_op jit(solution)/shard_map/all_gather | solution.py:486
  2024.5 59.8 %scatter_custom_fusion.1 = f32[1001,768]{1,0:T(8,128)S(1)} fusion(s32[8192]{0:T(1024)S(1)} %and_select_fusion, bf16[8192,768]{1,0:T(8,128)(2,1)} %all-gather.27.cloned.1.call-done, f32[]{:T(128)} %constant.193.clone.1), kind=kCustom, calls=%fused_computation.34 | custom fusion | flops 12582912 | bytes 15657988 | tf_op jit(solution)/shard_map/scatter-add | solution.py:490
  2085.7 776.9 %reduce-scatter.17.cloned.1.call-done = f32[6,192,768]{2,1,0:T(8,128)} async-done(((f32[192,192,768]{2,1,0:T(8,128)}), f32[6,192,768]{2,1,0:T(8,128)}) %reduce-scatter.17.cloned.1.call-update) | async-done | bytes 3538960 | tf_op jit(solution)/shard_map/reduce_scatter | solution.py:498
  2868.8 40.0 %all-reduce.1 = (f32[]{:T(128)}, f32[5,768]{1,0:T(8,128)S(1)}) all-reduce(f32[]{:T(128)S(6)} %add.403, f32[5,768]{1,0:T(8,128)S(1)} %concatenate.137), channel_id=1, replica_groups=mesh['dp'=8,'rep'=4] {'dp','rep'}, use_global_device_ids=true, to_apply=%region_42.43 | all-reduce | flops 3841 | bytes 30728 | tf_op jit(solution)/shard_map/psum | solution.py:505
  2911.4 8.8 fusion.205
  (611 shorter events, 278.5 us)
Async XLA Ops:
  7.2 276.7 %all-gather.13.cloned.1.call-start = ((), (), s32[]{:S(2)}) async-start(), calls=%async_computation.6 | async-start | bytes 50688000 | tf_op jit(solution)/shard_map/all_gather | solution.py:351
  10.6 581.0 %all-gather.15.cloned.1.call-start = ((), (), s32[]{:S(2)}) async-start(), calls=%async_computation.7 | async-start | bytes 58392576 | tf_op jit(solution)/shard_map/all_gather | solution.py:348
  12.1 726.9 %all-gather.19.cloned.1.call-start = ((), (), s32[]{:S(2)}) async-start(), calls=%async_computation.9 | async-start | bytes 1966080 | tf_op jit(solution)/shard_map/all_gather | solution.py:151
  12.9 616.3 %copy-start.98 = (pred[256]{0:T(512)(128)(4,1)}, pred[256]{0:T(512)(128)(4,1)S(1)}, u32[]{:S(2)}) copy-start(pred[256]{0:T(512)(128)(4,1)S(1)} %and_reduce_fusion) | copy-start | bytes 772
  14.5 676.9 %copy-start.78 = (f32[768]{0:T(1024)}, f32[768]{0:T(1024)S(1)}, u32[]{:S(2)}) copy-start(f32[768]{0:T(1024)S(1)} %get-tuple-element.363) | copy-start | bytes 9220
  14.5 766.7 %copy-start.68 = (f32[768]{0:T(1024)}, f32[768]{0:T(1024)S(1)}, u32[]{:S(2)}) copy-start(f32[768]{0:T(1024)S(1)} %get-tuple-element.362) | copy-start | bytes 9220
  14.5 776.7 %copy-start.72 = (f32[768]{0:T(1024)}, f32[768]{0:T(1024)S(1)}, u32[]{:S(2)}) copy-start(f32[768]{0:T(1024)S(1)} %get-tuple-element.361) | copy-start | bytes 9220
  14.5 614.7 %copy-start.102 = (pred[256]{0:T(512)(128)(4,1)}, pred[256]{0:T(512)(128)(4,1)S(1)}, u32[]{:S(2)}) copy-start(pred[256]{0:T(512)(128)(4,1)S(1)} %compare_and_fusion.2) | copy-start | bytes 772
  287.1 342.1 %copy-start.34 = (bf16[256,768]{1,0:T(8,128)(2,1)}, bf16[256,768]{1,0:T(8,128)(2,1)S(1)}, u32[]{:S(2)}) copy-start(bf16[256,768]{1,0:T(8,128)(2,1)S(1)} %gather_fusion) | copy-start | bytes 1179652
  288.0 403.4 %copy-start.92 = (f32[256]{0:T(256)}, f32[256]{0:T(256)S(1)}, u32[]{:S(2)}) copy-start(f32[256]{0:T(256)S(1)} %get-tuple-element.485) | copy-start | bytes 3076
  697.2 74.0 %all-gather.17.cloned.1.call-start = ((), (), s32[]{:S(2)}) async-start(), calls=%async_computation.8 | async-start | bytes 1966080 | tf_op jit(solution)/shard_map/all_gather | solution.py:152
  700.3 131.0 %all-gather.23.cloned.1.call-start = ((), (), s32[]{:S(2)}) async-start(), calls=%async_computation.11 | async-start | bytes 1966080 | tf_op jit(solution)/shard_map/all_gather | solution.py:151
  747.3 33.9 %slice-start = ((s8[9437184]{0:T(1024)(128)(4,1)}), s8[1048576]{0:T(1024)(128)(4,1)S(1)}, s32[]{:S(2)}) async-start(s8[9437184]{0:T(1024)(128)(4,1)} %bitcast.358), calls=%async_computation.20 | async-start | bytes 2097152
  790.6 85.7 %copy-start.19 = (f32[256,768]{1,0:T(8,128)}, f32[256,768]{1,0:T(8,128)S(1)}, u32[]{:S(2)}) copy-start(f32[256,768]{1,0:T(8,128)S(1)} %get-tuple-element.499) | copy-start | bytes 2359300
  795.1 74.1 %all-gather.21.cloned.1.call-start = ((), (), s32[]{:S(2)}) async-start(), calls=%async_computation.10 | async-start | bytes 1966080 | tf_op jit(solution)/shard_map/all_gather | solution.py:152
  797.2 153.5 %all-gather.25.cloned.1.call-start = ((), (), s32[]{:S(2)}) async-start(), calls=%async_computation.12 | async-start | bytes 4866048 | tf_op jit(solution)/shard_map/all_gather | solution.py:401
  839.5 38.9 %slice-start.6 = ((s8[9437184]{0:T(1024)(128)(4,1)}), s8[1048576]{0:T(1024)(128)(4,1)S(1)}, s32[]{:S(2)}) async-start(s8[9437184]{0:T(1024)(128)(4,1)} %bitcast.364), calls=%async_computation.26 | async-start | bytes 2097152
  878.3 518.8 %copy-start.7 = (f32[256,768]{1,0:T(8,128)}, f32[256,768]{1,0:T(8,128)S(1)}, u32[]{:S(2)}) copy-start(f32[256,768]{1,0:T(8,128)S(1)} %get-tuple-element.503) | copy-start | bytes 2359300
  878.3 518.8 %copy-start.83 = (f32[256]{0:T(256)}, f32[256]{0:T(256)S(1)}, u32[]{:S(2)}) copy-start(f32[256]{0:T(256)S(1)} %get-tuple-element.491) | copy-start | bytes 3076
  888.7 495.0 %reduce-scatter.7.cloned.1.call-start = ((), (), s32[]{:S(2)}) async-start(), calls=%async_computation.13 | async-start | bytes 9732096 | tf_op jit(solution)/shard_map/reduce_scatter | solution.py:460
  1250.6 143.0 %slice-start.9 = ((s8[9437184]{0:T(1024)(128)(4,1)}), s8[1048576]{0:T(1024)(128)(4,1)S(1)}, s32[]{:S(2)}) async-start(s8[9437184]{0:T(1024)(128)(4,1)} %bitcast.367), calls=%async_computation.29 | async-start | bytes 2097152
  1250.7 230.1 %reduce-scatter.9.cloned.1.call-start = ((), (), s32[]{:S(2)}) async-start(), calls=%async_computation.14 | async-start | bytes 1966080 | tf_op jit(solution)/shard_map/reduce_scatter | solution.py:271
  1442.8 71.7 %reduce-scatter.11.cloned.1.call-start = ((), (), s32[]{:S(2)}) async-start(), calls=%async_computation.15 | async-start | bytes 1966080 | tf_op jit(solution)/shard_map/reduce_scatter | solution.py:277
  1450.8 158.6 %reduce-scatter.13.cloned.1.call-start = ((), (), s32[]{:S(2)}) async-start(), calls=%async_computation.16 | async-start | bytes 1966080 | tf_op jit(solution)/shard_map/reduce_scatter | solution.py:271
  1480.7 33.8 %copy-start.73 = (f32[768]{0:T(1024)S(1)}, f32[768]{0:T(1024)}, u32[]{:S(2)}) copy-start(f32[768]{0:T(1024)} %copy-done.72) | copy-start | bytes 9220
  1480.7 33.8 %copy-start.90 = (f32[256]{0:T(256)S(1)}, f32[256]{0:T(256)}, u32[]{:S(2)}) copy-start(f32[256]{0:T(256)} %copy-done.89) | copy-start | bytes 3076
  1529.2 119.3 %copy-start.17 = (f32[256,768]{1,0:T(8,128)}, f32[256,768]{1,0:T(8,128)S(1)}, u32[]{:S(2)}) copy-start(f32[256,768]{1,0:T(8,128)S(1)} %subtract_add_fusion) | copy-start | bytes 2359300
  1572.9 71.6 %reduce-scatter.15.cloned.1.call-start = ((), (), s32[]{:S(2)}) async-start(), calls=%async_computation.17 | async-start | bytes 1966080 | tf_op jit(solution)/shard_map/reduce_scatter | solution.py:277
  1580.9 443.6 %all-gather.27.cloned.1.call-start = ((), (), s32[]{:S(2)}) async-start(), calls=%async_computation.19 | async-start | bytes 12976128 | tf_op jit(solution)/shard_map/all_gather | solution.py:487
  1609.3 35.1 %copy-start.36 = (bf16[256,768]{1,0:T(8,128)(2,1)S(1)}, bf16[256,768]{1,0:T(8,128)(2,1)}, u32[]{:S(2)}) copy-start(bf16[256,768]{1,0:T(8,128)(2,1)} %copy-done.34) | copy-start | bytes 1179652
  1609.3 35.1 %copy-start.79 = (f32[768]{0:T(1024)S(1)}, f32[768]{0:T(1024)}, u32[]{:S(2)}) copy-start(f32[768]{0:T(1024)} %copy-done.78) | copy-start | bytes 9220
  1609.3 35.1 %copy-start.93 = (f32[256]{0:T(256)S(1)}, f32[256]{0:T(256)}, u32[]{:S(2)}) copy-start(f32[256]{0:T(256)} %copy-done.92) | copy-start | bytes 3076
  1609.3 35.1 %copy-start.100 = (pred[256]{0:T(512)(128)(4,1)S(1)}, pred[256]{0:T(512)(128)(4,1)}, u32[]{:S(2)}) copy-start(pred[256]{0:T(512)(128)(4,1)} %copy-done.98) | copy-start | bytes 772
  1609.3 35.1 %copy-start.104 = (pred[256]{0:T(512)(128)(4,1)S(1)}, pred[256]{0:T(512)(128)(4,1)}, u32[]{:S(2)}) copy-start(pred[256]{0:T(512)(128)(4,1)} %copy-done.102) | copy-start | bytes 772
  1611.9 36.6 %copy-start.43 = (bf16[1,256,12,64]{1,3,2,0:T(8,128)(2,1)}, bf16[1,256,12,64]{1,3,2,0:T(8,128)(2,1)S(1)}, u32[]{:S(2)}) copy-start(bf16[1,256,12,64]{1,3,2,0:T(8,128)(2,1)S(1)} %pad_maximum_fusion.12) | copy-start | bytes 1179652
  1611.9 36.6 %copy-start.44 = (bf16[1,256,12,64]{1,3,2,0:T(8,128)(2,1)}, bf16[1,256,12,64]{1,3,2,0:T(8,128)(2,1)S(1)}, u32[]{:S(2)}) copy-start(bf16[1,256,12,64]{1,3,2,0:T(8,128)(2,1)S(1)} %pad_maximum_fusion.13) | copy-start | bytes 1179652
  1649.6 1213.0 %reduce-scatter.17.cloned.1.call-start = ((), (), s32[]{:S(2)}) async-start(), calls=%async_computation.18 | async-start | bytes 116785152 | tf_op jit(solution)/shard_map/reduce_scatter | solution.py:498
  1718.3 35.9 %copy-start.107 = (s32[32]{0:T(128)S(1)}, s32[32]{0:T(128)}, u32[]{:S(2)}) copy-start(s32[32]{0:T(128)} %copy-done.106) | copy-start | bytes 388
  1954.4 67.1 %copy-start.118 = (s32[32]{0:T(128)S(1)}, s32[32]{0:T(128)}, u32[]{:S(2)}) copy-start(s32[32]{0:T(128)} %param.28) | copy-start | bytes 388
  1954.4 68.5 %copy-start.22 = (f32[1000,768]{1,0:T(8,128)S(1)}, f32[1000,768]{1,0:T(8,128)}, u32[]{:S(2)}) copy-start(f32[1000,768]{1,0:T(8,128)} %get-tuple-element.294) | copy-start | bytes 9216004
  1954.4 69.9 %copy-start.111 = (f32[768]{0:T(1024)S(1)}, f32[768]{0:T(1024)}, u32[]{:S(2)}) copy-start(f32[768]{0:T(1024)} %get-tuple-element.351) | copy-start | bytes 9220
  1954.4 69.9 %copy-start.87 = (f32[768]{0:T(1024)S(1)}, f32[768]{0:T(1024)}, u32[]{:S(2)}) copy-start(f32[768]{0:T(1024)} %get-tuple-element.349) | copy-start | bytes 9220
  1954.5 69.9 %copy-start.113 = (f32[768]{0:T(1024)S(1)}, f32[768]{0:T(1024)}, u32[]{:S(2)}) copy-start(f32[768]{0:T(1024)} %get-tuple-element.355) | copy-start | bytes 9220
  1954.5 69.9 %copy-start.112 = (f32[768]{0:T(1024)S(1)}, f32[768]{0:T(1024)}, u32[]{:S(2)}) copy-start(f32[768]{0:T(1024)} %get-tuple-element.353) | copy-start | bytes 9220
  1954.5 69.9 %copy-start.114 = (f32[768]{0:T(1024)S(1)}, f32[768]{0:T(1024)}, u32[]{:S(2)}) copy-start(f32[768]{0:T(1024)} %get-tuple-element.357) | copy-start | bytes 9220
  2084.3 826.4 %copy-start.77 = (f32[5,768]{1,0:T(8,128)S(1)}, f32[5,768]{1,0:T(8,128)}, u32[]{:S(2)}) copy-start(f32[5,768]{1,0:T(8,128)} %param.39) | copy-start | bytes 46084
  2084.3 826.4 %copy-start.85 = (f32[5,768]{1,0:T(8,128)S(1)}, f32[5,768]{1,0:T(8,128)}, u32[]{:S(2)}) copy-start(f32[5,768]{1,0:T(8,128)} %param.41) | copy-start | bytes 46084
  2084.3 826.4 %copy-start.86 = (f32[5,768]{1,0:T(8,128)S(1)}, f32[5,768]{1,0:T(8,128)}, u32[]{:S(2)}) copy-start(f32[5,768]{1,0:T(8,128)} %param.40) | copy-start | bytes 46084
  (102 other events, 675.2 us)
Sparse Core Ops, SparseCore 0:
  11.4 272.4 all-gather.12
  287.3 304.2 all-gather.14
  697.4 35.8 all-gather.18
  735.3 35.9 all-gather.16
  795.2 35.9 all-gather.22
  833.2 35.9 all-gather.20
  888.8 61.8 all-gather.24
  1250.8 132.8 reduce-scatter.6
  1442.9 34.4 reduce-scatter.8
  1480.2 34.2 reduce-scatter.10
  1573.0 34.2 reduce-scatter.12
  1610.1 34.2 reduce-scatter.14
  1649.7 95.0 all-gather.26
  1954.6 907.9 reduce-scatter.16
where the time goes:
time: 2960 us; the launch traced here: 2950 us
  waiting for transfers between devices  1630 us (55%)
  local copies, waits for them, and re-layouts  436 us (15%)
  blocking collectives  350 us (12%)
  matrix products  334 us (11%)
  other arithmetic  171 us (6%)
    reduce_scatter x1, waiting for transfers between devices, shards(): lax.psum_scatter(grid, ('dp', 'rep'), scatter_dimension=0, tiled=True)  777 us
    all_gather x1, waiting for transfers between devices, shards(): lax.all_gather(tile_weight.astype(jnp.bfloat16), ('dp', 'rep'), axis=0, t...  304 us
    all_gather x1, waiting for transfers between devices, shards(): lax.all_gather(table_weight.astype(jnp.bfloat16), ('dp', 'rep'), axis=0,...  269 us
    all_gather x3, blocking collectives, joined(): gathered = jax.tree.map(lambda a: lax.all_gather(a, axis), part)  205 us
    reduce_scatter x1, waiting for transfers between devices, shards(): lax.psum_scatter(rows_grad.reshape(slot_total, D), ('dp', 'rep'), scatter...  133 us
    scatter x1, local copies, waits for them, and re-layouts, to_owners(): grid = jnp.zeros((dp_size * slots_cap,) + tiles.shape[1:], tiles.dtype).a...  127 us
    transpose x1, local copies, waits for them, and re-layouts, to_owners(): grid.reshape(dp_size, slots_cap, rep_size, -1, width)  73.6 us
    dot_general x2, matrix products, layer_backward(): jnp.einsum('bhqk,bqhd->bkhd', score_grad, query, preferred_element_type=j...  69.4 us
  transfers between devices with their start and end apart: 14, of which 10 were waited for; matrix products, arithmetic and copies ran while one was open for 18% of the time, Pallas kernels for 0%

commit v1 on v0

v1 whole, which is shorter than its diff:
```python
import jax
import jax.numpy as jnp
from jax import lax
from jax.sharding import Mesh, PartitionSpec as P

D = 768
HEADS = 12
HD = 64
FF = 3072
LAYERS = 2


EPS_NORM = 1e-05
EPS_ADAM = 1e-08
CLIP_NORM = 0.005
BETA_FIRST = 0.5
BETA_SECOND = 0.5
DECAY = 0.1
RATE_TILE = 0.02
RATE_HEAD = 0.05
RATE_TABLE = 0.5
RATE_GAIN = 0.3
MASKED = -1e30


def root_norm(training_state, gain):
    return (
        training_state
        * lax.rsqrt(jnp.mean(training_state * training_state, axis=-1, keepdims=True) + EPS_NORM)
        * gain
    )


def norm_back(training_state, gain, grad):
    scale = lax.rsqrt(jnp.mean(training_state * training_state, axis=-1, keepdims=True) + EPS_NORM)
    scaled = grad * gain
    state_grad = scale * scaled - training_state * scale**3 * jnp.mean(
        scaled * training_state, axis=-1, keepdims=True
    )
    gain_grad = jnp.sum(
        (grad * training_state * scale).reshape(-1, training_state.shape[-1]), axis=0
    )
    return (state_grad, gain_grad)


def rope_tables(places, width):
    half = width // 2
    freqs = jnp.power(10000.0, -2.0 * jnp.arange(half).astype(jnp.float32) / width)
    angle = places[:, None] * freqs[None, :]
    return (jnp.cos(angle), jnp.sin(angle))


def rotate(field, cosine, sine):
    half = field.shape[-1] // 2
    first, second = (field[..., :half], field[..., half:])
    cosine, sine = (cosine[:, None, :], sine[:, None, :])
    return jnp.concatenate(
        [first * cosine - second * sine, second * cosine + first * sine], axis=-1
    )


def rotate_back(field, cosine, sine):
    half = field.shape[-1] // 2
    first, second = (field[..., :half], field[..., half:])
    cosine, sine = (cosine[:, None, :], sine[:, None, :])
    return jnp.concatenate(
        [first * cosine + second * sine, second * cosine - first * sine], axis=-1
    )


def tile_slots(owners):
    order = jnp.arange(owners.shape[0], dtype=jnp.int32)
    same = (owners[:, None] == owners[None, :]) & (order[None, :] < order[:, None])
    return jnp.sum(same.astype(jnp.int32), axis=1)


def adam(weight, first, second, grad, factor, rate, decay, steps):
    grad = grad * factor
    first = BETA_FIRST * first + (1.0 - BETA_FIRST) * grad
    second = BETA_SECOND * second + (1.0 - BETA_SECOND) * grad * grad
    first_hat = first / (1.0 - jnp.power(BETA_FIRST, steps))
    second_hat = second / (1.0 - jnp.power(BETA_SECOND, steps))
    weight = weight - rate * (first_hat / (jnp.sqrt(second_hat) + EPS_ADAM) + decay * weight)
    return (weight, first, second)


ALL = ("a", "b", "rep")
DP = ("a", "b")
UNITS = FF // D
TILES_PER = 4 + 3 * UNITS


def mm(x, w):
    return jnp.einsum("ld,de->le", x, w, preferred_element_type=jnp.float32)


def mm_t(x, w):
    return jnp.einsum("le,de->ld", x, w, preferred_element_type=jnp.float32)


def mm_g(x, y):
    return jnp.einsum("ld,le->de", x, y, preferred_element_type=jnp.float32)


def heads(x):
    return x.reshape(x.shape[0], HEADS, HD)


def layer_forward(state, tiles, gain_pair, cosine, sine, allowed):
    rows = state.shape[0]
    normed = root_norm(state, gain_pair[0]).astype(jnp.bfloat16)
    query, keys, value = [mm(normed, tiles[i]) for i in range(3)]
    query = rotate(heads(query), cosine, sine).astype(jnp.bfloat16)
    keys = rotate(heads(keys), cosine, sine).astype(jnp.bfloat16).reshape(rows, D)
    both = jnp.concatenate([keys, value.astype(jnp.bfloat16)], axis=1)
    both = lax.all_gather(both, "b", axis=0, tiled=True)
    keys_all, value_all = heads(both[:, :D]), heads(both[:, D:])
    scores = jnp.einsum("qhd,khd->hqk", query, keys_all, preferred_element_type=jnp.float32) * HD ** (
        -0.5
    )
    scores = jnp.where(allowed, scores, MASKED)
    top = jnp.max(scores, axis=-1, keepdims=True)
    exponent = jnp.exp(scores - top)
    total = jnp.sum(exponent, axis=-1, keepdims=True)
    prob = (exponent / total).astype(jnp.bfloat16)
    log_total = top + jnp.log(total)
    attended = jnp.einsum("hqk,khd->qhd", prob, value_all, preferred_element_type=jnp.float32)
    attended = attended.reshape(rows, D).astype(jnp.bfloat16)
    middle = state + mm(attended, tiles[3])
    normed_feed = root_norm(middle, gain_pair[1]).astype(jnp.bfloat16)
    gates = [mm(normed_feed, tiles[4 + i]) for i in range(UNITS)]
    ups = [mm(normed_feed, tiles[4 + UNITS + i]) for i in range(UNITS)]
    hidden = [(jax.nn.silu(g) * u).astype(jnp.bfloat16) for g, u in zip(gates, ups)]
    output = middle + sum(mm(h, tiles[4 + 2 * UNITS + i]) for i, h in enumerate(hidden))
    return output, (
        state,
        middle,
        normed,
        normed_feed,
        query,
        keys_all,
        value_all,
        log_total,
        attended,
        gates,
        ups,
        hidden,
    )


def layer_backward(grad, kept, tiles, gain_pair, cosine, sine, allowed):
    (
        state,
        middle,
        normed,
        normed_feed,
        query,
        keys_all,
        value_all,
        log_total,
        attended,
        gates,
        ups,
        hidden,
    ) = kept
    rows = state.shape[0]
    branch = grad.astype(jnp.bfloat16)
    down_grads, gate_grads, up_grads = [], [], []
    feed_back = 0.0
    for i in range(UNITS):
        down_grads.append(mm_g(hidden[i], branch))
        hidden_grad = mm_t(branch, tiles[4 + 2 * UNITS + i])
        sigma = jax.nn.sigmoid(gates[i])
        gate_back = (hidden_grad * ups[i] * sigma * (1.0 + gates[i] * (1.0 - sigma))).astype(
            jnp.bfloat16
        )
        up_back = (hidden_grad * gates[i] * sigma).astype(jnp.bfloat16)
        gate_grads.append(mm_g(normed_feed, gate_back))
        up_grads.append(mm_g(normed_feed, up_back))
        feed_back = (
            feed_back + mm_t(gate_back, tiles[4 + i]) + mm_t(up_back, tiles[4 + UNITS + i])
        )
    back, feed_gain = norm_back(middle, gain_pair[1], feed_back)
    middle_grad = grad + back
    branch = middle_grad.astype(jnp.bfloat16)
    out_grad = mm_g(attended, branch)
    heads_grad = heads(mm_t(branch, tiles[3]).astype(jnp.bfloat16))
    scores = jnp.einsum("qhd,khd->hqk", query, keys_all, preferred_element_type=jnp.float32) * HD ** (
        -0.5
    )
    prob = jnp.exp(jnp.where(allowed, scores, MASKED) - log_total)
    value_part = jnp.einsum(
        "hqk,qhd->khd", prob.astype(jnp.bfloat16), heads_grad, preferred_element_type=jnp.float32
    )
    prob_grad = jnp.einsum("qhd,khd->hqk", heads_grad, value_all, preferred_element_type=jnp.float32)
    score_grad = (
        prob * (prob_grad - jnp.sum(prob * prob_grad, axis=-1, keepdims=True)) * HD ** (-0.5)
    ).astype(jnp.bfloat16)
    query_grad = jnp.einsum("hqk,khd->qhd", score_grad, keys_all, preferred_element_type=jnp.float32)
    keys_part = jnp.einsum("hqk,qhd->khd", score_grad, query, preferred_element_type=jnp.float32)
    length = keys_part.shape[0]
    both = jnp.concatenate([keys_part.reshape(length, D), value_part.reshape(length, D)], axis=1)
    both = lax.psum_scatter(both.astype(jnp.bfloat16), "b", scatter_dimension=0, tiled=True)
    keys_grad, value_grad = both[:, :D].astype(jnp.float32), both[:, D:]
    parts = [
        rotate_back(query_grad, cosine, sine).reshape(rows, D).astype(jnp.bfloat16),
        rotate_back(heads(keys_grad), cosine, sine).reshape(rows, D).astype(jnp.bfloat16),
        value_grad,
    ]
    input_grads = [mm_g(normed, p) for p in parts]
    back, attend_gain = norm_back(
        state, gain_pair[0], sum(mm_t(p, tiles[i]) for i, p in enumerate(parts))
    )
    tiles_grad = jnp.stack(
        [
            t.astype(jnp.bfloat16)
            for t in input_grads + [out_grad] + gate_grads + up_grads + down_grads
        ]
    )
    return middle_grad + back, tiles_grad, [attend_gain, feed_gain]


def shards(
    tokens,
    segments,
    completion,
    targets,
    owners,
    step_count,
    tile_weight,
    tile_first,
    tile_second,
    table_weight,
    table_first,
    table_second,
    head_weight,
    head_first,
    head_second,
    gain_weight,
    gain_first,
    gain_second,
):
    a_size, b_size, rep_size = [lax.axis_size(n) for n in ALL]
    a_index, b_index, rep_index = [lax.axis_index(n) for n in ALL]
    dp_size = a_size * b_size
    devices = dp_size * rep_size
    dp_index = a_index * b_size + b_index
    device = dp_index * rep_size + rep_index
    rows = tokens.shape[1]
    length = segments.shape[1]
    comp = completion.shape[1]
    slots_cap, tile_rows = tile_weight.shape[:2]
    tile_count = owners.shape[0]
    home_tiles = tile_count // dp_size
    vocab_rows = table_weight.shape[0]
    vocab_start = device * vocab_rows
    sequence = a_index * rep_size + rep_index

    own_part = jnp.concatenate(
        [
            tokens[0],
            lax.dynamic_slice_in_dim(segments[0], rep_index * rows, rows),
            lax.dynamic_slice_in_dim(completion[0], rep_index * (comp // rep_size), comp // rep_size),
            lax.dynamic_slice_in_dim(targets[0], rep_index * (comp // rep_size), comp // rep_size),
        ]
    )
    packed = lax.all_gather(own_part, ALL, axis=0, tiled=False).reshape(dp_size, rep_size, -1)
    tokens_all = packed[:, :, :rows].reshape(dp_size, length)
    segments_all = packed[:, :, rows : 2 * rows].reshape(dp_size, length)
    edge = 2 * rows + comp // rep_size
    completion_all = packed[:, :, 2 * rows : edge].reshape(dp_size, comp)
    targets_all = packed[:, :, edge:].reshape(dp_size, comp)

    slots = tile_slots(owners)
    mine = owners == dp_index
    tile_low = tile_weight.astype(jnp.bfloat16)
    placed = jnp.where(mine[:, None, None], jnp.take(tile_low, jnp.where(mine, slots, 0), axis=0), 0)
    home = lax.psum_scatter(placed, DP, scatter_dimension=0, tiled=True)
    spread = lax.all_gather(home, ALL, axis=0, tiled=True)
    spread = spread.reshape(dp_size, rep_size, home_tiles, tile_rows, D)
    tiles = spread.transpose(0, 2, 1, 3, 4).reshape(tile_count, D, D)

    order = tokens_all.reshape(a_size, rep_size, b_size, rows).transpose(0, 2, 1, 3).reshape(-1)
    place = order - vocab_start
    vocab_iota = jnp.arange(vocab_rows)
    token_hot = (place[:, None] == vocab_iota[None, :]).astype(jnp.bfloat16)
    picked = jnp.dot(
        token_hot, table_weight.astype(jnp.bfloat16), preferred_element_type=jnp.float32
    ).astype(jnp.bfloat16)
    state = lax.psum_scatter(picked, ALL, scatter_dimension=0, tiled=True).astype(jnp.float32)

    first_place = b_index * rows
    places = first_place + jnp.arange(rows)
    cosine, sine = rope_tables(places.astype(jnp.float32), HD)
    own_segments = lax.dynamic_index_in_dim(segments_all, sequence, 0, False)
    query_segments = lax.dynamic_slice_in_dim(own_segments, first_place, rows)
    allowed = (jnp.arange(length)[None, :] <= places[:, None]) & (
        query_segments[:, None] == own_segments[None, :]
    )
    allowed = allowed[None]
    kept_list = []
    for index in range(LAYERS):
        state, kept = layer_forward(
            state,
            tiles[index * TILES_PER : (index + 1) * TILES_PER],
            gain_weight[2 * index : 2 * index + 2],
            cosine,
            sine,
            allowed,
        )
        kept_list.append(kept)
    final_gain = gain_weight[2 * LAYERS]
    final = root_norm(state, final_gain).astype(jnp.bfloat16)

    capacity = 3 * comp // (2 * rep_size)
    block = completion_all // rows
    inside = block[:, None, :] == jnp.arange(b_size)[None, :, None]
    rank = jnp.cumsum(inside.astype(jnp.int32), axis=2) - 1
    slot_pick = inside[..., None] & (rank[..., None] == jnp.arange(capacity))
    filled = jnp.any(slot_pick, axis=2)
    wanted = jnp.where(
        filled, jnp.sum(jnp.where(slot_pick, targets_all[:, None, :, None], 0), axis=2), -1
    )
    spots = jnp.where(
        filled, jnp.sum(jnp.where(slot_pick, (completion_all % rows)[:, None, :, None], 0), axis=2), -1
    )
    all_wanted = (
        wanted.reshape(a_size, rep_size, b_size, capacity).transpose(0, 2, 1, 3).reshape(-1)
    )
    own_spots = lax.dynamic_index_in_dim(
        lax.dynamic_index_in_dim(spots, sequence, 0, False), b_index, 0, False
    )
    select = (own_spots[:, None] == jnp.arange(rows)[None, :]).astype(jnp.bfloat16)
    chosen = jnp.dot(select, final, preferred_element_type=jnp.float32).astype(jnp.bfloat16)
    all_rows = lax.all_gather(chosen, ALL, axis=0, tiled=True)
    head_low = head_weight.astype(jnp.bfloat16)
    logits = jnp.einsum("rd,vd->rv", all_rows, head_low, preferred_element_type=jnp.float32)
    hot = vocab_iota[None, :] == (all_wanted - vocab_start)[:, None]
    local_top = jnp.max(logits, axis=-1)
    local_total = jnp.sum(jnp.exp(logits - local_top[:, None]), axis=-1)
    local_hit = jnp.sum(jnp.where(hot, logits, 0.0), axis=-1)
    stats = lax.all_gather(
        jnp.stack([local_top, local_total, local_hit]), ALL, axis=0, tiled=False
    )
    top = jnp.max(stats[:, 0], axis=0)
    total = jnp.sum(stats[:, 1] * jnp.exp(stats[:, 0] - top[None]), axis=0)
    log_total = top + jnp.log(total)
    valid = all_wanted >= 0
    scored = dp_size * comp
    loss = jnp.sum(jnp.where(valid, log_total - jnp.sum(stats[:, 2], axis=0), 0.0)) / scored
    logit_grad = jnp.where(
        valid[:, None],
        (jnp.exp(logits - log_total[:, None]) - jnp.where(hot, 1.0, 0.0)) / scored,
        0.0,
    ).astype(jnp.bfloat16)
    rows_grad = jnp.dot(logit_grad, head_low, preferred_element_type=jnp.float32)
    own_rows = lax.psum_scatter(
        rows_grad.astype(jnp.bfloat16), ALL, scatter_dimension=0, tiled=True
    )
    head_grad = jnp.einsum("rv,rd->vd", logit_grad, all_rows, preferred_element_type=jnp.float32)
    final_grad = jnp.einsum("ct,cd->td", select, own_rows, preferred_element_type=jnp.float32)
    state_grad, final_gain_grad = norm_back(state, final_gain, final_grad)
    tile_parts = [None] * LAYERS
    gain_parts = [None] * LAYERS
    for index in reversed(range(LAYERS)):
        state_grad, tile_parts[index], gain_parts[index] = layer_backward(
            state_grad,
            kept_list[index],
            tiles[index * TILES_PER : (index + 1) * TILES_PER],
            gain_weight[2 * index : 2 * index + 2],
            cosine,
            sine,
            allowed,
        )
    piece_grads = lax.all_gather(state_grad.astype(jnp.bfloat16), ALL, axis=0, tiled=True)
    table_grad = jnp.einsum(
        "tv,td->vd", token_hot, piece_grads, preferred_element_type=jnp.float32
    )
    tile_grads = jnp.concatenate(tile_parts, axis=0).reshape(
        dp_size, home_tiles, rep_size, tile_rows, D
    )
    home_grad = lax.psum_scatter(
        tile_grads.transpose(0, 2, 1, 3, 4).reshape(-1, tile_rows, D),
        ALL,
        scatter_dimension=0,
        tiled=True,
    )
    plane_grad = lax.all_gather(home_grad, DP, axis=0, tiled=True)
    own_count = jnp.sum(mine.astype(jnp.int32))
    slot_ids = jnp.arange(slots_cap)
    tile_of_slot = jnp.sum(
        jnp.where(
            mine[None, :] & (slots[None, :] == slot_ids[:, None]), jnp.arange(tile_count)[None, :], 0
        ),
        axis=1,
    )
    slot_valid = (slot_ids < own_count)[:, None, None]
    own_grad = jnp.where(
        slot_valid, jnp.take(plane_grad, tile_of_slot, axis=0).astype(jnp.float32), 0.0
    )
    gain_grads = jnp.stack([g for pair in gain_parts for g in pair] + [final_gain_grad])
    square = (
        jnp.sum(own_grad * own_grad)
        + jnp.sum(table_grad * table_grad)
        + jnp.sum(head_grad * head_grad)
    )
    square, gain_grads = lax.psum((square, gain_grads), ALL)
    norm = jnp.sqrt(square + jnp.sum(gain_grads * gain_grads))
    factor = jnp.minimum(1.0, CLIP_NORM / norm)
    steps = step_count[0].astype(jnp.float32)
    tile_new, tile_first_new, tile_second_new = adam(
        tile_weight, tile_first, tile_second, own_grad, factor, RATE_TILE, DECAY, steps
    )
    tile_new = jnp.where(slot_valid, tile_new, 0.0)
    tile_first_new = jnp.where(slot_valid, tile_first_new, 0.0)
    tile_second_new = jnp.where(slot_valid, tile_second_new, 0.0)
    table_new, table_first_new, table_second_new = adam(
        table_weight, table_first, table_second, table_grad, factor, RATE_TABLE, DECAY, steps
    )
    head_new, head_first_new, head_second_new = adam(
        head_weight, head_first, head_second, head_grad, factor, RATE_HEAD, DECAY, steps
    )
    gain_new, gain_first_new, gain_second_new = adam(
        gain_weight, gain_first, gain_second, gain_grads, factor, RATE_GAIN, 0.0, steps
    )
    return (
        loss,
        norm,
        tile_new,
        tile_new.astype(jnp.bfloat16),
        tile_first_new,
        tile_second_new,
        table_new,
        table_new.astype(jnp.bfloat16),
        table_first_new,
        table_second_new,
        head_new,
        head_new.astype(jnp.bfloat16),
        head_first_new,
        head_second_new,
        gain_new,
        gain_first_new,
        gain_second_new,
    )


def solution(mesh):
    dp_size, rep_size = mesh.shape["dp"], mesh.shape["rep"]
    split = Mesh(mesh.devices.reshape(dp_size // rep_size, rep_size, rep_size), ALL)
    return jax.shard_map(
        shards,
        mesh=split,
        in_specs=(
            P(("a", "b"), "rep"),
            P(("a", "b"), None),
            P(("a", "b"), None),
            P(("a", "b"), None),
            P(),
            P(),
            P(("a", "b", "rep"), None, None),
            P(("a", "b", "rep"), None, None),
            P(("a", "b", "rep"), None, None),
            P(("a", "b", "rep"), None),
            P(("a", "b", "rep"), None),
            P(("a", "b", "rep"), None),
            P(("a", "b", "rep"), None),
            P(("a", "b", "rep"), None),
            P(("a", "b", "rep"), None),
            P(),
            P(),
            P(),
        ),
        out_specs=(
            P(),
            P(),
            P(("a", "b", "rep"), None, None),
            P(("a", "b", "rep"), None, None),
            P(("a", "b", "rep"), None, None),
            P(("a", "b", "rep"), None, None),
            P(("a", "b", "rep"), None),
            P(("a", "b", "rep"), None),
            P(("a", "b", "rep"), None),
            P(("a", "b", "rep"), None),
            P(("a", "b", "rep"), None),
            P(("a", "b", "rep"), None),
            P(("a", "b", "rep"), None),
            P(("a", "b", "rep"), None),
            P(),
            P(),
            P(),
        ),
        check_vma=False,
    )
```

time: 2960 us -> 1840 us (0.62)
  waiting for transfers between devices: 1630 us -> 1090 us
  local copies, waits for them, and re-layouts: 436 us -> 141 us
  blocking collectives: 350 us -> 112 us
  other arithmetic: 171 us -> 85.7 us
  matrix products: 334 us -> 384 us
    reduce_scatter x6, waiting for transfers between devices: 973 us -> 607 us  [the longest x1 341 us: shards(): lax.psum_scatter(tile_grads.transpose(0, 2, 1, 3, 4).reshape(-1, tile_row...]
    all_gather x4 -> x1, blocking collectives: 271 us -> 71.4 us  [shards(): lax.all_gather(own_part, ALL, axis=0, tiled=False)]
    all_gather x8 -> x7, waiting for transfers between devices: 658 us -> 477 us  [the longest x1 215 us: shards(): spread = lax.all_gather(home, ALL, axis=0, tiled=True)]
    transpose x8 -> x0, local copies, waits for them, and re-layouts: 166 us -> none  [the longest x1 73.6 us: to_owners(): grid.reshape(dp_size, slots_cap, rep_size, -1, width)]
    scatter x1 -> x0, local copies, waits for them, and re-layouts: 127 us -> none  [to_owners(): grid = jnp.zeros((dp_size * slots_cap,) + tiles.shape[1:], tiles.dtype).a...]
    scatter-add x1 -> x0, other arithmetic: 59.8 us -> none  [shards(): jax.ops.segment_sum(piece_grads.astype(jnp.float32), jnp.where(within, pl...]
    slice x4 -> x13, local copies, waits for them, and re-layouts: 12 us -> 63.9 us  [the longest x3 45.2 us: shards(): tiles[index * TILES_PER:(index + 1) * TILES_PER]]
    dot_general x51 -> x115, matrix products: 334 us -> 384 us  [the longest x2 69.5 us: layer_backward(): jnp.einsum('hqk,qhd->khd', score_grad, query, preferred_element_type=jnp....]
  transfers between devices with their start and end apart: 14 -> 13, of which waited for: 10 -> 12; matrix products, arithmetic and copies ran while one was open for 18% -> 8% of each run, Pallas kernels for 0% -> 0%
where the time goes in v1:
time: 1840 us; the launch traced here: 1830 us
  waiting for transfers between devices  1090 us (59%)
  matrix products  384 us (21%)
  local copies, waits for them, and re-layouts  141 us (8%)
  blocking collectives  112 us (6%)
  other arithmetic  85.7 us (5%)
  between operations  24.3 us (1%)
    reduce_scatter x1, waiting for transfers between devices, shards(): lax.psum_scatter(tile_grads.transpose(0, 2, 1, 3, 4).reshape(-1, tile_row...  341 us
    all_gather x1, waiting for transfers between devices, shards(): spread = lax.all_gather(home, ALL, axis=0, tiled=True)  215 us
    reduce_scatter x1, waiting for transfers between devices, shards(): lax.psum_scatter(picked, ALL, scatter_dimension=0, tiled=True)  151 us
    reduce_scatter x1, waiting for transfers between devices, shards(): lax.psum_scatter(rows_grad.astype(jnp.bfloat16), ALL, scatter_dimension=0...  104 us
    all_gather x1, waiting for transfers between devices, shards(): lax.all_gather(state_grad.astype(jnp.bfloat16), ALL, axis=0, tiled=True)  79.1 us
    all_gather x1, blocking collectives, shards(): lax.all_gather(own_part, ALL, axis=0, tiled=False)  71.4 us
    dot_general x2, matrix products, layer_backward(): jnp.einsum('hqk,qhd->khd', score_grad, query, preferred_element_type=jnp....  69.5 us
    dot_general x2, matrix products, layer_backward(): jnp.einsum('hqk,khd->qhd', score_grad, keys_all, preferred_element_type=j...  64.1 us
  transfers between devices with their start and end apart: 13, of which 12 were waited for; matrix products, arithmetic and copies ran while one was open for 8% of the time, Pallas kernels for 0%

profile of v1, /device:TPU:0, one launch (start us, length us, event | category | flops | bytes accessed | tf_op | source)
XLA Modules:
  0.0 1833.1 jit_solution(9074929124070509347)
XLA Ops:
  11.7 5.3 gather_fusion
  17.0 8.4 select_select_fusion
  26.3 71.4 %all-gather.2 = s32[32,1,640]{2,1,0:T(1,128)S(1)} all-gather(s32[1,1,640]{2,1,0:T(1,128)S(1)} %reshape.609), channel_id=2, replica_groups=mesh['a'=2,'b'=4,'rep'=4] {'a','b','rep'}, dimensions={0}, use_global_device_ids=true | all-gather | bytes 84480 | tf_op jit(solution)/shard_map/all_gather | solution.py:267
  98.0 17.5 fusion.6
  116.7 151.0 %reduce-scatter.7.cloned.1.call-done = bf16[256,768]{1,0:T(8,128)(2,1)} async-done(((bf16[8192,768]{1,0:T(8,128)(2,1)}), bf16[256,768]{1,0:T(8,128)(2,1)}) %reduce-scatter.7.cloned.1.call-update) | async-done | bytes 393232 | tf_op jit(solution)/shard_map/reduce_scatter | solution.py:290
  269.4 215.5 %all-gather.12.cloned.1.call-done = bf16[128,192,768]{2,1,0:T(8,128)(2,1)} async-done(((bf16[4,192,768]{2,1,0:T(8,128)(2,1)}), bf16[128,192,768]{2,1,0:T(8,128)(2,1)}) %all-gather.12.cloned.1.call-update) | async-done | bytes 37748752 | tf_op jit(solution)/shard_map/all_gather | solution.py:279
  484.9 25.4 %fusion.305 = (bf16[4,4,4,192,768]{4,3,1,2,0:T(8,128)(2,1)}, bf16[4,4,4,192,768]{4,3,1,2,0:T(8,128)(2,1)}) fusion(bf16[8,4,4,192,768]{4,3,1,2,0:T(8,128)(2,1)} %bitcast.623), kind=kLoop, calls=%fused_computation.542 | loop fusion | bytes 75497472 | tf_op jit(solution)/shard_map/slice | solution.py:305
  510.4 9.7 copy.148
  520.0 6.4 copy-done.3
  535.7 10.1 copy.154
  545.8 6.4 copy-done.2
  555.5 6.3 all-gather.14.cloned.1.call-done
  561.9 3.7 fusion.307
  570.8 3.7 fusion.11
  574.5 3.7 fusion.9
  580.8 7.0 fusion.163
  614.1 21.3 %all-gather.16.cloned.1.call-done = bf16[1024,1536]{1,0:T(8,128)(2,1)} async-done(((bf16[256,1536]{1,0:T(8,128)(2,1)}), bf16[1024,1536]{1,0:T(8,128)(2,1)}) %all-gather.16.cloned.1.call-update) | async-done | bytes 3145744 | tf_op jit(solution)/shard_map/all_gather | solution.py:116
  642.1 4.3 fusion.12
  652.1 6.9 fusion.162
  673.8 63.5 %all-gather.18.cloned.1.call-done = bf16[3072,768]{1,0:T(8,128)(2,1)} async-done(((bf16[96,768]{1,0:T(8,128)(2,1)}), bf16[3072,768]{1,0:T(8,128)(2,1)}) %all-gather.18.cloned.1.call-update) | async-done | bytes 4718608 | tf_op jit(solution)/shard_map/all_gather | solution.py:335
  737.3 7.8 fusion.311
  745.2 4.5 copy-done.14
  753.8 53.9 %all-gather.24.cloned.1.call-done = f32[32,3,3072]{2,1,0:T(4,128)} async-done(((f32[1,3,3072]{2,1,0:T(4,128)}), f32[32,3,3072]{2,1,0:T(4,128)}) %all-gather.24.cloned.1.call-update) | async-done | bytes 1179664 | tf_op jit(solution)/shard_map/all_gather | solution.py:342
  807.7 3.9 fusion.308
  812.4 12.6 convolution_convert_fusion
  826.6 104.4 %reduce-scatter.11.cloned.1.call-done = bf16[96,768]{1,0:T(8,128)(2,1)} async-done(((bf16[3072,768]{1,0:T(8,128)(2,1)}), bf16[96,768]{1,0:T(8,128)(2,1)}) %reduce-scatter.11.cloned.1.call-update) | async-done | bytes 147472 | tf_op jit(solution)/shard_map/reduce_scatter | solution.py:357
  951.0 7.7 fusion.313
  958.7 8.3 fusion.80
  967.0 34.5 %fusion.83 = bf16[12,64,1024]{2,1,0:T(8,128)(2,1)} fusion(f32[12,256,1024]{2,1,0:T(8,128)} %fusion.313, f32[12,256,1024]{2,1,0:T(8,128)} %copy-done.5, f32[12,256]{1,0:T(8,128)S(1)} %copy-done.160, pred[256,1024]{1,0:T(8,128)(4,1)S(1)} %fusion.170, bf16[256,12,32]{0,2,1:T(8,128)(2,1)S(1)} %copy-done.53, bf16[256,12,32]{0,2,1:T(8,128)(2,1)S(1)} %copy-done.51), kind=kOutput, calls=%fused_computation.97 | convolution fusion | flops 438833152 | bytes 27406336 | tf_op jit(solution)/shard_map/hqk,qhd->khd/dot_general | solution.py:200
  1001.5 4.0 pad_maximum_fusion
  1005.6 29.1 %fusion.154 = f32[256,12,64]{0,2,1:T(8,128)} fusion(bf16[1024,12,64]{0,2,1:T(8,128)(2,1)S(1)} %bitcast.635, f32[12,256,1024]{2,1,0:T(8,128)} %fusion.313, f32[12,256,1024]{2,1,0:T(8,128)} %copy-done.5, f32[12,256]{1,0:T(8,128)S(1)} %copy-done.160, pred[256,1024]{1,0:T(8,128)(4,1)S(1)} %fusion.170), kind=kOutput, calls=%fused_computation.196 | convolution fusion | flops 437260288 | bytes 27799552 | tf_op jit(solution)/shard_map/hqk,khd->qhd/dot_general | solution.py:199
  1034.7 8.1 reduce-scatter.13.cloned.1.call-done
  1068.8 7.8 fusion.314
  1076.6 8.1 fusion.77
  1084.7 35.0 %fusion.86 = bf16[12,64,1024]{2,1,0:T(8,128)(2,1)} fusion(f32[12,256,1024]{2,1,0:T(8,128)} %fusion.314, f32[12,256,1024]{2,1,0:T(8,128)} %copy-done.4, f32[12,256]{1,0:T(8,128)S(1)} %log_add_fusion.1, pred[256,1024]{1,0:T(8,128)(4,1)S(1)} %fusion.170, bf16[256,12,32]{0,2,1:T(8,128)(2,1)S(1)} %copy-done.49, bf16[256,12,32]{0,2,1:T(8,128)(2,1)S(1)} %copy-done.47), kind=kOutput, calls=%fused_computation.98 | convolution fusion | flops 438833152 | bytes 27406336 | tf_op jit(solution)/shard_map/hqk,qhd->khd/dot_general | solution.py:200
  1119.7 3.9 pad_maximum_fusion.1
  1123.6 35.0 %fusion.157 = f32[256,12,64]{0,2,1:T(8,128)} fusion(bf16[1024,12,64]{0,2,1:T(8,128)(2,1)} %bitcast.633, f32[12,256,1024]{2,1,0:T(8,128)} %fusion.314, f32[12,256,1024]{2,1,0:T(8,128)} %copy-done.4, f32[12,256]{1,0:T(8,128)S(1)} %log_add_fusion.1, pred[256,1024]{1,0:T(8,128)(4,1)S(1)} %fusion.170), kind=kOutput, calls=%fused_computation.197 | convolution fusion | flops 437260288 | bytes 27799552 | tf_op jit(solution)/shard_map/hqk,khd->qhd/dot_general | solution.py:199
  1214.7 25.6 %copy.166 = bf16[8,4,4,192,768]{4,3,1,2,0:T(8,128)(2,1)} copy(bf16[8,4,4,192,768]{4,3,2,1,0:T(8,128)(2,1)} %bitcast.130) | data formatting | bytes 75497472 | tf_op jit(solution)/shard_map/reshape | solution.py:379
  1248.4 340.8 %reduce-scatter.17.cloned.1.call-done = bf16[4,192,768]{2,1,0:T(8,128)(2,1)} async-done(((bf16[128,192,768]{2,1,0:T(8,128)(2,1)}), bf16[4,192,768]{2,1,0:T(8,128)(2,1)}) %reduce-scatter.17.cloned.1.call-update) | async-done | bytes 1179664 | tf_op jit(solution)/shard_map/reduce_scatter | solution.py:382
  1593.5 15.4 multiply_reduce_fusion.3
  1609.1 79.1 %all-gather.22.cloned.1.call-done = bf16[8192,768]{1,0:T(8,128)(2,1)} async-done(((bf16[256,768]{1,0:T(8,128)(2,1)}), bf16[8192,768]{1,0:T(8,128)(2,1)}) %all-gather.22.cloned.1.call-update) | async-done | bytes 12582928 | tf_op jit(solution)/shard_map/all_gather | solution.py:375
  1688.1 21.3 %multiply_reduce_fusion.4 = (f32[]{:T(128)}, f32[1000,768]{1,0:T(8,128)}) fusion(bf16[8192,768]{1,0:T(8,128)(2,1)} %all-gather.22.cloned.1.call-done, s32[8192]{0:T(1024)S(1)} %bitcast.671), kind=kOutput, calls=%fused_computation.85 | convolution fusion | flops 12592640000 | bytes 15687684 | tf_op jit(solution)/shard_map/tv,td->vd/dot_general | solution.py:376
  1709.4 37.9 %all-gather.20.cloned.1.call-done = bf16[32,192,768]{2,1,0:T(8,128)(2,1)} async-done(((bf16[4,192,768]{2,1,0:T(8,128)(2,1)}), bf16[32,192,768]{2,1,0:T(8,128)(2,1)}) %all-gather.20.cloned.1.call-update) | async-done | bytes 9437200 | tf_op jit(solution)/shard_map/all_gather | solution.py:388
  1747.3 4.3 gather_fusion.1
  1755.8 40.2 %all-reduce = (f32[]{:T(128)}, f32[5,768]{1,0:T(8,128)S(1)}) all-reduce(f32[]{:T(128)S(6)} %add.513, f32[5,768]{1,0:T(8,128)S(1)} %stack.167), channel_id=1, replica_groups=mesh['a'=2,'b'=4,'rep'=4] {'a','b','rep'}, use_global_device_ids=true, to_apply=%region_40.41 | all-reduce | flops 3841 | bytes 30728 | tf_op jit(solution)/shard_map/psum | solution.py:407
  1798.7 10.6 fusion.302
  1810.6 6.0 fusion.298
  1818.9 5.0 fusion.300
  (665 shorter events, 206.5 us)
Async XLA Ops:
  7.2 18.4 %copy-start = (s32[1,1024]{1,0:T(1,128)S(1)}, s32[1,1024]{1,0:T(1,128)}, u32[]{:S(2)}) copy-start(s32[1,1024]{1,0:T(1,128)} %param.19) | copy-start | bytes 12292
  7.2 108.4 %reduce-scatter.9.cloned.1.call-start = ((), (), s32[]{:S(2)}) async-start(), calls=%async_computation.7 | async-start | bytes 10616832 | tf_op jit(solution)/shard_map/reduce_scatter | solution.py:278
  25.4 72.5 %copy-start.30 = (f32[1000,768]{1,0:T(8,128)S(1)}, f32[1000,768]{1,0:T(8,128)}, u32[]{:S(2)}) copy-start(f32[1000,768]{1,0:T(8,128)} %param.27) | copy-start | bytes 9216004
  25.5 242.2 %reduce-scatter.7.cloned.1.call-start = ((), (), s32[]{:S(2)}) async-start(), calls=%async_computation.6 | async-start | bytes 12976128 | tf_op jit(solution)/shard_map/reduce_scatter | solution.py:290
  97.9 17.6 copy-start.71
  98.0 17.6 copy-start.148
  115.5 369.4 %all-gather.12.cloned.1.call-start = ((), (), s32[]{:S(2)}) async-start(), calls=%async_computation.8 | async-start | bytes 38928384 | tf_op jit(solution)/shard_map/all_gather | solution.py:279
  116.3 445.6 %all-gather.14.cloned.1.call-start = ((), (), s32[]{:S(2)}) async-start(), calls=%async_computation.9 | async-start | bytes 3932160 | tf_op jit(solution)/shard_map/all_gather | solution.py:116
  116.4 415.8 %copy-start.139 = (f32[768]{0:T(1024)}, f32[768]{0:T(1024)S(1)}, u32[]{:S(2)}) copy-start(f32[768]{0:T(1024)S(1)} %get-tuple-element.37) | copy-start | bytes 9220
  116.4 474.6 %copy-start.134 = (f32[768]{0:T(1024)}, f32[768]{0:T(1024)S(1)}, u32[]{:S(2)}) copy-start(f32[768]{0:T(1024)S(1)} %get-tuple-element.36) | copy-start | bytes 9220
  116.6 488.6 %copy-start.42 = (f32[256,32]{0,1:T(8,128)}, f32[256,32]{0,1:T(8,128)S(1)}, u32[]{:S(2)}) copy-start(f32[256,32]{0,1:T(8,128)S(1)} %get-tuple-element.125) | copy-start | bytes 98308
  116.7 488.6 %copy-start.44 = (f32[256,32]{0,1:T(8,128)}, f32[256,32]{0,1:T(8,128)S(1)}, u32[]{:S(2)}) copy-start(f32[256,32]{0,1:T(8,128)S(1)} %get-tuple-element.126) | copy-start | bytes 98308
  269.4 262.8 %copy-start.165 = (f32[256]{0:T(256)}, f32[256]{0:T(256)S(1)}, u32[]{:S(2)}) copy-start(f32[256]{0:T(256)S(1)} %get-tuple-element.128) | copy-start | bytes 3076
  535.0 100.5 %all-gather.16.cloned.1.call-start = ((), (), s32[]{:S(2)}) async-start(), calls=%async_computation.10 | async-start | bytes 3932160 | tf_op jit(solution)/shard_map/all_gather | solution.py:116
  555.5 15.2 copy-start.46
  555.5 15.2 copy-start.48
  600.8 58.2 %copy-start.6 = (f32[256,768]{1,0:T(8,128)}, f32[256,768]{1,0:T(8,128)S(1)}, u32[]{:S(2)}) copy-start(f32[256,768]{1,0:T(8,128)S(1)} %get-tuple-element.150) | copy-start | bytes 2359300
  605.6 36.5 %copy-start.50 = (bf16[256,12,32]{0,2,1:T(8,128)(2,1)}, bf16[256,12,32]{0,2,1:T(8,128)(2,1)S(1)}, u32[]{:S(2)}) copy-start(bf16[256,12,32]{0,2,1:T(8,128)(2,1)S(1)} %get-tuple-element.101) | copy-start | bytes 589828
  605.6 36.5 %copy-start.52 = (bf16[256,12,32]{0,2,1:T(8,128)(2,1)}, bf16[256,12,32]{0,2,1:T(8,128)(2,1)S(1)}, u32[]{:S(2)}) copy-start(bf16[256,12,32]{0,2,1:T(8,128)(2,1)S(1)} %get-tuple-element.102) | copy-start | bytes 589828
  606.8 130.6 %all-gather.18.cloned.1.call-start = ((), (), s32[]{:S(2)}) async-start(), calls=%async_computation.11 | async-start | bytes 4866048 | tf_op jit(solution)/shard_map/all_gather | solution.py:335
  612.8 29.2 %copy-start.129 = (s32[8,4,96]{2,1,0:T(4,128)}, s32[8,4,96]{2,1,0:T(4,128)S(1)}, u32[]{:S(2)}) copy-start(s32[8,4,96]{2,1,0:T(4,128)S(1)} %get-tuple-element.32) | copy-start | bytes 36868
  613.6 28.5 %copy-start.146 = (pred[8,4,96]{2,1,0:T(4,128)(4,1)}, pred[8,4,96]{2,1,0:T(4,128)(4,1)S(1)}, u32[]{:S(2)}) copy-start(pred[8,4,96]{2,1,0:T(4,128)(4,1)S(1)} %fusion.74) | copy-start | bytes 9220
  613.6 140.1 %copy-start.145 = (pred[8,4,96]{2,0,1:T(8,128)(4,1)}, pred[8,4,96]{2,0,1:T(8,128)(4,1)S(1)}, u32[]{:S(2)}) copy-start(pred[8,4,96]{2,0,1:T(8,128)(4,1)S(1)} %get-tuple-element.124) | copy-start | bytes 9220
  673.6 134.0 %all-gather.24.cloned.1.call-start = ((), (), s32[]{:S(2)}) async-start(), calls=%async_computation.18 | async-start | bytes 1622016 | tf_op jit(solution)/shard_map/all_gather | solution.py:342
  673.8 138.5 %copy-start.143 = (s32[3072]{0:T(1024)}, s32[3072]{0:T(1024)S(1)}, u32[]{:S(2)}) copy-start(s32[3072]{0:T(1024)S(1)} %sub.245) | copy-start | bytes 36868
  753.7 177.4 %reduce-scatter.11.cloned.1.call-start = ((), (), s32[]{:S(2)}) async-start(), calls=%async_computation.12 | async-start | bytes 4866048 | tf_op jit(solution)/shard_map/reduce_scatter | solution.py:357
  753.8 71.2 %copy-start.176 = (pred[3072]{0:T(1024)(128)(4,1)}, pred[3072]{0:T(1024)(128)(4,1)S(1)}, u32[]{:S(2)}) copy-start(pred[3072]{0:T(1024)(128)(4,1)S(1)} %ge.42) | copy-start | bytes 9220
  812.4 118.7 %copy-start.151 = (f32[256]{0:T(256)S(1)}, f32[256]{0:T(256)}, u32[]{:S(2)}) copy-start(f32[256]{0:T(256)} %copy-done.150) | copy-start | bytes 3076
  825.0 118.9 %slice-start.5 = ((s8[18874368]{0:T(1024)(128)(4,1)}), s8[2097152]{0:T(1024)(128)(4,1)S(1)}, s32[]{:S(2)}) async-start(s8[18874368]{0:T(1024)(128)(4,1)} %bitcast.577), calls=%async_computation.24 | async-start | bytes 4194304
  825.0 217.8 %reduce-scatter.13.cloned.1.call-start = ((), (), s32[]{:S(2)}) async-start(), calls=%async_computation.13 | async-start | bytes 3932160 | tf_op jit(solution)/shard_map/reduce_scatter | solution.py:203
  1005.5 156.2 %reduce-scatter.15.cloned.1.call-start = ((), (), s32[]{:S(2)}) async-start(), calls=%async_computation.14 | async-start | bytes 3932160 | tf_op jit(solution)/shard_map/reduce_scatter | solution.py:203
  1005.6 38.4 %copy-start.43 = (f32[256,32]{0,1:T(8,128)S(1)}, f32[256,32]{0,1:T(8,128)}, u32[]{:S(2)}) copy-start(f32[256,32]{0,1:T(8,128)} %copy-done.42) | copy-start | bytes 98308
  1005.6 38.4 %copy-start.45 = (f32[256,32]{0,1:T(8,128)S(1)}, f32[256,32]{0,1:T(8,128)}, u32[]{:S(2)}) copy-start(f32[256,32]{0,1:T(8,128)} %copy-done.44) | copy-start | bytes 98308
  1123.6 40.9 %copy-start.24 = (bf16[256,768]{1,0:T(8,128)(2,1)S(1)}, bf16[256,768]{1,0:T(8,128)(2,1)}, u32[]{:S(2)}) copy-start(bf16[256,768]{1,0:T(8,128)(2,1)} %reduce-scatter.7.cloned.1.call-done) | copy-start | bytes 1179652
  1123.6 40.9 %copy-start.140 = (f32[768]{0:T(1024)S(1)}, f32[768]{0:T(1024)}, u32[]{:S(2)}) copy-start(f32[768]{0:T(1024)} %copy-done.139) | copy-start | bytes 9220
  1123.6 40.9 %copy-start.166 = (f32[256]{0:T(256)S(1)}, f32[256]{0:T(256)}, u32[]{:S(2)}) copy-start(f32[256]{0:T(256)} %copy-done.165) | copy-start | bytes 3076
  1123.6 465.6 %reduce-scatter.17.cloned.1.call-start = ((), (), s32[]{:S(2)}) async-start(), calls=%async_computation.15 | async-start | bytes 38928384 | tf_op jit(solution)/shard_map/reduce_scatter | solution.py:382
  1240.4 353.1 %copy-start.144 = (s32[3072]{0:T(1024)S(1)}, s32[3072]{0:T(1024)}, u32[]{:S(2)}) copy-start(s32[3072]{0:T(1024)} %copy-done.143) | copy-start | bytes 36868
  1240.4 447.7 %all-gather.22.cloned.1.call-start = ((), (), s32[]{:S(2)}) async-start(), calls=%async_computation.17 | async-start | bytes 12976128 | tf_op jit(solution)/shard_map/all_gather | solution.py:375
  1248.4 498.9 %all-gather.20.cloned.1.call-start = ((), (), s32[]{:S(2)}) async-start(), calls=%async_computation.16 | async-start | bytes 10616832 | tf_op jit(solution)/shard_map/all_gather | solution.py:388
  1593.5 15.4 copy-start.156
  1593.5 15.4 copy-start.157
  1593.5 15.5 copy-start.158
  1593.5 15.5 copy-start.159
  1593.5 94.6 %copy-start.149 = (s32[8,2,4,128]{3,1,2,0:T(2,128)S(1)}, s32[8,2,4,128]{3,1,2,0:T(2,128)}, u32[]{:S(2)}) copy-start(s32[8,2,4,128]{3,1,2,0:T(2,128)} %copy-done.148) | copy-start | bytes 98308
  1609.0 189.0 %copy-start.142 = (f32[5,768]{1,0:T(8,128)S(1)}, f32[5,768]{1,0:T(8,128)}, u32[]{:S(2)}) copy-start(f32[5,768]{1,0:T(8,128)} %param.33) | copy-start | bytes 46084
  1609.1 189.0 %copy-start.152 = (f32[5,768]{1,0:T(8,128)S(1)}, f32[5,768]{1,0:T(8,128)}, u32[]{:S(2)}) copy-start(f32[5,768]{1,0:T(8,128)} %param.35) | copy-start | bytes 46084
  1609.1 189.0 %copy-start.153 = (f32[5,768]{1,0:T(8,128)S(1)}, f32[5,768]{1,0:T(8,128)}, u32[]{:S(2)}) copy-start(f32[5,768]{1,0:T(8,128)} %param.34) | copy-start | bytes 46084
  (173 other events, 1126.5 us)
Sparse Core Ops, SparseCore 0:
  25.6 79.4 reduce-scatter.8
  115.7 151.9 reduce-scatter.6
  270.9 214.0 all-gather.11
  535.1 26.6 all-gather.13
  606.9 28.5 all-gather.15
  673.8 63.5 all-gather.17
  753.8 53.8 all-gather.23
  825.2 105.8 reduce-scatter.10
  1005.6 37.1 reduce-scatter.12
  1123.7 37.9 reduce-scatter.14
  1240.5 348.6 reduce-scatter.16
  1592.9 95.1 all-gather.21
  1690.2 57.0 all-gather.19

commit v2 on v1

--- a/solution.py
+++ b/solution.py
@@ -1,6 +1,10 @@
+import functools
+
 import jax
 import jax.numpy as jnp
 from jax import lax
+from jax.experimental import pallas as pl
+from jax.experimental.pallas import tpu as pltpu
 from jax.sharding import Mesh, PartitionSpec as P
 
 D = 768
@@ -84,10 +88,473 @@
     return (weight, first, second)
 
 
-ALL = ("a", "b", "rep")
-DP = ("a", "b")
+ALL = ("y", "x", "c", "z")
+DP = ("y", "x", "c")
+PART = ("x", "c")
 UNITS = FF // D
 TILES_PER = 4 + 3 * UNITS
+
+
+MESH = pl.DeviceIdType.MESH
+
+
+def half_rows(rows):
+    return (rows // 2 + 15) // 16 * 16
+
+
+def remote(src, dst, ssem, rsem, **to):
+    return pltpu.make_async_remote_copy(
+        src_ref=src, dst_ref=dst, send_sem=ssem, recv_sem=rsem, device_id=to, device_id_type=MESH
+    )
+
+
+def greet(zn, y, x, c, z):
+    barrier = pltpu.get_barrier_semaphore()
+    for to in ({"x": 1 - x}, {"y": 1 - y}, {"c": 1 - c}):
+        pl.semaphore_signal(barrier, inc=1, device_id=to, device_id_type=MESH)
+    if zn > 1:
+
+        @pl.when(z < zn - 1)
+        def _():
+            pl.semaphore_signal(barrier, inc=1, device_id={"z": z + 1}, device_id_type=MESH)
+
+        @pl.when(z > 0)
+        def _():
+            pl.semaphore_signal(barrier, inc=1, device_id={"z": z - 1}, device_id_type=MESH)
+
+        @pl.when((z > 0) & (z < zn - 1))
+        def _():
+            pl.semaphore_wait(barrier, 5)
+
+        @pl.when((z == 0) | (z == zn - 1))
+        def _():
+            pl.semaphore_wait(barrier, 4)
+    else:
+        pl.semaphore_wait(barrier, 3)
+
+
+def gather_kernel(zn, x_ref, o_ref, hold, ssem, rsem, lsem):
+    y, x, c, z = [lax.axis_index(n) for n in ALL]
+    me = z if zn > 1 else 0
+    rows = x_ref.shape[0]
+    h0 = half_rows(rows)
+    lo, hi = pl.ds(0, h0), pl.ds(h0, rows - h0)
+    X, Y, DX, DY, CO, CX, CY, C0, C1, ZU, ZD = range(11)
+    nx, ny, nc = {"x": 1 - x}, {"y": 1 - y}, {"c": 1 - c}
+
+    def slot(yy, xx, zz):
+        return ((yy * 2 + xx) * 2 + c) * zn + zz
+
+    def copy(kind, k, src, dst, to):
+        return remote(src, dst, ssem.at[kind, k], rsem.at[kind, k], **to)
+
+    def block(s):
+        return o_ref.at[s]
+
+    greet(zn, y, x, c, z)
+    local = pltpu.make_async_copy(x_ref, hold, lsem)
+    local.start()
+    local.wait()
+    local = pltpu.make_async_copy(hold, o_ref.at[slot(y, x, me)], lsem)
+    local.start()
+
+    def spread(zb, src):
+        dst = block(slot(y, x, zb))
+        copy(X, zb, src, dst, nx).start()
+        copy(Y, zb, src, dst, ny).start()
+        copy(CO, zb, src, dst, nc).start()
+
+    def up(s):
+        zb = z - (s - 1)
+        b = block(slot(y, x, zb))
+        return copy(ZU, s, x_ref if s == 1 else b, b, {"z": z + 1})
+
+    def down(s):
+        zb = z + (s - 1)
+        b = block(slot(y, x, zb))
+        return copy(ZD, s, x_ref if s == 1 else b, b, {"z": z - 1})
+
+    for s in range(1, zn):
+
+        @pl.when((z < zn - 1) & (z - (s - 1) >= 0))
+        def _():
+            up(s).start()
+
+        @pl.when((z > 0) & (z + (s - 1) < zn))
+        def _():
+            down(s).start()
+
+        if s == 1:
+            spread(me, x_ref)
+
+        @pl.when(z - s >= 0)
+        def _():
+            copy(ZU, s, x_ref, x_ref, nx).wait_recv()
+            spread(z - s, block(slot(y, x, z - s)))
+
+        @pl.when(z + s < zn)
+        def _():
+            copy(ZD, s, x_ref, x_ref, nx).wait_recv()
+            spread(z + s, block(slot(y, x, z + s)))
+
+    if zn == 1:
+        spread(0, x_ref)
+    order = [lax.rem(z + j, zn) if zn > 1 else 0 for j in range(zn)]
+    for zb in order:
+        sx, sy = slot(y, 1 - x, zb), slot(1 - y, x, zb)
+        copy(X, zb, x_ref, x_ref, nx).wait_recv()
+        copy(DX, zb, o_ref.at[sx, lo], o_ref.at[sx, lo], ny).start()
+        copy(CX, zb, block(sx), block(sx), nc).start()
+        copy(Y, zb, x_ref, x_ref, nx).wait_recv()
+        copy(DY, zb, o_ref.at[sy, hi], o_ref.at[sy, hi], nx).start()
+        copy(CY, zb, block(sy), block(sy), nc).start()
+    for zb in order:
+        sd = slot(1 - y, 1 - x, zb)
+        copy(DX, zb, x_ref.at[lo], x_ref.at[lo], nx).wait_recv()
+        copy(C0, zb, o_ref.at[sd, lo], o_ref.at[sd, lo], nc).start()
+        copy(DY, zb, x_ref.at[hi], x_ref.at[hi], nx).wait_recv()
+        copy(C1, zb, o_ref.at[sd, hi], o_ref.at[sd, hi], nc).start()
+    for zb in range(zn):
+        for kind, part in ((CO, x_ref), (CX, x_ref), (CY, x_ref), (C0, x_ref.at[lo]), (C1, x_ref.at[hi])):
+            copy(kind, zb, part, part, nx).wait_recv()
+        for kind, part in (
+            (X, x_ref), (Y, x_ref), (CO, x_ref), (CX, x_ref), (CY, x_ref),
+            (DX, x_ref.at[lo]), (DY, x_ref.at[hi]), (C0, x_ref.at[lo]), (C1, x_ref.at[hi]),
+        ):
+            copy(kind, zb, part, part, nx).wait_send()
+    for s in range(1, zn):
+
+        @pl.when((z < zn - 1) & (z - (s - 1) >= 0))
+        def _():
+            up(s).wait_send()
+
+        @pl.when((z > 0) & (z + (s - 1) < zn))
+        def _():
+            down(s).wait_send()
+
+    local.wait()
+
+
+def all_gather(x, zn, ident, name):
+    sems = pltpu.SemaphoreType.DMA((11, zn))
+    return pl.pallas_call(
+        functools.partial(gather_kernel, zn),
+        out_shape=jax.ShapeDtypeStruct((8 * zn,) + x.shape, x.dtype),
+        in_specs=[pl.BlockSpec(memory_space=pl.ANY)],
+        out_specs=pl.BlockSpec(memory_space=pl.ANY),
+        scratch_shapes=[pltpu.VMEM(x.shape, x.dtype), sems, sems, pltpu.SemaphoreType.DMA],
+        compiler_params=pltpu.CompilerParams(collective_id=ident, has_side_effects=True),
+        name=name,
+    )(x)
+
+
+def reduce_kernel(zn, p_ref, o_ref, acc, crecv, dxr, dyr, xr, yr, zur, zdr, ssem, rsem, lsem):
+    y, x, c, z = [lax.axis_index(n) for n in ALL]
+    me = z if zn > 1 else 0
+    rows, cols = p_ref.shape[1:]
+    h0 = half_rows(rows)
+    h1 = rows - h0
+    X, Y, DX, DY, C0, ZU, ZD = 0, 1, 2, 3, 4, 8, 9
+    nx, ny, nc = {"x": 1 - x}, {"y": 1 - y}, {"c": 1 - c}
+    kinds = [(y, x), (y, 1 - x), (1 - y, x), (1 - y, 1 - x)]
+    step = 32 if rows % 32 == 0 else 16
+
+    def slot(k, cc, zz):
+        yy, xx = kinds[k]
+        return ((yy * 2 + xx) * 2 + cc) * zn + zz
+
+    def copy(kind, k, src, dst, to):
+        return remote(src, dst, ssem.at[kind, k], rsem.at[kind, k], **to)
+
+    def load(k, zb):
+        return pltpu.make_async_copy(p_ref.at[slot(k, c, zb)], acc.at[k * zn + zb], lsem.at[k * zn + zb])
+
+    def across(k, zb):
+        return copy(C0 + k, zb, p_ref.at[slot(k, 1 - c, zb)], crecv.at[k * zn + zb], nc)
+
+    def add(dst, start, count, terms):
+        size = step if count % step == 0 else 16
+
+        @pl.loop(0, count // size)
+        def _(i):
+            at = pl.ds(pl.multiple_of(start + i * size, 16), size)
+            total = None
+            for ref, base in terms:
+                part = ref[pl.ds(pl.multiple_of(start - base + i * size, 16), size), :].astype(jnp.float32)
+                total = part if total is None else total + part
+            dst[at, :] = total.astype(dst.dtype)
+
+    greet(zn, y, x, c, z)
+    zorder = [lax.rem(z + j, zn) if zn > 1 else 0 for j in range(zn)]
+    for k in (3, 1, 2, 0):
+        for zb in range(zn):
+            across(k, zb).start()
+            load(k, zb).start()
+
+    def ready(k, zb):
+        load(k, zb).wait()
+        across(k, zb).wait_recv()
+
+    for zb in range(zn):
+        ready(3, zb)
+        b = 3 * zn + zb
+        add(acc.at[b], 0, rows, [(acc.at[b], 0), (crecv.at[b], 0)])
+        copy(DX, zb, acc.at[b, pl.ds(0, h0)], dxr.at[zb], nx).start()
+        copy(DY, zb, acc.at[b, pl.ds(h0, h1)], dyr.at[zb], ny).start()
+    for zb in range(zn):
+        ready(1, zb)
+        b = zn + zb
+        add(acc.at[b], 0, h0, [(acc.at[b], 0), (crecv.at[b], 0)])
+        copy(DY, zb, dyr.at[zb], dyr.at[zb], ny).wait_recv()
+        add(acc.at[b], h0, h1, [(acc.at[b], 0), (crecv.at[b], 0), (dyr.at[zb], h0)])
+        copy(X, zb, acc.at[b], xr.at[zb], nx).start()
+        ready(2, zb)
+        b = 2 * zn + zb
+        add(acc.at[b], h0, h1, [(acc.at[b], 0), (crecv.at[b], 0)])
+        copy(DX, zb, dxr.at[zb], dxr.at[zb], nx).wait_recv()
+        add(acc.at[b], 0, h0, [(acc.at[b], 0), (crecv.at[b], 0), (dxr.at[zb], 0)])
+        copy(Y, zb, acc.at[b], yr.at[zb], ny).start()
+
+    def column(zb):
+        return [(acc.at[zb], 0), (crecv.at[zb], 0), (xr.at[zb], 0), (yr.at[zb], 0)]
+
+    for zb in range(zn):
+        ready(0, zb)
+        copy(X, zb, acc.at[zb], xr.at[zb], nx).wait_recv()
+        copy(Y, zb, acc.at[zb], yr.at[zb], ny).wait_recv()
+        if zn == 1:
+            add(o_ref, 0, rows, column(0))
+            continue
+
+        def upward(zb=zb):
+            return copy(ZU, zb, acc.at[zb], zur.at[zb], {"z": z + 1})
+
+        def downward(zb=zb):
+            return copy(ZD, zb, acc.at[zb], zdr.at[zb], {"z": z - 1})
+
+        @pl.when(z == zb)
+        def _():
+            add(acc.at[zb], 0, rows, column(zb))
+
+        @pl.when((z < zb) & (z == 0))
+        def _():
+            add(acc.at[zb], 0, rows, column(zb))
+            upward().start()
+
+        @pl.when((z < zb) & (z > 0))
+        def _():
+            upward().wait_recv()
+            add(acc.at[zb], 0, rows, column(zb) + [(zur.at[zb], 0)])
+            upward().start()
+
+        @pl.when((z > zb) & (z == zn - 1))
+        def _():
+            add(acc.at[zb], 0, rows, column(zb))
+            downward().start()
+
+        @pl.when((z > zb) & (z < zn - 1))
+        def _():
+            downward().wait_recv()
+            add(acc.at[zb], 0, rows, column(zb) + [(zdr.at[zb], 0)])
+            downward().start()
+
+    if zn > 1:
+
+        @pl.when(z == 0)
+        def _():
+            copy(ZD, me, acc.at[me], zdr.at[me], {"z": z + 1}).wait_recv()
+            add(o_ref, 0, rows, [(acc.at[me], 0), (zdr.at[me], 0)])
+
+        @pl.when(z == zn - 1)
+        def _():
+            copy(ZU, me, acc.at[me], zur.at[me], {"z": z - 1}).wait_recv()
+            add(o_ref, 0, rows, [(acc.at[me], 0), (zur.at[me], 0)])
+
+        @pl.when((z > 0) & (z < zn - 1))
+        def _():
+            copy(ZD, me, acc.at[me], zdr.at[me], {"z": z + 1}).wait_recv()
+            copy(ZU, me, acc.at[me], zur.at[me], {"z": z + 1}).wait_recv()
+            add(o_ref, 0, rows, [(acc.at[me], 0), (zdr.at[me], 0), (zur.at[me], 0)])
+
+    for zb in range(zn):
+        for k in range(4):
+            across(k, zb).wait_send()
+        copy(DX, zb, dxr.at[zb], dxr.at[zb], nx).wait_send()
+        copy(DY, zb, dyr.at[zb], dyr.at[zb], ny).wait_send()
+        copy(X, zb, xr.at[zb], xr.at[zb], nx).wait_send()
+        copy(Y, zb, yr.at[zb], yr.at[zb], ny).wait_send()
+        if zn > 1:
+
+            @pl.when(z < zb)
+            def _():
+                copy(ZU, zb, zur.at[zb], zur.at[zb], {"z": z + 1}).wait_send()
+
+            @pl.when(z > zb)
+            def _():
+                copy(ZD, zb, zdr.at[zb], zdr.at[zb], {"z": z - 1}).wait_send()
+
+
+def reduce_scatter(p, zn, ident, name, out_dtype=None):
+    count, rows, cols = p.shape
+    h0 = half_rows(rows)
+    sems = pltpu.SemaphoreType.DMA((10, zn))
+    vm = lambda n, r: pltpu.VMEM((n, r, cols), p.dtype)
+    return pl.pallas_call(
+        functools.partial(reduce_kernel, zn),
+        out_shape=jax.ShapeDtypeStruct((rows, cols), out_dtype or p.dtype),
+        in_specs=[pl.BlockSpec(memory_space=pl.ANY)],
+        out_specs=pl.BlockSpec(memory_space=pltpu.VMEM),
+        scratch_shapes=[
+            vm(4 * zn, rows), vm(4 * zn, rows), vm(zn, h0), vm(zn, rows - h0),
+            vm(zn, rows), vm(zn, rows), vm(zn, rows), vm(zn, rows),
+            sems, sems, pltpu.SemaphoreType.DMA((4 * zn,)),
+        ],
+        compiler_params=pltpu.CompilerParams(
+            collective_id=ident, has_side_effects=True, vmem_limit_bytes=56 << 20
+        ),
+        name=name,
+    )(p)
+
+
+def greet_pair(x, c):
+    barrier = pltpu.get_barrier_semaphore()
+    for to in ({"x": 1 - x}, {"c": 1 - c}):
+        pl.semaphore_signal(barrier, inc=1, device_id=to, device_id_type=MESH)
+    pl.semaphore_wait(barrier, 2)
+
+
+def keys_gather_kernel(x_ref, o_ref, hold, ssem, rsem, lsem):
+    x, c = lax.axis_index("x"), lax.axis_index("c")
+    me, far = x * 2 + c, (1 - x) * 2 + c
+    nx, nc = {"x": 1 - x}, {"c": 1 - c}
+    load = pltpu.make_async_copy(x_ref, hold, lsem.at[0])
+    load.start()
+    greet_pair(x, c)
+    out = remote(x_ref, o_ref.at[me], ssem.at[0], rsem.at[0], **nx)
+    out.start()
+    near = remote(x_ref, o_ref.at[me], ssem.at[1], rsem.at[1], **nc)
+    near.start()
+    load.wait()
+    keep = pltpu.make_async_copy(hold, o_ref.at[me], lsem.at[1])
+    keep.start()
+    out.wait_recv()
+    on = remote(o_ref.at[far], o_ref.at[far], ssem.at[2], rsem.at[2], **nc)
+    on.start()
+    near.wait_recv()
+    on.wait_recv()
+    keep.wait()
+    out.wait_send()
+    near.wait_send()
+    on.wait_send()
+
+
+def keys_gather(v, ident):
+    sems = pltpu.SemaphoreType.DMA((3,))
+    return pl.pallas_call(
+        keys_gather_kernel,
+        out_shape=jax.ShapeDtypeStruct((4,) + v.shape, v.dtype),
+        in_specs=[pl.BlockSpec(memory_space=pl.ANY)],
+        out_specs=pl.BlockSpec(memory_space=pl.ANY),
+        scratch_shapes=[pltpu.VMEM(v.shape, v.dtype), sems, sems, pltpu.SemaphoreType.DMA((2,))],
+        compiler_params=pltpu.CompilerParams(collective_id=ident, has_side_effects=True),
+        name="keys_gather",
+    )(v)
+
+
+def keys_reduce_kernel(p_ref, o_ref, acc, crecv, xr, ssem, rsem, lsem):
+    x, c = lax.axis_index("x"), lax.axis_index("c")
+    nx, nc = {"x": 1 - x}, {"c": 1 - c}
+    rows = p_ref.shape[1]
+    places = [(1 - x) * 2, x * 2]
+    loads = [pltpu.make_async_copy(p_ref.at[places[i] + c], acc.at[i], lsem.at[i]) for i in range(2)]
+    for load in loads:
+        load.start()
+    greet_pair(x, c)
+    across = [
+        remote(p_ref.at[places[i] + 1 - c], crecv.at[i], ssem.at[i], rsem.at[i], **nc) for i in range(2)
+    ]
+    for copy in across:
+        copy.start()
+
+    def add(dst, terms):
+        @pl.loop(0, rows // 16)
+        def _(i):
+            at = pl.ds(pl.multiple_of(i * 16, 16), 16)
+            total = terms[0][at, :].astype(jnp.float32)
+            for term in terms[1:]:
+                total = total + term[at, :].astype(jnp.float32)
+            dst[at, :] = total.astype(dst.dtype)
+
+    loads[0].wait()
+    across[0].wait_recv()
+    add(acc.at[0], [acc.at[0], crecv.at[0]])
+    out = remote(acc.at[0], xr, ssem.at[2], rsem.at[2], **nx)
+    out.start()
+    loads[1].wait()
+    across[1].wait_recv()
+    out.wait_recv()
+    add(o_ref, [acc.at[1], crecv.at[1], xr])
+    for copy in across + [out]:
+        copy.wait_send()
+
+
+def keys_reduce(p, ident):
+    block = p.shape[1:]
+    sems = pltpu.SemaphoreType.DMA((3,))
+    return pl.pallas_call(
+        keys_reduce_kernel,
+        out_shape=jax.ShapeDtypeStruct(block, p.dtype),
+        in_specs=[pl.BlockSpec(memory_space=pl.ANY)],
+        out_specs=pl.BlockSpec(memory_space=pltpu.VMEM),
+        scratch_shapes=[
+            pltpu.VMEM((2,) + block, p.dtype), pltpu.VMEM((2,) + block, p.dtype),
+            pltpu.VMEM(block, p.dtype), sems, sems, pltpu.SemaphoreType.DMA((2,)),
+        ],
+        compiler_params=pltpu.CompilerParams(
+            collective_id=ident, has_side_effects=True, vmem_limit_bytes=32 << 20
+        ),
+        name="keys_reduce",
+    )(p)
+
+
+def fits(axes):
+    return [lax.axis_size(n) for n in ALL] == [2, 2, 2, 4]
+
+
+def gather_all(v, ident, name):
+    if fits(ALL):
+        return all_gather(v, 4, ident, name)
+    return lax.all_gather(v, ALL, axis=0)
+
+
+def gather_plane(v, ident, name):
+    if fits(ALL):
+        return all_gather(v, 1, ident, name)
+    return lax.all_gather(v, DP, axis=0)
+
+
+def scatter_all(p, ident, name):
+    if fits(ALL):
+        return reduce_scatter(p, 4, ident, name)
+    return lax.psum_scatter(p, ALL, scatter_dimension=0)
+
+
+def scatter_plane(p, ident, name):
+    if fits(ALL):
+        return reduce_scatter(p, 1, ident, name)
+    return lax.psum_scatter(p, DP, scatter_dimension=0)
+
+
+def keys_all_gather(v):
+    if fits(ALL):
+        return keys_gather(v, 11).reshape(-1, v.shape[1])
+    return lax.all_gather(v, PART, axis=0, tiled=True)
+
+
+def keys_sum_scatter(p):
+    if fits(ALL):
+        return keys_reduce(p.reshape(4, -1, p.shape[1]), 12)
+    return lax.psum_scatter(p, PART, scatter_dimension=0, tiled=True)
 
 
 def mm(x, w):
@@ -113,7 +580,7 @@
     query = rotate(heads(query), cosine, sine).astype(jnp.bfloat16)
     keys = rotate(heads(keys), cosine, sine).astype(jnp.bfloat16).reshape(rows, D)
     both = jnp.concatenate([keys, value.astype(jnp.bfloat16)], axis=1)
-    both = lax.all_gather(both, "b", axis=0, tiled=True)
+    both = keys_all_gather(both)
     keys_all, value_all = heads(both[:, :D]), heads(both[:, D:])
     scores = jnp.einsum("qhd,khd->hqk", query, keys_all, preferred_element_type=jnp.float32) * HD ** (
         -0.5
@@ -200,7 +667,7 @@
     keys_part = jnp.einsum("hqk,qhd->khd", score_grad, query, preferred_element_type=jnp.float32)
     length = keys_part.shape[0]
     both = jnp.concatenate([keys_part.reshape(length, D), value_part.reshape(length, D)], axis=1)
-    both = lax.psum_scatter(both.astype(jnp.bfloat16), "b", scatter_dimension=0, tiled=True)
+    both = keys_sum_scatter(both.astype(jnp.bfloat16))
     keys_grad, value_grad = both[:, :D].astype(jnp.float32), both[:, D:]
     parts = [
         rotate_back(query_grad, cosine, sine).reshape(rows, D).astype(jnp.bfloat16),
@@ -218,6 +685,11 @@
         ]
     )
     return middle_grad + back, tiles_grad, [attend_gain, feed_gain]
+
+
+def padded(v):
+    count = -(-v.shape[0] // 4096) * 4096
+    return jnp.pad(v, (0, count - v.shape[0])).reshape(-1, 128)
 
 
 def shards(
@@ -240,8 +712,8 @@
     gain_first,
     gain_second,
 ):
-    a_size, b_size, rep_size = [lax.axis_size(n) for n in ALL]
-    a_index, b_index, rep_index = [lax.axis_index(n) for n in ALL]
+    a_size, b_size, rep_size = lax.axis_size("y"), lax.axis_size(PART), lax.axis_size("z")
+    a_index, b_index, rep_index = lax.axis_index("y"), lax.axis_index(PART), lax.axis_index("z")
     dp_size = a_size * b_size
     devices = dp_size * rep_size
     dp_index = a_index * b_size + b_index
@@ -264,7 +736,8 @@
             lax.dynamic_slice_in_dim(targets[0], rep_index * (comp // rep_size), comp // rep_size),
         ]
     )
-    packed = lax.all_gather(own_part, ALL, axis=0, tiled=False).reshape(dp_size, rep_size, -1)
+    packed = gather_all(padded(own_part), 0, "ids_gather").reshape(devices, -1)
+    packed = packed[:, : own_part.shape[0]].reshape(dp_size, rep_size, -1)
     tokens_all = packed[:, :, :rows].reshape(dp_size, length)
     segments_all = packed[:, :, rows : 2 * rows].reshape(dp_size, length)
     edge = 2 * rows + comp // rep_size
@@ -274,11 +747,19 @@
     slots = tile_slots(owners)
     mine = owners == dp_index
     tile_low = tile_weight.astype(jnp.bfloat16)
-    placed = jnp.where(mine[:, None, None], jnp.take(tile_low, jnp.where(mine, slots, 0), axis=0), 0)
-    home = lax.psum_scatter(placed, DP, scatter_dimension=0, tiled=True)
-    spread = lax.all_gather(home, ALL, axis=0, tiled=True)
-    spread = spread.reshape(dp_size, rep_size, home_tiles, tile_rows, D)
-    tiles = spread.transpose(0, 2, 1, 3, 4).reshape(tile_count, D, D)
+    per = TILES_PER // dp_size
+    home_ids = (
+        jnp.arange(LAYERS)[None, :, None] * TILES_PER
+        + jnp.arange(dp_size)[:, None, None] * per
+        + jnp.arange(per)[None, None, :]
+    ).reshape(-1)
+    home_mine = jnp.take(mine, home_ids)
+    home_slots = jnp.where(home_mine, jnp.take(slots, home_ids), 0)
+    placed = jnp.where(home_mine[:, None, None], jnp.take(tile_low, home_slots, axis=0), 0)
+    home = scatter_plane(placed.reshape(dp_size, -1, D), 7, "home_scatter")
+    spread = gather_all(home, 1, "weights_gather")
+    spread = spread.reshape(dp_size, rep_size, LAYERS, per, tile_rows, D)
+    tiles = spread.transpose(2, 0, 3, 1, 4, 5).reshape(tile_count, D, D)
 
     order = tokens_all.reshape(a_size, rep_size, b_size, rows).transpose(0, 2, 1, 3).reshape(-1)
     place = order - vocab_start
@@ -287,7 +768,7 @@
     picked = jnp.dot(
         token_hot, table_weight.astype(jnp.bfloat16), preferred_element_type=jnp.float32
     ).astype(jnp.bfloat16)
-    state = lax.psum_scatter(picked, ALL, scatter_dimension=0, tiled=True).astype(jnp.float32)
+    state = scatter_all(picked.reshape(devices, rows, D), 8, "rows_scatter").astype(jnp.float32)
 
     first_place = b_index * rows
     places = first_place + jnp.arange(rows)
@@ -332,16 +813,16 @@
     )
     select = (own_spots[:, None] == jnp.arange(rows)[None, :]).astype(jnp.bfloat16)
     chosen = jnp.dot(select, final, preferred_element_type=jnp.float32).astype(jnp.bfloat16)
-    all_rows = lax.all_gather(chosen, ALL, axis=0, tiled=True)
+    all_rows = gather_all(chosen, 3, "chosen_gather").reshape(-1, D)
     head_low = head_weight.astype(jnp.bfloat16)
     logits = jnp.einsum("rd,vd->rv", all_rows, head_low, preferred_element_type=jnp.float32)
     hot = vocab_iota[None, :] == (all_wanted - vocab_start)[:, None]
     local_top = jnp.max(logits, axis=-1)
     local_total = jnp.sum(jnp.exp(logits - local_top[:, None]), axis=-1)
     local_hit = jnp.sum(jnp.where(hot, logits, 0.0), axis=-1)
-    stats = lax.all_gather(
-        jnp.stack([local_top, local_total, local_hit]), ALL, axis=0, tiled=False
-    )
+    own_stats = jnp.concatenate([local_top, local_total, local_hit])
+    stats = gather_all(padded(own_stats), 4, "stats_gather").reshape(devices, -1)
+    stats = stats[:, : own_stats.shape[0]].reshape(devices, 3, -1)
     top = jnp.max(stats[:, 0], axis=0)
     total = jnp.sum(stats[:, 1] * jnp.exp(stats[:, 0] - top[None]), axis=0)
     log_total = top + jnp.log(total)
@@ -354,8 +835,8 @@
         0.0,
     ).astype(jnp.bfloat16)
     rows_grad = jnp.dot(logit_grad, head_low, preferred_element_type=jnp.float32)
-    own_rows = lax.psum_scatter(
-        rows_grad.astype(jnp.bfloat16), ALL, scatter_dimension=0, tiled=True
+    own_rows = scatter_all(
+        rows_grad.astype(jnp.bfloat16).reshape(devices, -1, D), 9, "back_scatter"
     )
     head_grad = jnp.einsum("rv,rd->vd", logit_grad, all_rows, preferred_element_type=jnp.float32)
     final_grad = jnp.einsum("ct,cd->td", select, own_rows, preferred_element_type=jnp.float32)
@@ -372,20 +853,18 @@
             sine,
             allowed,
         )
-    piece_grads = lax.all_gather(state_grad.astype(jnp.bfloat16), ALL, axis=0, tiled=True)
+    piece_grads = gather_all(state_grad.astype(jnp.bfloat16), 2, "entry_gather").reshape(-1, D)
     table_grad = jnp.einsum(
         "tv,td->vd", token_hot, piece_grads, preferred_element_type=jnp.float32
     )
-    tile_grads = jnp.concatenate(tile_parts, axis=0).reshape(
-        dp_size, home_tiles, rep_size, tile_rows, D
-    )
-    home_grad = lax.psum_scatter(
-        tile_grads.transpose(0, 2, 1, 3, 4).reshape(-1, tile_rows, D),
-        ALL,
-        scatter_dimension=0,
-        tiled=True,
-    )
-    plane_grad = lax.all_gather(home_grad, DP, axis=0, tiled=True)
+    home_grads = []
+    for index in range(LAYERS):
+        part = tile_parts[index].reshape(dp_size, per, rep_size, tile_rows, D)
+        part = part.transpose(0, 2, 1, 3, 4).reshape(devices, -1, D)
+        home_grads.append(scatter_all(part, 10, "grads_scatter"))
+    plane_grad = gather_plane(jnp.concatenate(home_grads), 6, "owners_gather")
+    plane_grad = plane_grad.reshape(dp_size, LAYERS, per, tile_rows, D)
+    plane_grad = plane_grad.transpose(1, 0, 2, 3, 4).reshape(tile_count, tile_rows, D)
     own_count = jnp.sum(mine.astype(jnp.int32))
     slot_ids = jnp.arange(slots_cap)
     tile_of_slot = jnp.sum(
@@ -404,7 +883,11 @@
         + jnp.sum(table_grad * table_grad)
         + jnp.sum(head_grad * head_grad)
     )
-    square, gain_grads = lax.psum((square, gain_grads), ALL)
+    sums = gather_all(
+        padded(jnp.concatenate([square[None], gain_grads.reshape(-1)])), 5, "sums_gather"
+    )
+    sums = jnp.sum(sums.reshape(devices, -1), axis=0)
+    square, gain_grads = sums[0], sums[1 : 1 + gain_grads.size].reshape(gain_grads.shape)
     norm = jnp.sqrt(square + jnp.sum(gain_grads * gain_grads))
     factor = jnp.minimum(1.0, CLIP_NORM / norm)
     steps = step_count[0].astype(jnp.float32)
@@ -446,26 +929,26 @@
 
 def solution(mesh):
     dp_size, rep_size = mesh.shape["dp"], mesh.shape["rep"]
-    split = Mesh(mesh.devices.reshape(dp_size // rep_size, rep_size, rep_size), ALL)
+    split = Mesh(mesh.devices.reshape(dp_size // rep_size, rep_size // 2, 2, rep_size), ALL)
     return jax.shard_map(
         shards,
         mesh=split,
         in_specs=(
-            P(("a", "b"), "rep"),
-            P(("a", "b"), None),
-            P(("a", "b"), None),
-            P(("a", "b"), None),
+            P(DP, "z"),
+            P(DP, None),
+            P(DP, None),
+            P(DP, None),
             P(),
             P(),
-            P(("a", "b", "rep"), None, None),
-            P(("a", "b", "rep"), None, None),
-            P(("a", "b", "rep"), None, None),
-            P(("a", "b", "rep"), None),
-            P(("a", "b", "rep"), None),
-            P(("a", "b", "rep"), None),
-            P(("a", "b", "rep"), None),
-            P(("a", "b", "rep"), None),
-            P(("a", "b", "rep"), None),
+            P(ALL, None, None),
+            P(ALL, None, None),
+            P(ALL, None, None),
+            P(ALL, None),
+            P(ALL, None),
+            P(ALL, None),
+            P(ALL, None),
+            P(ALL, None),
+            P(ALL, None),
             P(),
             P(),
             P(),
@@ -473,18 +956,18 @@
         out_specs=(
             P(),
             P(),
-            P(("a", "b", "rep"), None, None),
-            P(("a", "b", "rep"), None, None),
-            P(("a", "b", "rep"), None, None),
-            P(("a", "b", "rep"), None, None),
-            P(("a", "b", "rep"), None),
-            P(("a", "b", "rep"), None),
-            P(("a", "b", "rep"), None),
-            P(("a", "b", "rep"), None),
-            P(("a", "b", "rep"), None),
-            P(("a", "b", "rep"), None),
-            P(("a", "b", "rep"), None),
-            P(("a", "b", "rep"), None),
+            P(ALL, None, None),
+            P(ALL, None, None),
+            P(ALL, None, None),
+            P(ALL, None, None),
+            P(ALL, None),
+            P(ALL, None),
+            P(ALL, None),
+            P(ALL, None),
+            P(ALL, None),
+            P(ALL, None),
+            P(ALL, None),
+            P(ALL, None),
             P(),
             P(),
             P(),

time: 1840 us -> 1500 us (0.82)
  waiting for transfers between devices: 1090 us -> 0 us
  Pallas kernels: 0 us -> 875 us
  blocking collectives: 112 us -> 0 us
  matrix products: 384 us -> 347 us
  local copies, waits for them, and re-layouts: 141 us -> 178 us
    pallas_call x0 -> x16, Pallas kernels: none -> 875 us  [the longest x7 424 us: all_gather(): pl.pallas_call(functools.partial(gather_kernel, zn), out_shape=jax.ShapeD...]
    reduce_scatter x6 -> x0, waiting for transfers between devices: 607 us -> none  [the longest x1 341 us: shards(): lax.psum_scatter(tile_grads.transpose(0, 2, 1, 3, 4).reshape(-1, tile_row...]
    all_gather x7 -> x0, waiting for transfers between devices: 477 us -> none  [the longest x1 215 us: shards(): spread = lax.all_gather(home, ALL, axis=0, tiled=True)]
    all_gather x1 -> x0, blocking collectives: 71.4 us -> none  [shards(): lax.all_gather(own_part, ALL, axis=0, tiled=False)]
    psum x1 -> x0, blocking collectives: 40.2 us -> none  [shards(): square, gain_grads = lax.psum((square, gain_grads), ALL)]
    dot_general x32, matrix products: 50.1 us -> 18.8 us  [mm_g(): return jnp.einsum('ld,le->de', x, y, preferred_element_type=jnp.float32)]
    reshape x2 -> x10, local copies, waits for them, and re-layouts: 25.7 us -> 55.2 us  [the longest x1 25.7 us: shards(): spread = spread.reshape(dp_size, rep_size, LAYERS, per, tile_rows, D)]
    concatenate x0 -> x8, local copies, waits for them, and re-layouts: none -> 26.1 us  [layer_backward(): jnp.concatenate([keys_part.reshape(length, D), value_part.reshape(length,...]
  transfers between devices with their start and end apart: 13 -> 0, of which waited for: 12 -> 0; matrix products, arithmetic and copies ran while one was open for 8% -> 0% of each run, Pallas kernels for 0% -> 0%
where the time goes in v2:
time: 1500 us; the launch traced here: 1490 us
  Pallas kernels  875 us (58%)
  matrix products  347 us (23%)
  local copies, waits for them, and re-layouts  178 us (12%)
  other arithmetic  82.7 us (6%)
    pallas_call x7, Pallas kernels, all_gather(): pl.pallas_call(functools.partial(gather_kernel, zn), out_shape=jax.ShapeD...  424 us
    pallas_call x5, Pallas kernels, reduce_scatter(): pl.pallas_call(functools.partial(reduce_kernel, zn), out_shape=jax.ShapeD...  359 us
    dot_general x2, matrix products, layer_backward(): jnp.einsum('hqk,qhd->khd', score_grad, query, preferred_element_type=jnp....  69.7 us
    dot_general x2, matrix products, layer_backward(): jnp.einsum('hqk,khd->qhd', score_grad, keys_all, preferred_element_type=j...  62.9 us
    pallas_call x2, Pallas kernels, keys_gather(): pl.pallas_call(keys_gather_kernel, out_shape=jax.ShapeDtypeStruct((4,) +...  48.6 us
    pallas_call x2, Pallas kernels, keys_reduce(): pl.pallas_call(keys_reduce_kernel, out_shape=jax.ShapeDtypeStruct(block,...  44.4 us
    dot_general x32, matrix products, mm_t(): return jnp.einsum('le,de->ld', x, w, preferred_element_type=jnp.float32)  41.3 us

profile of v2, /device:TPU:0, one launch (start us, length us, event | category | flops | bytes accessed | tf_op | source)
XLA Modules:
  0.0 1493.6 jit_solution(6587508804806568957)
XLA Ops:
  12.2 22.7 %ids_gather.1 = s32[32,32,128]{2,1,0:T(8,128)} custom-call(s32[32,128]{1,0:T(8,128)} %pad_bitcast_fusion.x_ref), custom_call_target="tpu_custom_call" | custom-call | tf_op jit(solution)/shard_map/ids_gather/pallas_call | solution.py:240
  46.4 5.1 gather_fusion.2
  51.5 9.8 fusion.11.p_ref
  61.3 49.2 %home_scatter.1.x_ref = bf16[768,768]{1,0:T(8,128)(2,1)} custom-call(bf16[8,768,768]{2,1,0:T(8,128)(2,1)} %fusion.11.p_ref), custom_call_target="tpu_custom_call" | custom-call | tf_op jit(solution)/shard_map/home_scatter/pallas_call | solution.py:402
  110.6 17.7 %fusion.6 = bf16[8192,768]{1,0:T(8,128)(2,1)} fusion(s32[8192]{0:T(1024)S(1)} %bitcast.739, f32[1000,768]{1,0:T(8,128)S(1)} %copy-done.32), kind=kOutput, calls=%fused_computation.12 | convolution fusion | flops 12598163456 | bytes 15687680 | tf_op jit(solution)/shard_map/dot_general | solution.py:768
  128.3 66.7 %rows_scatter.1 = bf16[256,768]{1,0:T(8,128)(2,1)} custom-call(bf16[32,256,768]{2,1,0:T(8,128)(2,1)} %bitcast.685), custom_call_target="tpu_custom_call" | custom-call | tf_op jit(solution)/shard_map/rows_scatter/pallas_call | solution.py:402
  196.8 182.1 %weights_gather.1 = bf16[32,768,768]{2,1,0:T(8,128)(2,1)} custom-call(bf16[768,768]{1,0:T(8,128)(2,1)} %home_scatter.1.x_ref), custom_call_target="tpu_custom_call" | custom-call | tf_op jit(solution)/shard_map/weights_gather/pallas_call | solution.py:240
  378.9 25.7 %copy.238 = bf16[8,4,2,2,192,768]{5,4,1,3,0,2:T(8,128)(2,1)} copy(bf16[8,4,2,2,192,768]{5,4,3,2,1,0:T(8,128)(2,1)} %bitcast.606) | data formatting | bytes 75497472 | tf_op jit(solution)/shard_map/reshape | solution.py:761
  404.5 25.5 %fusion.323 = (bf16[1,8,2,4,192,768]{5,4,3,2,1,0:T(8,128)(2,1)}, bf16[1,8,2,4,192,768]{5,4,3,2,1,0:T(8,128)(2,1)}) fusion(bf16[2,8,2,4,192,768]{5,4,3,2,1,0:T(8,128)(2,1)} %bitcast.605), kind=kLoop, calls=%fused_computation.579 | loop fusion | bytes 75497472 | tf_op jit(solution)/shard_map/slice | solution.py:786
  442.0 26.1 %keys_gather.2 = bf16[4,256,1536]{2,1,0:T(8,128)(2,1)} custom-call(bf16[256,1536]{1,0:T(8,128)(2,1)} %pad_maximum_fusion.3.x_ref), custom_call_target="tpu_custom_call" | custom-call | tf_op jit(solution)/shard_map/keys_gather/pallas_call | solution.py:453
  491.2 6.9 fusion.176
  516.6 22.5 %keys_gather.3 = bf16[4,256,1536]{2,1,0:T(8,128)(2,1)} custom-call(bf16[256,1536]{1,0:T(8,128)(2,1)} %pad_maximum_fusion.4.x_ref), custom_call_target="tpu_custom_call" | custom-call | tf_op jit(solution)/shard_map/keys_gather/pallas_call | solution.py:453
  545.7 4.3 fusion.13
  555.7 7.2 fusion.175
  576.2 29.4 %chosen_gather.1 = bf16[32,96,768]{2,1,0:T(8,128)(2,1)} custom-call(bf16[96,768]{1,0:T(8,128)(2,1)} %convolution_convert_fusion.37.x_ref), custom_call_target="tpu_custom_call" | custom-call | tf_op jit(solution)/shard_map/chosen_gather/pallas_call | solution.py:240
  605.6 7.8 fusion.328
  613.5 4.4 copy-done.13
  621.9 21.2 %stats_gather.1 = f32[32,96,128]{2,1,0:T(8,128)} custom-call(f32[96,128]{1,0:T(8,128)} %fusion.254.x_ref), custom_call_target="tpu_custom_call" | custom-call | tf_op jit(solution)/shard_map/stats_gather/pallas_call | solution.py:240
  649.8 15.6 %multiply_reduce_fusion.3 = (f32[]{:T(128)}, f32[1000,768]{1,0:T(8,128)}) fusion(bf16[3072,768]{1,0:T(8,128)(2,1)} %bitcast.705, f32[3072,1000]{0,1:T(8,128)} %copy-done.13, f32[3072]{0:T(1024)S(1)} %get-tuple-element.56, s32[3072]{0:T(1024)S(1)} %copy-done.134, pred[3072]{0:T(1024)(128)(4,1)S(1)} %copy-done.153), kind=kOutput, calls=%fused_computation.88 | convolution fusion | flops 4741632000 | bytes 20106244 | tf_op jit(solution)/shard_map/rv,rd->vd/dot_general | solution.py:841
  665.4 9.0 convolution_convert_fusion
  674.4 30.5 %back_scatter.1 = bf16[96,768]{1,0:T(8,128)(2,1)} custom-call(bf16[32,96,768]{2,1,0:T(8,128)(2,1)} %bitcast.706), custom_call_target="tpu_custom_call" | custom-call | tf_op jit(solution)/shard_map/back_scatter/pallas_call | solution.py:402
  725.8 8.1 fusion.97
  739.2 7.4 fusion.330
  746.6 28.8 %fusion.167 = f32[256,12,64]{0,2,1:T(8,128)} fusion(bf16[1024,12,64]{0,2,1:T(8,128)(2,1)S(1)} %bitcast.702, f32[12,256,1024]{2,1,0:T(8,128)} %fusion.330, f32[12,256,1024]{2,1,0:T(8,128)} %copy-done.3, f32[12,256]{1,0:T(8,128)S(1)} %log_add_fusion, pred[256,1024]{1,0:T(8,128)(4,1)S(1)} %fusion.183), kind=kOutput, calls=%fused_computation.205 | convolution fusion | flops 437260288 | bytes 27799552 | tf_op jit(solution)/shard_map/hqk,khd->qhd/dot_general | solution.py:666
  775.4 35.1 %fusion.94 = bf16[1024,12,64]{0,2,1:T(8,128)(2,1)} fusion(f32[12,256,1024]{2,1,0:T(8,128)} %fusion.330, f32[12,256,1024]{2,1,0:T(8,128)} %copy-done.3, f32[12,256]{1,0:T(8,128)S(1)} %log_add_fusion, pred[256,1024]{1,0:T(8,128)(4,1)S(1)} %fusion.183, bf16[256,12,32]{0,2,1:T(8,128)(2,1)S(1)} %copy-done.54, bf16[256,12,32]{0,2,1:T(8,128)(2,1)S(1)} %copy-done.52), kind=kOutput, calls=%fused_computation.138 | convolution fusion | flops 438833152 | bytes 27406336 | tf_op jit(solution)/shard_map/hqk,qhd->khd/dot_general | solution.py:667
  817.4 21.4 %keys_reduce.2 = bf16[256,1536]{1,0:T(8,128)(2,1)S(1)} custom-call(bf16[4,256,1536]{2,1,0:T(8,128)(2,1)S(1)} %pad_maximum_fusion.p_ref), custom_call_target="tpu_custom_call" | custom-call | tf_op jit(solution)/shard_map/keys_reduce/pallas_call | solution.py:504
  865.1 7.9 fusion.100
  873.0 3.9 concatenate.79
  876.8 4.1 copy.198
  881.0 7.8 fusion.331
  888.8 34.1 %fusion.170 = f32[256,12,64]{0,2,1:T(8,128)} fusion(bf16[1024,12,64]{0,2,1:T(8,128)(2,1)} %bitcast.700, f32[12,256,1024]{2,1,0:T(8,128)} %fusion.331, f32[12,256,1024]{2,1,0:T(8,128)} %copy-done.2, f32[12,256]{1,0:T(8,128)S(1)} %copy-done.142, pred[256,1024]{1,0:T(8,128)(4,1)S(1)} %fusion.183), kind=kOutput, calls=%fused_computation.206 | convolution fusion | flops 437260288 | bytes 27799552 | tf_op jit(solution)/shard_map/hqk,khd->qhd/dot_general | solution.py:666
  922.9 34.5 %fusion.91 = bf16[1024,12,64]{0,2,1:T(8,128)(2,1)} fusion(f32[12,256,1024]{2,1,0:T(8,128)} %fusion.331, f32[12,256,1024]{2,1,0:T(8,128)} %copy-done.2, f32[12,256]{1,0:T(8,128)S(1)} %copy-done.142, pred[256,1024]{1,0:T(8,128)(4,1)S(1)} %fusion.183, bf16[256,12,32]{0,2,1:T(8,128)(2,1)S(1)} %copy-done.50, bf16[256,12,32]{0,2,1:T(8,128)(2,1)S(1)} %copy-done.48), kind=kOutput, calls=%fused_computation.137 | convolution fusion | flops 438833152 | bytes 27406336 | tf_op jit(solution)/shard_map/hqk,qhd->khd/dot_general | solution.py:667
  957.5 3.9 concatenate.78
  961.3 3.7 copy.197
  967.2 23.0 %keys_reduce.3 = bf16[256,1536]{1,0:T(8,128)(2,1)S(1)} custom-call(bf16[4,256,1536]{2,1,0:T(8,128)(2,1)S(1)} %pad_maximum_fusion.1.p_ref), custom_call_target="tpu_custom_call" | custom-call | tf_op jit(solution)/shard_map/keys_reduce/pallas_call | solution.py:504
  1005.9 70.0 %entry_gather.1 = bf16[32,256,768]{2,1,0:T(8,128)(2,1)} custom-call(bf16[256,768]{1,0:T(8,128)(2,1)} %fusion.222.x_ref), custom_call_target="tpu_custom_call" | custom-call | tf_op jit(solution)/shard_map/entry_gather/pallas_call | solution.py:240
  1075.9 21.3 %multiply_reduce_fusion.4 = (f32[]{:T(128)}, f32[1000,768]{1,0:T(8,128)}) fusion(bf16[8192,768]{1,0:T(8,128)(2,1)} %bitcast.684, s32[8192]{0:T(1024)} %bitcast.740), kind=kOutput, calls=%fused_computation.89 | convolution fusion | flops 12592640000 | bytes 15687684 | tf_op jit(solution)/shard_map/tv,td->vd/dot_general | solution.py:857
  1108.2 6.8 copy.200
  1115.0 96.8 %grads_scatter.2 = bf16[384,768]{1,0:T(8,128)(2,1)} custom-call(bf16[32,384,768]{2,1,0:T(8,128)(2,1)} %bitcast.677), custom_call_target="tpu_custom_call" | custom-call | tf_op jit(solution)/shard_map/grads_scatter/pallas_call | solution.py:402
  1220.4 6.8 copy.201
  1227.2 115.5 %grads_scatter.3 = bf16[384,768]{1,0:T(8,128)(2,1)} custom-call(bf16[32,384,768]{2,1,0:T(8,128)(2,1)} %bitcast.678), custom_call_target="tpu_custom_call" | custom-call | tf_op jit(solution)/shard_map/grads_scatter/pallas_call | solution.py:402
  1344.9 49.4 %owners_gather.1 = bf16[8,768,768]{2,1,0:T(8,128)(2,1)} custom-call(bf16[768,768]{1,0:T(8,128)(2,1)} %pad_maximum_fusion.2.x_ref), custom_call_target="tpu_custom_call" | custom-call | tf_op jit(solution)/shard_map/owners_gather/pallas_call | solution.py:240
  1394.3 8.4 copy.202
  1402.7 4.5 gather_fusion.3
  1411.5 49.0 %sums_gather.1 = f32[32,32,128]{2,1,0:T(8,128)} custom-call(f32[32,128]{1,0:T(8,128)} %fusion.259.x_ref), custom_call_target="tpu_custom_call" | custom-call | tf_op jit(solution)/shard_map/sums_gather/pallas_call | solution.py:240
  1464.9 8.8 fusion.316
  1476.7 6.0 fusion.318
  1484.5 6.7 fusion.320
  (632 shorter events, 219.2 us)
Async XLA Ops:
  12.0 426.2 %copy-start.131 = (f32[768]{0:T(1024)}, f32[768]{0:T(1024)S(1)}, u32[]{:S(2)}) copy-start(f32[768]{0:T(1024)S(1)} %get-tuple-element.37) | copy-start | bytes 9220
  12.0 489.4 %copy-start.125 = (f32[768]{0:T(1024)}, f32[768]{0:T(1024)S(1)}, u32[]{:S(2)}) copy-start(f32[768]{0:T(1024)S(1)} %get-tuple-element.36) | copy-start | bytes 9220
  12.2 827.8 %copy-start.45 = (f32[256,32]{0,1:T(8,128)}, f32[256,32]{0,1:T(8,128)S(1)}, u32[]{:S(2)}) copy-start(f32[256,32]{0,1:T(8,128)S(1)} %get-tuple-element.121) | copy-start | bytes 98308
  12.2 827.8 %copy-start.46 = (f32[256,32]{0,1:T(8,128)}, f32[256,32]{0,1:T(8,128)S(1)}, u32[]{:S(2)}) copy-start(f32[256,32]{0,1:T(8,128)S(1)} %get-tuple-element.122) | copy-start | bytes 98308
  36.6 74.0 %copy-start.137 = (s32[8,2,4,128]{3,1,2,0:T(2,128)}, s32[8,2,4,128]{3,1,2,0:T(2,128)S(1)}, u32[]{:S(2)}) copy-start(s32[8,2,4,128]{3,1,2,0:T(2,128)S(1)} %copy.210) | copy-start | bytes 98308
  61.3 49.3 %copy-start.32 = (f32[1000,768]{1,0:T(8,128)S(1)}, f32[1000,768]{1,0:T(8,128)}, u32[]{:S(2)}) copy-start(f32[1000,768]{1,0:T(8,128)} %param.27) | copy-start | bytes 9216004
  196.8 241.5 %copy-start.145 = (f32[256]{0:T(256)}, f32[256]{0:T(256)S(1)}, u32[]{:S(2)}) copy-start(f32[256]{0:T(256)S(1)} %get-tuple-element.124) | copy-start | bytes 3076
  404.5 25.5 %copy-start.18 = (bf16[256,768]{1,0:T(8,128)(2,1)S(1)}, bf16[256,768]{1,0:T(8,128)(2,1)}, u32[]{:S(2)}) copy-start(bf16[256,768]{1,0:T(8,128)(2,1)} %rows_scatter.1) | copy-start | bytes 1179652
  484.4 13.8 slice-start.10
  511.2 51.7 %copy-start.4 = (f32[256,768]{1,0:T(8,128)}, f32[256,768]{1,0:T(8,128)S(1)}, u32[]{:S(2)}) copy-start(f32[256,768]{1,0:T(8,128)S(1)} %get-tuple-element.146) | copy-start | bytes 2359300
  513.5 32.1 %copy-start.51 = (bf16[256,12,32]{0,2,1:T(8,128)(2,1)}, bf16[256,12,32]{0,2,1:T(8,128)(2,1)S(1)}, u32[]{:S(2)}) copy-start(bf16[256,12,32]{0,2,1:T(8,128)(2,1)S(1)} %get-tuple-element.97) | copy-start | bytes 589828
  513.5 32.1 %copy-start.53 = (bf16[256,12,32]{0,2,1:T(8,128)(2,1)}, bf16[256,12,32]{0,2,1:T(8,128)(2,1)S(1)}, u32[]{:S(2)}) copy-start(bf16[256,12,32]{0,2,1:T(8,128)(2,1)S(1)} %get-tuple-element.98) | copy-start | bytes 589828
  545.6 10.0 copy-start.21
  549.9 13.0 slice-start
  605.6 12.3 copy-start.134
  621.9 27.9 %copy-start.153 = (pred[3072]{0:T(1024)(128)(4,1)S(1)}, pred[3072]{0:T(1024)(128)(4,1)}, u32[]{:S(2)}) copy-start(pred[3072]{0:T(1024)(128)(4,1)} %ge.80) | copy-start | bytes 9220
  649.5 15.8 %slice-start.20 = ((s8[12288000]{0:T(1024)(128)(4,1)}), s8[4194304]{0:T(1024)(128)(4,1)S(1)}, s32[]{:S(2)}) async-start(s8[12288000]{0:T(1024)(128)(4,1)} %bitcast.688), calls=%async_computation.20 | async-start | bytes 8388608
  649.7 15.6 %slice-start.21 = ((s8[12288000]{0:T(1024)(128)(4,1)}), s8[4194304]{0:T(1024)(128)(4,1)S(1)}, s32[]{:S(2)}) async-start(s8[12288000]{0:T(1024)(128)(4,1)} %bitcast.688), calls=%async_computation.21 | async-start | bytes 8388608
  649.7 15.6 %slice-start.22 = ((s8[12288000]{0:T(1024)(128)(4,1)}), s8[3899392]{0:T(1024)(128)(4,1)S(1)}, s32[]{:S(2)}) async-start(s8[12288000]{0:T(1024)(128)(4,1)} %bitcast.688), calls=%async_computation.22 | async-start | bytes 7798784
  649.8 15.6 %copy-start.31 = (f32[1000,768]{1,0:T(8,128)S(1)}, f32[1000,768]{1,0:T(8,128)}, u32[]{:S(2)}) copy-start(f32[1000,768]{1,0:T(8,128)} %param.30) | copy-start | bytes 9216004
  665.4 39.5 %copy-start.136 = (pred[8,4,96]{2,0,1:T(8,128)(4,1)S(1)}, pred[8,4,96]{2,0,1:T(8,128)(4,1)}, u32[]{:S(2)}) copy-start(pred[8,4,96]{2,0,1:T(8,128)(4,1)} %copy-done.135) | copy-start | bytes 9220
  674.4 44.3 %slice-start.5 = ((s8[18874368]{0:T(1024)(128)(4,1)}), s8[2097152]{0:T(1024)(128)(4,1)S(1)}, s32[]{:S(2)}) async-start(s8[18874368]{0:T(1024)(128)(4,1)} %bitcast.631), calls=%async_computation.5 | async-start | bytes 4194304
  707.8 10.9 slice-start.6
  708.0 10.6 slice-start.7
  710.7 11.2 copy-start.92
  710.7 11.7 copy-start.88
  746.6 28.8 %copy-start.52 = (bf16[256,12,32]{0,2,1:T(8,128)(2,1)S(1)}, bf16[256,12,32]{0,2,1:T(8,128)(2,1)}, u32[]{:S(2)}) copy-start(bf16[256,12,32]{0,2,1:T(8,128)(2,1)} %copy-done.51) | copy-start | bytes 589828
  746.6 28.8 %copy-start.54 = (bf16[256,12,32]{0,2,1:T(8,128)(2,1)S(1)}, bf16[256,12,32]{0,2,1:T(8,128)(2,1)}, u32[]{:S(2)}) copy-start(bf16[256,12,32]{0,2,1:T(8,128)(2,1)} %copy-done.53) | copy-start | bytes 589828
  845.8 13.3 slice-start.15
  848.5 10.6 slice-start.16
  848.8 10.3 slice-start.17
  851.2 11.2 copy-start.108
  851.2 11.7 copy-start.104
  888.8 34.1 %copy-start.48 = (bf16[256,12,32]{0,2,1:T(8,128)(2,1)S(1)}, bf16[256,12,32]{0,2,1:T(8,128)(2,1)}, u32[]{:S(2)}) copy-start(bf16[256,12,32]{0,2,1:T(8,128)(2,1)} %get-tuple-element.101) | copy-start | bytes 589828
  888.8 34.1 %copy-start.50 = (bf16[256,12,32]{0,2,1:T(8,128)(2,1)S(1)}, bf16[256,12,32]{0,2,1:T(8,128)(2,1)}, u32[]{:S(2)}) copy-start(bf16[256,12,32]{0,2,1:T(8,128)(2,1)} %get-tuple-element.102) | copy-start | bytes 589828
  1115.0 96.8 %copy-start.25 = (bf16[256,768]{1,0:T(8,128)(2,1)S(1)}, bf16[256,768]{1,0:T(8,128)(2,1)}, u32[]{:S(2)}) copy-start(bf16[256,768]{1,0:T(8,128)(2,1)} %copy-done.24) | copy-start | bytes 1179652
  1115.0 96.8 %copy-start.39 = (bf16[256,12,64]{0,2,1:T(8,128)(2,1)S(1)}, bf16[256,12,64]{0,2,1:T(8,128)(2,1)}, u32[]{:S(2)}) copy-start(bf16[256,12,64]{0,2,1:T(8,128)(2,1)} %copy-done.38) | copy-start | bytes 1179652
  1115.0 97.4 %copy-start.30 = (bf16[256,12,64]{0,2,1:T(8,128)(2,1)S(1)}, bf16[256,12,64]{0,2,1:T(8,128)(2,1)}, u32[]{:S(2)}) copy-start(bf16[256,12,64]{0,2,1:T(8,128)(2,1)} %copy-done.29) | copy-start | bytes 1179652
  1227.2 115.5 %copy-start.37 = (bf16[384,768]{1,0:T(8,128)(2,1)S(1)}, bf16[384,768]{1,0:T(8,128)(2,1)}, u32[]{:S(2)}) copy-start(bf16[384,768]{1,0:T(8,128)(2,1)} %grads_scatter.2) | copy-start | bytes 1769476
  1394.3 12.9 copy-start.147
  1394.3 12.9 copy-start.148
  1394.3 16.5 %copy-start.127 = (f32[3840]{0:T(1024)S(1)}, f32[3840]{0:T(1024)}, u32[]{:S(2)}) copy-start(f32[3840]{0:T(1024)} %reshape.814) | copy-start | bytes 46084
  1402.7 61.5 %copy-start.133 = (f32[5,768]{1,0:T(8,128)S(1)}, f32[5,768]{1,0:T(8,128)}, u32[]{:S(2)}) copy-start(f32[5,768]{1,0:T(8,128)} %param.33) | copy-start | bytes 46084
  1402.7 61.5 %copy-start.138 = (f32[5,768]{1,0:T(8,128)S(1)}, f32[5,768]{1,0:T(8,128)}, u32[]{:S(2)}) copy-start(f32[5,768]{1,0:T(8,128)} %param.35) | copy-start | bytes 46084
  1402.7 61.5 %copy-start.139 = (f32[5,768]{1,0:T(8,128)S(1)}, f32[5,768]{1,0:T(8,128)}, u32[]{:S(2)}) copy-start(f32[5,768]{1,0:T(8,128)} %param.34) | copy-start | bytes 46084
  1464.9 10.1 copy-start.34
  1464.9 11.0 copy-start.35
  1464.9 11.8 copy-start.36
  (136 other events, 657.0 us)

commit v3 on v2

--- a/solution.py
+++ b/solution.py
@@ -47,29 +47,11 @@
     return (state_grad, gain_grad)
 
 
-def rope_tables(places, width):
-    half = width // 2
-    freqs = jnp.power(10000.0, -2.0 * jnp.arange(half).astype(jnp.float32) / width)
+def rope_tables(places):
+    freqs = jnp.power(10000.0, -2.0 * jnp.arange(HD // 2).astype(jnp.float32) / HD)
     angle = places[:, None] * freqs[None, :]
-    return (jnp.cos(angle), jnp.sin(angle))
-
-
-def rotate(field, cosine, sine):
-    half = field.shape[-1] // 2
-    first, second = (field[..., :half], field[..., half:])
-    cosine, sine = (cosine[:, None, :], sine[:, None, :])
-    return jnp.concatenate(
-        [first * cosine - second * sine, second * cosine + first * sine], axis=-1
-    )
-
-
-def rotate_back(field, cosine, sine):
-    half = field.shape[-1] // 2
-    first, second = (field[..., :half], field[..., half:])
-    cosine, sine = (cosine[:, None, :], sine[:, None, :])
-    return jnp.concatenate(
-        [first * cosine + second * sine, second * cosine - first * sine], axis=-1
-    )
+    cosine, sine = jnp.cos(angle), jnp.sin(angle)
+    return jnp.concatenate([cosine] * 4, axis=1), jnp.concatenate([-sine, sine] * 2, axis=1)
 
 
 def tile_slots(owners):
@@ -557,134 +539,409 @@
     return lax.psum_scatter(p, PART, scatter_dimension=0, tiled=True)
 
 
-def mm(x, w):
-    return jnp.einsum("ld,de->le", x, w, preferred_element_type=jnp.float32)
-
-
-def mm_t(x, w):
-    return jnp.einsum("le,de->ld", x, w, preferred_element_type=jnp.float32)
-
-
-def mm_g(x, y):
-    return jnp.einsum("ld,le->de", x, y, preferred_element_type=jnp.float32)
-
-
-def heads(x):
-    return x.reshape(x.shape[0], HEADS, HD)
-
-
-def layer_forward(state, tiles, gain_pair, cosine, sine, allowed):
+def tile_spec(layer, per, deep, tile_rows, index):
+    def place(t):
+        j = index(t)
+        return (j // per, 0, layer * per + j % per, 0, 0)
+
+    return pl.BlockSpec((None, deep, None, tile_rows, D), place)
+
+
+def whole(shape):
+    return pl.BlockSpec(shape, lambda t: (0,) * len(shape))
+
+
+def dot_nn(a, b):
+    return lax.dot_general(a, b, (((1,), (0,)), ((), ())), preferred_element_type=jnp.float32)
+
+
+def dot_nt(a, b):
+    return lax.dot_general(a, b, (((1,), (1,)), ((), ())), preferred_element_type=jnp.float32)
+
+
+def dot_tn(a, b):
+    return lax.dot_general(a, b, (((0,), (0,)), ((), ())), preferred_element_type=jnp.float32)
+
+
+def turned(u, cos, sin):
+    lane = lax.broadcasted_iota(jnp.int32, (u.shape[0], 128), 1)
+    low = (lane % HD) < HD // 2
+    parts = []
+    for i in range(D // 128):
+        v = u[:, i * 128 : (i + 1) * 128]
+        other = jnp.where(low, pltpu.roll(v, 128 - HD // 2, 1), pltpu.roll(v, HD // 2, 1))
+        parts.append(v * cos + other * sin)
+    return jnp.concatenate(parts, axis=1)
+
+
+def project_kernel(x_ref, g_ref, cos_ref, sin_ref, w_ref, q_ref, kv_ref, a_ref):
+    t = pl.program_id(0)
+
+    @pl.when(t == 0)
+    def _():
+        a_ref[...] = root_norm(x_ref[...], g_ref[...]).astype(jnp.bfloat16)
+
+    m = dot_nn(a_ref[...], w_ref[...].reshape(D, D))
+
+    @pl.when(t == 0)
+    def _():
+        q_ref[...] = turned(m, cos_ref[...], sin_ref[...]).astype(jnp.bfloat16)
+
+    @pl.when(t == 1)
+    def _():
+        kv_ref[...] = turned(m, cos_ref[...], sin_ref[...]).astype(jnp.bfloat16)
+
+    @pl.when(t == 2)
+    def _():
+        kv_ref[...] = m.astype(jnp.bfloat16)
+
+
+def project(x, gain, cos, sin, weights, layer, per):
+    rows = x.shape[0]
+    deep, tile_rows = weights.shape[1], weights.shape[3]
+    return pl.pallas_call(
+        project_kernel,
+        grid=(3,),
+        out_shape=(
+            jax.ShapeDtypeStruct((rows, D), jnp.bfloat16),
+            jax.ShapeDtypeStruct((2, rows, D), jnp.bfloat16),
+        ),
+        in_specs=[
+            whole((rows, D)), whole((1, D)), whole((rows, 128)), whole((rows, 128)),
+            tile_spec(layer, per, deep, tile_rows, lambda t: t),
+        ],
+        out_specs=(
+            whole((rows, D)),
+            pl.BlockSpec((None, rows, D), lambda t: (jnp.maximum(t - 1, 0), 0, 0)),
+        ),
+        scratch_shapes=[pltpu.VMEM((rows, D), jnp.bfloat16)],
+        compiler_params=pltpu.CompilerParams(vmem_limit_bytes=40 << 20),
+        name="project",
+    )(x, gain, cos, sin, weights)
+
+
+def mask_bias(bias_ref, kseg_ref, qseg_ref, qpos_ref):
+    kpos = lax.broadcasted_iota(jnp.int32, bias_ref.shape, 0)
+    allowed = (kpos <= qpos_ref[...]) & (kseg_ref[...] == qseg_ref[...])
+    bias_ref[...] = jnp.where(allowed, 0.0, MASKED)
+
+
+def head_lanes(shape, head):
+    return (lax.broadcasted_iota(jnp.int32, shape, 1) // HD) == head
+
+
+def attend_kernel(q_ref, k_ref, v_ref, kseg_ref, qseg_ref, qpos_ref, o_ref, lse_ref, bias_ref):
+    @pl.when(pl.program_id(0) == 0)
+    def _():
+        mask_bias(bias_ref, kseg_ref, qseg_ref, qpos_ref)
+
+    length = bias_ref.shape[0]
+    q = q_ref[...]
+    k, v = k_ref[...].reshape(length, 128), v_ref[...].reshape(length, 128)
+    outs = []
+    for head in range(2):
+        mine = head_lanes(q.shape, head)
+        s = dot_nt(k, jnp.where(mine, q, jnp.zeros_like(q))) * HD ** (-0.5) + bias_ref[...]
+        top = jnp.max(s, axis=0, keepdims=True)
+        e = jnp.exp(s - top)
+        total = jnp.sum(e, axis=0, keepdims=True)
+        p = (e * (1.0 / total)).astype(jnp.bfloat16)
+        outs.append(dot_tn(p, v))
+        lse_ref[head : head + 1, :] = top + jnp.log(total)
+    o_ref[...] = jnp.where(head_lanes(outs[0].shape, 0), outs[0], outs[1]).astype(jnp.bfloat16)
+
+
+def attend_specs(rows, parts):
+    length = parts * rows
+    pair = pl.BlockSpec((rows, 128), lambda t: (0, t))
+    return pair, [
+        pair,
+        pl.BlockSpec((parts, None, rows, 128), lambda t: (0, 0, 0, t)),
+        pl.BlockSpec((parts, None, rows, 128), lambda t: (0, 1, 0, t)),
+        whole((length, 1)), whole((1, rows)), whole((1, rows)),
+    ]
+
+
+def attend(q, kv, kseg, qseg, qpos):
+    rows, parts = q.shape[0], kv.shape[0]
+    pair, specs = attend_specs(rows, parts)
+    return pl.pallas_call(
+        attend_kernel,
+        grid=(HEADS // 2,),
+        out_shape=(
+            jax.ShapeDtypeStruct((rows, D), jnp.bfloat16),
+            jax.ShapeDtypeStruct((HEADS // 2, 8, rows), jnp.float32),
+        ),
+        in_specs=specs,
+        out_specs=(pair, pl.BlockSpec((None, 8, rows), lambda t: (t, 0, 0))),
+        scratch_shapes=[pltpu.VMEM((parts * rows, rows), jnp.float32)],
+        compiler_params=pltpu.CompilerParams(vmem_limit_bytes=40 << 20),
+        name="attend",
+    )(q, kv, kv, kseg, qseg, qpos)
+
+
+def feed_kernel(x_ref, o_ref, g_ref, wo_ref, wg_ref, wu_ref, wd_ref, mid_ref, out_ref, b_ref):
+    t = pl.program_id(0)
+
+    @pl.when(t == 0)
+    def _():
+        mid = x_ref[...] + dot_nn(o_ref[...], wo_ref[...].reshape(D, D))
+        mid_ref[...] = mid
+        out_ref[...] = mid
+        b_ref[...] = root_norm(mid, g_ref[...]).astype(jnp.bfloat16)
+
+    @pl.when(t > 0)
+    def _():
+        gate = dot_nn(b_ref[...], wg_ref[...].reshape(D, D))
+        up = dot_nn(b_ref[...], wu_ref[...].reshape(D, D))
+        h = (gate * jax.nn.sigmoid(gate) * up).astype(jnp.bfloat16)
+        out_ref[...] += dot_nn(h, wd_ref[...].reshape(D, D))
+
+
+def feed(x, o, gain, weights, layer, per):
+    rows = x.shape[0]
+    deep, tile_rows = weights.shape[1], weights.shape[3]
+    spec = functools.partial(tile_spec, layer, per, deep, tile_rows)
+    unit = lambda t: jnp.maximum(t - 1, 0)
+    state = jax.ShapeDtypeStruct((rows, D), jnp.float32)
+    return pl.pallas_call(
+        feed_kernel,
+        grid=(1 + UNITS,),
+        out_shape=(state, state),
+        in_specs=[
+            whole((rows, D)), whole((rows, D)), whole((1, D)),
+            spec(lambda t: 3 + 0 * t), spec(lambda t: 4 + unit(t)),
+            spec(lambda t: 4 + UNITS + unit(t)), spec(lambda t: 4 + 2 * UNITS + unit(t)),
+        ],
+        out_specs=(whole((rows, D)), whole((rows, D))),
+        scratch_shapes=[pltpu.VMEM((rows, D), jnp.bfloat16)],
+        compiler_params=pltpu.CompilerParams(vmem_limit_bytes=48 << 20),
+        name="feed",
+    )(x, o, gain, weights, weights, weights, weights)
+
+
+def feed_back_kernel(
+    dy_ref, mid_ref, g_ref, o_ref, wo_ref, wg_ref, wu_ref, wd_ref,
+    grad_ref, dx_ref, do_ref, dgain_ref,
+    b_ref, e_ref, dg_ref, du_ref, db_ref,
+):
+    t = pl.program_id(0)
+    last = pl.num_programs(0) - 1
+    deep, tile_rows = grad_ref.shape[0], grad_ref.shape[1]
+
+    def emit(g):
+        grad_ref[...] = g.astype(jnp.bfloat16).reshape(deep, tile_rows, D)
+
+    @pl.when(t == 0)
+    def _():
+        b_ref[...] = root_norm(mid_ref[...], g_ref[...]).astype(jnp.bfloat16)
+        e_ref[...] = dy_ref[...].astype(jnp.bfloat16)
+        db_ref[...] = jnp.zeros_like(db_ref)
+
+    @pl.when((t % 3 == 0) & (t < last))
+    def _():
+        gate = dot_nn(b_ref[...], wg_ref[...].reshape(D, D))
+        up = dot_nn(b_ref[...], wu_ref[...].reshape(D, D))
+        sigma = jax.nn.sigmoid(gate)
+        h = (gate * sigma * up).astype(jnp.bfloat16)
+        emit(dot_tn(h, e_ref[...]))
+        dh = dot_nt(e_ref[...], wd_ref[...].reshape(D, D))
+        dg_ref[...] = (dh * up * sigma * (1.0 + gate * (1.0 - sigma))).astype(jnp.bfloat16)
+        du_ref[...] = (dh * gate * sigma).astype(jnp.bfloat16)
+
+    @pl.when(t % 3 == 1)
+    def _():
+        emit(dot_tn(b_ref[...], dg_ref[...]))
+        db_ref[...] += dot_nt(dg_ref[...], wg_ref[...].reshape(D, D))
+
+    @pl.when(t % 3 == 2)
+    def _():
+        emit(dot_tn(b_ref[...], du_ref[...]))
+        db_ref[...] += dot_nt(du_ref[...], wu_ref[...].reshape(D, D))
+
+    @pl.when(t == last)
+    def _():
+        back, gain_back = norm_back(mid_ref[...], g_ref[...], db_ref[...])
+        dx = dy_ref[...] + back
+        dx_ref[...] = dx
+        dgain_ref[...] = jnp.broadcast_to(gain_back[None, :], dgain_ref.shape)
+        e1 = dx.astype(jnp.bfloat16)
+        emit(dot_tn(o_ref[...], e1))
+        do_ref[...] = dot_nt(e1, wo_ref[...].reshape(D, D)).astype(jnp.bfloat16)
+
+
+def feed_back(dy, mid, gain, o, weights, layer, per):
+    rows = dy.shape[0]
+    dp, deep, tile_rows = weights.shape[0], weights.shape[1], weights.shape[3]
+    spec = functools.partial(tile_spec, layer, per, deep, tile_rows)
+    unit = lambda t: jnp.minimum(t // 3, UNITS - 1)
+
+    def grad_tile(t):
+        kind = t % 3
+        base = jnp.where(kind == 0, 4 + 2 * UNITS, jnp.where(kind == 1, 4, 4 + UNITS))
+        return jnp.where(t == 3 * UNITS, 3, base + unit(t))
+
+    return pl.pallas_call(
+        feed_back_kernel,
+        grid=(3 * UNITS + 1,),
+        out_shape=(
+            jax.ShapeDtypeStruct((dp, deep, per, tile_rows, D), jnp.bfloat16),
+            jax.ShapeDtypeStruct((rows, D), jnp.float32),
+            jax.ShapeDtypeStruct((rows, D), jnp.bfloat16),
+            jax.ShapeDtypeStruct((8, D), jnp.float32),
+        ),
+        in_specs=[
+            whole((rows, D)), whole((rows, D)), whole((1, D)), whole((rows, D)),
+            spec(lambda t: 3 + 0 * t), spec(lambda t: 4 + unit(t)),
+            spec(lambda t: 4 + UNITS + unit(t)), spec(lambda t: 4 + 2 * UNITS + unit(t)),
+        ],
+        out_specs=(
+            tile_spec(0, per, deep, tile_rows, grad_tile),
+            whole((rows, D)), whole((rows, D)), whole((8, D)),
+        ),
+        scratch_shapes=[
+            pltpu.VMEM((rows, D), jnp.bfloat16), pltpu.VMEM((rows, D), jnp.bfloat16),
+            pltpu.VMEM((rows, D), jnp.bfloat16), pltpu.VMEM((rows, D), jnp.bfloat16),
+            pltpu.VMEM((rows, D), jnp.float32),
+        ],
+        compiler_params=pltpu.CompilerParams(vmem_limit_bytes=48 << 20),
+        name="feed_back",
+    )(dy, mid, gain, o, weights, weights, weights, weights)
+
+
+def attend_back_kernel(
+    q_ref, k_ref, v_ref, kseg_ref, qseg_ref, qpos_ref, do_ref, lse_ref, dq_ref, dkv_ref, bias_ref
+):
+    @pl.when(pl.program_id(0) == 0)
+    def _():
+        mask_bias(bias_ref, kseg_ref, qseg_ref, qpos_ref)
+
+    length = bias_ref.shape[0]
+    parts, rows = dkv_ref.shape[0], q_ref.shape[0]
+    q, do = q_ref[...], do_ref[...]
+    k, v = k_ref[...].reshape(length, 128), v_ref[...].reshape(length, 128)
+    dqs, dk, dv = [], None, None
+    for head in range(2):
+        mine = head_lanes(q.shape, head)
+        qm = jnp.where(mine, q, jnp.zeros_like(q))
+        dom = jnp.where(mine, do, jnp.zeros_like(do))
+        s = dot_nt(k, qm) * HD ** (-0.5) + bias_ref[...]
+        p = jnp.exp(s - lse_ref[head : head + 1, :])
+        dp = dot_nt(v, dom)
+        delta = jnp.sum(p * dp, axis=0, keepdims=True)
+        ds = (p * (dp - delta) * HD ** (-0.5)).astype(jnp.bfloat16)
+        dv_part = dot_nn(p.astype(jnp.bfloat16), dom)
+        dk_part = dot_nn(ds, qm)
+        dv = dv_part if dv is None else dv + dv_part
+        dk = dk_part if dk is None else dk + dk_part
+        dqs.append(dot_tn(ds, k))
+    dq_ref[...] = jnp.where(head_lanes(dqs[0].shape, 0), dqs[0], dqs[1])
+    dkv_ref[:, 0] = dk.astype(jnp.bfloat16).reshape(parts, rows, 128)
+    dkv_ref[:, 1] = dv.astype(jnp.bfloat16).reshape(parts, rows, 128)
+
+
+def attend_back(q, kv, kseg, qseg, qpos, do, lse):
+    rows, parts = q.shape[0], kv.shape[0]
+    pair, specs = attend_specs(rows, parts)
+    return pl.pallas_call(
+        attend_back_kernel,
+        grid=(HEADS // 2,),
+        out_shape=(
+            jax.ShapeDtypeStruct((rows, D), jnp.float32),
+            jax.ShapeDtypeStruct((parts, 2, rows, D), jnp.bfloat16),
+        ),
+        in_specs=specs + [pair, pl.BlockSpec((None, 8, rows), lambda t: (t, 0, 0))],
+        out_specs=(pair, pl.BlockSpec((parts, 2, rows, 128), lambda t: (0, 0, 0, t))),
+        scratch_shapes=[pltpu.VMEM((parts * rows, rows), jnp.float32)],
+        compiler_params=pltpu.CompilerParams(vmem_limit_bytes=48 << 20),
+        name="attend_back",
+    )(q, kv, kv, kseg, qseg, qpos, do, lse)
+
+
+def project_back_kernel(
+    dx_ref, x_ref, g_ref, cos_ref, sin_ref, dq_ref, dkv_ref, w_ref, held_ref,
+    grad_ref, out_ref, dgain_ref, a_ref, dm_ref, da_ref,
+):
+    t = pl.program_id(0)
+    deep, tile_rows = grad_ref.shape[0], grad_ref.shape[1]
+
+    @pl.when(t == 0)
+    def _():
+        a_ref[...] = root_norm(x_ref[...], g_ref[...]).astype(jnp.bfloat16)
+        da_ref[...] = jnp.zeros_like(da_ref)
+        dm_ref[...] = turned(dq_ref[...], cos_ref[...], -sin_ref[...]).astype(jnp.bfloat16)
+
+    @pl.when(t == 1)
+    def _():
+        dk = dkv_ref[0].astype(jnp.float32)
+        dm_ref[...] = turned(dk, cos_ref[...], -sin_ref[...]).astype(jnp.bfloat16)
+
+    @pl.when(t == 2)
+    def _():
+        dm_ref[...] = dkv_ref[1]
+
+    grad = dot_tn(a_ref[...], dm_ref[...])
+    grad_ref[...] = grad.astype(jnp.bfloat16).reshape(deep, tile_rows, D)
+    da_ref[...] += dot_nt(dm_ref[...], w_ref[...].reshape(D, D))
+
+    @pl.when(t == 2)
+    def _():
+        back, gain_back = norm_back(x_ref[...], g_ref[...], da_ref[...])
+        out_ref[...] = dx_ref[...] + back
+        dgain_ref[...] = jnp.broadcast_to(gain_back[None, :], dgain_ref.shape)
+
+
+def project_back(dx, x, gain, cos, sin, dq, dkv, weights, grads, layer, per):
+    rows = x.shape[0]
+    deep, tile_rows = weights.shape[1], weights.shape[3]
+    return pl.pallas_call(
+        project_back_kernel,
+        grid=(3,),
+        out_shape=(
+            jax.ShapeDtypeStruct(grads.shape, grads.dtype),
+            jax.ShapeDtypeStruct((rows, D), jnp.float32),
+            jax.ShapeDtypeStruct((8, D), jnp.float32),
+        ),
+        in_specs=[
+            whole((rows, D)), whole((rows, D)), whole((1, D)), whole((rows, 128)),
+            whole((rows, 128)), whole((rows, D)), whole((2, rows, D)),
+            tile_spec(layer, per, deep, tile_rows, lambda t: t),
+            pl.BlockSpec(memory_space=pl.ANY),
+        ],
+        out_specs=(
+            tile_spec(0, per, deep, tile_rows, lambda t: t), whole((rows, D)), whole((8, D)),
+        ),
+        scratch_shapes=[
+            pltpu.VMEM((rows, D), jnp.bfloat16), pltpu.VMEM((rows, D), jnp.bfloat16),
+            pltpu.VMEM((rows, D), jnp.float32),
+        ],
+        input_output_aliases={8: 0},
+        compiler_params=pltpu.CompilerParams(vmem_limit_bytes=40 << 20),
+        name="project_back",
+    )(dx, x, gain, cos, sin, dq, dkv, weights, grads)
+
+
+def layer_forward(state, weights, layer, per, gains, cos, sin, marks):
     rows = state.shape[0]
-    normed = root_norm(state, gain_pair[0]).astype(jnp.bfloat16)
-    query, keys, value = [mm(normed, tiles[i]) for i in range(3)]
-    query = rotate(heads(query), cosine, sine).astype(jnp.bfloat16)
-    keys = rotate(heads(keys), cosine, sine).astype(jnp.bfloat16).reshape(rows, D)
-    both = jnp.concatenate([keys, value.astype(jnp.bfloat16)], axis=1)
-    both = keys_all_gather(both)
-    keys_all, value_all = heads(both[:, :D]), heads(both[:, D:])
-    scores = jnp.einsum("qhd,khd->hqk", query, keys_all, preferred_element_type=jnp.float32) * HD ** (
-        -0.5
-    )
-    scores = jnp.where(allowed, scores, MASKED)
-    top = jnp.max(scores, axis=-1, keepdims=True)
-    exponent = jnp.exp(scores - top)
-    total = jnp.sum(exponent, axis=-1, keepdims=True)
-    prob = (exponent / total).astype(jnp.bfloat16)
-    log_total = top + jnp.log(total)
-    attended = jnp.einsum("hqk,khd->qhd", prob, value_all, preferred_element_type=jnp.float32)
-    attended = attended.reshape(rows, D).astype(jnp.bfloat16)
-    middle = state + mm(attended, tiles[3])
-    normed_feed = root_norm(middle, gain_pair[1]).astype(jnp.bfloat16)
-    gates = [mm(normed_feed, tiles[4 + i]) for i in range(UNITS)]
-    ups = [mm(normed_feed, tiles[4 + UNITS + i]) for i in range(UNITS)]
-    hidden = [(jax.nn.silu(g) * u).astype(jnp.bfloat16) for g, u in zip(gates, ups)]
-    output = middle + sum(mm(h, tiles[4 + 2 * UNITS + i]) for i, h in enumerate(hidden))
-    return output, (
-        state,
-        middle,
-        normed,
-        normed_feed,
-        query,
-        keys_all,
-        value_all,
-        log_total,
-        attended,
-        gates,
-        ups,
-        hidden,
-    )
-
-
-def layer_backward(grad, kept, tiles, gain_pair, cosine, sine, allowed):
-    (
-        state,
-        middle,
-        normed,
-        normed_feed,
-        query,
-        keys_all,
-        value_all,
-        log_total,
-        attended,
-        gates,
-        ups,
-        hidden,
-    ) = kept
+    q, kv = project(state, gains[2 * layer : 2 * layer + 1], cos, sin, weights, layer, per)
+    kv = keys_all_gather(kv.reshape(2 * rows, D)).reshape(-1, 2, rows, D)
+    o, lse = attend(q, kv, *marks)
+    mid, out = feed(state, o, gains[2 * layer + 1 : 2 * layer + 2], weights, layer, per)
+    return out, (state, mid, q, kv, lse, o)
+
+
+def layer_backward(grad, kept, weights, layer, per, gains, cos, sin, marks):
+    state, mid, q, kv, lse, o = kept
     rows = state.shape[0]
-    branch = grad.astype(jnp.bfloat16)
-    down_grads, gate_grads, up_grads = [], [], []
-    feed_back = 0.0
-    for i in range(UNITS):
-        down_grads.append(mm_g(hidden[i], branch))
-        hidden_grad = mm_t(branch, tiles[4 + 2 * UNITS + i])
-        sigma = jax.nn.sigmoid(gates[i])
-        gate_back = (hidden_grad * ups[i] * sigma * (1.0 + gates[i] * (1.0 - sigma))).astype(
-            jnp.bfloat16
-        )
-        up_back = (hidden_grad * gates[i] * sigma).astype(jnp.bfloat16)
-        gate_grads.append(mm_g(normed_feed, gate_back))
-        up_grads.append(mm_g(normed_feed, up_back))
-        feed_back = (
-            feed_back + mm_t(gate_back, tiles[4 + i]) + mm_t(up_back, tiles[4 + UNITS + i])
-        )
-    back, feed_gain = norm_back(middle, gain_pair[1], feed_back)
-    middle_grad = grad + back
-    branch = middle_grad.astype(jnp.bfloat16)
-    out_grad = mm_g(attended, branch)
-    heads_grad = heads(mm_t(branch, tiles[3]).astype(jnp.bfloat16))
-    scores = jnp.einsum("qhd,khd->hqk", query, keys_all, preferred_element_type=jnp.float32) * HD ** (
-        -0.5
-    )
-    prob = jnp.exp(jnp.where(allowed, scores, MASKED) - log_total)
-    value_part = jnp.einsum(
-        "hqk,qhd->khd", prob.astype(jnp.bfloat16), heads_grad, preferred_element_type=jnp.float32
-    )
-    prob_grad = jnp.einsum("qhd,khd->hqk", heads_grad, value_all, preferred_element_type=jnp.float32)
-    score_grad = (
-        prob * (prob_grad - jnp.sum(prob * prob_grad, axis=-1, keepdims=True)) * HD ** (-0.5)
-    ).astype(jnp.bfloat16)
-    query_grad = jnp.einsum("hqk,khd->qhd", score_grad, keys_all, preferred_element_type=jnp.float32)
-    keys_part = jnp.einsum("hqk,qhd->khd", score_grad, query, preferred_element_type=jnp.float32)
-    length = keys_part.shape[0]
-    both = jnp.concatenate([keys_part.reshape(length, D), value_part.reshape(length, D)], axis=1)
-    both = keys_sum_scatter(both.astype(jnp.bfloat16))
-    keys_grad, value_grad = both[:, :D].astype(jnp.float32), both[:, D:]
-    parts = [
-        rotate_back(query_grad, cosine, sine).reshape(rows, D).astype(jnp.bfloat16),
-        rotate_back(heads(keys_grad), cosine, sine).reshape(rows, D).astype(jnp.bfloat16),
-        value_grad,
-    ]
-    input_grads = [mm_g(normed, p) for p in parts]
-    back, attend_gain = norm_back(
-        state, gain_pair[0], sum(mm_t(p, tiles[i]) for i, p in enumerate(parts))
-    )
-    tiles_grad = jnp.stack(
-        [
-            t.astype(jnp.bfloat16)
-            for t in input_grads + [out_grad] + gate_grads + up_grads + down_grads
-        ]
-    )
-    return middle_grad + back, tiles_grad, [attend_gain, feed_gain]
+    grads, dx, do, feed_gain = feed_back(
+        grad, mid, gains[2 * layer + 1 : 2 * layer + 2], o, weights, layer, per
+    )
+    dq, dkv = attend_back(q, kv, *marks, do, lse)
+    dkv = keys_sum_scatter(dkv.reshape(-1, D)).reshape(2, rows, D)
+    grads, dx, input_gain = project_back(
+        dx, state, gains[2 * layer : 2 * layer + 1], cos, sin, dq, dkv, weights, grads, layer, per
+    )
+    return dx, grads, [input_gain[0], feed_gain[0]]
 
 
 def padded(v):
@@ -758,8 +1015,7 @@
     placed = jnp.where(home_mine[:, None, None], jnp.take(tile_low, home_slots, axis=0), 0)
     home = scatter_plane(placed.reshape(dp_size, -1, D), 7, "home_scatter")
     spread = gather_all(home, 1, "weights_gather")
-    spread = spread.reshape(dp_size, rep_size, LAYERS, per, tile_rows, D)
-    tiles = spread.transpose(2, 0, 3, 1, 4, 5).reshape(tile_count, D, D)
+    weights = spread.reshape(dp_size, rep_size, LAYERS * per, tile_rows, D)
 
     order = tokens_all.reshape(a_size, rep_size, b_size, rows).transpose(0, 2, 1, 3).reshape(-1)
     place = order - vocab_start
@@ -772,22 +1028,14 @@
 
     first_place = b_index * rows
     places = first_place + jnp.arange(rows)
-    cosine, sine = rope_tables(places.astype(jnp.float32), HD)
+    cosine, sine = rope_tables(places.astype(jnp.float32))
     own_segments = lax.dynamic_index_in_dim(segments_all, sequence, 0, False)
     query_segments = lax.dynamic_slice_in_dim(own_segments, first_place, rows)
-    allowed = (jnp.arange(length)[None, :] <= places[:, None]) & (
-        query_segments[:, None] == own_segments[None, :]
-    )
-    allowed = allowed[None]
+    marks = (own_segments[:, None], query_segments[None, :], places[None, :])
     kept_list = []
     for index in range(LAYERS):
         state, kept = layer_forward(
-            state,
-            tiles[index * TILES_PER : (index + 1) * TILES_PER],
-            gain_weight[2 * index : 2 * index + 2],
-            cosine,
-            sine,
-            allowed,
+            state, weights, index, per, gain_weight, cosine, sine, marks
         )
         kept_list.append(kept)
     final_gain = gain_weight[2 * LAYERS]
@@ -845,13 +1093,7 @@
     gain_parts = [None] * LAYERS
     for index in reversed(range(LAYERS)):
         state_grad, tile_parts[index], gain_parts[index] = layer_backward(
-            state_grad,
-            kept_list[index],
-            tiles[index * TILES_PER : (index + 1) * TILES_PER],
-            gain_weight[2 * index : 2 * index + 2],
-            cosine,
-            sine,
-            allowed,
+            state_grad, kept_list[index], weights, index, per, gain_weight, cosine, sine, marks
         )
     piece_grads = gather_all(state_grad.astype(jnp.bfloat16), 2, "entry_gather").reshape(-1, D)
     table_grad = jnp.einsum(
@@ -859,8 +1101,7 @@
     )
     home_grads = []
     for index in range(LAYERS):
-        part = tile_parts[index].reshape(dp_size, per, rep_size, tile_rows, D)
-        part = part.transpose(0, 2, 1, 3, 4).reshape(devices, -1, D)
+        part = tile_parts[index].reshape(devices, -1, D)
         home_grads.append(scatter_all(part, 10, "grads_scatter"))
     plane_grad = gather_plane(jnp.concatenate(home_grads), 6, "owners_gather")
     plane_grad = plane_grad.reshape(dp_size, LAYERS, per, tile_rows, D)

time: 1500 us -> 1240 us (0.83)
  matrix products: 347 us -> 73.7 us
  Pallas kernels: 875 us -> 1030 us
  local copies, waits for them, and re-layouts: 178 us -> 51.7 us
  other arithmetic: 82.7 us -> 66.1 us
    dot_general x108 -> x0, matrix products: 273 us -> none  [the longest x2 69.7 us: layer_backward(): jnp.einsum('hqk,qhd->khd', score_grad, query, preferred_element_type=jnp....]
    pallas_call x0 -> x12, Pallas kernels: none -> 146 us  [the longest x2 50.7 us: feed_back(): pl.pallas_call(feed_back_kernel, grid=(3 * UNITS + 1,), out_shape=(jax.Sh...]
    reshape x5 -> x0, local copies, waits for them, and re-layouts: 42.7 us -> none  [the longest x1 25.7 us: shards(): spread = spread.reshape(dp_size, rep_size, LAYERS, per, tile_rows, D)]
    slice x8 -> x5, local copies, waits for them, and re-layouts: 39.8 us -> 0.3 us  [the longest x1 25.5 us: shards(): tiles[index * TILES_PER:(index + 1) * TILES_PER]]
    concatenate x8 -> x0, local copies, waits for them, and re-layouts: 26.1 us -> none  [layer_backward(): jnp.concatenate([keys_part.reshape(length, D), value_part.reshape(length,...]
where the time goes in v3:
time: 1240 us; the launch traced here: 1230 us
  Pallas kernels  1030 us (83%)
  matrix products  73.7 us (6%)
  other arithmetic  66.1 us (5%)
  local copies, waits for them, and re-layouts  51.7 us (4%)
    pallas_call x7, Pallas kernels, all_gather(): pl.pallas_call(functools.partial(gather_kernel, zn), out_shape=jax.ShapeD...  422 us
    pallas_call x5, Pallas kernels, reduce_scatter(): pl.pallas_call(functools.partial(reduce_kernel, zn), out_shape=jax.ShapeD...  366 us
    pallas_call x2, Pallas kernels, feed_back(): pl.pallas_call(feed_back_kernel, grid=(3 * UNITS + 1,), out_shape=(jax.Sh...  50.7 us
    pallas_call x2, Pallas kernels, keys_gather(): pl.pallas_call(keys_gather_kernel, out_shape=jax.ShapeDtypeStruct((4,) +...  48.6 us
    pallas_call x2, Pallas kernels, keys_reduce(): pl.pallas_call(keys_reduce_kernel, out_shape=jax.ShapeDtypeStruct(block,...  44.4 us
    pallas_call x2, Pallas kernels, attend_back(): pl.pallas_call(attend_back_kernel, grid=(HEADS // 2,), out_shape=(jax.Sha...  27.6 us
    pallas_call x2, Pallas kernels, attend(): pl.pallas_call(attend_kernel, grid=(HEADS // 2,), out_shape=(jax.ShapeDty...  26.3 us

profile of v3, /device:TPU:0, one launch (start us, length us, event | category | flops | bytes accessed | tf_op | source)
XLA Modules:
  0.0 1228.3 jit_solution(14390951802911497671)
XLA Ops:
  12.7 22.7 %ids_gather.1 = s32[32,32,128]{2,1,0:T(8,128)} custom-call(s32[32,128]{1,0:T(8,128)} %pad_bitcast_fusion.x_ref), custom_call_target="tpu_custom_call" | custom-call | tf_op jit(solution)/shard_map/ids_gather/pallas_call | solution.py:222
  37.4 2.3 reduce-window.6
  44.6 3.4 convert_element_type.85
  48.0 6.8 gather_fusion.2
  54.8 9.8 fusion.5.p_ref
  64.6 49.3 %home_scatter.1.x_ref = bf16[768,768]{1,0:T(8,128)(2,1)} custom-call(bf16[8,768,768]{2,1,0:T(8,128)(2,1)} %fusion.5.p_ref), custom_call_target="tpu_custom_call" | custom-call | tf_op jit(solution)/shard_map/home_scatter/pallas_call | solution.py:384
  114.0 17.5 %fusion.4 = bf16[8192,768]{1,0:T(8,128)(2,1)} fusion(s32[8192]{0:T(1024)S(1)} %bitcast.165, f32[1000,768]{1,0:T(8,128)S(1)} %copy-done.29), kind=kOutput, calls=%fused_computation.9 | convolution fusion | flops 12598163456 | bytes 15687680 | tf_op jit(solution)/shard_map/dot_general | solution.py:1024
  131.5 66.5 %rows_scatter.1 = bf16[256,768]{1,0:T(8,128)(2,1)} custom-call(bf16[32,256,768]{2,1,0:T(8,128)(2,1)} %bitcast.145), custom_call_target="tpu_custom_call" | custom-call | tf_op jit(solution)/shard_map/rows_scatter/pallas_call | solution.py:384
  199.1 182.1 %weights_gather.1 = bf16[32,768,768]{2,1,0:T(8,128)(2,1)} custom-call(bf16[768,768]{1,0:T(8,128)(2,1)} %home_scatter.1.x_ref), custom_call_target="tpu_custom_call" | custom-call | tf_op jit(solution)/shard_map/weights_gather/pallas_call | solution.py:222
  381.2 4.3 project.2
  386.4 26.1 %keys_gather.2 = bf16[4,512,768]{2,1,0:T(8,128)(2,1)} custom-call(bf16[512,768]{1,0:T(8,128)(2,1)} %bitcast.117), custom_call_target="tpu_custom_call" | custom-call | tf_op jit(solution)/shard_map/keys_gather/pallas_call | solution.py:435
  412.5 1.9 copy-done.2
  414.4 13.1 %attend.2 = (bf16[256,768]{1,0:T(8,128)(2,1)S(1)}, f32[6,8,256]{2,1,0:T(8,128)S(1)}) custom-call(bf16[256,768]{1,0:T(8,128)(2,1)S(1)} %get-tuple-element.47.q_ref, bf16[4,2,256,768]{3,2,1,0:T(8,128)(2,1)S(1)} %bitcast.107, bf16[4,2,256,768]{3,2,1,0:T(8,128)(2,1)S(1)} %bitcast.108, s32[1024,1]{1,0:T(8,128)S(1)} %copy.110.kseg_ref, ...), custom_call_target="tpu_custom_call" | custom-call | tf_op jit(solution)/shard_map/attend/pallas_call | solution.py:668
  428.2 9.7 feed.2
  438.0 4.6 project.3
  443.4 22.5 %keys_gather.3 = bf16[4,512,768]{2,1,0:T(8,128)(2,1)} custom-call(bf16[512,768]{1,0:T(8,128)(2,1)} %bitcast.118), custom_call_target="tpu_custom_call" | custom-call | tf_op jit(solution)/shard_map/keys_gather/pallas_call | solution.py:435
  467.8 13.2 %attend.3 = (bf16[256,768]{1,0:T(8,128)(2,1)S(1)}, f32[6,8,256]{2,1,0:T(8,128)S(1)}) custom-call(bf16[256,768]{1,0:T(8,128)(2,1)S(1)} %get-tuple-element.51.q_ref, bf16[4,2,256,768]{3,2,1,0:T(8,128)(2,1)S(1)} %bitcast.111, bf16[4,2,256,768]{3,2,1,0:T(8,128)(2,1)S(1)} %bitcast.112, s32[1024,1]{1,0:T(8,128)S(1)} %copy.110.kseg_ref, ...), custom_call_target="tpu_custom_call" | custom-call | tf_op jit(solution)/shard_map/attend/pallas_call | solution.py:668
  481.6 9.8 feed.3
  494.5 41.5 %chosen_gather.1 = bf16[32,96,768]{2,1,0:T(8,128)(2,1)} custom-call(bf16[96,768]{1,0:T(8,128)(2,1)} %convolution_convert_fusion.1.x_ref), custom_call_target="tpu_custom_call" | custom-call | tf_op jit(solution)/shard_map/chosen_gather/pallas_call | solution.py:222
  535.9 7.8 fusion.54
  543.8 3.3 exponential_reduce_fusion
  548.8 21.2 %stats_gather.1 = f32[32,96,128]{2,1,0:T(8,128)} custom-call(f32[96,128]{1,0:T(8,128)} %fusion.23.x_ref), custom_call_target="tpu_custom_call" | custom-call | tf_op jit(solution)/shard_map/stats_gather/pallas_call | solution.py:222
  570.0 2.3 copy.153
  573.4 2.8 reshape.503
  576.2 4.0 slice_reduce_fusion
  581.0 15.8 %multiply_reduce_fusion.1 = (f32[]{:T(128)}, f32[1000,768]{1,0:T(8,128)}) fusion(bf16[3072,768]{1,0:T(8,128)(2,1)} %bitcast.151, f32[3072,1000]{0,1:T(8,128)} %copy-done.25, f32[3072]{0:T(1024)S(1)} %get-tuple-element.101, s32[3072]{0:T(1024)} %sub.129, pred[3072]{0:T(1024)(128)(4,1)} %ge.80), kind=kOutput, calls=%fused_computation.37 | convolution fusion | flops 4741632000 | bytes 20106244 | tf_op jit(solution)/shard_map/rv,rd->vd/dot_general | solution.py:1089
  596.8 8.8 convolution_convert_fusion
  605.6 31.2 %back_scatter.1 = bf16[96,768]{1,0:T(8,128)(2,1)} custom-call(bf16[32,96,768]{2,1,0:T(8,128)(2,1)} %bitcast.152), custom_call_target="tpu_custom_call" | custom-call | tf_op jit(solution)/shard_map/back_scatter/pallas_call | solution.py:384
  643.3 25.4 %feed_back.2 = (bf16[8,4,2,192,768]{4,3,2,1,0:T(8,128)(2,1)}, f32[256,768]{1,0:T(8,128)S(1)}, bf16[256,768]{1,0:T(8,128)(2,1)S(1)}, f32[8,768]{1,0:T(8,128)S(1)}) custom-call(f32[256,768]{1,0:T(8,128)S(1)} %multiply_subtract_fusion.2.dy_ref, f32[256,768]{1,0:T(8,128)S(1)} %copy-done.13, f32[1,768]{1,0:T(1,128)S(1)} %get-tuple-element.113.g_ref, ...), custom_call_target="tpu_custom_call" | custom-call | tf_op jit(solution)/shard_map/feed_back/pallas_call | solution.py:784
  668.7 13.8 %attend_back.2 = (f32[256,768]{1,0:T(8,128)S(1)}, bf16[4,2,256,768]{3,2,1,0:T(8,128)(2,1)S(1)}) custom-call(bf16[256,768]{1,0:T(8,128)(2,1)S(1)} %get-tuple-element.51.q_ref, bf16[4,2,256,768]{3,2,1,0:T(8,128)(2,1)} %bitcast.109, bf16[4,2,256,768]{3,2,1,0:T(8,128)(2,1)} %bitcast.110, s32[1024,1]{1,0:T(8,128)S(1)} %copy.110.kseg_ref, ...), custom_call_target="tpu_custom_call" | custom-call | tf_op jit(solution)/shard_map/attend_back/pallas_call | solution.py:846
  682.5 21.2 %keys_reduce.2 = bf16[512,768]{1,0:T(8,128)(2,1)S(1)} custom-call(bf16[4,512,768]{2,1,0:T(8,128)(2,1)S(1)} %bitcast.116), custom_call_target="tpu_custom_call" | custom-call | tf_op jit(solution)/shard_map/keys_reduce/pallas_call | solution.py:486
  703.8 6.7 project_back.2
  710.5 99.0 %grads_scatter.3 = bf16[384,768]{1,0:T(8,128)(2,1)} custom-call(bf16[32,384,768]{2,1,0:T(8,128)(2,1)} %bitcast.140), custom_call_target="tpu_custom_call" | custom-call | tf_op jit(solution)/shard_map/grads_scatter/pallas_call | solution.py:384
  809.5 25.3 %feed_back.3 = (bf16[8,4,2,192,768]{4,3,2,1,0:T(8,128)(2,1)}, f32[256,768]{1,0:T(8,128)S(1)}, bf16[256,768]{1,0:T(8,128)(2,1)S(1)}, f32[8,768]{1,0:T(8,128)S(1)}) custom-call(f32[256,768]{1,0:T(8,128)S(1)} %get-tuple-element.62.dy_ref, f32[256,768]{1,0:T(8,128)S(1)} %copy-done.11, f32[1,768]{1,0:T(1,128)S(1)} %copy-done.23, bf16[256,768]{1,0:T(8,128)(2,1)S(1)} %copy-done.7, ...), custom_call_target="tpu_custom_call" | custom-call | tf_op jit(solution)/shard_map/feed_back/pallas_call | solution.py:784
  834.9 13.8 %attend_back.3 = (f32[256,768]{1,0:T(8,128)S(1)}, bf16[4,2,256,768]{3,2,1,0:T(8,128)(2,1)S(1)}) custom-call(bf16[256,768]{1,0:T(8,128)(2,1)S(1)} %copy-done.5, bf16[4,2,256,768]{3,2,1,0:T(8,128)(2,1)} %bitcast.105, bf16[4,2,256,768]{3,2,1,0:T(8,128)(2,1)} %bitcast.106, s32[1024,1]{1,0:T(8,128)S(1)} %copy.110.kseg_ref, s32[1,256]{1,0:T(1,128)S(1)} %dynamic_slice.36.qseg_ref, ...), custom_call_target="tpu_custom_call" | custom-call | tf_op jit(solution)/shard_map/attend_back/pallas_call | solution.py:846
  848.7 23.1 %keys_reduce.3 = bf16[512,768]{1,0:T(8,128)(2,1)S(1)} custom-call(bf16[4,512,768]{2,1,0:T(8,128)(2,1)S(1)} %bitcast.115), custom_call_target="tpu_custom_call" | custom-call | tf_op jit(solution)/shard_map/keys_reduce/pallas_call | solution.py:486
  871.9 6.7 project_back.3
  878.6 120.1 %grads_scatter.2 = bf16[384,768]{1,0:T(8,128)(2,1)} custom-call(bf16[32,384,768]{2,1,0:T(8,128)(2,1)} %bitcast.139), custom_call_target="tpu_custom_call" | custom-call | tf_op jit(solution)/shard_map/grads_scatter/pallas_call | solution.py:384
  998.7 2.2 pad_maximum_fusion.x_ref
  1001.7 47.0 %owners_gather.1 = bf16[8,768,768]{2,1,0:T(8,128)(2,1)} custom-call(bf16[768,768]{1,0:T(8,128)(2,1)} %pad_maximum_fusion.x_ref), custom_call_target="tpu_custom_call" | custom-call | tf_op jit(solution)/shard_map/owners_gather/pallas_call | solution.py:222
  1048.7 8.3 copy.118
  1057.0 4.5 gather_fusion.3
  1063.1 88.8 %entry_gather.1 = bf16[32,256,768]{2,1,0:T(8,128)(2,1)} custom-call(bf16[256,768]{1,0:T(8,128)(2,1)} %convert_element_type.93.x_ref), custom_call_target="tpu_custom_call" | custom-call | tf_op jit(solution)/shard_map/entry_gather/pallas_call | solution.py:222
  1151.9 21.3 %multiply_reduce_fusion.2 = (f32[]{:T(128)}, f32[1000,768]{1,0:T(8,128)}) fusion(bf16[8192,768]{1,0:T(8,128)(2,1)} %bitcast.144, s32[8192]{0:T(1024)S(1)} %bitcast.166), kind=kOutput, calls=%fused_computation.38 | convolution fusion | flops 12592640000 | bytes 15687684 | tf_op jit(solution)/shard_map/tv,td->vd/dot_general | solution.py:1099
  1175.9 19.0 %sums_gather.1 = f32[32,32,128]{2,1,0:T(8,128)} custom-call(f32[32,128]{1,0:T(8,128)} %fusion.29.x_ref), custom_call_target="tpu_custom_call" | custom-call | tf_op jit(solution)/shard_map/sums_gather/pallas_call | solution.py:222
  1199.3 8.8 fusion.46
  1211.2 6.0 fusion.48
  1219.0 6.7 fusion.50
  (210 shorter events, 47.4 us)
Async XLA Ops:
  0.7 1.6 copy-start
  11.9 369.2 %copy-start.20 = (f32[1,768]{1,0:T(1,128)}, f32[1,768]{1,0:T(1,128)S(1)}, u32[]{:S(2)}) copy-start(f32[1,768]{1,0:T(1,128)S(1)} %get-tuple-element.116.g_ref) | copy-start | bytes 9220
  11.9 416.3 %copy-start.22 = (f32[1,768]{1,0:T(1,128)}, f32[1,768]{1,0:T(1,128)S(1)}, u32[]{:S(2)}) copy-start(f32[1,768]{1,0:T(1,128)S(1)} %get-tuple-element.115.g_ref) | copy-start | bytes 9220
  37.1 76.9 %copy-start.40 = (s32[8,2,4,128]{3,1,2,0:T(2,128)}, s32[8,2,4,128]{3,1,2,0:T(2,128)S(1)}, u32[]{:S(2)}) copy-start(s32[8,2,4,128]{3,1,2,0:T(2,128)S(1)} %copy.126) | copy-start | bytes 98308
  42.5 12.3 %copy-start.39 = (pred[8,4,96]{2,0,1:T(8,128)(4,1)}, pred[8,4,96]{2,0,1:T(8,128)(4,1)S(1)}, u32[]{:S(2)}) copy-start(pred[8,4,96]{2,0,1:T(8,128)(4,1)S(1)} %get-tuple-element.120) | copy-start | bytes 9220
  64.6 49.3 %copy-start.29 = (f32[1000,768]{1,0:T(8,128)S(1)}, f32[1000,768]{1,0:T(8,128)}, u32[]{:S(2)}) copy-start(f32[1000,768]{1,0:T(8,128)} %param.27) | copy-start | bytes 9216004
  385.5 0.9 copy-start.14
  386.4 41.2 %copy-start.4 = (bf16[256,768]{1,0:T(8,128)(2,1)}, bf16[256,768]{1,0:T(8,128)(2,1)S(1)}, u32[]{:S(2)}) copy-start(bf16[256,768]{1,0:T(8,128)(2,1)S(1)} %get-tuple-element.47.q_ref) | copy-start | bytes 1179652
  412.5 1.9 copy-start.2
  428.2 9.8 copy-start.6
  438.0 4.6 copy-start.10
  465.9 1.9 copy-start.3
  481.6 9.8 copy-start.8
  481.6 11.9 copy-start.35
  481.6 11.9 copy-start.48
  535.9 7.8 copy-start.37
  543.8 4.4 copy-start.25
  580.1 16.6 %slice-start = ((s8[12288000]{0:T(1024)(128)(4,1)}), s8[4194304]{0:T(1024)(128)(4,1)S(1)}, s32[]{:S(2)}) async-start(s8[12288000]{0:T(1024)(128)(4,1)} %bitcast.146), calls=%async_computation | async-start | bytes 8388608
  580.9 15.8 %slice-start.1 = ((s8[12288000]{0:T(1024)(128)(4,1)}), s8[4194304]{0:T(1024)(128)(4,1)S(1)}, s32[]{:S(2)}) async-start(s8[12288000]{0:T(1024)(128)(4,1)} %bitcast.146), calls=%async_computation.1 | async-start | bytes 8388608
  580.9 15.8 %slice-start.2 = ((s8[12288000]{0:T(1024)(128)(4,1)}), s8[3899392]{0:T(1024)(128)(4,1)S(1)}, s32[]{:S(2)}) async-start(s8[12288000]{0:T(1024)(128)(4,1)} %bitcast.146), calls=%async_computation.2 | async-start | bytes 7798784
  580.9 15.8 %copy-start.28 = (f32[1000,768]{1,0:T(8,128)S(1)}, f32[1000,768]{1,0:T(8,128)}, u32[]{:S(2)}) copy-start(f32[1000,768]{1,0:T(8,128)} %param.30) | copy-start | bytes 9216004
  580.9 15.8 %copy-start.38 = (s32[3072]{0:T(1024)S(1)}, s32[3072]{0:T(1024)}, u32[]{:S(2)}) copy-start(s32[3072]{0:T(1024)} %sub.129) | copy-start | bytes 36868
  580.9 15.8 %copy-start.49 = (pred[3072]{0:T(1024)(128)(4,1)S(1)}, pred[3072]{0:T(1024)(128)(4,1)}, u32[]{:S(2)}) copy-start(pred[3072]{0:T(1024)(128)(4,1)} %ge.80) | copy-start | bytes 9220
  640.2 3.0 copy-start.9
  640.2 3.0 copy-start.13
  643.3 25.4 %copy-start.19 = (f32[6,8,256]{2,1,0:T(8,128)S(1)}, f32[6,8,256]{2,1,0:T(8,128)}, u32[]{:S(2)}) copy-start(f32[6,8,256]{2,1,0:T(8,128)} %copy-done.18) | copy-start | bytes 147460
  710.5 99.0 %copy-start.7 = (bf16[256,768]{1,0:T(8,128)(2,1)S(1)}, bf16[256,768]{1,0:T(8,128)(2,1)}, u32[]{:S(2)}) copy-start(bf16[256,768]{1,0:T(8,128)(2,1)} %copy-done.6) | copy-start | bytes 1179652
  710.5 99.0 %copy-start.11 = (f32[256,768]{1,0:T(8,128)S(1)}, f32[256,768]{1,0:T(8,128)}, u32[]{:S(2)}) copy-start(f32[256,768]{1,0:T(8,128)} %copy-done.10) | copy-start | bytes 2359300
  710.5 99.0 %copy-start.23 = (f32[1,768]{1,0:T(1,128)S(1)}, f32[1,768]{1,0:T(1,128)}, u32[]{:S(2)}) copy-start(f32[1,768]{1,0:T(1,128)} %copy-done.22) | copy-start | bytes 9220
  809.5 25.3 %copy-start.5 = (bf16[256,768]{1,0:T(8,128)(2,1)S(1)}, bf16[256,768]{1,0:T(8,128)(2,1)}, u32[]{:S(2)}) copy-start(bf16[256,768]{1,0:T(8,128)(2,1)} %copy-done.4) | copy-start | bytes 1179652
  809.5 25.3 %copy-start.17 = (f32[6,8,256]{2,1,0:T(8,128)S(1)}, f32[6,8,256]{2,1,0:T(8,128)}, u32[]{:S(2)}) copy-start(f32[6,8,256]{2,1,0:T(8,128)} %copy-done.16) | copy-start | bytes 147460
  848.7 23.2 %copy-start.21 = (f32[1,768]{1,0:T(1,128)S(1)}, f32[1,768]{1,0:T(1,128)}, u32[]{:S(2)}) copy-start(f32[1,768]{1,0:T(1,128)} %copy-done.20) | copy-start | bytes 9220
  878.6 120.1 %copy-start.34 = (bf16[384,768]{1,0:T(8,128)(2,1)S(1)}, bf16[384,768]{1,0:T(8,128)(2,1)}, u32[]{:S(2)}) copy-start(bf16[384,768]{1,0:T(8,128)(2,1)} %grads_scatter.3) | copy-start | bytes 1769476
  878.6 122.2 %copy-start.45 = (f32[1,768]{1,0:T(1,128)S(1)}, f32[1,768]{1,0:T(1,128)}, u32[]{:S(2)}) copy-start(f32[1,768]{1,0:T(1,128)} %stack.6) | copy-start | bytes 9220
  1057.0 4.5 copy-start.46
  1057.0 4.5 copy-start.47
  1063.1 88.8 %copy-start.41 = (s32[8,2,4,128]{3,1,2,0:T(2,128)S(1)}, s32[8,2,4,128]{3,1,2,0:T(2,128)}, u32[]{:S(2)}) copy-start(s32[8,2,4,128]{3,1,2,0:T(2,128)} %copy-done.40) | copy-start | bytes 98308
  1151.9 46.7 %copy-start.36 = (f32[5,768]{1,0:T(8,128)S(1)}, f32[5,768]{1,0:T(8,128)}, u32[]{:S(2)}) copy-start(f32[5,768]{1,0:T(8,128)} %param.33) | copy-start | bytes 46084
  1151.9 46.7 %copy-start.42 = (f32[5,768]{1,0:T(8,128)S(1)}, f32[5,768]{1,0:T(8,128)}, u32[]{:S(2)}) copy-start(f32[5,768]{1,0:T(8,128)} %param.35) | copy-start | bytes 46084
  1151.9 46.7 %copy-start.43 = (f32[5,768]{1,0:T(8,128)S(1)}, f32[5,768]{1,0:T(8,128)}, u32[]{:S(2)}) copy-start(f32[5,768]{1,0:T(8,128)} %param.34) | copy-start | bytes 46084
  1199.3 8.8 copy-start.30
  1199.3 10.1 copy-start.31
  1199.3 11.0 copy-start.32
  1199.3 11.8 copy-start.33
  1211.2 6.0 copy-start.24
  1211.2 6.4 copy-start.26
  1211.2 7.8 copy-start.27
  1218.9 6.7 copy-start.1
  (5 other events, 3.6 us)

commit v4 on v3

--- a/solution.py
+++ b/solution.py
@@ -80,8 +80,9 @@
 MESH = pl.DeviceIdType.MESH
 
 
-def half_rows(rows):
-    return (rows // 2 + 15) // 16 * 16
+def half_rows(rows, dtype):
+    unit = 16 if jnp.dtype(dtype).itemsize == 2 else 8
+    return (rows // 2 + unit - 1) // unit * unit
 
 
 def remote(src, dst, ssem, rsem, **to):
@@ -115,11 +116,11 @@
         pl.semaphore_wait(barrier, 3)
 
 
-def gather_kernel(zn, x_ref, o_ref, hold, ssem, rsem, lsem):
+def gather_steps(zn, x_ref, o_ref, hold, ssem, rsem, lsem):
     y, x, c, z = [lax.axis_index(n) for n in ALL]
     me = z if zn > 1 else 0
     rows = x_ref.shape[0]
-    h0 = half_rows(rows)
+    h0 = half_rows(rows, x_ref.dtype)
     lo, hi = pl.ds(0, h0), pl.ds(h0, rows - h0)
     X, Y, DX, DY, CO, CX, CY, C0, C1, ZU, ZD = range(11)
     nx, ny, nc = {"x": 1 - x}, {"y": 1 - y}, {"c": 1 - c}
@@ -133,12 +134,9 @@
     def block(s):
         return o_ref.at[s]
 
-    greet(zn, y, x, c, z)
-    local = pltpu.make_async_copy(x_ref, hold, lsem)
+    local = pltpu.make_async_copy(x_ref, hold, lsem.at[0])
     local.start()
-    local.wait()
-    local = pltpu.make_async_copy(hold, o_ref.at[slot(y, x, me)], lsem)
-    local.start()
+    keep = pltpu.make_async_copy(hold, o_ref.at[slot(y, x, me)], lsem.at[1])
 
     def spread(zb, src):
         dst = block(slot(y, x, zb))
@@ -168,6 +166,9 @@
 
         if s == 1:
             spread(me, x_ref)
+            local.wait()
+            keep.start()
+        yield
 
         @pl.when(z - s >= 0)
         def _():
@@ -181,8 +182,11 @@
 
     if zn == 1:
         spread(0, x_ref)
+        local.wait()
+        keep.start()
     order = [lax.rem(z + j, zn) if zn > 1 else 0 for j in range(zn)]
     for zb in order:
+        yield
         sx, sy = slot(y, 1 - x, zb), slot(1 - y, x, zb)
         copy(X, zb, x_ref, x_ref, nx).wait_recv()
         copy(DX, zb, o_ref.at[sx, lo], o_ref.at[sx, lo], ny).start()
@@ -191,11 +195,13 @@
         copy(DY, zb, o_ref.at[sy, hi], o_ref.at[sy, hi], nx).start()
         copy(CY, zb, block(sy), block(sy), nc).start()
     for zb in order:
+        yield
         sd = slot(1 - y, 1 - x, zb)
         copy(DX, zb, x_ref.at[lo], x_ref.at[lo], nx).wait_recv()
         copy(C0, zb, o_ref.at[sd, lo], o_ref.at[sd, lo], nc).start()
         copy(DY, zb, x_ref.at[hi], x_ref.at[hi], nx).wait_recv()
         copy(C1, zb, o_ref.at[sd, hi], o_ref.at[sd, hi], nc).start()
+    yield
     for zb in range(zn):
         for kind, part in ((CO, x_ref), (CX, x_ref), (CY, x_ref), (C0, x_ref.at[lo]), (C1, x_ref.at[hi])):
             copy(kind, zb, part, part, nx).wait_recv()
@@ -214,27 +220,44 @@
         def _():
             down(s).wait_send()
 
-    local.wait()
+    keep.wait()
+
+
+def run_steps(*parts):
+    parts = list(parts)
+    while parts:
+        for part in list(parts):
+            if next(part, part) is part:
+                parts.remove(part)
+
+
+def gather_kernel(zn, *refs):
+    greet(zn, *[lax.axis_index(n) for n in ALL])
+    run_steps(gather_steps(zn, *refs))
+
+
+def gather_scratch(zn, shape, dtype):
+    sems = pltpu.SemaphoreType.DMA((11, zn))
+    return [pltpu.VMEM(shape, dtype), sems, sems, pltpu.SemaphoreType.DMA((2,))]
 
 
 def all_gather(x, zn, ident, name):
-    sems = pltpu.SemaphoreType.DMA((11, zn))
     return pl.pallas_call(
         functools.partial(gather_kernel, zn),
         out_shape=jax.ShapeDtypeStruct((8 * zn,) + x.shape, x.dtype),
         in_specs=[pl.BlockSpec(memory_space=pl.ANY)],
         out_specs=pl.BlockSpec(memory_space=pl.ANY),
-        scratch_shapes=[pltpu.VMEM(x.shape, x.dtype), sems, sems, pltpu.SemaphoreType.DMA],
+        scratch_shapes=gather_scratch(zn, x.shape, x.dtype),
         compiler_params=pltpu.CompilerParams(collective_id=ident, has_side_effects=True),
         name=name,
     )(x)
 
 
-def reduce_kernel(zn, p_ref, o_ref, acc, crecv, dxr, dyr, xr, yr, zur, zdr, ssem, rsem, lsem):
+def reduce_steps(zn, p_ref, o_ref, acc, crecv, dxr, dyr, xr, yr, zur, zdr, ssem, rsem, lsem):
     y, x, c, z = [lax.axis_index(n) for n in ALL]
     me = z if zn > 1 else 0
     rows, cols = p_ref.shape[1:]
-    h0 = half_rows(rows)
+    h0 = half_rows(rows, p_ref.dtype)
     h1 = rows - h0
     X, Y, DX, DY, C0, ZU, ZD = 0, 1, 2, 3, 4, 8, 9
     nx, ny, nc = {"x": 1 - x}, {"y": 1 - y}, {"c": 1 - c}
@@ -266,7 +289,6 @@
                 total = part if total is None else total + part
             dst[at, :] = total.astype(dst.dtype)
 
-    greet(zn, y, x, c, z)
     zorder = [lax.rem(z + j, zn) if zn > 1 else 0 for j in range(zn)]
     for k in (3, 1, 2, 0):
         for zb in range(zn):
@@ -278,18 +300,21 @@
         across(k, zb).wait_recv()
 
     for zb in range(zn):
+        yield
         ready(3, zb)
         b = 3 * zn + zb
         add(acc.at[b], 0, rows, [(acc.at[b], 0), (crecv.at[b], 0)])
         copy(DX, zb, acc.at[b, pl.ds(0, h0)], dxr.at[zb], nx).start()
         copy(DY, zb, acc.at[b, pl.ds(h0, h1)], dyr.at[zb], ny).start()
     for zb in range(zn):
+        yield
         ready(1, zb)
         b = zn + zb
         add(acc.at[b], 0, h0, [(acc.at[b], 0), (crecv.at[b], 0)])
         copy(DY, zb, dyr.at[zb], dyr.at[zb], ny).wait_recv()
         add(acc.at[b], h0, h1, [(acc.at[b], 0), (crecv.at[b], 0), (dyr.at[zb], h0)])
         copy(X, zb, acc.at[b], xr.at[zb], nx).start()
+        yield
         ready(2, zb)
         b = 2 * zn + zb
         add(acc.at[b], h0, h1, [(acc.at[b], 0), (crecv.at[b], 0)])
@@ -301,6 +326,7 @@
         return [(acc.at[zb], 0), (crecv.at[zb], 0), (xr.at[zb], 0), (yr.at[zb], 0)]
 
     for zb in range(zn):
+        yield
         ready(0, zb)
         copy(X, zb, acc.at[zb], xr.at[zb], nx).wait_recv()
         copy(Y, zb, acc.at[zb], yr.at[zb], ny).wait_recv()
@@ -340,6 +366,7 @@
             add(acc.at[zb], 0, rows, column(zb) + [(zdr.at[zb], 0)])
             downward().start()
 
+    yield
     if zn > 1:
 
         @pl.when(z == 0)
@@ -376,26 +403,59 @@
                 copy(ZD, zb, zdr.at[zb], zdr.at[zb], {"z": z - 1}).wait_send()
 
 
+def reduce_kernel(zn, *refs):
+    greet(zn, *[lax.axis_index(n) for n in ALL])
+    run_steps(reduce_steps(zn, *refs))
+
+
+def reduce_scratch(zn, rows, cols, dtype):
+    h0 = half_rows(rows, dtype)
+    sems = pltpu.SemaphoreType.DMA((10, zn))
+    counts = [(4 * zn, rows), (4 * zn, rows), (zn, h0), (zn, rows - h0)] + [(zn, rows)] * 4
+    blocks = [pltpu.VMEM((n, r, cols), dtype) for n, r in counts]
+    return blocks + [sems, sems, pltpu.SemaphoreType.DMA((4 * zn,))]
+
+
 def reduce_scatter(p, zn, ident, name, out_dtype=None):
     count, rows, cols = p.shape
-    h0 = half_rows(rows)
-    sems = pltpu.SemaphoreType.DMA((10, zn))
-    vm = lambda n, r: pltpu.VMEM((n, r, cols), p.dtype)
     return pl.pallas_call(
         functools.partial(reduce_kernel, zn),
         out_shape=jax.ShapeDtypeStruct((rows, cols), out_dtype or p.dtype),
         in_specs=[pl.BlockSpec(memory_space=pl.ANY)],
         out_specs=pl.BlockSpec(memory_space=pltpu.VMEM),
-        scratch_shapes=[
-            vm(4 * zn, rows), vm(4 * zn, rows), vm(zn, h0), vm(zn, rows - h0),
-            vm(zn, rows), vm(zn, rows), vm(zn, rows), vm(zn, rows),
-            sems, sems, pltpu.SemaphoreType.DMA((4 * zn,)),
-        ],
+        scratch_shapes=reduce_scratch(zn, rows, cols, p.dtype),
         compiler_params=pltpu.CompilerParams(
             collective_id=ident, has_side_effects=True, vmem_limit_bytes=56 << 20
         ),
         name=name,
     )(p)
+
+
+def both_kernel(zr, zg, p_ref, x_ref, r_ref, o_ref, *scratch):
+    greet(max(zr, zg), *[lax.axis_index(n) for n in ALL])
+    count = len(reduce_scratch(1, 32, 128, jnp.float32))
+    run_steps(
+        reduce_steps(zr, p_ref, r_ref, *scratch[:count]),
+        gather_steps(zg, x_ref, o_ref, *scratch[count:]),
+    )
+
+
+def scatter_and_gather(p, zr, x, zg, ident, name):
+    count, rows, cols = p.shape
+    return pl.pallas_call(
+        functools.partial(both_kernel, zr, zg),
+        out_shape=(
+            jax.ShapeDtypeStruct((rows, cols), p.dtype),
+            jax.ShapeDtypeStruct((8 * zg,) + x.shape, x.dtype),
+        ),
+        in_specs=[pl.BlockSpec(memory_space=pl.ANY)] * 2,
+        out_specs=(pl.BlockSpec(memory_space=pltpu.VMEM), pl.BlockSpec(memory_space=pl.ANY)),
+        scratch_shapes=reduce_scratch(zr, rows, cols, p.dtype) + gather_scratch(zg, x.shape, x.dtype),
+        compiler_params=pltpu.CompilerParams(
+            collective_id=ident, has_side_effects=True, vmem_limit_bytes=56 << 20
+        ),
+        name=name,
+    )(p, x)
 
 
 def greet_pair(x, c):
@@ -499,52 +559,64 @@
     )(p)
 
 
-def fits(axes):
+def fits():
     return [lax.axis_size(n) for n in ALL] == [2, 2, 2, 4]
 
 
 def gather_all(v, ident, name):
-    if fits(ALL):
+    if fits():
         return all_gather(v, 4, ident, name)
     return lax.all_gather(v, ALL, axis=0)
 
 
 def gather_plane(v, ident, name):
-    if fits(ALL):
+    if fits():
         return all_gather(v, 1, ident, name)
     return lax.all_gather(v, DP, axis=0)
 
 
 def scatter_all(p, ident, name):
-    if fits(ALL):
+    if fits():
         return reduce_scatter(p, 4, ident, name)
     return lax.psum_scatter(p, ALL, scatter_dimension=0)
 
 
 def scatter_plane(p, ident, name):
-    if fits(ALL):
+    if fits():
         return reduce_scatter(p, 1, ident, name)
     return lax.psum_scatter(p, DP, scatter_dimension=0)
 
 
 def keys_all_gather(v):
-    if fits(ALL):
+    if fits():
         return keys_gather(v, 11).reshape(-1, v.shape[1])
     return lax.all_gather(v, PART, axis=0, tiled=True)
 
 
 def keys_sum_scatter(p):
-    if fits(ALL):
+    if fits():
         return keys_reduce(p.reshape(4, -1, p.shape[1]), 12)
     return lax.psum_scatter(p, PART, scatter_dimension=0, tiled=True)
 
 
-def tile_spec(layer, per, deep, tile_rows, index):
+def tile_spec(dp, deep, tile_rows, index, local=None):
     def place(t):
         j = index(t)
-        return (j // per, 0, layer * per + j % per, 0, 0)
+        return (j % dp, 0, j // dp if local is None else local, 0, 0)
 
     return pl.BlockSpec((None, deep, None, tile_rows, D), place)
+
+
+def weight_specs(weights, *groups):
+    arrays, specs = [], []
+    for first, offset in groups:
+        array, local = weights[first // weights[0][0].shape[0]]
+        dp, deep, _, tile_rows, _ = array.shape
+        arrays.append(array)
+        specs.append(
+            tile_spec(dp, deep, tile_rows, lambda t, f=first, o=offset: f + o(t), local)
+        )
+    return arrays, specs
 
 
 def whole(shape):
@@ -596,9 +668,9 @@
         kv_ref[...] = m.astype(jnp.bfloat16)
 
 
-def project(x, gain, cos, sin, weights, layer, per):
+def project(x, gain, cos, sin, weights):
     rows = x.shape[0]
-    deep, tile_rows = weights.shape[1], weights.shape[3]
+    arrays, specs = weight_specs(weights, (0, lambda t: t))
     return pl.pallas_call(
         project_kernel,
         grid=(3,),
@@ -607,8 +679,7 @@
             jax.ShapeDtypeStruct((2, rows, D), jnp.bfloat16),
         ),
         in_specs=[
-            whole((rows, D)), whole((1, D)), whole((rows, 128)), whole((rows, 128)),
-            tile_spec(layer, per, deep, tile_rows, lambda t: t),
+            whole((rows, D)), whole((1, D)), whole((rows, 128)), whole((rows, 128)), *specs,
         ],
         out_specs=(
             whole((rows, D)),
@@ -617,7 +688,7 @@
         scratch_shapes=[pltpu.VMEM((rows, D), jnp.bfloat16)],
         compiler_params=pltpu.CompilerParams(vmem_limit_bytes=40 << 20),
         name="project",
-    )(x, gain, cos, sin, weights)
+    )(x, gain, cos, sin, *arrays)
 
 
 def mask_bias(bias_ref, kseg_ref, qseg_ref, qpos_ref):
@@ -698,26 +769,25 @@
         out_ref[...] += dot_nn(h, wd_ref[...].reshape(D, D))
 
 
-def feed(x, o, gain, weights, layer, per):
+def feed(x, o, gain, weights):
     rows = x.shape[0]
-    deep, tile_rows = weights.shape[1], weights.shape[3]
-    spec = functools.partial(tile_spec, layer, per, deep, tile_rows)
     unit = lambda t: jnp.maximum(t - 1, 0)
+    arrays, specs = weight_specs(
+        weights, (3, lambda t: 0 * t), (4, unit), (4 + UNITS, unit), (4 + 2 * UNITS, unit)
+    )
     state = jax.ShapeDtypeStruct((rows, D), jnp.float32)
     return pl.pallas_call(
         feed_kernel,
         grid=(1 + UNITS,),
         out_shape=(state, state),
         in_specs=[
-            whole((rows, D)), whole((rows, D)), whole((1, D)),
-            spec(lambda t: 3 + 0 * t), spec(lambda t: 4 + unit(t)),
-            spec(lambda t: 4 + UNITS + unit(t)), spec(lambda t: 4 + 2 * UNITS + unit(t)),
+            whole((rows, D)), whole((rows, D)), whole((1, D)), *specs,
         ],
         out_specs=(whole((rows, D)), whole((rows, D))),
         scratch_shapes=[pltpu.VMEM((rows, D), jnp.bfloat16)],
         compiler_params=pltpu.CompilerParams(vmem_limit_bytes=48 << 20),
         name="feed",
-    )(x, o, gain, weights, weights, weights, weights)
+    )(x, o, gain, *arrays)
 
 
 def feed_back_kernel(
@@ -770,11 +840,13 @@
         do_ref[...] = dot_nt(e1, wo_ref[...].reshape(D, D)).astype(jnp.bfloat16)
 
 
-def feed_back(dy, mid, gain, o, weights, layer, per):
+def feed_back(dy, mid, gain, o, weights):
     rows = dy.shape[0]
-    dp, deep, tile_rows = weights.shape[0], weights.shape[1], weights.shape[3]
-    spec = functools.partial(tile_spec, layer, per, deep, tile_rows)
+    dp, deep, _, tile_rows, _ = weights[0][0].shape
     unit = lambda t: jnp.minimum(t // 3, UNITS - 1)
+    arrays, specs = weight_specs(
+        weights, (3, lambda t: 0 * t), (4, unit), (4 + UNITS, unit), (4 + 2 * UNITS, unit)
+    )
 
     def grad_tile(t):
         kind = t % 3
@@ -785,18 +857,16 @@
         feed_back_kernel,
         grid=(3 * UNITS + 1,),
         out_shape=(
-            jax.ShapeDtypeStruct((dp, deep, per, tile_rows, D), jnp.bfloat16),
+            jax.ShapeDtypeStruct((dp, deep, len(weights), tile_rows, D), jnp.bfloat16),
             jax.ShapeDtypeStruct((rows, D), jnp.float32),
             jax.ShapeDtypeStruct((rows, D), jnp.bfloat16),
             jax.ShapeDtypeStruct((8, D), jnp.float32),
         ),
         in_specs=[
-            whole((rows, D)), whole((rows, D)), whole((1, D)), whole((rows, D)),
-            spec(lambda t: 3 + 0 * t), spec(lambda t: 4 + unit(t)),
-            spec(lambda t: 4 + UNITS + unit(t)), spec(lambda t: 4 + 2 * UNITS + unit(t)),
+            whole((rows, D)), whole((rows, D)), whole((1, D)), whole((rows, D)), *specs,
         ],
         out_specs=(
-            tile_spec(0, per, deep, tile_rows, grad_tile),
+            tile_spec(dp, deep, tile_rows, grad_tile),
             whole((rows, D)), whole((rows, D)), whole((8, D)),
         ),
         scratch_shapes=[
@@ -806,7 +876,7 @@
         ],
         compiler_params=pltpu.CompilerParams(vmem_limit_bytes=48 << 20),
         name="feed_back",
-    )(dy, mid, gain, o, weights, weights, weights, weights)
+    )(dy, mid, gain, o, *arrays)
 
 
 def attend_back_kernel(
@@ -891,9 +961,10 @@
         dgain_ref[...] = jnp.broadcast_to(gain_back[None, :], dgain_ref.shape)
 
 
-def project_back(dx, x, gain, cos, sin, dq, dkv, weights, grads, layer, per):
+def project_back(dx, x, gain, cos, sin, dq, dkv, weights, grads):
     rows = x.shape[0]
-    deep, tile_rows = weights.shape[1], weights.shape[3]
+    dp, deep, _, tile_rows, _ = weights[0][0].shape
+    arrays, specs = weight_specs(weights, (0, lambda t: t))
     return pl.pallas_call(
         project_back_kernel,
         grid=(3,),
@@ -905,11 +976,11 @@
         in_specs=[
             whole((rows, D)), whole((rows, D)), whole((1, D)), whole((rows, 128)),
             whole((rows, 128)), whole((rows, D)), whole((2, rows, D)),
-            tile_spec(layer, per, deep, tile_rows, lambda t: t),
+            *specs,
             pl.BlockSpec(memory_space=pl.ANY),
         ],
         out_specs=(
-            tile_spec(0, per, deep, tile_rows, lambda t: t), whole((rows, D)), whole((8, D)),
+            tile_spec(dp, deep, tile_rows, lambda t: t), whole((rows, D)), whole((8, D)),
         ),
         scratch_shapes=[
             pltpu.VMEM((rows, D), jnp.bfloat16), pltpu.VMEM((rows, D), jnp.bfloat16),
@@ -918,35 +989,60 @@
         input_output_aliases={8: 0},
         compiler_params=pltpu.CompilerParams(vmem_limit_bytes=40 << 20),
         name="project_back",
-    )(dx, x, gain, cos, sin, dq, dkv, weights, grads)
-
-
-def layer_forward(state, weights, layer, per, gains, cos, sin, marks):
+    )(dx, x, gain, cos, sin, dq, dkv, *arrays, grads)
+
+
+def layer_forward(state, weights, layer, gains, cos, sin, marks):
     rows = state.shape[0]
-    q, kv = project(state, gains[2 * layer : 2 * layer + 1], cos, sin, weights, layer, per)
+    q, kv = project(state, gains[2 * layer : 2 * layer + 1], cos, sin, weights)
     kv = keys_all_gather(kv.reshape(2 * rows, D)).reshape(-1, 2, rows, D)
     o, lse = attend(q, kv, *marks)
-    mid, out = feed(state, o, gains[2 * layer + 1 : 2 * layer + 2], weights, layer, per)
+    mid, out = feed(state, o, gains[2 * layer + 1 : 2 * layer + 2], weights)
     return out, (state, mid, q, kv, lse, o)
 
 
-def layer_backward(grad, kept, weights, layer, per, gains, cos, sin, marks):
+def layer_backward(grad, kept, weights, layer, gains, cos, sin, marks):
     state, mid, q, kv, lse, o = kept
     rows = state.shape[0]
     grads, dx, do, feed_gain = feed_back(
-        grad, mid, gains[2 * layer + 1 : 2 * layer + 2], o, weights, layer, per
+        grad, mid, gains[2 * layer + 1 : 2 * layer + 2], o, weights
     )
     dq, dkv = attend_back(q, kv, *marks, do, lse)
     dkv = keys_sum_scatter(dkv.reshape(-1, D)).reshape(2, rows, D)
     grads, dx, input_gain = project_back(
-        dx, state, gains[2 * layer : 2 * layer + 1], cos, sin, dq, dkv, weights, grads, layer, per
+        dx, state, gains[2 * layer : 2 * layer + 1], cos, sin, dq, dkv, weights, grads
     )
     return dx, grads, [input_gain[0], feed_gain[0]]
 
 
 def padded(v):
-    count = -(-v.shape[0] // 4096) * 4096
+    count = -(-v.shape[0] // 2048) * 2048
     return jnp.pad(v, (0, count - v.shape[0])).reshape(-1, 128)
+
+
+def place_kernel(slot_ref, mine_ref, w_ref, o_ref):
+    g = pl.program_id(0)
+    count = o_ref.shape[0]
+    for i in range(count):
+        t = g * count + i
+        o_ref[i] = jnp.where(mine_ref[t] > 0, w_ref[slot_ref[t]], 0.0).astype(jnp.bfloat16)
+
+
+def place_tiles(tile_weight, slots, mine, dp_size):
+    count = slots.shape[0] // dp_size
+    cap, rows, cols = tile_weight.shape
+    return pl.pallas_call(
+        place_kernel,
+        grid_spec=pltpu.PrefetchScalarGridSpec(
+            num_scalar_prefetch=2,
+            grid=(dp_size,),
+            in_specs=[pl.BlockSpec((cap, rows, cols), lambda g, *_: (0, 0, 0))],
+            out_specs=pl.BlockSpec((count, rows, cols), lambda g, *_: (g, 0, 0)),
+        ),
+        out_shape=jax.ShapeDtypeStruct((dp_size * count, rows, cols), jnp.bfloat16),
+        compiler_params=pltpu.CompilerParams(vmem_limit_bytes=24 << 20),
+        name="place_tiles",
+    )(slots, mine, tile_weight)
 
 
 def shards(
@@ -993,29 +1089,36 @@
             lax.dynamic_slice_in_dim(targets[0], rep_index * (comp // rep_size), comp // rep_size),
         ]
     )
-    packed = gather_all(padded(own_part), 0, "ids_gather").reshape(devices, -1)
-    packed = packed[:, : own_part.shape[0]].reshape(dp_size, rep_size, -1)
+    slots = tile_slots(owners)
+    mine = owners == dp_index
+    per = TILES_PER // dp_size
+    home_ids = (
+        jnp.arange(LAYERS)[None, :, None] * TILES_PER
+        + jnp.arange(per)[None, None, :] * dp_size
+        + jnp.arange(dp_size)[:, None, None]
+    ).reshape(-1)
+    home_mine = jnp.take(mine, home_ids)
+    home_slots = jnp.where(home_mine, jnp.take(slots, home_ids), 0)
+    placed = place_tiles(tile_weight, home_slots, home_mine.astype(jnp.int32), dp_size)
+    placed = placed.reshape(dp_size, -1, D)
+    if fits():
+        home, packed = scatter_and_gather(placed, 1, padded(own_part), 4, 0, "home_and_ids")
+    else:
+        home = lax.psum_scatter(placed, DP, scatter_dimension=0)
+        packed = lax.all_gather(padded(own_part), ALL, axis=0)
+    packed = packed.reshape(devices, -1)[:, : own_part.shape[0]]
+    packed = packed.reshape(dp_size, rep_size, -1)
     tokens_all = packed[:, :, :rows].reshape(dp_size, length)
     segments_all = packed[:, :, rows : 2 * rows].reshape(dp_size, length)
     edge = 2 * rows + comp // rep_size
     completion_all = packed[:, :, 2 * rows : edge].reshape(dp_size, comp)
     targets_all = packed[:, :, edge:].reshape(dp_size, comp)
 
-    slots = tile_slots(owners)
-    mine = owners == dp_index
-    tile_low = tile_weight.astype(jnp.bfloat16)
-    per = TILES_PER // dp_size
-    home_ids = (
-        jnp.arange(LAYERS)[None, :, None] * TILES_PER
-        + jnp.arange(dp_size)[:, None, None] * per
-        + jnp.arange(per)[None, None, :]
-    ).reshape(-1)
-    home_mine = jnp.take(mine, home_ids)
-    home_slots = jnp.where(home_mine, jnp.take(slots, home_ids), 0)
-    placed = jnp.where(home_mine[:, None, None], jnp.take(tile_low, home_slots, axis=0), 0)
-    home = scatter_plane(placed.reshape(dp_size, -1, D), 7, "home_scatter")
-    spread = gather_all(home, 1, "weights_gather")
-    weights = spread.reshape(dp_size, rep_size, LAYERS * per, tile_rows, D)
+    home = home.reshape(LAYERS, per, tile_rows, D)
+    spread = lax.all_gather(home[0], ALL, axis=0)
+    spread = spread.reshape(dp_size, rep_size, per, tile_rows, D)
+    weights = [[(spread, i) for i in range(per)]]
+    later = [[lax.all_gather(home[index, i], ALL, axis=0) for i in range(1, per)] for index in range(1, LAYERS)]
 
     order = tokens_all.reshape(a_size, rep_size, b_size, rows).transpose(0, 2, 1, 3).reshape(-1)
     place = order - vocab_start
@@ -1026,6 +1129,15 @@
     ).astype(jnp.bfloat16)
     state = scatter_all(picked.reshape(devices, rows, D), 8, "rows_scatter").astype(jnp.float32)
 
+    for index in range(1, LAYERS):
+        first, state = lax.optimization_barrier((home[index, 0], state))
+        first = gather_all(first, 1, "weights_gather")
+        weights.append(
+            [
+                (array.reshape(dp_size, rep_size, 1, tile_rows, D), 0)
+                for array in [first] + later[index - 1]
+            ]
+        )
     first_place = b_index * rows
     places = first_place + jnp.arange(rows)
     cosine, sine = rope_tables(places.astype(jnp.float32))
@@ -1035,7 +1147,7 @@
     kept_list = []
     for index in range(LAYERS):
         state, kept = layer_forward(
-            state, weights, index, per, gain_weight, cosine, sine, marks
+            state, weights[index], index, gain_weight, cosine, sine, marks
         )
         kept_list.append(kept)
     final_gain = gain_weight[2 * LAYERS]
@@ -1068,15 +1180,18 @@
     local_top = jnp.max(logits, axis=-1)
     local_total = jnp.sum(jnp.exp(logits - local_top[:, None]), axis=-1)
     local_hit = jnp.sum(jnp.where(hot, logits, 0.0), axis=-1)
-    own_stats = jnp.concatenate([local_top, local_total, local_hit])
-    stats = gather_all(padded(own_stats), 4, "stats_gather").reshape(devices, -1)
-    stats = stats[:, : own_stats.shape[0]].reshape(devices, 3, -1)
-    top = jnp.max(stats[:, 0], axis=0)
-    total = jnp.sum(stats[:, 1] * jnp.exp(stats[:, 0] - top[None]), axis=0)
-    log_total = top + jnp.log(total)
+    own_stats = jnp.concatenate(
+        [v.reshape(-1, 128) for v in (local_top, local_total, local_hit)]
+    )
+    stats = gather_all(own_stats, 4, "stats_gather")
+    tops, totals, hits = jnp.split(stats, 3, axis=1)
+    top = jnp.max(tops, axis=0)
+    total = jnp.sum(totals * jnp.exp(tops - top[None]), axis=0)
+    log_total = (top + jnp.log(total)).reshape(-1)
+    target_hit = jnp.sum(hits, axis=0).reshape(-1)
     valid = all_wanted >= 0
     scored = dp_size * comp
-    loss = jnp.sum(jnp.where(valid, log_total - jnp.sum(stats[:, 2], axis=0), 0.0)) / scored
+    loss = jnp.sum(jnp.where(valid, log_total - target_hit, 0.0)) / scored
     logit_grad = jnp.where(
         valid[:, None],
         (jnp.exp(logits - log_total[:, None]) - jnp.where(hot, 1.0, 0.0)) / scored,
@@ -1093,27 +1208,27 @@
     gain_parts = [None] * LAYERS
     for index in reversed(range(LAYERS)):
         state_grad, tile_parts[index], gain_parts[index] = layer_backward(
-            state_grad, kept_list[index], weights, index, per, gain_weight, cosine, sine, marks
+            state_grad, kept_list[index], weights[index], index, gain_weight, cosine, sine, marks
         )
-    piece_grads = gather_all(state_grad.astype(jnp.bfloat16), 2, "entry_gather").reshape(-1, D)
+    entry = state_grad.astype(jnp.bfloat16)
+    parts = [part.reshape(devices, -1, D) for part in tile_parts]
+    home_grads = [None] + [
+        lax.psum_scatter(part, ALL, scatter_dimension=0) for part in parts[1:]
+    ]
+    if fits():
+        home_grads[0], piece_grads = scatter_and_gather(parts[0], 4, entry, 4, 2, "grads_and_entry")
+    else:
+        home_grads[0] = lax.psum_scatter(parts[0], ALL, scatter_dimension=0)
+        piece_grads = lax.all_gather(entry, ALL, axis=0)
     table_grad = jnp.einsum(
-        "tv,td->vd", token_hot, piece_grads, preferred_element_type=jnp.float32
-    )
-    home_grads = []
-    for index in range(LAYERS):
-        part = tile_parts[index].reshape(devices, -1, D)
-        home_grads.append(scatter_all(part, 10, "grads_scatter"))
+        "tv,td->vd", token_hot, piece_grads.reshape(-1, D), preferred_element_type=jnp.float32
+    )
     plane_grad = gather_plane(jnp.concatenate(home_grads), 6, "owners_gather")
-    plane_grad = plane_grad.reshape(dp_size, LAYERS, per, tile_rows, D)
-    plane_grad = plane_grad.transpose(1, 0, 2, 3, 4).reshape(tile_count, tile_rows, D)
+    plane_grad = plane_grad.reshape(tile_count, tile_rows, D)
     own_count = jnp.sum(mine.astype(jnp.int32))
     slot_ids = jnp.arange(slots_cap)
-    tile_of_slot = jnp.sum(
-        jnp.where(
-            mine[None, :] & (slots[None, :] == slot_ids[:, None]), jnp.arange(tile_count)[None, :], 0
-        ),
-        axis=1,
-    )
+    picks = mine[home_ids][None, :] & (slots[home_ids][None, :] == slot_ids[:, None])
+    tile_of_slot = jnp.sum(jnp.where(picks, jnp.arange(tile_count)[None, :], 0), axis=1)
     slot_valid = (slot_ids < own_count)[:, None, None]
     own_grad = jnp.where(
         slot_valid, jnp.take(plane_grad, tile_of_slot, axis=0).astype(jnp.float32), 0.0

time: 1240 us -> 1110 us (0.90)
  Pallas kernels: 1030 us -> 897 us
  other arithmetic: 66.1 us -> 52.2 us
  between operations: 8.98 us -> 22.5 us
    pallas_call x0 -> x3, Pallas kernels: none -> 275 us  [the longest x2 272 us: scatter_and_gather(): pl.pallas_call(functools.partial(both_kernel, zr, zg), out_shape=(jax.Sha...]
    pallas_call x5 -> x2, Pallas kernels: 366 us -> 138 us  [reduce_scatter(): pl.pallas_call(functools.partial(reduce_kernel, zn), out_shape=jax.ShapeD...]
    pallas_call x7 -> x5, Pallas kernels: 422 us -> 241 us  [all_gather(): pl.pallas_call(functools.partial(gather_kernel, zn), out_shape=jax.ShapeD...]
    unnamed x110 -> x183, local copies, waits for them, and re-layouts: 17.9 us -> 27.9 us
  transfers between devices with their start and end apart: 0 -> 3, of which waited for: 0 -> 0; matrix products, arithmetic and copies ran while one was open for 0% -> 7% of each run, Pallas kernels for 0% -> 53%
where the time goes in v4:
time: 1110 us; the launch traced here: 1100 us
  Pallas kernels  897 us (81%)
  matrix products  79.6 us (7%)
  other arithmetic  52.2 us (5%)
  local copies, waits for them, and re-layouts  49.5 us (4%)
  between operations  22.5 us (2%)
    pallas_call x2, Pallas kernels, scatter_and_gather(): pl.pallas_call(functools.partial(both_kernel, zr, zg), out_shape=(jax.Sha...  272 us
    pallas_call x5, Pallas kernels, all_gather(): pl.pallas_call(functools.partial(gather_kernel, zn), out_shape=jax.ShapeD...  241 us
    pallas_call x2, Pallas kernels, reduce_scatter(): pl.pallas_call(functools.partial(reduce_kernel, zn), out_shape=jax.ShapeD...  138 us
    pallas_call x2, Pallas kernels, keys_gather(): pl.pallas_call(keys_gather_kernel, out_shape=jax.ShapeDtypeStruct((4,) +...  52.5 us
    pallas_call x2, Pallas kernels, feed_back(): pl.pallas_call(feed_back_kernel, grid=(3 * UNITS + 1,), out_shape=(jax.Sh...  51.7 us
    pallas_call x2, Pallas kernels, keys_reduce(): pl.pallas_call(keys_reduce_kernel, out_shape=jax.ShapeDtypeStruct(block,...  45 us
    unnamed x183, local copies, waits for them, and re-layouts  27.9 us
    pallas_call x2, Pallas kernels, attend_back(): pl.pallas_call(attend_back_kernel, grid=(HEADS // 2,), out_shape=(jax.Sha...  27.7 us
  transfers between devices with their start and end apart: 3, of which 0 were waited for; matrix products, arithmetic and copies ran while one was open for 7% of the time, Pallas kernels for 53%

profile of v4, /device:TPU:0, one launch (start us, length us, event | category | flops | bytes accessed | tf_op | source)
XLA Modules:
  0.0 1100.7 jit_solution(3536762817939649175)
XLA Ops:
  13.3 2.0 copy-done.5
  15.3 2.5 place_tiles.1
  17.9 3.7 copy-done.4
  21.5 56.6 %home_and_ids.1 = (bf16[768,768]{1,0:T(8,128)(2,1)}, s32[32,16,128]{2,1,0:T(8,128)}) custom-call(bf16[8,768,768]{2,1,0:T(8,128)(2,1)} %bitcast.93, s32[16,128]{1,0:T(8,128)} %pad_bitcast_fusion.x_ref), custom_call_target="tpu_custom_call" | custom-call | tf_op jit(solution)/shard_map/home_and_ids/pallas_call | solution.py:445
  78.1 2.0 slice.78
  80.1 1.9 fusion.46
  82.8 2.3 reduce-window.6
  86.2 1.6 select_reduce_fusion.1
  89.5 19.5 %fusion.4 = bf16[8192,768]{1,0:T(8,128)(2,1)} fusion(s32[8192]{0:T(1024)S(1)} %bitcast.139, f32[1000,768]{1,0:T(8,128)} %param.27), kind=kOutput, calls=%fused_computation.8 | convolution fusion | flops 12598163456 | bytes 15687680 | tf_op jit(solution)/shard_map/dot_general | solution.py:1127
  109.0 107.9 %rows_scatter.1 = bf16[256,768]{1,0:T(8,128)(2,1)} custom-call(bf16[32,256,768]{2,1,0:T(8,128)(2,1)} %bitcast.117), custom_call_target="tpu_custom_call" | custom-call | tf_op jit(solution)/shard_map/rows_scatter/pallas_call | solution.py:421
  217.9 98.3 %weights_gather.1 = bf16[32,192,768]{2,1,0:T(8,128)(2,1)} custom-call(bf16[192,768]{1,0:T(8,128)(2,1)} %get-tuple-element.60.refs_0_), custom_call_target="tpu_custom_call" | custom-call | tf_op jit(solution)/shard_map/weights_gather/pallas_call | solution.py:245
  318.3 4.7 project.2
  324.0 30.0 %keys_gather.2 = bf16[4,512,768]{2,1,0:T(8,128)(2,1)} custom-call(bf16[512,768]{1,0:T(8,128)(2,1)} %bitcast.98), custom_call_target="tpu_custom_call" | custom-call | tf_op jit(solution)/shard_map/keys_gather/pallas_call | solution.py:495
  354.0 1.9 copy-done.2
  355.9 13.1 %attend.2 = (bf16[256,768]{1,0:T(8,128)(2,1)S(1)}, f32[6,8,256]{2,1,0:T(8,128)S(1)}) custom-call(bf16[256,768]{1,0:T(8,128)(2,1)S(1)} %get-tuple-element.56.q_ref, bf16[4,2,256,768]{3,2,1,0:T(8,128)(2,1)S(1)} %bitcast.87, bf16[4,2,256,768]{3,2,1,0:T(8,128)(2,1)S(1)} %bitcast.88, s32[1024,1]{1,0:T(8,128)S(1)} %copy.100.kseg_ref, ...), custom_call_target="tpu_custom_call" | custom-call | tf_op jit(solution)/shard_map/attend/pallas_call | solution.py:739
  369.7 10.7 feed.2
  380.4 2.8 project.3
  384.1 22.5 %keys_gather.3 = bf16[4,512,768]{2,1,0:T(8,128)(2,1)} custom-call(bf16[512,768]{1,0:T(8,128)(2,1)} %bitcast.99), custom_call_target="tpu_custom_call" | custom-call | tf_op jit(solution)/shard_map/keys_gather/pallas_call | solution.py:495
  406.6 1.9 copy-done.3
  408.5 13.1 %attend.3 = (bf16[256,768]{1,0:T(8,128)(2,1)S(1)}, f32[6,8,256]{2,1,0:T(8,128)S(1)}) custom-call(bf16[256,768]{1,0:T(8,128)(2,1)S(1)} %get-tuple-element.61.q_ref, bf16[4,2,256,768]{3,2,1,0:T(8,128)(2,1)S(1)} %bitcast.91, bf16[4,2,256,768]{3,2,1,0:T(8,128)(2,1)S(1)} %bitcast.92, s32[1024,1]{1,0:T(8,128)S(1)} %copy.100.kseg_ref, ...), custom_call_target="tpu_custom_call" | custom-call | tf_op jit(solution)/shard_map/attend/pallas_call | solution.py:739
  424.1 9.5 feed.3
  436.1 28.3 %chosen_gather.1 = bf16[32,96,768]{2,1,0:T(8,128)(2,1)} custom-call(bf16[96,768]{1,0:T(8,128)(2,1)} %convolution_convert_fusion.1.refs_0_), custom_call_target="tpu_custom_call" | custom-call | tf_op jit(solution)/shard_map/chosen_gather/pallas_call | solution.py:245
  464.4 8.0 fusion.49
  472.4 3.3 exponential_reduce_fusion
  477.5 19.7 %stats_gather.1 = f32[32,72,128]{2,1,0:T(8,128)} custom-call(f32[72,128]{1,0:T(8,128)} %pad_maximum_fusion.3.refs_0_), custom_call_target="tpu_custom_call" | custom-call | tf_op jit(solution)/shard_map/stats_gather/pallas_call | solution.py:245
  500.2 12.4 %convolution_convert_fusion = bf16[3072,768]{1,0:T(8,128)(2,1)} fusion(f32[1000,768]{1,0:T(8,128)} %param.30, f32[3072,1000]{0,1:T(8,128)} %copy-done.46, f32[3072]{0:T(1024)S(1)} %get-tuple-element.120, s32[3072]{0:T(1024)S(1)} %copy-done.62, pred[3072]{0:T(1024)(128)(4,1)S(1)} %copy-done.78), kind=kOutput, calls=%fused_computation.15 | convolution fusion | flops 4743223296 | bytes 20106240 | tf_op jit(solution)/shard_map/dot_general | solution.py:1200
  512.6 30.2 %back_scatter.1 = bf16[96,768]{1,0:T(8,128)(2,1)} custom-call(bf16[32,96,768]{2,1,0:T(8,128)(2,1)} %bitcast.120), custom_call_target="tpu_custom_call" | custom-call | tf_op jit(solution)/shard_map/back_scatter/pallas_call | solution.py:421
  542.8 2.1 multiply_reduce_fusion.3
  545.2 25.4 %feed_back.2 = (bf16[8,4,2,192,768]{4,3,2,1,0:T(8,128)(2,1)}, f32[256,768]{1,0:T(8,128)S(1)}, bf16[256,768]{1,0:T(8,128)(2,1)S(1)}, f32[8,768]{1,0:T(8,128)S(1)}) custom-call(f32[256,768]{1,0:T(8,128)S(1)} %multiply_subtract_fusion.2.dy_ref, f32[256,768]{1,0:T(8,128)S(1)} %copy-done.23, f32[1,768]{1,0:T(1,128)S(1)} %copy-done.35, ...), custom_call_target="tpu_custom_call" | custom-call | tf_op jit(solution)/shard_map/feed_back/pallas_call | solution.py:856
  576.8 13.8 %attend_back.2 = (f32[256,768]{1,0:T(8,128)S(1)}, bf16[4,2,256,768]{3,2,1,0:T(8,128)(2,1)S(1)}) custom-call(bf16[256,768]{1,0:T(8,128)(2,1)S(1)} %copy-done.15, bf16[4,2,256,768]{3,2,1,0:T(8,128)(2,1)} %bitcast.89, bf16[4,2,256,768]{3,2,1,0:T(8,128)(2,1)} %bitcast.90, s32[1024,1]{1,0:T(8,128)S(1)} %copy.100.kseg_ref, s32[1,256]{1,0:T(1,128)S(1)} %copy-done.39, ...), custom_call_target="tpu_custom_call" | custom-call | tf_op jit(solution)/shard_map/attend_back/pallas_call | solution.py:916
  590.6 21.9 %keys_reduce.2 = bf16[512,768]{1,0:T(8,128)(2,1)S(1)} custom-call(bf16[4,512,768]{2,1,0:T(8,128)(2,1)S(1)} %bitcast.95), custom_call_target="tpu_custom_call" | custom-call | tf_op jit(solution)/shard_map/keys_reduce/pallas_call | solution.py:546
  613.7 5.0 project_back.2
  623.5 1.4 sub.133
  627.5 26.3 %feed_back.3 = (bf16[8,4,2,192,768]{4,3,2,1,0:T(8,128)(2,1)}, f32[256,768]{1,0:T(8,128)S(1)}, bf16[256,768]{1,0:T(8,128)(2,1)S(1)}, f32[8,768]{1,0:T(8,128)S(1)}) custom-call(f32[256,768]{1,0:T(8,128)S(1)} %copy-done.19, f32[256,768]{1,0:T(8,128)S(1)} %copy-done.17, f32[1,768]{1,0:T(1,128)S(1)} %get-tuple-element.125.g_ref, ...), custom_call_target="tpu_custom_call" | custom-call | tf_op jit(solution)/shard_map/feed_back/pallas_call | solution.py:856
  653.9 13.9 %attend_back.3 = (f32[256,768]{1,0:T(8,128)S(1)}, bf16[4,2,256,768]{3,2,1,0:T(8,128)(2,1)S(1)}) custom-call(bf16[256,768]{1,0:T(8,128)(2,1)S(1)} %copy-done.13, bf16[4,2,256,768]{3,2,1,0:T(8,128)(2,1)} %bitcast.85, bf16[4,2,256,768]{3,2,1,0:T(8,128)(2,1)} %bitcast.86, s32[1024,1]{1,0:T(8,128)S(1)} %copy.100.kseg_ref, s32[1,256]{1,0:T(1,128)S(1)} %copy-done.40, ...), custom_call_target="tpu_custom_call" | custom-call | tf_op jit(solution)/shard_map/attend_back/pallas_call | solution.py:916
  667.8 23.1 %keys_reduce.3 = bf16[512,768]{1,0:T(8,128)(2,1)S(1)} custom-call(bf16[4,512,768]{2,1,0:T(8,128)(2,1)S(1)} %bitcast.94), custom_call_target="tpu_custom_call" | custom-call | tf_op jit(solution)/shard_map/keys_reduce/pallas_call | solution.py:546
  691.0 6.7 project_back.3
  699.9 215.7 %grads_and_entry.1 = (bf16[384,768]{1,0:T(8,128)(2,1)}, bf16[32,256,768]{2,1,0:T(8,128)(2,1)}) custom-call(bf16[32,384,768]{2,1,0:T(8,128)(2,1)} %bitcast.114, bf16[256,768]{1,0:T(8,128)(2,1)} %convert_element_type.88.x_ref), custom_call_target="tpu_custom_call" | custom-call | tf_op jit(solution)/shard_map/grads_and_entry/pallas_call | solution.py:445
  915.6 15.4 %multiply_reduce_fusion.1 = (f32[]{:T(128)}, f32[1000,768]{1,0:T(8,128)}) fusion(bf16[3072,768]{1,0:T(8,128)(2,1)} %bitcast.119, f32[3072,1000]{0,1:T(8,128)} %copy-done.46, f32[3072]{0:T(1024)S(1)} %copy-done.74, s32[3072]{0:T(1024)S(1)} %copy-done.63, pred[3072]{0:T(1024)(128)(4,1)S(1)} %copy-done.79), kind=kOutput, calls=%fused_computation.34 | convolution fusion | flops 4741632000 | bytes 20106244 | tf_op jit(solution)/shard_map/rv,rd->vd/dot_general | solution.py:1204
  930.9 21.3 %multiply_reduce_fusion.2 = (f32[]{:T(128)}, f32[1000,768]{1,0:T(8,128)}) fusion(bf16[8192,768]{1,0:T(8,128)(2,1)} %bitcast.143, s32[8192]{0:T(1024)S(1)} %bitcast.140), kind=kOutput, calls=%fused_computation.35 | convolution fusion | flops 12592640000 | bytes 15687684 | tf_op jit(solution)/shard_map/tv,td->vd/dot_general | solution.py:1223
  952.3 2.2 pad_maximum_fusion.refs_0_
  954.4 44.9 %owners_gather.1 = bf16[8,768,768]{2,1,0:T(8,128)(2,1)} custom-call(bf16[768,768]{1,0:T(8,128)(2,1)} %pad_maximum_fusion.refs_0_), custom_call_target="tpu_custom_call" | custom-call | tf_op jit(solution)/shard_map/owners_gather/pallas_call | solution.py:245
  999.4 5.9 gather_fusion.2
  1005.2 3.1 multiply_reduce_fusion
  1010.9 50.2 %sums_gather.1 = f32[32,32,128]{2,1,0:T(8,128)} custom-call(f32[32,128]{1,0:T(8,128)} %fusion.23.refs_0_), custom_call_target="tpu_custom_call" | custom-call | tf_op jit(solution)/shard_map/sums_gather/pallas_call | solution.py:245
  1066.8 10.4 fusion.45
  1078.2 6.0 fusion.41
  1086.5 4.9 fusion.43
  (275 shorter events, 48.5 us)
Async XLA Ops:
  7.2 311.1 %all-gather.4.cloned.1.call-start = ((), (), s32[]{:S(2)}) async-start(), calls=%async_computation.1 | async-start | bytes 19464192 | tf_op jit(solution)/shard_map/all_gather | solution.py:1118
  80.1 343.0 %all-gather.6.cloned.1.call-start = ((), (), s32[]{:S(2)}) async-start(), calls=%async_computation.3 | async-start | bytes 9732096 | tf_op jit(solution)/shard_map/all_gather | solution.py:1121
  82.1 870.2 %reduce-scatter.2.cloned.1.call-start = ((), (), s32[]{:S(2)}) async-start(), calls=%async_computation.2 | async-start | bytes 19464192 | tf_op jit(solution)/shard_map/reduce_scatter | solution.py:1216
  82.7 26.3 %copy-start.66 = (s32[8,2,4,128]{3,1,2,0:T(2,128)}, s32[8,2,4,128]{3,1,2,0:T(2,128)S(1)}, u32[]{:S(2)}) copy-start(s32[8,2,4,128]{3,1,2,0:T(2,128)S(1)} %copy.111) | copy-start | bytes 98308
  88.5 20.4 %copy-start.64 = (pred[8,4,96]{2,0,1:T(8,128)(4,1)}, pred[8,4,96]{2,0,1:T(8,128)(4,1)S(1)}, u32[]{:S(2)}) copy-start(pred[8,4,96]{2,0,1:T(8,128)(4,1)S(1)} %get-tuple-element.130) | copy-start | bytes 9220
  217.9 99.8 %copy-start.60 = (f32[5,768]{1,0:T(8,128)S(1)}, f32[5,768]{1,0:T(8,128)}, u32[]{:S(2)}) copy-start(f32[5,768]{1,0:T(8,128)} %param.33) | copy-start | bytes 46084
  316.3 90.3 %copy-start.38 = (s32[1,256]{1,0:T(1,128)}, s32[1,256]{1,0:T(1,128)S(1)}, u32[]{:S(2)}) copy-start(s32[1,256]{1,0:T(1,128)S(1)} %dynamic_slice.36.qseg_ref) | copy-start | bytes 3076
  316.3 90.3 %copy-start.41 = (s32[1,256]{1,0:T(1,128)}, s32[1,256]{1,0:T(1,128)S(1)}, u32[]{:S(2)}) copy-start(s32[1,256]{1,0:T(1,128)S(1)} %iota_add_fusion.1.qpos_ref) | copy-start | bytes 3076
  318.3 104.7 %copy-start.34 = (f32[1,768]{1,0:T(1,128)}, f32[1,768]{1,0:T(1,128)S(1)}, u32[]{:S(2)}) copy-start(f32[1,768]{1,0:T(1,128)S(1)} %get-tuple-element.123.g_ref) | copy-start | bytes 9220
  324.0 45.1 %copy-start.12 = (bf16[256,768]{1,0:T(8,128)(2,1)}, bf16[256,768]{1,0:T(8,128)(2,1)S(1)}, u32[]{:S(2)}) copy-start(bf16[256,768]{1,0:T(8,128)(2,1)S(1)} %get-tuple-element.56.q_ref) | copy-start | bytes 1179652
  369.7 10.7 slice-start
  369.7 10.7 slice-start.1
  369.7 10.7 slice-start.2
  380.4 42.7 %copy-start.7 = (f32[256,768]{1,0:T(8,128)}, f32[256,768]{1,0:T(8,128)S(1)}, u32[]{:S(2)}) copy-start(f32[256,768]{1,0:T(8,128)S(1)} %get-tuple-element.59.x_ref) | copy-start | bytes 2359300
  384.1 37.5 %copy-start.14 = (bf16[256,768]{1,0:T(8,128)(2,1)}, bf16[256,768]{1,0:T(8,128)(2,1)S(1)}, u32[]{:S(2)}) copy-start(bf16[256,768]{1,0:T(8,128)(2,1)S(1)} %get-tuple-element.61.q_ref) | copy-start | bytes 1179652
  424.1 11.1 %copy-start.58 = (f32[768]{0:T(1024)S(1)}, f32[768]{0:T(1024)}, u32[]{:S(2)}) copy-start(f32[768]{0:T(1024)} %get-tuple-element.122) | copy-start | bytes 9220
  424.1 11.1 %copy-start.75 = (s32[96]{0:T(128)S(1)}, s32[96]{0:T(128)}, u32[]{:S(2)}) copy-start(s32[96]{0:T(128)} %fusion.35) | copy-start | bytes 1156
  464.4 8.0 copy-start.62
  472.4 27.8 %copy-start.78 = (pred[3072]{0:T(1024)(128)(4,1)S(1)}, pred[3072]{0:T(1024)(128)(4,1)}, u32[]{:S(2)}) copy-start(pred[3072]{0:T(1024)(128)(4,1)} %ge.50) | copy-start | bytes 9220
  500.2 12.4 %copy-start.73 = (f32[3072]{0:T(1024)}, f32[3072]{0:T(1024)S(1)}, u32[]{:S(2)}) copy-start(f32[3072]{0:T(1024)S(1)} %get-tuple-element.120) | copy-start | bytes 36868
  512.6 30.2 %copy-start.76 = (s32[96]{0:T(128)S(1)}, s32[96]{0:T(128)}, u32[]{:S(2)}) copy-start(s32[96]{0:T(128)} %fusion.35) | copy-start | bytes 1156
  512.6 32.3 %copy-start.77 = (f32[256]{0:T(256)S(1)}, f32[256]{0:T(256)}, u32[]{:S(2)}) copy-start(f32[256]{0:T(256)} %get-tuple-element.134) | copy-start | bytes 3076
  545.1 67.4 %slice-start.3 = ((s8[9437184]{0:T(1024)(128)(4,1)}), s8[4194304]{0:T(1024)(128)(4,1)S(1)}, s32[]{:S(2)}) async-start(s8[9437184]{0:T(1024)(128)(4,1)} %bitcast.82), calls=%async_computation.7 | async-start | bytes 8388608
  545.2 67.4 %slice-start.4 = ((s8[9437184]{0:T(1024)(128)(4,1)}), s8[4194304]{0:T(1024)(128)(4,1)S(1)}, s32[]{:S(2)}) async-start(s8[9437184]{0:T(1024)(128)(4,1)} %bitcast.82), calls=%async_computation.8 | async-start | bytes 8388608
  545.2 67.4 %slice-start.5 = ((s8[9437184]{0:T(1024)(128)(4,1)}), s8[1048576]{0:T(1024)(128)(4,1)S(1)}, s32[]{:S(2)}) async-start(s8[9437184]{0:T(1024)(128)(4,1)} %bitcast.82), calls=%async_computation.9 | async-start | bytes 2097152
  590.6 21.9 %copy-start.26 = (f32[256,768]{1,0:T(8,128)}, f32[256,768]{1,0:T(8,128)S(1)}, u32[]{:S(2)}) copy-start(f32[256,768]{1,0:T(8,128)S(1)} %get-tuple-element.69.dq_ref) | copy-start | bytes 2359300
  590.6 22.0 %copy-start.8 = (f32[256,768]{1,0:T(8,128)S(1)}, f32[256,768]{1,0:T(8,128)}, u32[]{:S(2)}) copy-start(f32[256,768]{1,0:T(8,128)} %copy-done.7) | copy-start | bytes 2359300
  590.6 22.0 %copy-start.25 = (f32[256,768]{1,0:T(8,128)S(1)}, f32[256,768]{1,0:T(8,128)}, u32[]{:S(2)}) copy-start(f32[256,768]{1,0:T(8,128)} %copy-done.24) | copy-start | bytes 2359300
  627.5 26.4 %copy-start.13 = (bf16[256,768]{1,0:T(8,128)(2,1)S(1)}, bf16[256,768]{1,0:T(8,128)(2,1)}, u32[]{:S(2)}) copy-start(bf16[256,768]{1,0:T(8,128)(2,1)} %copy-done.12) | copy-start | bytes 1179652
  627.5 26.4 %copy-start.31 = (f32[6,8,256]{2,1,0:T(8,128)S(1)}, f32[6,8,256]{2,1,0:T(8,128)}, u32[]{:S(2)}) copy-start(f32[6,8,256]{2,1,0:T(8,128)} %copy-done.30) | copy-start | bytes 147460
  627.5 26.4 %copy-start.40 = (s32[1,256]{1,0:T(1,128)S(1)}, s32[1,256]{1,0:T(1,128)}, u32[]{:S(2)}) copy-start(s32[1,256]{1,0:T(1,128)} %copy-done.38) | copy-start | bytes 3076
  627.5 26.4 %copy-start.43 = (s32[1,256]{1,0:T(1,128)S(1)}, s32[1,256]{1,0:T(1,128)}, u32[]{:S(2)}) copy-start(s32[1,256]{1,0:T(1,128)} %copy-done.41) | copy-start | bytes 3076
  667.8 23.1 %copy-start.37 = (f32[1,768]{1,0:T(1,128)S(1)}, f32[1,768]{1,0:T(1,128)}, u32[]{:S(2)}) copy-start(f32[1,768]{1,0:T(1,128)} %copy-done.36) | copy-start | bytes 9220
  699.8 215.7 %copy-start.63 = (s32[3072]{0:T(1024)S(1)}, s32[3072]{0:T(1024)}, u32[]{:S(2)}) copy-start(s32[3072]{0:T(1024)} %sub.129) | copy-start | bytes 36868
  699.9 215.7 %copy-start.74 = (f32[3072]{0:T(1024)S(1)}, f32[3072]{0:T(1024)}, u32[]{:S(2)}) copy-start(f32[3072]{0:T(1024)} %copy-done.73) | copy-start | bytes 36868
  699.9 215.7 %copy-start.79 = (pred[3072]{0:T(1024)(128)(4,1)S(1)}, pred[3072]{0:T(1024)(128)(4,1)}, u32[]{:S(2)}) copy-start(pred[3072]{0:T(1024)(128)(4,1)} %ge.50) | copy-start | bytes 9220
  915.6 15.4 %copy-start.67 = (s32[8,2,4,128]{3,1,2,0:T(2,128)S(1)}, s32[8,2,4,128]{3,1,2,0:T(2,128)}, u32[]{:S(2)}) copy-start(s32[8,2,4,128]{3,1,2,0:T(2,128)} %copy-done.66) | copy-start | bytes 98308
  930.9 21.3 %copy-start.55 = (bf16[384,768]{1,0:T(8,128)(2,1)S(1)}, bf16[384,768]{1,0:T(8,128)(2,1)}, u32[]{:S(2)}) copy-start(bf16[384,768]{1,0:T(8,128)(2,1)} %get-tuple-element.82) | copy-start | bytes 1769476
  999.3 67.4 %copy-start.6 = (f32[6,192,768]{2,1,0:T(8,128)S(1)}, f32[6,192,768]{2,1,0:T(8,128)}, u32[]{:S(2)}) copy-start(f32[6,192,768]{2,1,0:T(8,128)} %w_ref.1) | copy-start | bytes 10616836
  1066.8 10.5 copy-start.57
  1066.8 10.5 copy-start.61
  1066.8 10.5 copy-start.68
  1066.8 10.5 copy-start.69
  1066.8 11.1 %copy-start.47 = (f32[1000,768]{1,0:T(8,128)S(1)}, f32[1000,768]{1,0:T(8,128)}, u32[]{:S(2)}) copy-start(f32[1000,768]{1,0:T(8,128)} %param.30) | copy-start | bytes 9216004
  1066.8 11.1 %copy-start.48 = (f32[1000,768]{1,0:T(8,128)S(1)}, f32[1000,768]{1,0:T(8,128)}, u32[]{:S(2)}) copy-start(f32[1000,768]{1,0:T(8,128)} %param.32) | copy-start | bytes 9216004
  1066.8 11.1 %copy-start.49 = (f32[1000,768]{1,0:T(8,128)S(1)}, f32[1000,768]{1,0:T(8,128)}, u32[]{:S(2)}) copy-start(f32[1000,768]{1,0:T(8,128)} %param.31) | copy-start | bytes 9216004
  1066.8 11.4 %copy-start.53 = (f32[1000,768]{1,0:T(8,128)S(1)}, f32[1000,768]{1,0:T(8,128)}, u32[]{:S(2)}) copy-start(f32[1000,768]{1,0:T(8,128)} %get-tuple-element.142) | copy-start | bytes 9216004
  1078.2 8.3 copy-start.54
  (45 other events, 136.1 us)
Sparse Core Ops, SparseCore 0:
  80.2 159.0 all-gather.3
  242.6 112.1 all-gather.5
  620.4 267.7 reduce-scatter.1

commit v5 on v4

--- a/solution.py
+++ b/solution.py
@@ -253,13 +253,13 @@
     )(x)
 
 
-def reduce_steps(zn, p_ref, o_ref, acc, crecv, dxr, dyr, xr, yr, zur, zdr, ssem, rsem, lsem):
+def reduce_steps(zn, p_refs, o_ref, acc, crecv, dxr, dyr, xr, yr, zur, zdr, ssem, rsem, lsem):
     y, x, c, z = [lax.axis_index(n) for n in ALL]
     me = z if zn > 1 else 0
-    rows, cols = p_ref.shape[1:]
-    h0 = half_rows(rows, p_ref.dtype)
+    rows, each = acc.shape[1], p_refs[0].shape[1]
+    h0 = half_rows(rows, acc.dtype)
     h1 = rows - h0
-    X, Y, DX, DY, C0, ZU, ZD = 0, 1, 2, 3, 4, 8, 9
+    X, Y, DX, DY, ZU, ZD = range(6)
     nx, ny, nc = {"x": 1 - x}, {"y": 1 - y}, {"c": 1 - c}
     kinds = [(y, x), (y, 1 - x), (1 - y, x), (1 - y, 1 - x)]
     step = 32 if rows % 32 == 0 else 16
@@ -272,10 +272,20 @@
         return remote(src, dst, ssem.at[kind, k], rsem.at[kind, k], **to)
 
     def load(k, zb):
-        return pltpu.make_async_copy(p_ref.at[slot(k, c, zb)], acc.at[k * zn + zb], lsem.at[k * zn + zb])
+        b = k * zn + zb
+        return [
+            pltpu.make_async_copy(
+                p.at[slot(k, c, zb)], acc.at[b, pl.ds(i * each, each)], lsem.at[b, i]
+            )
+            for i, p in enumerate(p_refs)
+        ]
 
     def across(k, zb):
-        return copy(C0 + k, zb, p_ref.at[slot(k, 1 - c, zb)], crecv.at[k * zn + zb], nc)
+        b = k * zn + zb
+        return [
+            copy(10 + 4 * i + k, zb, p.at[slot(k, 1 - c, zb)], crecv.at[b, pl.ds(i * each, each)], nc)
+            for i, p in enumerate(p_refs)
+        ]
 
     def add(dst, start, count, terms):
         size = step if count % step == 0 else 16
@@ -292,12 +302,14 @@
     zorder = [lax.rem(z + j, zn) if zn > 1 else 0 for j in range(zn)]
     for k in (3, 1, 2, 0):
         for zb in range(zn):
-            across(k, zb).start()
-            load(k, zb).start()
+            for over, near in zip(across(k, zb), load(k, zb)):
+                over.start()
+                near.start()
 
     def ready(k, zb):
-        load(k, zb).wait()
-        across(k, zb).wait_recv()
+        for over, near in zip(across(k, zb), load(k, zb)):
+            near.wait()
+            over.wait_recv()
 
     for zb in range(zn):
         yield
@@ -387,7 +399,8 @@
 
     for zb in range(zn):
         for k in range(4):
-            across(k, zb).wait_send()
+            for over in across(k, zb):
+                over.wait_send()
         copy(DX, zb, dxr.at[zb], dxr.at[zb], nx).wait_send()
         copy(DY, zb, dyr.at[zb], dyr.at[zb], ny).wait_send()
         copy(X, zb, xr.at[zb], xr.at[zb], nx).wait_send()
@@ -403,17 +416,17 @@
                 copy(ZD, zb, zdr.at[zb], zdr.at[zb], {"z": z - 1}).wait_send()
 
 
-def reduce_kernel(zn, *refs):
+def reduce_kernel(zn, p_ref, *refs):
     greet(zn, *[lax.axis_index(n) for n in ALL])
-    run_steps(reduce_steps(zn, *refs))
-
-
-def reduce_scratch(zn, rows, cols, dtype):
+    run_steps(reduce_steps(zn, [p_ref], *refs))
+
+
+def reduce_scratch(zn, rows, cols, dtype, inputs=1):
     h0 = half_rows(rows, dtype)
-    sems = pltpu.SemaphoreType.DMA((10, zn))
+    sems = pltpu.SemaphoreType.DMA((10 + 4 * inputs, zn))
     counts = [(4 * zn, rows), (4 * zn, rows), (zn, h0), (zn, rows - h0)] + [(zn, rows)] * 4
     blocks = [pltpu.VMEM((n, r, cols), dtype) for n, r in counts]
-    return blocks + [sems, sems, pltpu.SemaphoreType.DMA((4 * zn,))]
+    return blocks + [sems, sems, pltpu.SemaphoreType.DMA((4 * zn, inputs))]
 
 
 def reduce_scatter(p, zn, ident, name, out_dtype=None):
@@ -431,31 +444,35 @@
     )(p)
 
 
-def both_kernel(zr, zg, p_ref, x_ref, r_ref, o_ref, *scratch):
+def both_kernel(inputs, zr, zg, *refs):
+    p_refs, (x_ref, r_ref, o_ref), scratch = refs[:inputs], refs[inputs : inputs + 3], refs[inputs + 3 :]
     greet(max(zr, zg), *[lax.axis_index(n) for n in ALL])
     count = len(reduce_scratch(1, 32, 128, jnp.float32))
     run_steps(
-        reduce_steps(zr, p_ref, r_ref, *scratch[:count]),
+        reduce_steps(zr, p_refs, r_ref, *scratch[:count]),
         gather_steps(zg, x_ref, o_ref, *scratch[count:]),
     )
 
 
-def scatter_and_gather(p, zr, x, zg, ident, name):
-    count, rows, cols = p.shape
+def scatter_and_gather(parts, zr, x, zg, ident, name):
+    inputs = len(parts)
+    count, each, cols = parts[0].shape
+    rows, dtype = inputs * each, parts[0].dtype
     return pl.pallas_call(
-        functools.partial(both_kernel, zr, zg),
+        functools.partial(both_kernel, inputs, zr, zg),
         out_shape=(
-            jax.ShapeDtypeStruct((rows, cols), p.dtype),
+            jax.ShapeDtypeStruct((rows, cols), dtype),
             jax.ShapeDtypeStruct((8 * zg,) + x.shape, x.dtype),
         ),
-        in_specs=[pl.BlockSpec(memory_space=pl.ANY)] * 2,
+        in_specs=[pl.BlockSpec(memory_space=pl.ANY)] * (inputs + 1),
         out_specs=(pl.BlockSpec(memory_space=pltpu.VMEM), pl.BlockSpec(memory_space=pl.ANY)),
-        scratch_shapes=reduce_scratch(zr, rows, cols, p.dtype) + gather_scratch(zg, x.shape, x.dtype),
+        scratch_shapes=reduce_scratch(zr, rows, cols, dtype, inputs)
+        + gather_scratch(zg, x.shape, x.dtype),
         compiler_params=pltpu.CompilerParams(
             collective_id=ident, has_side_effects=True, vmem_limit_bytes=56 << 20
         ),
         name=name,
-    )(p, x)
+    )(*parts, x)
 
 
 def greet_pair(x, c):
@@ -707,12 +724,12 @@
         mask_bias(bias_ref, kseg_ref, qseg_ref, qpos_ref)
 
     length = bias_ref.shape[0]
-    q = q_ref[...]
+    q = q_ref[...] * HD ** (-0.5)
     k, v = k_ref[...].reshape(length, 128), v_ref[...].reshape(length, 128)
     outs = []
     for head in range(2):
         mine = head_lanes(q.shape, head)
-        s = dot_nt(k, jnp.where(mine, q, jnp.zeros_like(q))) * HD ** (-0.5) + bias_ref[...]
+        s = dot_nt(k, jnp.where(mine, q, jnp.zeros_like(q))) + bias_ref[...]
         top = jnp.max(s, axis=0, keepdims=True)
         e = jnp.exp(s - top)
         total = jnp.sum(e, axis=0, keepdims=True)
@@ -791,20 +808,22 @@
 
 
 def feed_back_kernel(
-    dy_ref, mid_ref, g_ref, o_ref, wo_ref, wg_ref, wu_ref, wd_ref,
-    grad_ref, dx_ref, do_ref, dgain_ref,
-    b_ref, e_ref, dg_ref, du_ref, db_ref,
+    groups, dy_ref, mid_ref, g_ref, o_ref, wo_ref, wg_ref, wu_ref, wd_ref, dx_ref, do_ref, dgain_ref,
+    *refs,
 ):
+    grad_refs, (b_ref, bt_ref, e_ref, dg_ref, du_ref, db_ref) = refs[:-6], refs[-6:]
     t = pl.program_id(0)
     last = pl.num_programs(0) - 1
-    deep, tile_rows = grad_ref.shape[0], grad_ref.shape[1]
-
-    def emit(g):
-        grad_ref[...] = g.astype(jnp.bfloat16).reshape(deep, tile_rows, D)
+
+    def emit(kind, g):
+        ref = grad_refs[groups[kind]]
+        ref[...] = g.astype(jnp.bfloat16).reshape(ref.shape)
 
     @pl.when(t == 0)
     def _():
-        b_ref[...] = root_norm(mid_ref[...], g_ref[...]).astype(jnp.bfloat16)
+        b = root_norm(mid_ref[...], g_ref[...])
+        b_ref[...] = b.astype(jnp.bfloat16)
+        bt_ref[...] = b.T.astype(jnp.bfloat16)
         e_ref[...] = dy_ref[...].astype(jnp.bfloat16)
         db_ref[...] = jnp.zeros_like(db_ref)
 
@@ -814,19 +833,19 @@
         up = dot_nn(b_ref[...], wu_ref[...].reshape(D, D))
         sigma = jax.nn.sigmoid(gate)
         h = (gate * sigma * up).astype(jnp.bfloat16)
-        emit(dot_tn(h, e_ref[...]))
+        emit(0, dot_tn(h, e_ref[...]))
         dh = dot_nt(e_ref[...], wd_ref[...].reshape(D, D))
         dg_ref[...] = (dh * up * sigma * (1.0 + gate * (1.0 - sigma))).astype(jnp.bfloat16)
         du_ref[...] = (dh * gate * sigma).astype(jnp.bfloat16)
 
     @pl.when(t % 3 == 1)
     def _():
-        emit(dot_tn(b_ref[...], dg_ref[...]))
+        emit(1, dot_nn(bt_ref[...], dg_ref[...]))
         db_ref[...] += dot_nt(dg_ref[...], wg_ref[...].reshape(D, D))
 
     @pl.when(t % 3 == 2)
     def _():
-        emit(dot_tn(b_ref[...], du_ref[...]))
+        emit(2, dot_nn(bt_ref[...], du_ref[...]))
         db_ref[...] += dot_nt(du_ref[...], wu_ref[...].reshape(D, D))
 
     @pl.when(t == last)
@@ -836,7 +855,7 @@
         dx_ref[...] = dx
         dgain_ref[...] = jnp.broadcast_to(gain_back[None, :], dgain_ref.shape)
         e1 = dx.astype(jnp.bfloat16)
-        emit(dot_tn(o_ref[...], e1))
+        emit(3, dot_tn(o_ref[...], e1))
         do_ref[...] = dot_nt(e1, wo_ref[...].reshape(D, D)).astype(jnp.bfloat16)
 
 
@@ -847,32 +866,39 @@
     arrays, specs = weight_specs(
         weights, (3, lambda t: 0 * t), (4, unit), (4 + UNITS, unit), (4 + 2 * UNITS, unit)
     )
-
-    def grad_tile(t):
-        kind = t % 3
-        base = jnp.where(kind == 0, 4 + 2 * UNITS, jnp.where(kind == 1, 4, 4 + UNITS))
-        return jnp.where(t == 3 * UNITS, 3, base + unit(t))
+    firsts = [4 + 2 * UNITS, 4, 4 + UNITS, 3]
+    groups = [first // dp for first in firsts]
+
+    def grad_tile(group, t):
+        kinds = [k for k in range(3) if groups[k] == group]
+        s, k = unit(t), t % 3
+        tile = firsts[kinds[0]] + jnp.where(k < kinds[0], jnp.maximum(s - 1, 0), s)
+        for kind in kinds[1:]:
+            tile = jnp.where(k >= kind, firsts[kind] + s, tile)
+        final = 3 if groups[3] == group else firsts[kinds[-1]] + UNITS - 1
+        return jnp.where(t == 3 * UNITS, final, tile)
 
     return pl.pallas_call(
-        feed_back_kernel,
+        functools.partial(feed_back_kernel, groups),
         grid=(3 * UNITS + 1,),
         out_shape=(
-            jax.ShapeDtypeStruct((dp, deep, len(weights), tile_rows, D), jnp.bfloat16),
             jax.ShapeDtypeStruct((rows, D), jnp.float32),
             jax.ShapeDtypeStruct((rows, D), jnp.bfloat16),
             jax.ShapeDtypeStruct((8, D), jnp.float32),
-        ),
+        )
+        + (jax.ShapeDtypeStruct((dp, deep, 1, tile_rows, D), jnp.bfloat16),) * len(weights),
         in_specs=[
             whole((rows, D)), whole((rows, D)), whole((1, D)), whole((rows, D)), *specs,
         ],
-        out_specs=(
-            tile_spec(dp, deep, tile_rows, grad_tile),
-            whole((rows, D)), whole((rows, D)), whole((8, D)),
+        out_specs=(whole((rows, D)), whole((rows, D)), whole((8, D)))
+        + tuple(
+            tile_spec(dp, deep, tile_rows, functools.partial(grad_tile, group), 0)
+            for group in range(len(weights))
         ),
         scratch_shapes=[
+            pltpu.VMEM((rows, D), jnp.bfloat16), pltpu.VMEM((D, rows), jnp.bfloat16),
             pltpu.VMEM((rows, D), jnp.bfloat16), pltpu.VMEM((rows, D), jnp.bfloat16),
-            pltpu.VMEM((rows, D), jnp.bfloat16), pltpu.VMEM((rows, D), jnp.bfloat16),
-            pltpu.VMEM((rows, D), jnp.float32),
+            pltpu.VMEM((rows, D), jnp.bfloat16), pltpu.VMEM((rows, D), jnp.float32),
         ],
         compiler_params=pltpu.CompilerParams(vmem_limit_bytes=48 << 20),
         name="feed_back",
@@ -888,24 +914,24 @@
 
     length = bias_ref.shape[0]
     parts, rows = dkv_ref.shape[0], q_ref.shape[0]
-    q, do = q_ref[...], do_ref[...]
+    q, do = q_ref[...] * HD ** (-0.5), do_ref[...]
     k, v = k_ref[...].reshape(length, 128), v_ref[...].reshape(length, 128)
     dqs, dk, dv = [], None, None
     for head in range(2):
         mine = head_lanes(q.shape, head)
         qm = jnp.where(mine, q, jnp.zeros_like(q))
         dom = jnp.where(mine, do, jnp.zeros_like(do))
-        s = dot_nt(k, qm) * HD ** (-0.5) + bias_ref[...]
+        s = dot_nt(k, qm) + bias_ref[...]
         p = jnp.exp(s - lse_ref[head : head + 1, :])
         dp = dot_nt(v, dom)
         delta = jnp.sum(p * dp, axis=0, keepdims=True)
-        ds = (p * (dp - delta) * HD ** (-0.5)).astype(jnp.bfloat16)
+        ds = (p * (dp - delta)).astype(jnp.bfloat16)
         dv_part = dot_nn(p.astype(jnp.bfloat16), dom)
         dk_part = dot_nn(ds, qm)
         dv = dv_part if dv is None else dv + dv_part
         dk = dk_part if dk is None else dk + dk_part
         dqs.append(dot_tn(ds, k))
-    dq_ref[...] = jnp.where(head_lanes(dqs[0].shape, 0), dqs[0], dqs[1])
+    dq_ref[...] = jnp.where(head_lanes(dqs[0].shape, 0), dqs[0], dqs[1]) * HD ** (-0.5)
     dkv_ref[:, 0] = dk.astype(jnp.bfloat16).reshape(parts, rows, 128)
     dkv_ref[:, 1] = dv.astype(jnp.bfloat16).reshape(parts, rows, 128)
 
@@ -980,7 +1006,7 @@
             pl.BlockSpec(memory_space=pl.ANY),
         ],
         out_specs=(
-            tile_spec(dp, deep, tile_rows, lambda t: t), whole((rows, D)), whole((8, D)),
+            tile_spec(dp, deep, tile_rows, lambda t: t, 0), whole((rows, D)), whole((8, D)),
         ),
         scratch_shapes=[
             pltpu.VMEM((rows, D), jnp.bfloat16), pltpu.VMEM((rows, D), jnp.bfloat16),
@@ -1004,13 +1030,13 @@
 def layer_backward(grad, kept, weights, layer, gains, cos, sin, marks):
     state, mid, q, kv, lse, o = kept
     rows = state.shape[0]
-    grads, dx, do, feed_gain = feed_back(
+    dx, do, feed_gain, *grads = feed_back(
         grad, mid, gains[2 * layer + 1 : 2 * layer + 2], o, weights
     )
     dq, dkv = attend_back(q, kv, *marks, do, lse)
     dkv = keys_sum_scatter(dkv.reshape(-1, D)).reshape(2, rows, D)
-    grads, dx, input_gain = project_back(
-        dx, state, gains[2 * layer : 2 * layer + 1], cos, sin, dq, dkv, weights, grads
+    grads[0], dx, input_gain = project_back(
+        dx, state, gains[2 * layer : 2 * layer + 1], cos, sin, dq, dkv, weights, grads[0]
     )
     return dx, grads, [input_gain[0], feed_gain[0]]
 
@@ -1102,7 +1128,7 @@
     placed = place_tiles(tile_weight, home_slots, home_mine.astype(jnp.int32), dp_size)
     placed = placed.reshape(dp_size, -1, D)
     if fits():
-        home, packed = scatter_and_gather(placed, 1, padded(own_part), 4, 0, "home_and_ids")
+        home, packed = scatter_and_gather([placed], 1, padded(own_part), 4, 0, "home_and_ids")
     else:
         home = lax.psum_scatter(placed, DP, scatter_dimension=0)
         packed = lax.all_gather(padded(own_part), ALL, axis=0)
@@ -1156,7 +1182,8 @@
     capacity = 3 * comp // (2 * rep_size)
     block = completion_all // rows
     inside = block[:, None, :] == jnp.arange(b_size)[None, :, None]
-    rank = jnp.cumsum(inside.astype(jnp.int32), axis=2) - 1
+    before = jnp.sum((block[:, None, :] < jnp.arange(b_size)[None, :, None]).astype(jnp.int32), axis=2)
+    rank = jnp.arange(comp)[None, None, :] - before[:, :, None]
     slot_pick = inside[..., None] & (rank[..., None] == jnp.arange(capacity))
     filled = jnp.any(slot_pick, axis=2)
     wanted = jnp.where(
@@ -1197,6 +1224,7 @@
         (jnp.exp(logits - log_total[:, None]) - jnp.where(hot, 1.0, 0.0)) / scored,
         0.0,
     ).astype(jnp.bfloat16)
+    logit_grad = lax.optimization_barrier(logit_grad)
     rows_grad = jnp.dot(logit_grad, head_low, preferred_element_type=jnp.float32)
     own_rows = scatter_all(
         rows_grad.astype(jnp.bfloat16).reshape(devices, -1, D), 9, "back_scatter"
@@ -1211,14 +1239,16 @@
             state_grad, kept_list[index], weights[index], index, gain_weight, cosine, sine, marks
         )
     entry = state_grad.astype(jnp.bfloat16)
-    parts = [part.reshape(devices, -1, D) for part in tile_parts]
-    home_grads = [None] + [
-        lax.psum_scatter(part, ALL, scatter_dimension=0) for part in parts[1:]
-    ]
+    flat = [[part.reshape(devices, -1, D) for part in layer] for layer in tile_parts]
     if fits():
-        home_grads[0], piece_grads = scatter_and_gather(parts[0], 4, entry, 4, 2, "grads_and_entry")
+        tail = [lax.psum_scatter(flat[-1][-1], ALL, scatter_dimension=0)]
+        firsts = [part for layer in flat for part in layer][:-1]
+        body, piece_grads = scatter_and_gather(firsts, 4, entry, 4, 2, "grads_and_entry")
+        home_grads = [body] + tail
     else:
-        home_grads[0] = lax.psum_scatter(parts[0], ALL, scatter_dimension=0)
+        home_grads = [
+            lax.psum_scatter(part, ALL, scatter_dimension=0) for layer in flat for part in layer
+        ]
         piece_grads = lax.all_gather(entry, ALL, axis=0)
     table_grad = jnp.einsum(
         "tv,td->vd", token_hot, piece_grads.reshape(-1, D), preferred_element_type=jnp.float32

time: 1110 us -> 1120 us (level)
  local copies, waits for them, and re-layouts: 49.5 us -> 62.8 us
    unnamed x183 -> x193, local copies, waits for them, and re-layouts: 27.9 us -> 42.4 us
  transfers between devices with their start and end apart: 3 -> 3, of which waited for: 0 -> 0; matrix products, arithmetic and copies ran while one was open for 7% -> 6% of each run, Pallas kernels for 53% -> 56%
where the time goes in v5:
time: 1120 us; the launch traced here: 1110 us
  Pallas kernels  900 us (80%)
  matrix products  70.6 us (6%)
  local copies, waits for them, and re-layouts  62.8 us (6%)
  other arithmetic  58.2 us (5%)
  between operations  22.3 us (2%)
    pallas_call x2, Pallas kernels, scatter_and_gather(): pl.pallas_call(functools.partial(both_kernel, inputs, zr, zg), out_shape=...  266 us
    pallas_call x5, Pallas kernels, all_gather(): pl.pallas_call(functools.partial(gather_kernel, zn), out_shape=jax.ShapeD...  246 us
    pallas_call x2, Pallas kernels, reduce_scatter(): pl.pallas_call(functools.partial(reduce_kernel, zn), out_shape=jax.ShapeD...  138 us
    pallas_call x2, Pallas kernels, feed_back(): pl.pallas_call(functools.partial(feed_back_kernel, groups), grid=(3 * UNI...  54.6 us
    pallas_call x2, Pallas kernels, keys_gather(): pl.pallas_call(keys_gather_kernel, out_shape=jax.ShapeDtypeStruct((4,) +...  52.5 us
    pallas_call x2, Pallas kernels, keys_reduce(): pl.pallas_call(keys_reduce_kernel, out_shape=jax.ShapeDtypeStruct(block,...  46.1 us
    unnamed x193, local copies, waits for them, and re-layouts  42.4 us
    pallas_call x2, Pallas kernels, attend_back(): pl.pallas_call(attend_back_kernel, grid=(HEADS // 2,), out_shape=(jax.Sha...  28.1 us
  transfers between devices with their start and end apart: 3, of which 0 were waited for; matrix products, arithmetic and copies ran while one was open for 6% of the time, Pallas kernels for 56%

profile of v5, /device:TPU:0, one launch (start us, length us, event | category | flops | bytes accessed | tf_op | source)
XLA Modules:
  0.0 1113.9 jit_solution(3017158987962565865)
XLA Ops:
  13.3 2.0 copy-done.9
  15.3 2.5 place_tiles.1
  17.9 3.7 copy-done.8
  21.5 56.7 %home_and_ids.1 = (bf16[768,768]{1,0:T(8,128)(2,1)}, s32[32,16,128]{2,1,0:T(8,128)}) custom-call(bf16[8,768,768]{2,1,0:T(8,128)(2,1)} %bitcast.96, s32[16,128]{1,0:T(8,128)} %pad_bitcast_fusion.refs_1_), custom_call_target="tpu_custom_call" | custom-call | tf_op jit(solution)/shard_map/home_and_ids/pallas_call | solution.py:461
  78.3 2.0 slice.70
  80.3 1.9 fusion.44
  87.1 19.6 %fusion.4 = bf16[8192,768]{1,0:T(8,128)(2,1)} fusion(s32[8192]{0:T(1024)S(1)} %bitcast.142, f32[1000,768]{1,0:T(8,128)} %param.27), kind=kOutput, calls=%fused_computation.8 | convolution fusion | flops 12598163456 | bytes 15687680 | tf_op jit(solution)/shard_map/dot_general | solution.py:1153
  106.7 108.0 %rows_scatter.1 = bf16[256,768]{1,0:T(8,128)(2,1)} custom-call(bf16[32,256,768]{2,1,0:T(8,128)(2,1)} %bitcast.118), custom_call_target="tpu_custom_call" | custom-call | tf_op jit(solution)/shard_map/rows_scatter/pallas_call | solution.py:434
  215.8 93.5 %weights_gather.1 = bf16[32,192,768]{2,1,0:T(8,128)(2,1)} custom-call(bf16[192,768]{1,0:T(8,128)(2,1)} %get-tuple-element.62.refs_0_), custom_call_target="tpu_custom_call" | custom-call | tf_op jit(solution)/shard_map/weights_gather/pallas_call | solution.py:245
  311.5 4.8 project.2
  317.1 29.8 %keys_gather.2 = bf16[4,512,768]{2,1,0:T(8,128)(2,1)} custom-call(bf16[512,768]{1,0:T(8,128)(2,1)} %bitcast.101), custom_call_target="tpu_custom_call" | custom-call | tf_op jit(solution)/shard_map/keys_gather/pallas_call | solution.py:512
  348.9 13.1 %attend.2 = (bf16[256,768]{1,0:T(8,128)(2,1)S(1)}, f32[6,8,256]{2,1,0:T(8,128)S(1)}) custom-call(bf16[256,768]{1,0:T(8,128)(2,1)S(1)} %get-tuple-element.58.q_ref, bf16[4,2,256,768]{3,2,1,0:T(8,128)(2,1)S(1)} %bitcast.88, bf16[4,2,256,768]{3,2,1,0:T(8,128)(2,1)S(1)} %bitcast.89, s32[1024,1]{1,0:T(8,128)S(1)} %copy.86.kseg_ref, ...), custom_call_target="tpu_custom_call" | custom-call | tf_op jit(solution)/shard_map/attend/pallas_call | solution.py:756
  362.6 10.7 feed.2
  373.3 2.8 project.3
  377.0 22.6 %keys_gather.3 = bf16[4,512,768]{2,1,0:T(8,128)(2,1)} custom-call(bf16[512,768]{1,0:T(8,128)(2,1)} %bitcast.102), custom_call_target="tpu_custom_call" | custom-call | tf_op jit(solution)/shard_map/keys_gather/pallas_call | solution.py:512
  401.6 13.1 %attend.3 = (bf16[256,768]{1,0:T(8,128)(2,1)S(1)}, f32[6,8,256]{2,1,0:T(8,128)S(1)}) custom-call(bf16[256,768]{1,0:T(8,128)(2,1)S(1)} %get-tuple-element.63.q_ref, bf16[4,2,256,768]{3,2,1,0:T(8,128)(2,1)S(1)} %bitcast.92, bf16[4,2,256,768]{3,2,1,0:T(8,128)(2,1)S(1)} %bitcast.93, s32[1024,1]{1,0:T(8,128)S(1)} %copy.86.kseg_ref, ...), custom_call_target="tpu_custom_call" | custom-call | tf_op jit(solution)/shard_map/attend/pallas_call | solution.py:756
  417.0 9.5 feed.3
  429.1 30.3 %chosen_gather.1 = bf16[32,96,768]{2,1,0:T(8,128)(2,1)} custom-call(bf16[96,768]{1,0:T(8,128)(2,1)} %convolution_convert_fusion.1.refs_0_), custom_call_target="tpu_custom_call" | custom-call | tf_op jit(solution)/shard_map/chosen_gather/pallas_call | solution.py:245
  459.3 8.0 fusion.47
  467.4 4.5 copy-done.52
  471.8 3.3 exponential_reduce_fusion
  475.8 19.6 %stats_gather.1 = f32[32,72,128]{2,1,0:T(8,128)} custom-call(f32[72,128]{1,0:T(8,128)} %pad_maximum_fusion.3.refs_0_), custom_call_target="tpu_custom_call" | custom-call | tf_op jit(solution)/shard_map/stats_gather/pallas_call | solution.py:245
  498.4 7.0 select_convert_fusion
  505.5 7.4 convolution_convert_fusion
  512.9 30.5 %back_scatter.1 = bf16[96,768]{1,0:T(8,128)(2,1)} custom-call(bf16[32,96,768]{2,1,0:T(8,128)(2,1)} %bitcast.123), custom_call_target="tpu_custom_call" | custom-call | tf_op jit(solution)/shard_map/back_scatter/pallas_call | solution.py:434
  543.5 2.1 multiply_reduce_fusion.3
  545.8 25.8 %feed_back.2 = (f32[256,768]{1,0:T(8,128)S(1)}, bf16[256,768]{1,0:T(8,128)(2,1)S(1)}, f32[8,768]{1,0:T(8,128)S(1)}, bf16[8,4,1,192,768]{4,3,2,1,0:T(8,128)(2,1)}, bf16[8,4,1,192,768]{4,3,2,1,0:T(8,128)(2,1)}) custom-call(f32[256,768]{1,0:T(8,128)S(1)} %multiply_subtract_fusion.2.dy_ref, f32[256,768]{1,0:T(8,128)S(1)} %copy-done.32, ...), custom_call_target="tpu_custom_call" | custom-call | tf_op jit(solution)/shard_map/feed_back/pallas_call | solution.py:881
  582.3 14.0 %attend_back.2 = (f32[256,768]{1,0:T(8,128)S(1)}, bf16[4,2,256,768]{3,2,1,0:T(8,128)(2,1)S(1)}) custom-call(bf16[256,768]{1,0:T(8,128)(2,1)S(1)} %copy-done.21, bf16[4,2,256,768]{3,2,1,0:T(8,128)(2,1)} %bitcast.90, bf16[4,2,256,768]{3,2,1,0:T(8,128)(2,1)} %bitcast.91, s32[1024,1]{1,0:T(8,128)S(1)} %copy.86.kseg_ref, s32[1,256]{1,0:T(1,128)S(1)} %copy-done.46, ...), custom_call_target="tpu_custom_call" | custom-call | tf_op jit(solution)/shard_map/attend_back/pallas_call | solution.py:942
  598.0 2.3 copy-done.14
  600.4 21.6 %keys_reduce.2 = bf16[512,768]{1,0:T(8,128)(2,1)S(1)} custom-call(bf16[4,512,768]{2,1,0:T(8,128)(2,1)S(1)} %bitcast.99), custom_call_target="tpu_custom_call" | custom-call | tf_op jit(solution)/shard_map/keys_reduce/pallas_call | solution.py:563
  623.2 5.3 project_back.2
  629.2 28.9 %feed_back.3 = (f32[256,768]{1,0:T(8,128)S(1)}, bf16[256,768]{1,0:T(8,128)(2,1)S(1)}, f32[8,768]{1,0:T(8,128)S(1)}, bf16[8,4,1,192,768]{4,3,2,1,0:T(8,128)(2,1)}, bf16[8,4,1,192,768]{4,3,2,1,0:T(8,128)(2,1)}) custom-call(f32[256,768]{1,0:T(8,128)S(1)} %get-tuple-element.74.dy_ref, f32[256,768]{1,0:T(8,128)S(1)} %copy-done.23, ...), custom_call_target="tpu_custom_call" | custom-call | tf_op jit(solution)/shard_map/feed_back/pallas_call | solution.py:881
  662.7 14.0 %attend_back.3 = (f32[256,768]{1,0:T(8,128)S(1)}, bf16[4,2,256,768]{3,2,1,0:T(8,128)(2,1)S(1)}) custom-call(bf16[256,768]{1,0:T(8,128)(2,1)S(1)} %copy-done.19, bf16[4,2,256,768]{3,2,1,0:T(8,128)(2,1)} %bitcast.86, bf16[4,2,256,768]{3,2,1,0:T(8,128)(2,1)} %bitcast.87, s32[1024,1]{1,0:T(8,128)S(1)} %copy.86.kseg_ref, s32[1,256]{1,0:T(1,128)S(1)} %copy-done.47, ...), custom_call_target="tpu_custom_call" | custom-call | tf_op jit(solution)/shard_map/attend_back/pallas_call | solution.py:942
  676.8 24.5 %keys_reduce.3 = bf16[512,768]{1,0:T(8,128)(2,1)S(1)} custom-call(bf16[4,512,768]{2,1,0:T(8,128)(2,1)S(1)} %bitcast.98), custom_call_target="tpu_custom_call" | custom-call | tf_op jit(solution)/shard_map/keys_reduce/pallas_call | solution.py:563
  701.4 5.5 project_back.3
  706.9 3.6 copy-done.5
  712.1 1.9 convert_element_type.87.refs_3_
  715.3 209.7 %grads_and_entry.1 = (bf16[576,768]{1,0:T(8,128)(2,1)}, bf16[32,256,768]{2,1,0:T(8,128)(2,1)}) custom-call(bf16[32,192,768]{2,1,0:T(8,128)(2,1)} %bitcast.94, bf16[32,192,768]{2,1,0:T(8,128)(2,1)} %bitcast.119, bf16[32,192,768]{2,1,0:T(8,128)(2,1)} %bitcast.95, bf16[256,768]{1,0:T(8,128)(2,1)} %convert_element_type.87.refs_3_), custom_call_target="tpu_custom_call" | custom-call | tf_op jit(solution)/shard_map/grads_and_entry/pallas_call | solution.py:461
  925.1 11.3 %multiply_reduce_fusion.1 = (f32[]{:T(128)}, f32[1000,768]{1,0:T(8,128)}) fusion(bf16[3072,1000]{0,1:T(8,128)(2,1)} %copy-done.53, bf16[3072,768]{1,0:T(8,128)(2,1)} %bitcast.122), kind=kOutput, calls=%fused_computation.34 | convolution fusion | flops 4720128000 | bytes 13934596 | tf_op jit(solution)/shard_map/rv,rd->vd/dot_general | solution.py:1232
  936.4 21.3 %multiply_reduce_fusion.2 = (f32[]{:T(128)}, f32[1000,768]{1,0:T(8,128)}) fusion(bf16[8192,768]{1,0:T(8,128)(2,1)} %bitcast.146, s32[8192]{0:T(1024)S(1)} %bitcast.143), kind=kOutput, calls=%fused_computation.35 | convolution fusion | flops 12592640000 | bytes 15687684 | tf_op jit(solution)/shard_map/tv,td->vd/dot_general | solution.py:1253
  957.7 2.1 pad_maximum_fusion.refs_0_
  959.7 45.0 %owners_gather.1 = bf16[8,768,768]{2,1,0:T(8,128)(2,1)} custom-call(bf16[768,768]{1,0:T(8,128)(2,1)} %pad_maximum_fusion.refs_0_), custom_call_target="tpu_custom_call" | custom-call | tf_op jit(solution)/shard_map/owners_gather/pallas_call | solution.py:245
  1004.8 5.9 gather_fusion.2
  1010.7 3.1 multiply_reduce_fusion
  1016.4 58.0 %sums_gather.1 = f32[32,32,128]{2,1,0:T(8,128)} custom-call(f32[32,128]{1,0:T(8,128)} %fusion.22.refs_0_), custom_call_target="tpu_custom_call" | custom-call | tf_op jit(solution)/shard_map/sums_gather/pallas_call | solution.py:245
  1080.1 10.4 fusion.43
  1091.5 6.0 fusion.39
  1099.7 4.9 fusion.41
  (278 shorter events, 57.8 us)
Async XLA Ops:
  7.2 304.2 %all-gather.4.cloned.1.call-start = ((), (), s32[]{:S(2)}) async-start(), calls=%async_computation.1 | async-start | bytes 19464192 | tf_op jit(solution)/shard_map/all_gather | solution.py:1144
  80.2 335.7 %all-gather.6.cloned.1.call-start = ((), (), s32[]{:S(2)}) async-start(), calls=%async_computation.3 | async-start | bytes 9732096 | tf_op jit(solution)/shard_map/all_gather | solution.py:1147
  82.2 875.5 %reduce-scatter.2.cloned.1.call-start = ((), (), s32[]{:S(2)}) async-start(), calls=%async_computation.2 | async-start | bytes 9732096 | tf_op jit(solution)/shard_map/reduce_scatter | solution.py:1244
  82.5 24.2 %copy-start.74 = (s32[8,2,4,128]{3,1,2,0:T(2,128)}, s32[8,2,4,128]{3,1,2,0:T(2,128)S(1)}, u32[]{:S(2)}) copy-start(s32[8,2,4,128]{3,1,2,0:T(2,128)S(1)} %copy.95) | copy-start | bytes 98308
  86.2 20.5 %copy-start.72 = (pred[8,4,96]{2,0,1:T(8,128)(4,1)}, pred[8,4,96]{2,0,1:T(8,128)(4,1)S(1)}, u32[]{:S(2)}) copy-start(pred[8,4,96]{2,0,1:T(8,128)(4,1)S(1)} %get-tuple-element.134) | copy-start | bytes 9220
  215.8 95.0 %copy-start.69 = (f32[5,768]{1,0:T(8,128)S(1)}, f32[5,768]{1,0:T(8,128)}, u32[]{:S(2)}) copy-start(f32[5,768]{1,0:T(8,128)} %param.33) | copy-start | bytes 46084
  309.4 90.2 %copy-start.45 = (s32[1,256]{1,0:T(1,128)}, s32[1,256]{1,0:T(1,128)S(1)}, u32[]{:S(2)}) copy-start(s32[1,256]{1,0:T(1,128)S(1)} %dynamic_slice.36.qseg_ref) | copy-start | bytes 3076
  309.5 90.2 %copy-start.48 = (s32[1,256]{1,0:T(1,128)}, s32[1,256]{1,0:T(1,128)S(1)}, u32[]{:S(2)}) copy-start(s32[1,256]{1,0:T(1,128)S(1)} %iota_add_fusion.1.qpos_ref) | copy-start | bytes 3076
  311.4 61.8 %copy-start.43 = (f32[1,768]{1,0:T(1,128)}, f32[1,768]{1,0:T(1,128)S(1)}, u32[]{:S(2)}) copy-start(f32[1,768]{1,0:T(1,128)S(1)} %get-tuple-element.128.g_ref) | copy-start | bytes 9220
  317.1 44.8 %copy-start.18 = (bf16[256,768]{1,0:T(8,128)(2,1)}, bf16[256,768]{1,0:T(8,128)(2,1)S(1)}, u32[]{:S(2)}) copy-start(bf16[256,768]{1,0:T(8,128)(2,1)S(1)} %get-tuple-element.58.q_ref) | copy-start | bytes 1179652
  362.6 10.7 slice-start
  362.6 10.7 slice-start.1
  362.6 10.7 slice-start.2
  373.3 42.7 %copy-start.11 = (f32[256,768]{1,0:T(8,128)}, f32[256,768]{1,0:T(8,128)S(1)}, u32[]{:S(2)}) copy-start(f32[256,768]{1,0:T(8,128)S(1)} %get-tuple-element.61.x_ref) | copy-start | bytes 2359300
  377.0 37.6 %copy-start.20 = (bf16[256,768]{1,0:T(8,128)(2,1)}, bf16[256,768]{1,0:T(8,128)(2,1)S(1)}, u32[]{:S(2)}) copy-start(bf16[256,768]{1,0:T(8,128)(2,1)S(1)} %get-tuple-element.63.q_ref) | copy-start | bytes 1179652
  417.0 11.1 copy-start.67
  417.0 11.1 copy-start.85
  428.1 31.2 %copy-start.78 = (f32[256]{0:T(256)}, f32[256]{0:T(256)S(1)}, u32[]{:S(2)}) copy-start(f32[256]{0:T(256)S(1)} %get-tuple-element.139) | copy-start | bytes 3076
  459.3 12.5 %copy-start.65 = (s32[3072]{0:T(1024)S(1)}, s32[3072]{0:T(1024)}, u32[]{:S(2)}) copy-start(s32[3072]{0:T(1024)} %sub.138) | copy-start | bytes 36868
  471.8 26.6 %copy-start.81 = (pred[3072]{0:T(1024)(128)(4,1)S(1)}, pred[3072]{0:T(1024)(128)(4,1)}, u32[]{:S(2)}) copy-start(pred[3072]{0:T(1024)(128)(4,1)} %ge.50) | copy-start | bytes 9220
  512.9 30.5 %copy-start.79 = (f32[256]{0:T(256)S(1)}, f32[256]{0:T(256)}, u32[]{:S(2)}) copy-start(f32[256]{0:T(256)} %copy-done.78) | copy-start | bytes 3076
  512.9 30.6 %copy-start.86 = (s32[96]{0:T(128)S(1)}, s32[96]{0:T(128)}, u32[]{:S(2)}) copy-start(s32[96]{0:T(128)} %fusion.34) | copy-start | bytes 1156
  512.9 32.7 %copy-start.87 = (f32[256]{0:T(256)S(1)}, f32[256]{0:T(256)}, u32[]{:S(2)}) copy-start(f32[256]{0:T(256)} %get-tuple-element.138) | copy-start | bytes 3076
  582.3 39.7 %copy-start.6 = (bf16[8,4,1,192,768]{4,3,2,1,0:T(8,128)(2,1)S(1)}, bf16[8,4,1,192,768]{4,3,2,1,0:T(8,128)(2,1)}, u32[]{:S(2)}) copy-start(bf16[8,4,1,192,768]{4,3,2,1,0:T(8,128)(2,1)} %get-tuple-element.73.held_ref) | copy-start | bytes 28311556
  598.0 23.9 %copy-start.26 = (f32[256,768]{1,0:T(8,128)}, f32[256,768]{1,0:T(8,128)S(1)}, u32[]{:S(2)}) copy-start(f32[256,768]{1,0:T(8,128)S(1)} %get-tuple-element.71.dq_ref) | copy-start | bytes 2359300
  598.0 24.0 %copy-start.12 = (f32[256,768]{1,0:T(8,128)S(1)}, f32[256,768]{1,0:T(8,128)}, u32[]{:S(2)}) copy-start(f32[256,768]{1,0:T(8,128)} %copy-done.11) | copy-start | bytes 2359300
  600.4 21.6 %copy-start.25 = (f32[256,768]{1,0:T(8,128)S(1)}, f32[256,768]{1,0:T(8,128)}, u32[]{:S(2)}) copy-start(f32[256,768]{1,0:T(8,128)} %copy-done.24) | copy-start | bytes 2359300
  600.4 21.6 %copy-start.44 = (f32[1,768]{1,0:T(1,128)S(1)}, f32[1,768]{1,0:T(1,128)}, u32[]{:S(2)}) copy-start(f32[1,768]{1,0:T(1,128)} %copy-done.43) | copy-start | bytes 9220
  628.5 29.5 %copy-start.7 = (bf16[8,4,1,192,768]{4,3,2,1,0:T(8,128)(2,1)}, bf16[8,4,1,192,768]{4,3,2,1,0:T(8,128)(2,1)S(1)}, u32[]{:S(2)}) copy-start(bf16[8,4,1,192,768]{4,3,2,1,0:T(8,128)(2,1)S(1)} %get-tuple-element.84) | copy-start | bytes 28311556
  629.2 31.1 %copy-start.19 = (bf16[256,768]{1,0:T(8,128)(2,1)S(1)}, bf16[256,768]{1,0:T(8,128)(2,1)}, u32[]{:S(2)}) copy-start(bf16[256,768]{1,0:T(8,128)(2,1)} %copy-done.18) | copy-start | bytes 1179652
  629.2 31.1 %copy-start.47 = (s32[1,256]{1,0:T(1,128)S(1)}, s32[1,256]{1,0:T(1,128)}, u32[]{:S(2)}) copy-start(s32[1,256]{1,0:T(1,128)} %copy-done.45) | copy-start | bytes 3076
  662.7 38.6 %copy-start.4 = (bf16[8,4,1,192,768]{4,3,2,1,0:T(8,128)(2,1)S(1)}, bf16[8,4,1,192,768]{4,3,2,1,0:T(8,128)(2,1)}, u32[]{:S(2)}) copy-start(bf16[8,4,1,192,768]{4,3,2,1,0:T(8,128)(2,1)} %get-tuple-element.81.held_ref) | copy-start | bytes 28311556
  676.8 24.6 %copy-start.34 = (f32[256,768]{1,0:T(8,128)S(1)}, f32[256,768]{1,0:T(8,128)}, u32[]{:S(2)}) copy-start(f32[256,768]{1,0:T(8,128)} %copy-done.33) | copy-start | bytes 2359300
  701.3 10.7 copy-start.82
  701.4 10.7 copy-start.83
  701.4 10.7 copy-start.84
  701.4 12.7 %copy-start.68 = (f32[2,4,4,96]{3,2,1,0:T(4,128)S(1)}, f32[2,4,4,96]{3,2,1,0:T(4,128)}, u32[]{:S(2)}) copy-start(f32[2,4,4,96]{3,2,1,0:T(4,128)} %sub.142) | copy-start | bytes 36868
  701.4 12.7 %copy-start.73 = (pred[8,4,96]{2,0,1:T(8,128)(4,1)S(1)}, pred[8,4,96]{2,0,1:T(8,128)(4,1)}, u32[]{:S(2)}) copy-start(pred[8,4,96]{2,0,1:T(8,128)(4,1)} %copy-done.72) | copy-start | bytes 9220
  925.1 11.3 %copy-start.75 = (s32[8,2,4,128]{3,1,2,0:T(2,128)S(1)}, s32[8,2,4,128]{3,1,2,0:T(2,128)}, u32[]{:S(2)}) copy-start(s32[8,2,4,128]{3,1,2,0:T(2,128)} %copy-done.74) | copy-start | bytes 98308
  936.4 21.3 %copy-start.63 = (bf16[576,768]{1,0:T(8,128)(2,1)S(1)}, bf16[576,768]{1,0:T(8,128)(2,1)}, u32[]{:S(2)}) copy-start(bf16[576,768]{1,0:T(8,128)(2,1)} %get-tuple-element.86) | copy-start | bytes 2654212
  1004.8 75.3 %copy-start.10 = (f32[6,192,768]{2,1,0:T(8,128)S(1)}, f32[6,192,768]{2,1,0:T(8,128)}, u32[]{:S(2)}) copy-start(f32[6,192,768]{2,1,0:T(8,128)} %w_ref.1) | copy-start | bytes 10616836
  1080.0 10.5 copy-start.70
  1080.0 10.5 copy-start.76
  1080.0 10.5 copy-start.77
  1080.0 11.1 copy-start.55
  1080.1 11.1 copy-start.56
  1080.1 11.1 copy-start.57
  1080.1 11.4 %copy-start.62 = (f32[1000,768]{1,0:T(8,128)S(1)}, f32[1000,768]{1,0:T(8,128)}, u32[]{:S(2)}) copy-start(f32[1000,768]{1,0:T(8,128)} %get-tuple-element.146) | copy-start | bytes 9216004
  (50 other events, 138.1 us)
Sparse Core Ops, SparseCore 0:
  80.4 162.6 all-gather.3
  246.4 107.2 all-gather.5
  573.3 144.5 reduce-scatter.1

commit v6 on v5

--- a/solution.py
+++ b/solution.py
@@ -78,6 +78,8 @@
 
 
 MESH = pl.DeviceIdType.MESH
+LAG = 8
+VMEM = 60 << 20
 
 
 def half_rows(rows, dtype):
@@ -224,16 +226,17 @@
 
 
 def run_steps(*parts):
-    parts = list(parts)
+    parts, turn = list(parts), 0
     while parts:
         for part in list(parts):
-            if next(part, part) is part:
+            if turn >= part[0] and next(part[1], part) is part:
                 parts.remove(part)
+        turn += 1
 
 
 def gather_kernel(zn, *refs):
     greet(zn, *[lax.axis_index(n) for n in ALL])
-    run_steps(gather_steps(zn, *refs))
+    run_steps((0, gather_steps(zn, *refs)))
 
 
 def gather_scratch(zn, shape, dtype):
@@ -248,21 +251,25 @@
         in_specs=[pl.BlockSpec(memory_space=pl.ANY)],
         out_specs=pl.BlockSpec(memory_space=pl.ANY),
         scratch_shapes=gather_scratch(zn, x.shape, x.dtype),
-        compiler_params=pltpu.CompilerParams(collective_id=ident, has_side_effects=True),
+        compiler_params=pltpu.CompilerParams(
+            collective_id=ident, has_side_effects=True, vmem_limit_bytes=VMEM
+        ),
         name=name,
     )(x)
 
 
-def reduce_steps(zn, p_refs, o_ref, acc, crecv, dxr, dyr, xr, yr, zur, zdr, ssem, rsem, lsem):
+def reduce_steps(zn, p_ref, at, o_ref, to, acc, crecv, dxr, dyr, xr, yr, zur, zdr, ssem, rsem, lsem):
     y, x, c, z = [lax.axis_index(n) for n in ALL]
     me = z if zn > 1 else 0
-    rows, each = acc.shape[1], p_refs[0].shape[1]
+    rows = acc.shape[1]
     h0 = half_rows(rows, acc.dtype)
     h1 = rows - h0
-    X, Y, DX, DY, ZU, ZD = range(6)
+    X, Y, DX, DY, ZU, ZD, C0 = range(7)
     nx, ny, nc = {"x": 1 - x}, {"y": 1 - y}, {"c": 1 - c}
     kinds = [(y, x), (y, 1 - x), (1 - y, x), (1 - y, 1 - x)]
     step = 32 if rows % 32 == 0 else 16
+    zorder = sorted(range(zn), key=lambda zb: (abs(2 * zb - zn + 1), zb), reverse=True)
+    out_rows = o_ref.at[pl.ds(to, rows)]
 
     def slot(k, cc, zz):
         yy, xx = kinds[k]
@@ -273,52 +280,41 @@
 
     def load(k, zb):
         b = k * zn + zb
-        return [
-            pltpu.make_async_copy(
-                p.at[slot(k, c, zb)], acc.at[b, pl.ds(i * each, each)], lsem.at[b, i]
-            )
-            for i, p in enumerate(p_refs)
-        ]
+        return pltpu.make_async_copy(p_ref.at[slot(k, c, zb), pl.ds(at, rows)], acc.at[b], lsem.at[b])
 
     def across(k, zb):
-        b = k * zn + zb
-        return [
-            copy(10 + 4 * i + k, zb, p.at[slot(k, 1 - c, zb)], crecv.at[b, pl.ds(i * each, each)], nc)
-            for i, p in enumerate(p_refs)
-        ]
+        source = p_ref.at[slot(k, 1 - c, zb), pl.ds(at, rows)]
+        return copy(C0 + k, zb, source, crecv.at[k * zn + zb], nc)
 
     def add(dst, start, count, terms):
         size = step if count % step == 0 else 16
 
         @pl.loop(0, count // size)
         def _(i):
-            at = pl.ds(pl.multiple_of(start + i * size, 16), size)
+            here = pl.ds(pl.multiple_of(start + i * size, 16), size)
             total = None
             for ref, base in terms:
                 part = ref[pl.ds(pl.multiple_of(start - base + i * size, 16), size), :].astype(jnp.float32)
                 total = part if total is None else total + part
-            dst[at, :] = total.astype(dst.dtype)
-
-    zorder = [lax.rem(z + j, zn) if zn > 1 else 0 for j in range(zn)]
+            dst[here, :] = total.astype(dst.dtype)
+
     for k in (3, 1, 2, 0):
-        for zb in range(zn):
-            for over, near in zip(across(k, zb), load(k, zb)):
-                over.start()
-                near.start()
+        for zb in zorder:
+            across(k, zb).start()
+            load(k, zb).start()
 
     def ready(k, zb):
-        for over, near in zip(across(k, zb), load(k, zb)):
-            near.wait()
-            over.wait_recv()
-
-    for zb in range(zn):
+        load(k, zb).wait()
+        across(k, zb).wait_recv()
+
+    for zb in zorder:
         yield
         ready(3, zb)
         b = 3 * zn + zb
         add(acc.at[b], 0, rows, [(acc.at[b], 0), (crecv.at[b], 0)])
         copy(DX, zb, acc.at[b, pl.ds(0, h0)], dxr.at[zb], nx).start()
         copy(DY, zb, acc.at[b, pl.ds(h0, h1)], dyr.at[zb], ny).start()
-    for zb in range(zn):
+    for zb in zorder:
         yield
         ready(1, zb)
         b = zn + zb
@@ -337,13 +333,13 @@
     def column(zb):
         return [(acc.at[zb], 0), (crecv.at[zb], 0), (xr.at[zb], 0), (yr.at[zb], 0)]
 
-    for zb in range(zn):
+    for zb in zorder:
         yield
         ready(0, zb)
         copy(X, zb, acc.at[zb], xr.at[zb], nx).wait_recv()
         copy(Y, zb, acc.at[zb], yr.at[zb], ny).wait_recv()
         if zn == 1:
-            add(o_ref, 0, rows, column(0))
+            add(out_rows, 0, rows, column(0))
             continue
 
         def upward(zb=zb):
@@ -384,23 +380,22 @@
         @pl.when(z == 0)
         def _():
             copy(ZD, me, acc.at[me], zdr.at[me], {"z": z + 1}).wait_recv()
-            add(o_ref, 0, rows, [(acc.at[me], 0), (zdr.at[me], 0)])
+            add(out_rows, 0, rows, [(acc.at[me], 0), (zdr.at[me], 0)])
 
         @pl.when(z == zn - 1)
         def _():
             copy(ZU, me, acc.at[me], zur.at[me], {"z": z - 1}).wait_recv()
-            add(o_ref, 0, rows, [(acc.at[me], 0), (zur.at[me], 0)])
+            add(out_rows, 0, rows, [(acc.at[me], 0), (zur.at[me], 0)])
 
         @pl.when((z > 0) & (z < zn - 1))
         def _():
             copy(ZD, me, acc.at[me], zdr.at[me], {"z": z + 1}).wait_recv()
             copy(ZU, me, acc.at[me], zur.at[me], {"z": z + 1}).wait_recv()
-            add(o_ref, 0, rows, [(acc.at[me], 0), (zdr.at[me], 0), (zur.at[me], 0)])
+            add(out_rows, 0, rows, [(acc.at[me], 0), (zdr.at[me], 0), (zur.at[me], 0)])
 
     for zb in range(zn):
         for k in range(4):
-            for over in across(k, zb):
-                over.wait_send()
+            across(k, zb).wait_send()
         copy(DX, zb, dxr.at[zb], dxr.at[zb], nx).wait_send()
         copy(DY, zb, dyr.at[zb], dyr.at[zb], ny).wait_send()
         copy(X, zb, xr.at[zb], xr.at[zb], nx).wait_send()
@@ -416,17 +411,37 @@
                 copy(ZD, zb, zdr.at[zb], zdr.at[zb], {"z": z - 1}).wait_send()
 
 
-def reduce_kernel(zn, p_ref, *refs):
+def segments_of(rows):
+    if rows < 192:
+        return [(0, rows)]
+    first = (rows // 2 + 31) // 32 * 32
+    return [(0, first), (first, rows - first)]
+
+
+def reduce_plan(zn, p_refs, o_ref, scratch):
+    parts, base = [], 0
+    for p_ref in p_refs:
+        for at, rows in segments_of(p_ref.shape[1]):
+            mine, scratch = scratch[:11], scratch[11:]
+            parts.append((LAG * len(parts), reduce_steps(zn, p_ref, at, o_ref, base + at, *mine)))
+        base += p_ref.shape[1]
+    return parts
+
+
+def reduce_kernel(zn, p_ref, o_ref, *scratch):
     greet(zn, *[lax.axis_index(n) for n in ALL])
-    run_steps(reduce_steps(zn, [p_ref], *refs))
-
-
-def reduce_scratch(zn, rows, cols, dtype, inputs=1):
-    h0 = half_rows(rows, dtype)
-    sems = pltpu.SemaphoreType.DMA((10 + 4 * inputs, zn))
-    counts = [(4 * zn, rows), (4 * zn, rows), (zn, h0), (zn, rows - h0)] + [(zn, rows)] * 4
-    blocks = [pltpu.VMEM((n, r, cols), dtype) for n, r in counts]
-    return blocks + [sems, sems, pltpu.SemaphoreType.DMA((4 * zn, inputs))]
+    run_steps(*reduce_plan(zn, [p_ref], o_ref, scratch))
+
+
+def reduce_scratch(zn, rows, cols, dtype):
+    entries = []
+    for _, n in segments_of(rows):
+        h0 = half_rows(n, dtype)
+        sems = pltpu.SemaphoreType.DMA((10, zn))
+        counts = [(4 * zn, n), (4 * zn, n), (zn, h0), (zn, n - h0)] + [(zn, n)] * 4
+        entries += [pltpu.VMEM((m, r, cols), dtype) for m, r in counts]
+        entries += [sems, sems, pltpu.SemaphoreType.DMA((4 * zn,))]
+    return entries
 
 
 def reduce_scatter(p, zn, ident, name, out_dtype=None):
@@ -438,7 +453,7 @@
         out_specs=pl.BlockSpec(memory_space=pltpu.VMEM),
         scratch_shapes=reduce_scratch(zn, rows, cols, p.dtype),
         compiler_params=pltpu.CompilerParams(
-            collective_id=ident, has_side_effects=True, vmem_limit_bytes=56 << 20
+            collective_id=ident, has_side_effects=True, vmem_limit_bytes=VMEM
         ),
         name=name,
     )(p)
@@ -447,11 +462,8 @@
 def both_kernel(inputs, zr, zg, *refs):
     p_refs, (x_ref, r_ref, o_ref), scratch = refs[:inputs], refs[inputs : inputs + 3], refs[inputs + 3 :]
     greet(max(zr, zg), *[lax.axis_index(n) for n in ALL])
-    count = len(reduce_scratch(1, 32, 128, jnp.float32))
-    run_steps(
-        reduce_steps(zr, p_refs, r_ref, *scratch[:count]),
-        gather_steps(zg, x_ref, o_ref, *scratch[count:]),
-    )
+    gather = (0, gather_steps(zg, x_ref, o_ref, *scratch[-4:]))
+    run_steps(gather, *reduce_plan(zr, p_refs, r_ref, scratch[:-4]))
 
 
 def scatter_and_gather(parts, zr, x, zg, ident, name):
@@ -466,10 +478,10 @@
         ),
         in_specs=[pl.BlockSpec(memory_space=pl.ANY)] * (inputs + 1),
         out_specs=(pl.BlockSpec(memory_space=pltpu.VMEM), pl.BlockSpec(memory_space=pl.ANY)),
-        scratch_shapes=reduce_scratch(zr, rows, cols, dtype, inputs)
+        scratch_shapes=reduce_scratch(zr, each, cols, dtype) * inputs
         + gather_scratch(zg, x.shape, x.dtype),
         compiler_params=pltpu.CompilerParams(
-            collective_id=ident, has_side_effects=True, vmem_limit_bytes=56 << 20
+            collective_id=ident, has_side_effects=True, vmem_limit_bytes=VMEM
         ),
         name=name,
     )(*parts, x)
@@ -515,7 +527,9 @@
         in_specs=[pl.BlockSpec(memory_space=pl.ANY)],
         out_specs=pl.BlockSpec(memory_space=pl.ANY),
         scratch_shapes=[pltpu.VMEM(v.shape, v.dtype), sems, sems, pltpu.SemaphoreType.DMA((2,))],
-        compiler_params=pltpu.CompilerParams(collective_id=ident, has_side_effects=True),
+        compiler_params=pltpu.CompilerParams(
+            collective_id=ident, has_side_effects=True, vmem_limit_bytes=VMEM
+        ),
         name="keys_gather",
     )(v)
 
@@ -570,7 +584,7 @@
             pltpu.VMEM(block, p.dtype), sems, sems, pltpu.SemaphoreType.DMA((2,)),
         ],
         compiler_params=pltpu.CompilerParams(
-            collective_id=ident, has_side_effects=True, vmem_limit_bytes=32 << 20
+            collective_id=ident, has_side_effects=True, vmem_limit_bytes=VMEM
         ),
         name="keys_reduce",
     )(p)
@@ -703,7 +717,7 @@
             pl.BlockSpec((None, rows, D), lambda t: (jnp.maximum(t - 1, 0), 0, 0)),
         ),
         scratch_shapes=[pltpu.VMEM((rows, D), jnp.bfloat16)],
-        compiler_params=pltpu.CompilerParams(vmem_limit_bytes=40 << 20),
+        compiler_params=pltpu.CompilerParams(vmem_limit_bytes=VMEM),
         name="project",
     )(x, gain, cos, sin, *arrays)
 
@@ -763,7 +777,7 @@
         in_specs=specs,
         out_specs=(pair, pl.BlockSpec((None, 8, rows), lambda t: (t, 0, 0))),
         scratch_shapes=[pltpu.VMEM((parts * rows, rows), jnp.float32)],
-        compiler_params=pltpu.CompilerParams(vmem_limit_bytes=40 << 20),
+        compiler_params=pltpu.CompilerParams(vmem_limit_bytes=VMEM),
         name="attend",
     )(q, kv, kv, kseg, qseg, qpos)
 
@@ -802,7 +816,7 @@
         ],
         out_specs=(whole((rows, D)), whole((rows, D))),
         scratch_shapes=[pltpu.VMEM((rows, D), jnp.bfloat16)],
-        compiler_params=pltpu.CompilerParams(vmem_limit_bytes=48 << 20),
+        compiler_params=pltpu.CompilerParams(vmem_limit_bytes=VMEM),
         name="feed",
     )(x, o, gain, *arrays)
 
@@ -900,7 +914,7 @@
             pltpu.VMEM((rows, D), jnp.bfloat16), pltpu.VMEM((rows, D), jnp.bfloat16),
             pltpu.VMEM((rows, D), jnp.bfloat16), pltpu.VMEM((rows, D), jnp.float32),
         ],
-        compiler_params=pltpu.CompilerParams(vmem_limit_bytes=48 << 20),
+        compiler_params=pltpu.CompilerParams(vmem_limit_bytes=VMEM),
         name="feed_back",
     )(dy, mid, gain, o, *arrays)
 
@@ -949,7 +963,7 @@
         in_specs=specs + [pair, pl.BlockSpec((None, 8, rows), lambda t: (t, 0, 0))],
         out_specs=(pair, pl.BlockSpec((parts, 2, rows, 128), lambda t: (0, 0, 0, t))),
         scratch_shapes=[pltpu.VMEM((parts * rows, rows), jnp.float32)],
-        compiler_params=pltpu.CompilerParams(vmem_limit_bytes=48 << 20),
+        compiler_params=pltpu.CompilerParams(vmem_limit_bytes=VMEM),
         name="attend_back",
     )(q, kv, kv, kseg, qseg, qpos, do, lse)
 
@@ -1013,7 +1027,7 @@
             pltpu.VMEM((rows, D), jnp.float32),
         ],
         input_output_aliases={8: 0},
-        compiler_params=pltpu.CompilerParams(vmem_limit_bytes=40 << 20),
+        compiler_params=pltpu.CompilerParams(vmem_limit_bytes=VMEM),
         name="project_back",
     )(dx, x, gain, cos, sin, dq, dkv, *arrays, grads)
 
@@ -1066,7 +1080,7 @@
             out_specs=pl.BlockSpec((count, rows, cols), lambda g, *_: (g, 0, 0)),
         ),
         out_shape=jax.ShapeDtypeStruct((dp_size * count, rows, cols), jnp.bfloat16),
-        compiler_params=pltpu.CompilerParams(vmem_limit_bytes=24 << 20),
+        compiler_params=pltpu.CompilerParams(vmem_limit_bytes=VMEM),
         name="place_tiles",
     )(slots, mine, tile_weight)
 

time: 1120 us -> 1030 us (0.920)
  Pallas kernels: 900 us -> 853 us
  local copies, waits for them, and re-layouts: 62.8 us -> 22.9 us
    pallas_call x5, Pallas kernels: 246 us -> 182 us  [all_gather(): pl.pallas_call(functools.partial(gather_kernel, zn), out_shape=jax.ShapeD...]
    unnamed x193 -> x51, local copies, waits for them, and re-layouts: 42.4 us -> 5.19 us
    pallas_call x2, Pallas kernels: 266 us -> 252 us  [scatter_and_gather(): pl.pallas_call(functools.partial(both_kernel, inputs, zr, zg), out_shape=...]
  transfers between devices with their start and end apart: 3 -> 3, of which waited for: 0 -> 0; matrix products, arithmetic and copies ran while one was open for 6% -> 7% of each run, Pallas kernels for 56% -> 59%
where the time goes in v6:
time: 1030 us; the launch traced here: 1020 us
  Pallas kernels  853 us (83%)
  matrix products  68.4 us (7%)
  other arithmetic  58.1 us (6%)
  local copies, waits for them, and re-layouts  22.9 us (2%)
  between operations  21.7 us (2%)
    pallas_call x2, Pallas kernels, scatter_and_gather(): pl.pallas_call(functools.partial(both_kernel, inputs, zr, zg), out_shape=...  252 us
    pallas_call x5, Pallas kernels, all_gather(): pl.pallas_call(functools.partial(gather_kernel, zn), out_shape=jax.ShapeD...  182 us
    pallas_call x2, Pallas kernels, reduce_scatter(): pl.pallas_call(functools.partial(reduce_kernel, zn), out_shape=jax.ShapeD...  140 us
    pallas_call x2, Pallas kernels, keys_gather(): pl.pallas_call(keys_gather_kernel, out_shape=jax.ShapeDtypeStruct((4,) +...  59.3 us
    pallas_call x2, Pallas kernels, feed_back(): pl.pallas_call(functools.partial(feed_back_kernel, groups), grid=(3 * UNI...  54.7 us
    pallas_call x2, Pallas kernels, keys_reduce(): pl.pallas_call(keys_reduce_kernel, out_shape=jax.ShapeDtypeStruct(block,...  51.2 us
    pallas_call x2, Pallas kernels, attend(): pl.pallas_call(attend_kernel, grid=(HEADS // 2,), out_shape=(jax.ShapeDty...  29.1 us
    pallas_call x2, Pallas kernels, attend_back(): pl.pallas_call(attend_back_kernel, grid=(HEADS // 2,), out_shape=(jax.Sha...  28.4 us
  transfers between devices with their start and end apart: 3, of which 0 were waited for; matrix products, arithmetic and copies ran while one was open for 7% of the time, Pallas kernels for 59%

profile of v6, /device:TPU:0, one launch (start us, length us, event | category | flops | bytes accessed | tf_op | source)
XLA Modules:
  0.0 1024.5 jit_solution(17027791687904768198)
XLA Ops:
  14.3 8.2 place_tiles.1
  22.5 57.1 %home_and_ids.1 = (bf16[768,768]{1,0:T(8,128)(2,1)}, s32[32,16,128]{2,1,0:T(8,128)}) custom-call(bf16[8,768,768]{2,1,0:T(8,128)(2,1)} %bitcast.108, s32[16,128]{1,0:T(8,128)} %pad_bitcast_fusion.refs_1_), custom_call_target="tpu_custom_call" | custom-call | tf_op jit(solution)/shard_map/home_and_ids/pallas_call | solution.py:473
  79.7 2.1 slice.70
  81.8 1.9 fusion.44
  86.3 1.6 select_reduce_fusion.1
  89.2 17.7 %fusion.4 = bf16[8192,768]{1,0:T(8,128)(2,1)} fusion(s32[8192]{0:T(1024)S(1)} %bitcast.140, f32[1000,768]{1,0:T(8,128)S(1)} %copy-done.9), kind=kOutput, calls=%fused_computation.8 | convolution fusion | flops 12598163456 | bytes 15687680 | tf_op jit(solution)/shard_map/dot_general | solution.py:1167
  106.8 106.3 %rows_scatter.1 = bf16[256,768]{1,0:T(8,128)(2,1)} custom-call(bf16[32,256,768]{2,1,0:T(8,128)(2,1)} %bitcast.110), custom_call_target="tpu_custom_call" | custom-call | tf_op jit(solution)/shard_map/rows_scatter/pallas_call | solution.py:449
  213.1 1.9 convert_element_type.78.x_ref
  215.1 69.5 %weights_gather.1 = bf16[32,192,768]{2,1,0:T(8,128)(2,1)} custom-call(bf16[192,768]{1,0:T(8,128)(2,1)} %get-tuple-element.62.refs_0_), custom_call_target="tpu_custom_call" | custom-call | tf_op jit(solution)/shard_map/weights_gather/pallas_call | solution.py:248
  287.9 5.4 project.2
  293.4 35.5 %keys_gather.2 = bf16[4,512,768]{2,1,0:T(8,128)(2,1)} custom-call(bf16[512,768]{1,0:T(8,128)(2,1)} %bitcast.122), custom_call_target="tpu_custom_call" | custom-call | tf_op jit(solution)/shard_map/keys_gather/pallas_call | solution.py:524
  328.9 14.5 %attend.2 = (bf16[256,768]{1,0:T(8,128)(2,1)}, f32[6,8,256]{2,1,0:T(8,128)}) custom-call(bf16[256,768]{1,0:T(8,128)(2,1)} %get-tuple-element.58.q_ref, bf16[4,2,256,768]{3,2,1,0:T(8,128)(2,1)} %bitcast.98, bf16[4,2,256,768]{3,2,1,0:T(8,128)(2,1)} %bitcast.99, s32[1024,1]{1,0:T(8,128)} %copy.86.kseg_ref, s32[1,256]{1,0:T(1,128)} %dynamic_slice.36.qseg_ref, ...), custom_call_target="tpu_custom_call" | custom-call | tf_op jit(solution)/shard_map/attend/pallas_call | solution.py:770
  343.4 11.1 %feed.2 = (f32[256,768]{1,0:T(8,128)}, f32[256,768]{1,0:T(8,128)}) custom-call(f32[256,768]{1,0:T(8,128)} %convert_element_type.78.x_ref, bf16[256,768]{1,0:T(8,128)(2,1)} %get-tuple-element.60.o_ref, f32[1,768]{1,0:T(1,128)} %get-tuple-element.129.g_ref, bf16[8,4,2,192,768]{4,3,2,1,0:T(8,128)(2,1)} %bitcast.79, bf16[8,4,2,192,768]{4,3,2,1,0:T(8,128)(2,1)} %bitcast.80, ...), custom_call_target="tpu_custom_call" | custom-call | tf_op jit(solution)/shard_map/feed/pallas_call | solution.py:810
  354.5 5.4 project.3
  359.9 23.8 %keys_gather.3 = bf16[4,512,768]{2,1,0:T(8,128)(2,1)} custom-call(bf16[512,768]{1,0:T(8,128)(2,1)} %bitcast.123), custom_call_target="tpu_custom_call" | custom-call | tf_op jit(solution)/shard_map/keys_gather/pallas_call | solution.py:524
  383.7 14.5 %attend.3 = (bf16[256,768]{1,0:T(8,128)(2,1)}, f32[6,8,256]{2,1,0:T(8,128)}) custom-call(bf16[256,768]{1,0:T(8,128)(2,1)} %get-tuple-element.63.q_ref, bf16[4,2,256,768]{3,2,1,0:T(8,128)(2,1)} %bitcast.102, bf16[4,2,256,768]{3,2,1,0:T(8,128)(2,1)} %bitcast.103, s32[1024,1]{1,0:T(8,128)} %copy.86.kseg_ref, s32[1,256]{1,0:T(1,128)} %dynamic_slice.36.qseg_ref, ...), custom_call_target="tpu_custom_call" | custom-call | tf_op jit(solution)/shard_map/attend/pallas_call | solution.py:770
  398.3 11.0 %feed.3 = (f32[256,768]{1,0:T(8,128)}, f32[256,768]{1,0:T(8,128)}) custom-call(f32[256,768]{1,0:T(8,128)} %get-tuple-element.61.x_ref, bf16[256,768]{1,0:T(8,128)(2,1)} %get-tuple-element.65.o_ref, f32[1,768]{1,0:T(1,128)} %get-tuple-element.127.g_ref, bf16[8,4,1,192,768]{4,3,2,1,0:T(8,128)(2,1)} %bitcast.89, bf16[8,4,1,192,768]{4,3,2,1,0:T(8,128)(2,1)} %bitcast.90, ...), custom_call_target="tpu_custom_call" | custom-call | tf_op jit(solution)/shard_map/feed/pallas_call | solution.py:810
  409.2 1.4 multiply_reduce_fusion.5
  410.7 2.1 convolution_convert_fusion.1.refs_0_
  412.7 28.4 %chosen_gather.1 = bf16[32,96,768]{2,1,0:T(8,128)(2,1)} custom-call(bf16[96,768]{1,0:T(8,128)(2,1)} %convolution_convert_fusion.1.refs_0_), custom_call_target="tpu_custom_call" | custom-call | tf_op jit(solution)/shard_map/chosen_gather/pallas_call | solution.py:248
  441.2 7.3 fusion.47
  448.5 3.3 exponential_reduce_fusion
  453.6 20.0 %stats_gather.1 = f32[32,72,128]{2,1,0:T(8,128)} custom-call(f32[72,128]{1,0:T(8,128)} %pad_maximum_fusion.3.refs_0_), custom_call_target="tpu_custom_call" | custom-call | tf_op jit(solution)/shard_map/stats_gather/pallas_call | solution.py:248
  476.0 6.9 select_convert_fusion
  482.9 7.3 convolution_convert_fusion
  490.2 33.4 %back_scatter.1 = bf16[96,768]{1,0:T(8,128)(2,1)} custom-call(bf16[32,96,768]{2,1,0:T(8,128)(2,1)} %bitcast.115), custom_call_target="tpu_custom_call" | custom-call | tf_op jit(solution)/shard_map/back_scatter/pallas_call | solution.py:449
  523.6 1.4 multiply_reduce_fusion.3
  526.2 26.9 %feed_back.2 = (f32[256,768]{1,0:T(8,128)}, bf16[256,768]{1,0:T(8,128)(2,1)}, f32[8,768]{1,0:T(8,128)}, bf16[8,4,1,192,768]{4,3,2,1,0:T(8,128)(2,1)}, bf16[8,4,1,192,768]{4,3,2,1,0:T(8,128)(2,1)}) custom-call(f32[256,768]{1,0:T(8,128)} %multiply_subtract_fusion.2.dy_ref, f32[256,768]{1,0:T(8,128)} %get-tuple-element.67.mid_ref, ...), custom_call_target="tpu_custom_call" | custom-call | tf_op jit(solution)/shard_map/feed_back/pallas_call | solution.py:895
  555.4 14.2 %attend_back.2 = (f32[256,768]{1,0:T(8,128)}, bf16[4,2,256,768]{3,2,1,0:T(8,128)(2,1)}) custom-call(bf16[256,768]{1,0:T(8,128)(2,1)} %get-tuple-element.63.q_ref, bf16[4,2,256,768]{3,2,1,0:T(8,128)(2,1)} %bitcast.104, bf16[4,2,256,768]{3,2,1,0:T(8,128)(2,1)} %bitcast.105, s32[1024,1]{1,0:T(8,128)} %copy.86.kseg_ref, s32[1,256]{1,0:T(1,128)} %dynamic_slice.36.qseg_ref, ...), custom_call_target="tpu_custom_call" | custom-call | tf_op jit(solution)/shard_map/attend_back/pallas_call | solution.py:956
  569.6 24.0 %keys_reduce.2 = bf16[512,768]{1,0:T(8,128)(2,1)} custom-call(bf16[4,512,768]{2,1,0:T(8,128)(2,1)} %bitcast.118), custom_call_target="tpu_custom_call" | custom-call | tf_op jit(solution)/shard_map/keys_reduce/pallas_call | solution.py:577
  593.6 8.1 project_back.2
  602.5 27.8 %feed_back.3 = (f32[256,768]{1,0:T(8,128)}, bf16[256,768]{1,0:T(8,128)(2,1)}, f32[8,768]{1,0:T(8,128)}, bf16[8,4,1,192,768]{4,3,2,1,0:T(8,128)(2,1)}, bf16[8,4,1,192,768]{4,3,2,1,0:T(8,128)(2,1)}) custom-call(f32[256,768]{1,0:T(8,128)} %get-tuple-element.74.dy_ref, f32[256,768]{1,0:T(8,128)} %get-tuple-element.75.mid_ref, ...), custom_call_target="tpu_custom_call" | custom-call | tf_op jit(solution)/shard_map/feed_back/pallas_call | solution.py:895
  630.2 14.2 %attend_back.3 = (f32[256,768]{1,0:T(8,128)}, bf16[4,2,256,768]{3,2,1,0:T(8,128)(2,1)}) custom-call(bf16[256,768]{1,0:T(8,128)(2,1)} %get-tuple-element.58.q_ref, bf16[4,2,256,768]{3,2,1,0:T(8,128)(2,1)} %bitcast.100, bf16[4,2,256,768]{3,2,1,0:T(8,128)(2,1)} %bitcast.101, s32[1024,1]{1,0:T(8,128)} %copy.86.kseg_ref, s32[1,256]{1,0:T(1,128)} %dynamic_slice.36.qseg_ref, ...), custom_call_target="tpu_custom_call" | custom-call | tf_op jit(solution)/shard_map/attend_back/pallas_call | solution.py:956
  644.4 27.2 %keys_reduce.3 = bf16[512,768]{1,0:T(8,128)(2,1)} custom-call(bf16[4,512,768]{2,1,0:T(8,128)(2,1)} %bitcast.117), custom_call_target="tpu_custom_call" | custom-call | tf_op jit(solution)/shard_map/keys_reduce/pallas_call | solution.py:577
  671.7 8.0 project_back.3
  681.2 1.9 convert_element_type.87.refs_3_
  684.4 194.7 %grads_and_entry.1 = (bf16[576,768]{1,0:T(8,128)(2,1)}, bf16[32,256,768]{2,1,0:T(8,128)(2,1)}) custom-call(bf16[32,192,768]{2,1,0:T(8,128)(2,1)} %bitcast.106, bf16[32,192,768]{2,1,0:T(8,128)(2,1)} %bitcast.111, bf16[32,192,768]{2,1,0:T(8,128)(2,1)} %bitcast.107, bf16[256,768]{1,0:T(8,128)(2,1)} %convert_element_type.87.refs_3_), custom_call_target="tpu_custom_call" | custom-call | tf_op jit(solution)/shard_map/grads_and_entry/pallas_call | solution.py:473
  879.0 11.3 %multiply_reduce_fusion.1 = (f32[]{:T(128)}, f32[1000,768]{1,0:T(8,128)}) fusion(bf16[3072,1000]{0,1:T(8,128)(2,1)} %copy-done.4, bf16[3072,768]{1,0:T(8,128)(2,1)} %bitcast.114), kind=kOutput, calls=%fused_computation.34 | convolution fusion | flops 4720128000 | bytes 13934596 | tf_op jit(solution)/shard_map/rv,rd->vd/dot_general | solution.py:1246
  890.3 21.3 %multiply_reduce_fusion.2 = (f32[]{:T(128)}, f32[1000,768]{1,0:T(8,128)}) fusion(bf16[8192,768]{1,0:T(8,128)(2,1)} %bitcast.144, s32[8192]{0:T(1024)S(1)} %bitcast.141), kind=kOutput, calls=%fused_computation.35 | convolution fusion | flops 12592640000 | bytes 15687684 | tf_op jit(solution)/shard_map/tv,td->vd/dot_general | solution.py:1267
  911.7 2.1 pad_maximum_fusion.refs_0_
  913.7 45.3 %owners_gather.1 = bf16[8,768,768]{2,1,0:T(8,128)(2,1)} custom-call(bf16[768,768]{1,0:T(8,128)(2,1)} %pad_maximum_fusion.refs_0_), custom_call_target="tpu_custom_call" | custom-call | tf_op jit(solution)/shard_map/owners_gather/pallas_call | solution.py:248
  959.0 4.3 gather_fusion.2
  963.3 1.6 multiply_reduce_fusion
  967.6 18.7 %sums_gather.1 = f32[32,32,128]{2,1,0:T(8,128)} custom-call(f32[32,128]{1,0:T(8,128)} %fusion.22.refs_0_), custom_call_target="tpu_custom_call" | custom-call | tf_op jit(solution)/shard_map/sums_gather/pallas_call | solution.py:248
  990.1 10.6 %fusion.43 = (bf16[6,192,768]{2,1,0:T(8,128)(2,1)}, f32[6,192,768]{2,1,0:T(8,128)}, f32[6,192,768]{2,1,0:T(8,128)}, f32[6,192,768]{2,1,0:T(8,128)}) fusion(f32[6,192,768]{2,1,0:T(8,128)} %w_ref.1, f32[6,192,768]{2,1,0:T(8,128)} %param.26, f32[]{:T(128)} %bitcast.50, f32[]{:T(128)S(6)} %min.3, bf16[6,192,768]{2,1,0:T(8,128)(2,1)S(1)} %gather_fusion.2, ...), kind=kLoop, calls=%fused_computation.144 | loop fusion | flops 19464192 | bytes 24772628 | tf_op jit(solution)/shard_map/convert_element_type | solution.py:1313
  1002.0 6.0 fusion.39
  1008.0 1.4 copy-done.12
  1010.3 4.9 fusion.41
  (135 shorter events, 29.1 us)
Async XLA Ops:
  7.2 2.6 copy-start
  7.2 280.7 %all-gather.4.cloned.1.call-start = ((), (), s32[]{:S(2)}) async-start(), calls=%async_computation.1 | async-start | bytes 19464192 | tf_op jit(solution)/shard_map/all_gather | solution.py:1158
  79.7 9.5 copy-start.9
  81.8 316.5 %all-gather.6.cloned.1.call-start = ((), (), s32[]{:S(2)}) async-start(), calls=%async_computation.3 | async-start | bytes 9732096 | tf_op jit(solution)/shard_map/all_gather | solution.py:1161
  83.7 827.9 %reduce-scatter.2.cloned.1.call-start = ((), (), s32[]{:S(2)}) async-start(), calls=%async_computation.2 | async-start | bytes 9732096 | tf_op jit(solution)/shard_map/reduce_scatter | solution.py:1258
  85.0 21.9 %copy-start.20 = (s32[8,2,4,128]{3,1,2,0:T(2,128)}, s32[8,2,4,128]{3,1,2,0:T(2,128)S(1)}, u32[]{:S(2)}) copy-start(s32[8,2,4,128]{3,1,2,0:T(2,128)S(1)} %copy.95) | copy-start | bytes 98308
  88.0 18.8 %copy-start.18 = (pred[8,4,96]{2,0,1:T(8,128)(4,1)}, pred[8,4,96]{2,0,1:T(8,128)(4,1)S(1)}, u32[]{:S(2)}) copy-start(pred[8,4,96]{2,0,1:T(8,128)(4,1)S(1)} %get-tuple-element.134) | copy-start | bytes 9220
  215.1 72.2 %copy-start.16 = (f32[5,768]{1,0:T(8,128)S(1)}, f32[5,768]{1,0:T(8,128)}, u32[]{:S(2)}) copy-start(f32[5,768]{1,0:T(8,128)} %param.33) | copy-start | bytes 46084
  409.2 31.9 %copy-start.5 = (f32[1000,768]{1,0:T(8,128)S(1)}, f32[1000,768]{1,0:T(8,128)}, u32[]{:S(2)}) copy-start(f32[1000,768]{1,0:T(8,128)} %param.30) | copy-start | bytes 9216004
  448.5 4.5 copy-start.2
  482.8 7.3 copy-start.4
  490.2 33.5 %copy-start.3 = (f32[256,768]{1,0:T(8,128)S(1)}, f32[256,768]{1,0:T(8,128)}, u32[]{:S(2)}) copy-start(f32[256,768]{1,0:T(8,128)} %get-tuple-element.66) | copy-start | bytes 2359300
  671.7 11.4 %copy-start.19 = (pred[8,4,96]{2,0,1:T(8,128)(4,1)S(1)}, pred[8,4,96]{2,0,1:T(8,128)(4,1)}, u32[]{:S(2)}) copy-start(pred[8,4,96]{2,0,1:T(8,128)(4,1)} %copy-done.18) | copy-start | bytes 9220
  879.0 11.3 %copy-start.21 = (s32[8,2,4,128]{3,1,2,0:T(2,128)S(1)}, s32[8,2,4,128]{3,1,2,0:T(2,128)}, u32[]{:S(2)}) copy-start(s32[8,2,4,128]{3,1,2,0:T(2,128)} %copy-done.20) | copy-start | bytes 98308
  890.3 21.3 %copy-start.15 = (bf16[576,768]{1,0:T(8,128)(2,1)S(1)}, bf16[576,768]{1,0:T(8,128)(2,1)}, u32[]{:S(2)}) copy-start(bf16[576,768]{1,0:T(8,128)(2,1)} %get-tuple-element.86) | copy-start | bytes 2654212
  990.0 10.7 %copy-start.17 = (f32[5,768]{1,0:T(8,128)S(1)}, f32[5,768]{1,0:T(8,128)}, u32[]{:S(2)}) copy-start(f32[5,768]{1,0:T(8,128)} %param.33) | copy-start | bytes 46084
  990.0 10.7 %copy-start.22 = (f32[5,768]{1,0:T(8,128)S(1)}, f32[5,768]{1,0:T(8,128)}, u32[]{:S(2)}) copy-start(f32[5,768]{1,0:T(8,128)} %param.35) | copy-start | bytes 46084
  990.0 10.7 %copy-start.23 = (f32[5,768]{1,0:T(8,128)S(1)}, f32[5,768]{1,0:T(8,128)}, u32[]{:S(2)}) copy-start(f32[5,768]{1,0:T(8,128)} %param.34) | copy-start | bytes 46084
  990.0 11.4 %copy-start.6 = (f32[1000,768]{1,0:T(8,128)S(1)}, f32[1000,768]{1,0:T(8,128)}, u32[]{:S(2)}) copy-start(f32[1000,768]{1,0:T(8,128)} %param.30) | copy-start | bytes 9216004
  990.1 11.4 %copy-start.7 = (f32[1000,768]{1,0:T(8,128)S(1)}, f32[1000,768]{1,0:T(8,128)}, u32[]{:S(2)}) copy-start(f32[1000,768]{1,0:T(8,128)} %param.32) | copy-start | bytes 9216004
  990.1 11.3 %copy-start.8 = (f32[1000,768]{1,0:T(8,128)S(1)}, f32[1000,768]{1,0:T(8,128)}, u32[]{:S(2)}) copy-start(f32[1000,768]{1,0:T(8,128)} %param.31) | copy-start | bytes 9216004
  990.1 11.9 %copy-start.14 = (f32[1000,768]{1,0:T(8,128)S(1)}, f32[1000,768]{1,0:T(8,128)}, u32[]{:S(2)}) copy-start(f32[1000,768]{1,0:T(8,128)} %get-tuple-element.146) | copy-start | bytes 9216004
  1002.0 6.0 copy-start.10
  1002.0 6.0 copy-start.11
  1002.0 7.4 copy-start.12
  1002.0 8.3 copy-start.13
  1010.3 4.9 copy-start.1
Sparse Core Ops, SparseCore 0:
  81.9 165.9 all-gather.3
  251.3 89.3 all-gather.5
  553.2 135.8 reduce-scatter.1

commit v7 on v6

--- a/solution.py
+++ b/solution.py
@@ -78,7 +78,7 @@
 
 
 MESH = pl.DeviceIdType.MESH
-LAG = 8
+LAG_ONE, LAG_MANY = 8, 6
 VMEM = 60 << 20
 
 
@@ -411,19 +411,158 @@
                 copy(ZD, zb, zdr.at[zb], zdr.at[zb], {"z": z - 1}).wait_send()
 
 
-def segments_of(rows):
-    if rows < 192:
+def reduce_z_first_steps(
+    zn, p_ref, at, o_ref, to, acc, crecv, zur, zdr, dxr, dyr, xr, yr, ssem, rsem, lsem
+):
+    y, x, c, z = [lax.axis_index(n) for n in ALL]
+    rows = acc.shape[1]
+    h0 = half_rows(rows, acc.dtype)
+    h1 = rows - h0
+    X, Y, DX, DY, C, ZU, ZD = range(7)
+    nx, ny, nc = {"x": 1 - x}, {"y": 1 - y}, {"c": 1 - c}
+    up, down = {"z": z + 1}, {"z": z - 1}
+    kinds = [(y, x), (y, 1 - x), (1 - y, x), (1 - y, 1 - x)]
+    zorder = sorted(range(zn), key=lambda zb: (abs(2 * zb - zn + 1), zb), reverse=True)
+    blocks = [(k, zb) for k in range(4) for zb in range(zn)]
+
+    def slot(k, cc, zz):
+        yy, xx = kinds[k]
+        return ((yy * 2 + xx) * 2 + cc) * zn + zz
+
+    def copy(kind, k, src, dst, to):
+        return remote(src, dst, ssem.at[kind, k], rsem.at[kind, k], **to)
+
+    def load(k, zb):
+        b = k * zn + zb
+        return pltpu.make_async_copy(p_ref.at[slot(k, c, zb), pl.ds(at, rows)], acc.at[b], lsem.at[b])
+
+    def across(k, zb):
+        b = k * zn + zb
+        return copy(C, b, p_ref.at[slot(k, 1 - c, zb), pl.ds(at, rows)], crecv.at[b], nc)
+
+    def upward(b):
+        return copy(ZU, b, acc.at[b], zur.at[b], up)
+
+    def downward(b):
+        return copy(ZD, b, acc.at[b], zdr.at[b], down)
+
+    def add(dst, start, count, terms):
+        @pl.loop(0, count // 16)
+        def _(i):
+            total = None
+            for ref, base in terms:
+                part = ref[pl.ds(pl.multiple_of(start - base + i * 16, 16), 16), :]
+                part = part.astype(jnp.float32)
+                total = part if total is None else total + part
+            dst[pl.ds(pl.multiple_of(start + i * 16, 16), 16), :] = total.astype(dst.dtype)
+
+    def flow(k, zb):
+        b = k * zn + zb
+        load(k, zb).wait()
+        across(k, zb).wait_recv()
+        both = [(acc.at[b], 0), (crecv.at[b], 0)]
+
+        @pl.when((z == zb) | ((z < zb) & (z == 0)) | ((z > zb) & (z == zn - 1)))
+        def _():
+            add(acc.at[b], 0, rows, both)
+
+        @pl.when((z < zb) & (z > 0))
+        def _():
+            upward(b).wait_recv()
+            add(acc.at[b], 0, rows, both + [(zur.at[b], 0)])
+
+        @pl.when((z > zb) & (z < zn - 1))
+        def _():
+            downward(b).wait_recv()
+            add(acc.at[b], 0, rows, both + [(zdr.at[b], 0)])
+
+        @pl.when(z < zb)
+        def _():
+            upward(b).start()
+
+        @pl.when(z > zb)
+        def _():
+            downward(b).start()
+
+    def settle(k):
+        b = k * zn + z
+
+        @pl.when(z > 0)
+        def _():
+            upward(b).wait_recv()
+            add(acc.at[b], 0, rows, [(acc.at[b], 0), (zur.at[b], 0)])
+
+        @pl.when(z < zn - 1)
+        def _():
+            downward(b).wait_recv()
+            add(acc.at[b], 0, rows, [(acc.at[b], 0), (zdr.at[b], 0)])
+
+        return acc.at[b]
+
+    for k in (3, 1, 2, 0):
+        for zb in zorder:
+            across(k, zb).start()
+            load(k, zb).start()
+    lo, hi = pl.ds(0, h0), pl.ds(h0, h1)
+    for k in (3, 1):
+        for zb in zorder:
+            yield
+            flow(k, zb)
+    yield
+    block = settle(3)
+    copy(DX, 0, block.at[lo], dxr, nx).start()
+    copy(DY, 0, block.at[hi], dyr, ny).start()
+    for k in (2, 0):
+        for zb in zorder:
+            yield
+            flow(k, zb)
+    yield
+    block = settle(1)
+    copy(DY, 0, dyr, dyr, ny).wait_recv()
+    add(block, h0, h1, [(block, 0), (dyr, h0)])
+    copy(X, 0, block, xr, nx).start()
+    yield
+    block = settle(2)
+    copy(DX, 0, dxr, dxr, nx).wait_recv()
+    add(block, 0, h0, [(block, 0), (dxr, 0)])
+    copy(Y, 0, block, yr, ny).start()
+    yield
+    block = settle(0)
+    copy(X, 0, xr, xr, nx).wait_recv()
+    copy(Y, 0, yr, yr, ny).wait_recv()
+    add(o_ref.at[pl.ds(to, rows)], 0, rows, [(block, 0), (xr, 0), (yr, 0)])
+    for kind, ref in ((DX, dxr), (DY, dyr), (X, xr), (Y, yr)):
+        copy(kind, 0, ref, ref, nx).wait_send()
+    for k, zb in blocks:
+        b = k * zn + zb
+        across(k, zb).wait_send()
+
+        @pl.when(z < zb)
+        def _():
+            upward(b).wait_send()
+
+        @pl.when(z > zb)
+        def _():
+            downward(b).wait_send()
+
+
+def segments_of(rows, inputs=1):
+    if rows < 192 or inputs > 1:
         return [(0, rows)]
     first = (rows // 2 + 31) // 32 * 32
     return [(0, first), (first, rows - first)]
 
 
-def reduce_plan(zn, p_refs, o_ref, scratch):
-    parts, base = [], 0
-    for p_ref in p_refs:
-        for at, rows in segments_of(p_ref.shape[1]):
+def reduce_plan(zn, p_refs, o_ref, scratch, z_first=()):
+    parts, base, lag = [], 0, 0
+    for i, p_ref in enumerate(p_refs):
+        for at, rows in segments_of(p_ref.shape[1], len(p_refs)):
             mine, scratch = scratch[:11], scratch[11:]
-            parts.append((LAG * len(parts), reduce_steps(zn, p_ref, at, o_ref, base + at, *mine)))
+            if i in z_first:
+                parts.append((0, reduce_z_first_steps(zn, p_ref, at, o_ref, base + at, *mine)))
+                continue
+            parts.append((lag, reduce_steps(zn, p_ref, at, o_ref, base + at, *mine)))
+            lag += LAG_ONE if len(p_refs) == 1 else LAG_MANY
         base += p_ref.shape[1]
     return parts
 
@@ -433,13 +572,18 @@
     run_steps(*reduce_plan(zn, [p_ref], o_ref, scratch))
 
 
-def reduce_scratch(zn, rows, cols, dtype):
+def reduce_scratch(zn, rows, cols, dtype, inputs=1, z_first=False):
     entries = []
-    for _, n in segments_of(rows):
+    for _, n in segments_of(rows, inputs):
         h0 = half_rows(n, dtype)
-        sems = pltpu.SemaphoreType.DMA((10, zn))
-        counts = [(4 * zn, n), (4 * zn, n), (zn, h0), (zn, n - h0)] + [(zn, n)] * 4
-        entries += [pltpu.VMEM((m, r, cols), dtype) for m, r in counts]
+        if z_first:
+            shapes = [(4 * zn, n, cols)] * 4 + [(h0, cols), (n - h0, cols), (n, cols), (n, cols)]
+            sems = pltpu.SemaphoreType.DMA((7, 4 * zn))
+        else:
+            counts = [(4 * zn, n), (4 * zn, n), (zn, h0), (zn, n - h0)] + [(zn, n)] * 4
+            shapes = [(m, r, cols) for m, r in counts]
+            sems = pltpu.SemaphoreType.DMA((10, zn))
+        entries += [pltpu.VMEM(shape, dtype) for shape in shapes]
         entries += [sems, sems, pltpu.SemaphoreType.DMA((4 * zn,))]
     return entries
 
@@ -459,26 +603,28 @@
     )(p)
 
 
-def both_kernel(inputs, zr, zg, *refs):
+def both_kernel(inputs, z_first, zr, zg, *refs):
     p_refs, (x_ref, r_ref, o_ref), scratch = refs[:inputs], refs[inputs : inputs + 3], refs[inputs + 3 :]
     greet(max(zr, zg), *[lax.axis_index(n) for n in ALL])
     gather = (0, gather_steps(zg, x_ref, o_ref, *scratch[-4:]))
-    run_steps(gather, *reduce_plan(zr, p_refs, r_ref, scratch[:-4]))
-
-
-def scatter_and_gather(parts, zr, x, zg, ident, name):
+    run_steps(gather, *reduce_plan(zr, p_refs, r_ref, scratch[:-4], z_first))
+
+
+def scatter_and_gather(parts, zr, x, zg, ident, name, z_first=()):
     inputs = len(parts)
     count, each, cols = parts[0].shape
     rows, dtype = inputs * each, parts[0].dtype
     return pl.pallas_call(
-        functools.partial(both_kernel, inputs, zr, zg),
+        functools.partial(both_kernel, inputs, z_first, zr, zg),
         out_shape=(
             jax.ShapeDtypeStruct((rows, cols), dtype),
             jax.ShapeDtypeStruct((8 * zg,) + x.shape, x.dtype),
         ),
         in_specs=[pl.BlockSpec(memory_space=pl.ANY)] * (inputs + 1),
         out_specs=(pl.BlockSpec(memory_space=pltpu.VMEM), pl.BlockSpec(memory_space=pl.ANY)),
-        scratch_shapes=reduce_scratch(zr, each, cols, dtype) * inputs
+        scratch_shapes=[
+            entry for i in range(inputs) for entry in reduce_scratch(zr, each, cols, dtype, inputs, i in z_first)
+        ]
         + gather_scratch(zg, x.shape, x.dtype),
         compiler_params=pltpu.CompilerParams(
             collective_id=ident, has_side_effects=True, vmem_limit_bytes=VMEM
@@ -1167,11 +1313,16 @@
     picked = jnp.dot(
         token_hot, table_weight.astype(jnp.bfloat16), preferred_element_type=jnp.float32
     ).astype(jnp.bfloat16)
-    state = scatter_all(picked.reshape(devices, rows, D), 8, "rows_scatter").astype(jnp.float32)
+    picked = picked.reshape(devices, rows, D)
+    early = {}
+    if fits():
+        state, early[1] = scatter_and_gather([picked], 4, home[1, 0], 4, 8, "rows_and_weights")
+    else:
+        state = lax.psum_scatter(picked, ALL, scatter_dimension=0)
+    state = state.astype(jnp.float32)
 
     for index in range(1, LAYERS):
-        first, state = lax.optimization_barrier((home[index, 0], state))
-        first = gather_all(first, 1, "weights_gather")
+        first = early[index] if index in early else gather_all(home[index, 0], 1, "weights_gather")
         weights.append(
             [
                 (array.reshape(dp_size, rep_size, 1, tile_rows, D), 0)
@@ -1257,7 +1408,7 @@
     if fits():
         tail = [lax.psum_scatter(flat[-1][-1], ALL, scatter_dimension=0)]
         firsts = [part for layer in flat for part in layer][:-1]
-        body, piece_grads = scatter_and_gather(firsts, 4, entry, 4, 2, "grads_and_entry")
+        body, piece_grads = scatter_and_gather(firsts, 4, entry, 4, 2, "grads_and_entry", (2,))
         home_grads = [body] + tail
     else:
         home_grads = [
@@ -1267,7 +1418,7 @@
     table_grad = jnp.einsum(
         "tv,td->vd", token_hot, piece_grads.reshape(-1, D), preferred_element_type=jnp.float32
     )
-    plane_grad = gather_plane(jnp.concatenate(home_grads), 6, "owners_gather")
+    plane_grad = lax.all_gather(jnp.concatenate(home_grads), DP, axis=0)
     plane_grad = plane_grad.reshape(tile_count, tile_rows, D)
     own_count = jnp.sum(mine.astype(jnp.int32))
     slot_ids = jnp.arange(slots_cap)

time: 1030 us -> 997 us (0.968)
  Pallas kernels: 853 us -> 783 us
  waiting for transfers between devices: 0.05 us -> 22.4 us
  matrix products: 68.4 us -> 78.8 us
    pallas_call x2 -> x3, Pallas kernels: 252 us -> 403 us  [scatter_and_gather(): pl.pallas_call(functools.partial(both_kernel, inputs, z_first, zr, zg), o...]
    pallas_call x5 -> x3, Pallas kernels: 182 us -> 75.2 us  [all_gather(): pl.pallas_call(functools.partial(gather_kernel, zn), out_shape=jax.ShapeD...]
    pallas_call x2 -> x1, Pallas kernels: 140 us -> 33.4 us  [reduce_scatter(): pl.pallas_call(functools.partial(reduce_kernel, zn), out_shape=jax.ShapeD...]
    all_gather x0 -> x1, waiting for transfers between devices: none -> 22.3 us  [shards(): plane_grad = lax.all_gather(jnp.concatenate(home_grads), DP, axis=0)]
  transfers between devices with their start and end apart: 3 -> 4, of which waited for: 0 -> 1; matrix products, arithmetic and copies ran while one was open for 7% -> 7% of each run, Pallas kernels for 59% -> 58%
where the time goes in v7:
time: 997 us; the launch traced here: 987 us
  Pallas kernels  783 us (79%)
  matrix products  78.8 us (8%)
  other arithmetic  58.4 us (6%)
  local copies, waits for them, and re-layouts  22.9 us (2%)
  waiting for transfers between devices  22.4 us (2%)
  between operations  21.7 us (2%)
    pallas_call x3, Pallas kernels, scatter_and_gather(): pl.pallas_call(functools.partial(both_kernel, inputs, z_first, zr, zg), o...  403 us
    pallas_call x3, Pallas kernels, all_gather(): pl.pallas_call(functools.partial(gather_kernel, zn), out_shape=jax.ShapeD...  75.2 us
    pallas_call x2, Pallas kernels, feed_back(): pl.pallas_call(functools.partial(feed_back_kernel, groups), grid=(3 * UNI...  53.5 us
    pallas_call x2, Pallas kernels, keys_reduce(): pl.pallas_call(keys_reduce_kernel, out_shape=jax.ShapeDtypeStruct(block,...  52.3 us
    pallas_call x2, Pallas kernels, keys_gather(): pl.pallas_call(keys_gather_kernel, out_shape=jax.ShapeDtypeStruct((4,) +...  49.3 us
    pallas_call x1, Pallas kernels, reduce_scatter(): pl.pallas_call(functools.partial(reduce_kernel, zn), out_shape=jax.ShapeD...  33.4 us
    pallas_call x2, Pallas kernels, attend(): pl.pallas_call(attend_kernel, grid=(HEADS // 2,), out_shape=(jax.ShapeDty...  29 us
    pallas_call x2, Pallas kernels, attend_back(): pl.pallas_call(attend_back_kernel, grid=(HEADS // 2,), out_shape=(jax.Sha...  28.6 us
  transfers between devices with their start and end apart: 4, of which 1 were waited for; matrix products, arithmetic and copies ran while one was open for 7% of the time, Pallas kernels for 58%

profile of v7, /device:TPU:0, one launch (start us, length us, event | category | flops | bytes accessed | tf_op | source)
XLA Modules:
  0.0 986.9 jit_solution(9144851228908788103)
XLA Ops:
  14.3 8.2 place_tiles.1
  22.5 57.1 %home_and_ids.1 = (bf16[768,768]{1,0:T(8,128)(2,1)}, s32[32,16,128]{2,1,0:T(8,128)}) custom-call(bf16[8,768,768]{2,1,0:T(8,128)(2,1)} %bitcast.108, s32[16,128]{1,0:T(8,128)} %pad_bitcast_fusion.refs_1_), custom_call_target="tpu_custom_call" | custom-call | tf_op jit(solution)/shard_map/home_and_ids/pallas_call | solution.py:617
  79.7 2.1 slice.70
  81.8 1.9 fusion.44
  86.3 1.6 select_reduce_fusion.1
  89.2 17.6 %fusion.4 = bf16[8192,768]{1,0:T(8,128)(2,1)} fusion(s32[8192]{0:T(1024)S(1)} %bitcast.140, f32[1000,768]{1,0:T(8,128)S(1)} %copy-done.9), kind=kOutput, calls=%fused_computation.8 | convolution fusion | flops 12598163456 | bytes 15687680 | tf_op jit(solution)/shard_map/dot_general | solution.py:1313
  106.8 169.1 %rows_and_weights.1 = (bf16[256,768]{1,0:T(8,128)(2,1)}, bf16[32,192,768]{2,1,0:T(8,128)(2,1)}) custom-call(bf16[32,256,768]{2,1,0:T(8,128)(2,1)} %bitcast.109, bf16[192,768]{1,0:T(8,128)(2,1)} %get-tuple-element.119.refs_1_), custom_call_target="tpu_custom_call" | custom-call | tf_op jit(solution)/shard_map/rows_and_weights/pallas_call | solution.py:617
  275.9 1.9 convert_element_type.78.x_ref
  281.2 5.5 project.2
  286.7 23.3 %keys_gather.2 = bf16[4,512,768]{2,1,0:T(8,128)(2,1)} custom-call(bf16[512,768]{1,0:T(8,128)(2,1)} %bitcast.121), custom_call_target="tpu_custom_call" | custom-call | tf_op jit(solution)/shard_map/keys_gather/pallas_call | solution.py:670
  310.0 14.5 %attend.2 = (bf16[256,768]{1,0:T(8,128)(2,1)}, f32[6,8,256]{2,1,0:T(8,128)}) custom-call(bf16[256,768]{1,0:T(8,128)(2,1)} %get-tuple-element.58.q_ref, bf16[4,2,256,768]{3,2,1,0:T(8,128)(2,1)} %bitcast.98, bf16[4,2,256,768]{3,2,1,0:T(8,128)(2,1)} %bitcast.99, s32[1024,1]{1,0:T(8,128)} %copy.86.kseg_ref, s32[1,256]{1,0:T(1,128)} %dynamic_slice.36.qseg_ref, ...), custom_call_target="tpu_custom_call" | custom-call | tf_op jit(solution)/shard_map/attend/pallas_call | solution.py:916
  324.5 11.7 %feed.2 = (f32[256,768]{1,0:T(8,128)}, f32[256,768]{1,0:T(8,128)}) custom-call(f32[256,768]{1,0:T(8,128)} %convert_element_type.78.x_ref, bf16[256,768]{1,0:T(8,128)(2,1)} %get-tuple-element.60.o_ref, f32[1,768]{1,0:T(1,128)} %get-tuple-element.129.g_ref, bf16[8,4,2,192,768]{4,3,2,1,0:T(8,128)(2,1)} %bitcast.79, bf16[8,4,2,192,768]{4,3,2,1,0:T(8,128)(2,1)} %bitcast.80, ...), custom_call_target="tpu_custom_call" | custom-call | tf_op jit(solution)/shard_map/feed/pallas_call | solution.py:956
  336.3 5.5 project.3
  341.7 25.9 %keys_gather.3 = bf16[4,512,768]{2,1,0:T(8,128)(2,1)} custom-call(bf16[512,768]{1,0:T(8,128)(2,1)} %bitcast.122), custom_call_target="tpu_custom_call" | custom-call | tf_op jit(solution)/shard_map/keys_gather/pallas_call | solution.py:670
  367.7 14.5 %attend.3 = (bf16[256,768]{1,0:T(8,128)(2,1)}, f32[6,8,256]{2,1,0:T(8,128)}) custom-call(bf16[256,768]{1,0:T(8,128)(2,1)} %get-tuple-element.63.q_ref, bf16[4,2,256,768]{3,2,1,0:T(8,128)(2,1)} %bitcast.102, bf16[4,2,256,768]{3,2,1,0:T(8,128)(2,1)} %bitcast.103, s32[1024,1]{1,0:T(8,128)} %copy.86.kseg_ref, s32[1,256]{1,0:T(1,128)} %dynamic_slice.36.qseg_ref, ...), custom_call_target="tpu_custom_call" | custom-call | tf_op jit(solution)/shard_map/attend/pallas_call | solution.py:916
  382.2 11.0 %feed.3 = (f32[256,768]{1,0:T(8,128)}, f32[256,768]{1,0:T(8,128)}) custom-call(f32[256,768]{1,0:T(8,128)} %get-tuple-element.61.x_ref, bf16[256,768]{1,0:T(8,128)(2,1)} %get-tuple-element.65.o_ref, f32[1,768]{1,0:T(1,128)} %get-tuple-element.127.g_ref, bf16[8,4,1,192,768]{4,3,2,1,0:T(8,128)(2,1)} %bitcast.89, bf16[8,4,1,192,768]{4,3,2,1,0:T(8,128)(2,1)} %bitcast.90, ...), custom_call_target="tpu_custom_call" | custom-call | tf_op jit(solution)/shard_map/feed/pallas_call | solution.py:956
  393.2 1.4 multiply_reduce_fusion.5
  394.6 2.1 convolution_convert_fusion.1.refs_0_
  396.7 35.0 %chosen_gather.1 = bf16[32,96,768]{2,1,0:T(8,128)(2,1)} custom-call(bf16[96,768]{1,0:T(8,128)(2,1)} %convolution_convert_fusion.1.refs_0_), custom_call_target="tpu_custom_call" | custom-call | tf_op jit(solution)/shard_map/chosen_gather/pallas_call | solution.py:248
  431.7 17.3 %fusion.47 = (f32[3072]{0:T(1024)S(1)}, f32[3072,1000]{0,1:T(8,128)S(1)}) fusion(bf16[3072,768]{1,0:T(8,128)(2,1)} %bitcast.112, f32[1000,768]{1,0:T(8,128)S(1)} %copy-done.5), kind=kOutput, calls=%fused_computation.148 | convolution fusion | flops 4722428928 | bytes 20090880 | tf_op jit(solution)/shard_map/rd,vd->rv/dot_general | solution.py:1370
  449.0 3.3 exponential_reduce_fusion
  454.1 19.8 %stats_gather.1 = f32[32,72,128]{2,1,0:T(8,128)} custom-call(f32[72,128]{1,0:T(8,128)} %pad_maximum_fusion.3.refs_0_), custom_call_target="tpu_custom_call" | custom-call | tf_op jit(solution)/shard_map/stats_gather/pallas_call | solution.py:248
  474.9 1.3 multiply_reduce_fusion.6
  476.2 6.9 select_convert_fusion
  483.1 7.3 convolution_convert_fusion
  490.4 33.4 %back_scatter.1 = bf16[96,768]{1,0:T(8,128)(2,1)} custom-call(bf16[32,96,768]{2,1,0:T(8,128)(2,1)} %bitcast.114), custom_call_target="tpu_custom_call" | custom-call | tf_op jit(solution)/shard_map/back_scatter/pallas_call | solution.py:593
  523.9 1.4 multiply_reduce_fusion.3
  526.4 26.7 %feed_back.2 = (f32[256,768]{1,0:T(8,128)}, bf16[256,768]{1,0:T(8,128)(2,1)}, f32[8,768]{1,0:T(8,128)}, bf16[8,4,1,192,768]{4,3,2,1,0:T(8,128)(2,1)}, bf16[8,4,1,192,768]{4,3,2,1,0:T(8,128)(2,1)}) custom-call(f32[256,768]{1,0:T(8,128)} %multiply_subtract_fusion.2.dy_ref, f32[256,768]{1,0:T(8,128)} %get-tuple-element.67.mid_ref, ...), custom_call_target="tpu_custom_call" | custom-call | tf_op jit(solution)/shard_map/feed_back/pallas_call | solution.py:1041
  553.2 14.4 %attend_back.2 = (f32[256,768]{1,0:T(8,128)}, bf16[4,2,256,768]{3,2,1,0:T(8,128)(2,1)}) custom-call(bf16[256,768]{1,0:T(8,128)(2,1)} %get-tuple-element.63.q_ref, bf16[4,2,256,768]{3,2,1,0:T(8,128)(2,1)} %bitcast.104, bf16[4,2,256,768]{3,2,1,0:T(8,128)(2,1)} %bitcast.105, s32[1024,1]{1,0:T(8,128)} %copy.86.kseg_ref, s32[1,256]{1,0:T(1,128)} %dynamic_slice.36.qseg_ref, ...), custom_call_target="tpu_custom_call" | custom-call | tf_op jit(solution)/shard_map/attend_back/pallas_call | solution.py:1102
  567.6 24.0 %keys_reduce.2 = bf16[512,768]{1,0:T(8,128)(2,1)} custom-call(bf16[4,512,768]{2,1,0:T(8,128)(2,1)} %bitcast.117), custom_call_target="tpu_custom_call" | custom-call | tf_op jit(solution)/shard_map/keys_reduce/pallas_call | solution.py:723
  591.6 8.2 project_back.2
  599.8 26.8 %feed_back.3 = (f32[256,768]{1,0:T(8,128)}, bf16[256,768]{1,0:T(8,128)(2,1)}, f32[8,768]{1,0:T(8,128)}, bf16[8,4,1,192,768]{4,3,2,1,0:T(8,128)(2,1)}, bf16[8,4,1,192,768]{4,3,2,1,0:T(8,128)(2,1)}) custom-call(f32[256,768]{1,0:T(8,128)} %get-tuple-element.74.dy_ref, f32[256,768]{1,0:T(8,128)} %get-tuple-element.75.mid_ref, ...), custom_call_target="tpu_custom_call" | custom-call | tf_op jit(solution)/shard_map/feed_back/pallas_call | solution.py:1041
  626.6 14.2 %attend_back.3 = (f32[256,768]{1,0:T(8,128)}, bf16[4,2,256,768]{3,2,1,0:T(8,128)(2,1)}) custom-call(bf16[256,768]{1,0:T(8,128)(2,1)} %get-tuple-element.58.q_ref, bf16[4,2,256,768]{3,2,1,0:T(8,128)(2,1)} %bitcast.100, bf16[4,2,256,768]{3,2,1,0:T(8,128)(2,1)} %bitcast.101, s32[1024,1]{1,0:T(8,128)} %copy.86.kseg_ref, s32[1,256]{1,0:T(1,128)} %dynamic_slice.36.qseg_ref, ...), custom_call_target="tpu_custom_call" | custom-call | tf_op jit(solution)/shard_map/attend_back/pallas_call | solution.py:1102
  640.8 28.3 %keys_reduce.3 = bf16[512,768]{1,0:T(8,128)(2,1)} custom-call(bf16[4,512,768]{2,1,0:T(8,128)(2,1)} %bitcast.116), custom_call_target="tpu_custom_call" | custom-call | tf_op jit(solution)/shard_map/keys_reduce/pallas_call | solution.py:723
  669.1 8.4 project_back.3
  677.4 1.9 convert_element_type.87.refs_3_
  679.4 176.6 %grads_and_entry.1 = (bf16[576,768]{1,0:T(8,128)(2,1)}, bf16[32,256,768]{2,1,0:T(8,128)(2,1)}) custom-call(bf16[32,192,768]{2,1,0:T(8,128)(2,1)} %bitcast.106, bf16[32,192,768]{2,1,0:T(8,128)(2,1)} %bitcast.110, bf16[32,192,768]{2,1,0:T(8,128)(2,1)} %bitcast.107, bf16[256,768]{1,0:T(8,128)(2,1)} %convert_element_type.87.refs_3_), custom_call_target="tpu_custom_call" | custom-call | tf_op jit(solution)/shard_map/grads_and_entry/pallas_call | solution.py:617
  856.0 2.4 pad_maximum_fusion
  864.3 11.8 %multiply_reduce_fusion.1 = (f32[]{:T(128)}, f32[1000,768]{1,0:T(8,128)}) fusion(bf16[3072,1000]{0,1:T(8,128)(2,1)} %copy-done.4, bf16[3072,768]{1,0:T(8,128)(2,1)} %bitcast.113), kind=kOutput, calls=%fused_computation.34 | convolution fusion | flops 4720128000 | bytes 13934596 | tf_op jit(solution)/shard_map/rv,rd->vd/dot_general | solution.py:1397
  876.1 21.3 %multiply_reduce_fusion.2 = (f32[]{:T(128)}, f32[1000,768]{1,0:T(8,128)}) fusion(bf16[8192,768]{1,0:T(8,128)(2,1)} %bitcast.144, s32[8192]{0:T(1024)S(1)} %bitcast.141), kind=kOutput, calls=%fused_computation.35 | convolution fusion | flops 12592640000 | bytes 15687684 | tf_op jit(solution)/shard_map/tv,td->vd/dot_general | solution.py:1418
  897.4 22.3 %all-gather.10.cloned.1.call-done = bf16[6144,768]{1,0:T(8,128)(2,1)} async-done(((bf16[768,768]{1,0:T(8,128)(2,1)}), bf16[6144,768]{1,0:T(8,128)(2,1)}) %all-gather.10.cloned.1.call-update) | async-done | bytes 9437200 | tf_op jit(solution)/shard_map/all_gather | solution.py:1421
  919.7 4.3 gather_fusion.2
  924.0 1.6 multiply_reduce_fusion
  928.2 20.5 %sums_gather.1 = f32[32,32,128]{2,1,0:T(8,128)} custom-call(f32[32,128]{1,0:T(8,128)} %fusion.22.refs_0_), custom_call_target="tpu_custom_call" | custom-call | tf_op jit(solution)/shard_map/sums_gather/pallas_call | solution.py:248
  952.5 10.6 %fusion.43 = (bf16[6,192,768]{2,1,0:T(8,128)(2,1)}, f32[6,192,768]{2,1,0:T(8,128)}, f32[6,192,768]{2,1,0:T(8,128)}, f32[6,192,768]{2,1,0:T(8,128)}) fusion(f32[6,192,768]{2,1,0:T(8,128)} %w_ref.1, f32[6,192,768]{2,1,0:T(8,128)} %param.26, f32[]{:T(128)} %bitcast.50, f32[]{:T(128)S(6)} %min.3, bf16[6,192,768]{2,1,0:T(8,128)(2,1)S(1)} %gather_fusion.2, ...), kind=kLoop, calls=%fused_computation.144 | loop fusion | flops 19464192 | bytes 24772628 | tf_op jit(solution)/shard_map/convert_element_type | solution.py:1464
  964.5 6.0 fusion.39
  970.4 1.4 copy-done.12
  972.7 4.9 fusion.41
  (142 shorter events, 27.9 us)
Async XLA Ops:
  7.2 2.6 copy-start
  7.2 274.0 %all-gather.6.cloned.1.call-start = ((), (), s32[]{:S(2)}) async-start(), calls=%async_computation.1 | async-start | bytes 19464192 | tf_op jit(solution)/shard_map/all_gather | solution.py:1304
  12.6 9.9 %copy-start.23 = (pred[32]{0:T(512)(128)(4,1)}, pred[32]{0:T(512)(128)(4,1)S(1)}, u32[]{:S(2)}) copy-start(pred[32]{0:T(512)(128)(4,1)S(1)} %gather_fusion) | copy-start | bytes 100
  13.3 9.2 copy-start.25
  79.7 9.5 copy-start.9
  81.8 300.4 %all-gather.8.cloned.1.call-start = ((), (), s32[]{:S(2)}) async-start(), calls=%async_computation.3 | async-start | bytes 9732096 | tf_op jit(solution)/shard_map/all_gather | solution.py:1307
  83.8 772.3 %reduce-scatter.2.cloned.1.call-start = ((), (), s32[]{:S(2)}) async-start(), calls=%async_computation.2 | async-start | bytes 9732096 | tf_op jit(solution)/shard_map/reduce_scatter | solution.py:1409
  85.0 21.8 %copy-start.19 = (s32[8,2,4,128]{3,1,2,0:T(2,128)}, s32[8,2,4,128]{3,1,2,0:T(2,128)S(1)}, u32[]{:S(2)}) copy-start(s32[8,2,4,128]{3,1,2,0:T(2,128)S(1)} %copy.95) | copy-start | bytes 98308
  88.0 18.8 %copy-start.17 = (pred[8,4,96]{2,0,1:T(8,128)(4,1)}, pred[8,4,96]{2,0,1:T(8,128)(4,1)S(1)}, u32[]{:S(2)}) copy-start(pred[8,4,96]{2,0,1:T(8,128)(4,1)S(1)} %get-tuple-element.134) | copy-start | bytes 9220
  106.8 173.7 %copy-start.15 = (f32[5,768]{1,0:T(8,128)S(1)}, f32[5,768]{1,0:T(8,128)}, u32[]{:S(2)}) copy-start(f32[5,768]{1,0:T(8,128)} %param.33) | copy-start | bytes 46084
  393.2 38.5 %copy-start.5 = (f32[1000,768]{1,0:T(8,128)S(1)}, f32[1000,768]{1,0:T(8,128)}, u32[]{:S(2)}) copy-start(f32[1000,768]{1,0:T(8,128)} %param.30) | copy-start | bytes 9216004
  448.9 4.5 copy-start.2
  483.1 7.3 copy-start.4
  490.4 33.5 %copy-start.3 = (f32[256,768]{1,0:T(8,128)S(1)}, f32[256,768]{1,0:T(8,128)}, u32[]{:S(2)}) copy-start(f32[256,768]{1,0:T(8,128)} %get-tuple-element.66) | copy-start | bytes 2359300
  553.1 366.5 %all-gather.10.cloned.1.call-start = ((), (), s32[]{:S(2)}) async-start(), calls=%async_computation.4 | async-start | bytes 10616832 | tf_op jit(solution)/shard_map/all_gather | solution.py:1421
  856.0 3.8 copy-start.24
  856.0 3.8 copy-start.26
  856.0 7.0 copy-start.18
  864.3 11.8 %copy-start.20 = (s32[8,2,4,128]{3,1,2,0:T(2,128)S(1)}, s32[8,2,4,128]{3,1,2,0:T(2,128)}, u32[]{:S(2)}) copy-start(s32[8,2,4,128]{3,1,2,0:T(2,128)} %copy-done.19) | copy-start | bytes 98308
  952.4 10.7 %copy-start.16 = (f32[5,768]{1,0:T(8,128)S(1)}, f32[5,768]{1,0:T(8,128)}, u32[]{:S(2)}) copy-start(f32[5,768]{1,0:T(8,128)} %param.33) | copy-start | bytes 46084
  952.5 10.7 %copy-start.21 = (f32[5,768]{1,0:T(8,128)S(1)}, f32[5,768]{1,0:T(8,128)}, u32[]{:S(2)}) copy-start(f32[5,768]{1,0:T(8,128)} %param.35) | copy-start | bytes 46084
  952.5 10.7 %copy-start.22 = (f32[5,768]{1,0:T(8,128)S(1)}, f32[5,768]{1,0:T(8,128)}, u32[]{:S(2)}) copy-start(f32[5,768]{1,0:T(8,128)} %param.34) | copy-start | bytes 46084
  952.5 11.4 %copy-start.6 = (f32[1000,768]{1,0:T(8,128)S(1)}, f32[1000,768]{1,0:T(8,128)}, u32[]{:S(2)}) copy-start(f32[1000,768]{1,0:T(8,128)} %param.30) | copy-start | bytes 9216004
  952.5 11.4 %copy-start.7 = (f32[1000,768]{1,0:T(8,128)S(1)}, f32[1000,768]{1,0:T(8,128)}, u32[]{:S(2)}) copy-start(f32[1000,768]{1,0:T(8,128)} %param.32) | copy-start | bytes 9216004
  952.5 11.3 %copy-start.8 = (f32[1000,768]{1,0:T(8,128)S(1)}, f32[1000,768]{1,0:T(8,128)}, u32[]{:S(2)}) copy-start(f32[1000,768]{1,0:T(8,128)} %param.31) | copy-start | bytes 9216004
  952.5 11.9 %copy-start.14 = (f32[1000,768]{1,0:T(8,128)S(1)}, f32[1000,768]{1,0:T(8,128)}, u32[]{:S(2)}) copy-start(f32[1000,768]{1,0:T(8,128)} %get-tuple-element.146) | copy-start | bytes 9216004
  964.4 6.0 copy-start.10
  964.4 6.0 copy-start.11
  964.4 7.4 copy-start.12
  964.4 8.3 copy-start.13
  972.7 4.9 copy-start.1
Sparse Core Ops, SparseCore 0:
  81.9 183.3 all-gather.5
  268.7 92.9 all-gather.7
  553.3 137.4 reduce-scatter.1
  858.5 61.0 all-gather.9

commit v8 on v7

--- a/solution.py
+++ b/solution.py
@@ -79,7 +79,7 @@
 
 MESH = pl.DeviceIdType.MESH
 LAG_ONE, LAG_MANY = 8, 6
-VMEM = 60 << 20
+VMEM, VMEM_LAYER = 60 << 20, 44 << 20
 
 
 def half_rows(rows, dtype):
@@ -863,7 +863,7 @@
             pl.BlockSpec((None, rows, D), lambda t: (jnp.maximum(t - 1, 0), 0, 0)),
         ),
         scratch_shapes=[pltpu.VMEM((rows, D), jnp.bfloat16)],
-        compiler_params=pltpu.CompilerParams(vmem_limit_bytes=VMEM),
+        compiler_params=pltpu.CompilerParams(vmem_limit_bytes=VMEM_LAYER),
         name="project",
     )(x, gain, cos, sin, *arrays)
 
@@ -886,6 +886,7 @@
     length = bias_ref.shape[0]
     q = q_ref[...] * HD ** (-0.5)
     k, v = k_ref[...].reshape(length, 128), v_ref[...].reshape(length, 128)
+    vt = v.T
     outs = []
     for head in range(2):
         mine = head_lanes(q.shape, head)
@@ -894,9 +895,9 @@
         e = jnp.exp(s - top)
         total = jnp.sum(e, axis=0, keepdims=True)
         p = (e * (1.0 / total)).astype(jnp.bfloat16)
-        outs.append(dot_tn(p, v))
+        outs.append(dot_nn(vt[head * HD : (head + 1) * HD], p))
         lse_ref[head : head + 1, :] = top + jnp.log(total)
-    o_ref[...] = jnp.where(head_lanes(outs[0].shape, 0), outs[0], outs[1]).astype(jnp.bfloat16)
+    o_ref[...] = jnp.concatenate(outs, axis=0).T.astype(jnp.bfloat16)
 
 
 def attend_specs(rows, parts):
@@ -923,7 +924,7 @@
         in_specs=specs,
         out_specs=(pair, pl.BlockSpec((None, 8, rows), lambda t: (t, 0, 0))),
         scratch_shapes=[pltpu.VMEM((parts * rows, rows), jnp.float32)],
-        compiler_params=pltpu.CompilerParams(vmem_limit_bytes=VMEM),
+        compiler_params=pltpu.CompilerParams(vmem_limit_bytes=VMEM_LAYER),
         name="attend",
     )(q, kv, kv, kseg, qseg, qpos)
 
@@ -962,7 +963,7 @@
         ],
         out_specs=(whole((rows, D)), whole((rows, D))),
         scratch_shapes=[pltpu.VMEM((rows, D), jnp.bfloat16)],
-        compiler_params=pltpu.CompilerParams(vmem_limit_bytes=VMEM),
+        compiler_params=pltpu.CompilerParams(vmem_limit_bytes=VMEM_LAYER),
         name="feed",
     )(x, o, gain, *arrays)
 
@@ -1060,7 +1061,7 @@
             pltpu.VMEM((rows, D), jnp.bfloat16), pltpu.VMEM((rows, D), jnp.bfloat16),
             pltpu.VMEM((rows, D), jnp.bfloat16), pltpu.VMEM((rows, D), jnp.float32),
         ],
-        compiler_params=pltpu.CompilerParams(vmem_limit_bytes=VMEM),
+        compiler_params=pltpu.CompilerParams(vmem_limit_bytes=VMEM_LAYER),
         name="feed_back",
     )(dy, mid, gain, o, *arrays)
 
@@ -1076,6 +1077,7 @@
     parts, rows = dkv_ref.shape[0], q_ref.shape[0]
     q, do = q_ref[...] * HD ** (-0.5), do_ref[...]
     k, v = k_ref[...].reshape(length, 128), v_ref[...].reshape(length, 128)
+    kt = k.T
     dqs, dk, dv = [], None, None
     for head in range(2):
         mine = head_lanes(q.shape, head)
@@ -1090,8 +1092,8 @@
         dk_part = dot_nn(ds, qm)
         dv = dv_part if dv is None else dv + dv_part
         dk = dk_part if dk is None else dk + dk_part
-        dqs.append(dot_tn(ds, k))
-    dq_ref[...] = jnp.where(head_lanes(dqs[0].shape, 0), dqs[0], dqs[1]) * HD ** (-0.5)
+        dqs.append(dot_nn(kt[head * HD : (head + 1) * HD], ds))
+    dq_ref[...] = jnp.concatenate(dqs, axis=0).T * HD ** (-0.5)
     dkv_ref[:, 0] = dk.astype(jnp.bfloat16).reshape(parts, rows, 128)
     dkv_ref[:, 1] = dv.astype(jnp.bfloat16).reshape(parts, rows, 128)
 
@@ -1109,7 +1111,7 @@
         in_specs=specs + [pair, pl.BlockSpec((None, 8, rows), lambda t: (t, 0, 0))],
         out_specs=(pair, pl.BlockSpec((parts, 2, rows, 128), lambda t: (0, 0, 0, t))),
         scratch_shapes=[pltpu.VMEM((parts * rows, rows), jnp.float32)],
-        compiler_params=pltpu.CompilerParams(vmem_limit_bytes=VMEM),
+        compiler_params=pltpu.CompilerParams(vmem_limit_bytes=VMEM_LAYER),
         name="attend_back",
     )(q, kv, kv, kseg, qseg, qpos, do, lse)
 
@@ -1173,7 +1175,7 @@
             pltpu.VMEM((rows, D), jnp.float32),
         ],
         input_output_aliases={8: 0},
-        compiler_params=pltpu.CompilerParams(vmem_limit_bytes=VMEM),
+        compiler_params=pltpu.CompilerParams(vmem_limit_bytes=VMEM_LAYER),
         name="project_back",
     )(dx, x, gain, cos, sin, dq, dkv, *arrays, grads)
 

time: 997 us -> 993 us (level)
  local copies, waits for them, and re-layouts: 22.9 us -> 39.9 us
  Pallas kernels: 783 us -> 771 us
    unnamed x57 -> x119, local copies, waits for them, and re-layouts: 5.22 us -> 27.2 us
  transfers between devices with their start and end apart: 4 -> 4, of which waited for: 1 -> 1; matrix products, arithmetic and copies ran while one was open for 7% -> 6% of each run, Pallas kernels for 58% -> 57%
where the time goes in v8:
time: 993 us; the launch traced here: 983 us
  Pallas kernels  771 us (78%)
  matrix products  69.7 us (7%)
  other arithmetic  53.7 us (5%)
  local copies, waits for them, and re-layouts  39.9 us (4%)
  waiting for transfers between devices  26.2 us (3%)
  between operations  22.1 us (2%)
    pallas_call x3, Pallas kernels, scatter_and_gather(): pl.pallas_call(functools.partial(both_kernel, inputs, z_first, zr, zg), o...  404 us
    pallas_call x3, Pallas kernels, all_gather(): pl.pallas_call(functools.partial(gather_kernel, zn), out_shape=jax.ShapeD...  80.3 us
    pallas_call x2, Pallas kernels, feed_back(): pl.pallas_call(functools.partial(feed_back_kernel, groups), grid=(3 * UNI...  51.5 us
    pallas_call x2, Pallas kernels, keys_reduce(): pl.pallas_call(keys_reduce_kernel, out_shape=jax.ShapeDtypeStruct(block,...  50.9 us
    pallas_call x2, Pallas kernels, keys_gather(): pl.pallas_call(keys_gather_kernel, out_shape=jax.ShapeDtypeStruct((4,) +...  49.2 us
    pallas_call x1, Pallas kernels, reduce_scatter(): pl.pallas_call(functools.partial(reduce_kernel, zn), out_shape=jax.ShapeD...  33.4 us
    unnamed x119, local copies, waits for them, and re-layouts  27.2 us
    pallas_call x2, Pallas kernels, attend_back(): pl.pallas_call(attend_back_kernel, grid=(HEADS // 2,), out_shape=(jax.Sha...  26.2 us
  transfers between devices with their start and end apart: 4, of which 1 were waited for; matrix products, arithmetic and copies ran while one was open for 6% of the time, Pallas kernels for 57%

profile of v8, /device:TPU:0, one launch (start us, length us, event | category | flops | bytes accessed | tf_op | source)
XLA Modules:
  0.0 983.4 jit_solution(10698483454555417617)
XLA Ops:
  14.3 8.2 place_tiles.1
  22.5 57.2 %home_and_ids.1 = (bf16[768,768]{1,0:T(8,128)(2,1)}, s32[32,16,128]{2,1,0:T(8,128)}) custom-call(bf16[8,768,768]{2,1,0:T(8,128)(2,1)} %bitcast.114, s32[16,128]{1,0:T(8,128)} %pad_bitcast_fusion.refs_1_), custom_call_target="tpu_custom_call" | custom-call | tf_op jit(solution)/shard_map/home_and_ids/pallas_call | solution.py:617
  79.7 2.0 slice.70
  81.8 1.9 fusion.44
  85.3 1.6 select_reduce_fusion.1
  87.4 19.6 %fusion.4 = bf16[8192,768]{1,0:T(8,128)(2,1)} fusion(s32[8192]{0:T(1024)S(1)} %bitcast.140, f32[1000,768]{1,0:T(8,128)} %param.27), kind=kOutput, calls=%fused_computation.8 | convolution fusion | flops 12598163456 | bytes 15687680 | tf_op jit(solution)/shard_map/dot_general | solution.py:1315
  107.0 173.9 %rows_and_weights.1 = (bf16[256,768]{1,0:T(8,128)(2,1)}, bf16[32,192,768]{2,1,0:T(8,128)(2,1)}) custom-call(bf16[32,256,768]{2,1,0:T(8,128)(2,1)} %bitcast.115, bf16[192,768]{1,0:T(8,128)(2,1)} %get-tuple-element.119.refs_1_), custom_call_target="tpu_custom_call" | custom-call | tf_op jit(solution)/shard_map/rows_and_weights/pallas_call | solution.py:617
  283.0 4.3 project.2
  288.2 24.5 %keys_gather.2 = bf16[4,512,768]{2,1,0:T(8,128)(2,1)} custom-call(bf16[512,768]{1,0:T(8,128)(2,1)} %bitcast.90), custom_call_target="tpu_custom_call" | custom-call | tf_op jit(solution)/shard_map/keys_gather/pallas_call | solution.py:670
  312.7 1.9 copy-done.2
  314.6 12.2 %attend.2 = (bf16[256,768]{1,0:T(8,128)(2,1)S(1)}, f32[6,8,256]{2,1,0:T(8,128)S(1)}) custom-call(bf16[256,768]{1,0:T(8,128)(2,1)S(1)} %get-tuple-element.58.q_ref, bf16[4,2,256,768]{3,2,1,0:T(8,128)(2,1)S(1)} %bitcast.78, bf16[4,2,256,768]{3,2,1,0:T(8,128)(2,1)S(1)} %bitcast.79, s32[1024,1]{1,0:T(8,128)S(1)} %copy.86.kseg_ref, ...), custom_call_target="tpu_custom_call" | custom-call | tf_op jit(solution)/shard_map/attend/pallas_call | solution.py:917
  326.9 10.7 %feed.2 = (f32[256,768]{1,0:T(8,128)S(1)}, f32[256,768]{1,0:T(8,128)S(1)}) custom-call(f32[256,768]{1,0:T(8,128)S(1)} %convert_element_type.78.x_ref, bf16[256,768]{1,0:T(8,128)(2,1)S(1)} %get-tuple-element.60.o_ref, f32[1,768]{1,0:T(1,128)S(1)} %get-tuple-element.129.g_ref, bf16[8,4,2,192,768]{4,3,2,1,0:T(8,128)(2,1)} %bitcast.93, ...), custom_call_target="tpu_custom_call" | custom-call | tf_op jit(solution)/shard_map/feed/pallas_call | solution.py:957
  337.6 4.8 project.3
  343.3 24.7 %keys_gather.3 = bf16[4,512,768]{2,1,0:T(8,128)(2,1)} custom-call(bf16[512,768]{1,0:T(8,128)(2,1)} %bitcast.91), custom_call_target="tpu_custom_call" | custom-call | tf_op jit(solution)/shard_map/keys_gather/pallas_call | solution.py:670
  368.1 1.9 copy-done.4
  369.9 12.2 %attend.3 = (bf16[256,768]{1,0:T(8,128)(2,1)S(1)}, f32[6,8,256]{2,1,0:T(8,128)S(1)}) custom-call(bf16[256,768]{1,0:T(8,128)(2,1)S(1)} %get-tuple-element.63.q_ref, bf16[4,2,256,768]{3,2,1,0:T(8,128)(2,1)S(1)} %bitcast.82, bf16[4,2,256,768]{3,2,1,0:T(8,128)(2,1)S(1)} %bitcast.83, s32[1024,1]{1,0:T(8,128)S(1)} %copy.86.kseg_ref, ...), custom_call_target="tpu_custom_call" | custom-call | tf_op jit(solution)/shard_map/attend/pallas_call | solution.py:917
  382.2 9.5 feed.3
  392.8 39.9 %chosen_gather.1 = bf16[32,96,768]{2,1,0:T(8,128)(2,1)} custom-call(bf16[96,768]{1,0:T(8,128)(2,1)} %convolution_convert_fusion.1.refs_0_), custom_call_target="tpu_custom_call" | custom-call | tf_op jit(solution)/shard_map/chosen_gather/pallas_call | solution.py:248
  432.7 7.8 fusion.47
  440.6 4.5 copy-done.33
  445.1 3.3 exponential_reduce_fusion
  449.0 19.9 %stats_gather.1 = f32[32,72,128]{2,1,0:T(8,128)} custom-call(f32[72,128]{1,0:T(8,128)} %pad_maximum_fusion.3.refs_0_), custom_call_target="tpu_custom_call" | custom-call | tf_op jit(solution)/shard_map/stats_gather/pallas_call | solution.py:248
  472.0 7.0 select_convert_fusion
  479.0 7.4 convolution_convert_fusion
  486.4 33.4 %back_scatter.1 = bf16[96,768]{1,0:T(8,128)(2,1)} custom-call(bf16[32,96,768]{2,1,0:T(8,128)(2,1)} %bitcast.120), custom_call_target="tpu_custom_call" | custom-call | tf_op jit(solution)/shard_map/back_scatter/pallas_call | solution.py:593
  519.8 1.4 multiply_reduce_fusion.3
  521.5 25.5 %feed_back.2 = (f32[256,768]{1,0:T(8,128)S(1)}, bf16[256,768]{1,0:T(8,128)(2,1)S(1)}, f32[8,768]{1,0:T(8,128)S(1)}, bf16[8,4,1,192,768]{4,3,2,1,0:T(8,128)(2,1)}, bf16[8,4,1,192,768]{4,3,2,1,0:T(8,128)(2,1)}) custom-call(f32[256,768]{1,0:T(8,128)S(1)} %multiply_subtract_fusion.2.dy_ref, f32[256,768]{1,0:T(8,128)S(1)} %get-tuple-element.67.mid_ref, ...), custom_call_target="tpu_custom_call" | custom-call | tf_op jit(solution)/shard_map/feed_back/pallas_call | solution.py:1042
  548.9 1.6 copy-done.5
  553.6 13.1 %attend_back.2 = (f32[256,768]{1,0:T(8,128)S(1)}, bf16[4,2,256,768]{3,2,1,0:T(8,128)(2,1)S(1)}) custom-call(bf16[256,768]{1,0:T(8,128)(2,1)S(1)} %copy-done.22, bf16[4,2,256,768]{3,2,1,0:T(8,128)(2,1)S(1)} %bitcast.84, bf16[4,2,256,768]{3,2,1,0:T(8,128)(2,1)S(1)} %bitcast.85, s32[1024,1]{1,0:T(8,128)S(1)} %copy-done.7, s32[1,256]{1,0:T(1,128)S(1)} %dynamic_slice.36.qseg_ref, ...), custom_call_target="tpu_custom_call" | custom-call | tf_op jit(solution)/shard_map/attend_back/pallas_call | solution.py:1104
  566.7 1.7 copy-done.15
  569.2 24.0 %keys_reduce.2 = bf16[512,768]{1,0:T(8,128)(2,1)} custom-call(bf16[4,512,768]{2,1,0:T(8,128)(2,1)} %bitcast.88), custom_call_target="tpu_custom_call" | custom-call | tf_op jit(solution)/shard_map/keys_reduce/pallas_call | solution.py:723
  595.6 6.8 project_back.2
  602.4 25.9 %feed_back.3 = (f32[256,768]{1,0:T(8,128)S(1)}, bf16[256,768]{1,0:T(8,128)(2,1)S(1)}, f32[8,768]{1,0:T(8,128)S(1)}, bf16[8,4,1,192,768]{4,3,2,1,0:T(8,128)(2,1)}, bf16[8,4,1,192,768]{4,3,2,1,0:T(8,128)(2,1)}) custom-call(f32[256,768]{1,0:T(8,128)S(1)} %get-tuple-element.74.dy_ref, f32[256,768]{1,0:T(8,128)S(1)} %copy-done.24, ...), custom_call_target="tpu_custom_call" | custom-call | tf_op jit(solution)/shard_map/feed_back/pallas_call | solution.py:1042
  628.3 13.1 %attend_back.3 = (f32[256,768]{1,0:T(8,128)S(1)}, bf16[4,2,256,768]{3,2,1,0:T(8,128)(2,1)S(1)}) custom-call(bf16[256,768]{1,0:T(8,128)(2,1)S(1)} %copy-done.20, bf16[4,2,256,768]{3,2,1,0:T(8,128)(2,1)S(1)} %bitcast.80, bf16[4,2,256,768]{3,2,1,0:T(8,128)(2,1)S(1)} %bitcast.81, s32[1024,1]{1,0:T(8,128)S(1)} %copy-done.8, s32[1,256]{1,0:T(1,128)S(1)} %dynamic_slice.36.qseg_ref, ...), custom_call_target="tpu_custom_call" | custom-call | tf_op jit(solution)/shard_map/attend_back/pallas_call | solution.py:1104
  641.4 1.7 copy-done.14
  643.1 26.9 %keys_reduce.3 = bf16[512,768]{1,0:T(8,128)(2,1)} custom-call(bf16[4,512,768]{2,1,0:T(8,128)(2,1)} %bitcast.87), custom_call_target="tpu_custom_call" | custom-call | tf_op jit(solution)/shard_map/keys_reduce/pallas_call | solution.py:723
  671.2 7.0 project_back.3
  679.0 173.1 %grads_and_entry.1 = (bf16[576,768]{1,0:T(8,128)(2,1)}, bf16[32,256,768]{2,1,0:T(8,128)(2,1)}) custom-call(bf16[32,192,768]{2,1,0:T(8,128)(2,1)} %bitcast.112, bf16[32,192,768]{2,1,0:T(8,128)(2,1)} %bitcast.116, bf16[32,192,768]{2,1,0:T(8,128)(2,1)} %bitcast.113, bf16[256,768]{1,0:T(8,128)(2,1)} %convert_element_type.87.refs_3_), custom_call_target="tpu_custom_call" | custom-call | tf_op jit(solution)/shard_map/grads_and_entry/pallas_call | solution.py:617
  852.2 2.4 pad_maximum_fusion
  857.6 11.3 %multiply_reduce_fusion.1 = (f32[]{:T(128)}, f32[1000,768]{1,0:T(8,128)}) fusion(bf16[3072,1000]{0,1:T(8,128)(2,1)} %copy-done.34, bf16[3072,768]{1,0:T(8,128)(2,1)} %bitcast.119), kind=kOutput, calls=%fused_computation.34 | convolution fusion | flops 4720128000 | bytes 13934596 | tf_op jit(solution)/shard_map/rv,rd->vd/dot_general | solution.py:1399
  868.9 21.2 %multiply_reduce_fusion.2 = (f32[]{:T(128)}, f32[1000,768]{1,0:T(8,128)}) fusion(bf16[8192,768]{1,0:T(8,128)(2,1)} %bitcast.144, s32[8192]{0:T(1024)S(1)} %bitcast.141), kind=kOutput, calls=%fused_computation.35 | convolution fusion | flops 12592640000 | bytes 15687684 | tf_op jit(solution)/shard_map/tv,td->vd/dot_general | solution.py:1420
  890.1 26.1 %all-gather.10.cloned.1.call-done = bf16[6144,768]{1,0:T(8,128)(2,1)} async-done(((bf16[768,768]{1,0:T(8,128)(2,1)}), bf16[6144,768]{1,0:T(8,128)(2,1)}) %all-gather.10.cloned.1.call-update) | async-done | bytes 9437200 | tf_op jit(solution)/shard_map/all_gather | solution.py:1423
  916.2 4.3 gather_fusion.2
  920.6 1.6 multiply_reduce_fusion
  924.8 20.5 %sums_gather.1 = f32[32,32,128]{2,1,0:T(8,128)} custom-call(f32[32,128]{1,0:T(8,128)} %fusion.22.refs_0_), custom_call_target="tpu_custom_call" | custom-call | tf_op jit(solution)/shard_map/sums_gather/pallas_call | solution.py:248
  949.1 10.6 %fusion.43 = (bf16[6,192,768]{2,1,0:T(8,128)(2,1)}, f32[6,192,768]{2,1,0:T(8,128)}, f32[6,192,768]{2,1,0:T(8,128)}, f32[6,192,768]{2,1,0:T(8,128)}) fusion(f32[6,192,768]{2,1,0:T(8,128)} %w_ref.1, f32[6,192,768]{2,1,0:T(8,128)} %param.26, f32[]{:T(128)} %bitcast.50, f32[]{:T(128)S(6)} %min.3, bf16[6,192,768]{2,1,0:T(8,128)(2,1)S(1)} %gather_fusion.2, ...), kind=kLoop, calls=%fused_computation.144 | loop fusion | flops 19464192 | bytes 24772628 | tf_op jit(solution)/shard_map/convert_element_type | solution.py:1466
  961.0 6.0 fusion.39
  969.3 4.9 fusion.41
  (204 shorter events, 36.3 us)
Async XLA Ops:
  7.2 2.6 copy-start
  7.2 275.8 %all-gather.6.cloned.1.call-start = ((), (), s32[]{:S(2)}) async-start(), calls=%async_computation.1 | async-start | bytes 19464192 | tf_op jit(solution)/shard_map/all_gather | solution.py:1306
  12.6 10.0 %copy-start.54 = (pred[32]{0:T(512)(128)(4,1)}, pred[32]{0:T(512)(128)(4,1)S(1)}, u32[]{:S(2)}) copy-start(pred[32]{0:T(512)(128)(4,1)S(1)} %gather_fusion) | copy-start | bytes 100
  13.3 9.3 copy-start.56
  79.7 4.0 copy-start.44
  81.7 300.5 %all-gather.8.cloned.1.call-start = ((), (), s32[]{:S(2)}) async-start(), calls=%async_computation.3 | async-start | bytes 9732096 | tf_op jit(solution)/shard_map/all_gather | solution.py:1309
  83.7 768.5 %reduce-scatter.2.cloned.1.call-start = ((), (), s32[]{:S(2)}) async-start(), calls=%async_computation.2 | async-start | bytes 9732096 | tf_op jit(solution)/shard_map/reduce_scatter | solution.py:1411
  84.0 23.0 %copy-start.50 = (s32[8,2,4,128]{3,1,2,0:T(2,128)}, s32[8,2,4,128]{3,1,2,0:T(2,128)S(1)}, u32[]{:S(2)}) copy-start(s32[8,2,4,128]{3,1,2,0:T(2,128)S(1)} %copy.95) | copy-start | bytes 98308
  87.0 20.0 %copy-start.48 = (pred[8,4,96]{2,0,1:T(8,128)(4,1)}, pred[8,4,96]{2,0,1:T(8,128)(4,1)S(1)}, u32[]{:S(2)}) copy-start(pred[8,4,96]{2,0,1:T(8,128)(4,1)S(1)} %get-tuple-element.134) | copy-start | bytes 9220
  87.4 280.7 %copy-start.6 = (s32[1024,1]{1,0:T(8,128)}, s32[1024,1]{1,0:T(8,128)S(1)}, u32[]{:S(2)}) copy-start(s32[1024,1]{1,0:T(8,128)S(1)} %copy.86.kseg_ref) | copy-start | bytes 12292
  107.0 176.0 %copy-start.45 = (f32[5,768]{1,0:T(8,128)S(1)}, f32[5,768]{1,0:T(8,128)}, u32[]{:S(2)}) copy-start(f32[5,768]{1,0:T(8,128)} %param.33) | copy-start | bytes 46084
  282.0 44.9 %copy-start.9 = (f32[256,768]{1,0:T(8,128)}, f32[256,768]{1,0:T(8,128)S(1)}, u32[]{:S(2)}) copy-start(f32[256,768]{1,0:T(8,128)S(1)} %convert_element_type.78.x_ref) | copy-start | bytes 2359300
  288.2 38.6 %copy-start.19 = (bf16[256,768]{1,0:T(8,128)(2,1)}, bf16[256,768]{1,0:T(8,128)(2,1)S(1)}, u32[]{:S(2)}) copy-start(bf16[256,768]{1,0:T(8,128)(2,1)S(1)} %get-tuple-element.58.q_ref) | copy-start | bytes 1179652
  312.7 1.9 copy-start.2
  326.9 10.7 %copy-start.17 = (bf16[256,768]{1,0:T(8,128)(2,1)}, bf16[256,768]{1,0:T(8,128)(2,1)S(1)}, u32[]{:S(2)}) copy-start(bf16[256,768]{1,0:T(8,128)(2,1)S(1)} %get-tuple-element.60.o_ref) | copy-start | bytes 1179652
  337.6 4.9 copy-start.23
  337.6 44.6 %copy-start.11 = (f32[256,768]{1,0:T(8,128)}, f32[256,768]{1,0:T(8,128)S(1)}, u32[]{:S(2)}) copy-start(f32[256,768]{1,0:T(8,128)S(1)} %get-tuple-element.61.x_ref) | copy-start | bytes 2359300
  343.3 38.8 %copy-start.21 = (bf16[256,768]{1,0:T(8,128)(2,1)}, bf16[256,768]{1,0:T(8,128)(2,1)S(1)}, u32[]{:S(2)}) copy-start(bf16[256,768]{1,0:T(8,128)(2,1)S(1)} %get-tuple-element.63.q_ref) | copy-start | bytes 1179652
  368.0 1.9 copy-start.4
  440.6 4.5 copy-start.33
  472.0 7.0 copy-start.35
  479.0 7.4 copy-start.34
  548.7 367.5 %all-gather.10.cloned.1.call-start = ((), (), s32[]{:S(2)}) async-start(), calls=%async_computation.4 | async-start | bytes 10616832 | tf_op jit(solution)/shard_map/all_gather | solution.py:1423
  569.2 24.0 %copy-start.12 = (f32[256,768]{1,0:T(8,128)S(1)}, f32[256,768]{1,0:T(8,128)}, u32[]{:S(2)}) copy-start(f32[256,768]{1,0:T(8,128)} %copy-done.11) | copy-start | bytes 2359300
  569.2 24.0 %copy-start.26 = (f32[256,768]{1,0:T(8,128)S(1)}, f32[256,768]{1,0:T(8,128)}, u32[]{:S(2)}) copy-start(f32[256,768]{1,0:T(8,128)} %copy-done.25) | copy-start | bytes 2359300
  595.6 6.8 copy-start.18
  595.6 6.8 copy-start.24
  602.3 26.0 %copy-start.3 = (bf16[4,512,768]{2,1,0:T(8,128)(2,1)S(1)}, bf16[4,512,768]{2,1,0:T(8,128)(2,1)}, u32[]{:S(2)}) copy-start(bf16[4,512,768]{2,1,0:T(8,128)(2,1)} %keys_gather.2) | copy-start | bytes 9437188
  602.3 26.0 %copy-start.8 = (s32[1024,1]{1,0:T(8,128)S(1)}, s32[1024,1]{1,0:T(8,128)}, u32[]{:S(2)}) copy-start(s32[1024,1]{1,0:T(8,128)} %copy-done.6) | copy-start | bytes 12292
  602.4 25.9 %copy-start.20 = (bf16[256,768]{1,0:T(8,128)(2,1)S(1)}, bf16[256,768]{1,0:T(8,128)(2,1)}, u32[]{:S(2)}) copy-start(bf16[256,768]{1,0:T(8,128)(2,1)} %copy-done.19) | copy-start | bytes 1179652
  643.1 26.9 %copy-start.10 = (f32[256,768]{1,0:T(8,128)S(1)}, f32[256,768]{1,0:T(8,128)}, u32[]{:S(2)}) copy-start(f32[256,768]{1,0:T(8,128)} %copy-done.9) | copy-start | bytes 2359300
  852.2 3.8 copy-start.55
  852.2 3.8 copy-start.57
  852.2 4.0 copy-start.47
  852.2 4.1 copy-start.49
  857.6 11.3 %copy-start.51 = (s32[8,2,4,128]{3,1,2,0:T(2,128)S(1)}, s32[8,2,4,128]{3,1,2,0:T(2,128)}, u32[]{:S(2)}) copy-start(s32[8,2,4,128]{3,1,2,0:T(2,128)} %copy-done.50) | copy-start | bytes 98308
  949.0 10.7 %copy-start.46 = (f32[5,768]{1,0:T(8,128)S(1)}, f32[5,768]{1,0:T(8,128)}, u32[]{:S(2)}) copy-start(f32[5,768]{1,0:T(8,128)} %param.33) | copy-start | bytes 46084
  949.0 10.7 %copy-start.52 = (f32[5,768]{1,0:T(8,128)S(1)}, f32[5,768]{1,0:T(8,128)}, u32[]{:S(2)}) copy-start(f32[5,768]{1,0:T(8,128)} %param.35) | copy-start | bytes 46084
  949.0 10.7 %copy-start.53 = (f32[5,768]{1,0:T(8,128)S(1)}, f32[5,768]{1,0:T(8,128)}, u32[]{:S(2)}) copy-start(f32[5,768]{1,0:T(8,128)} %param.34) | copy-start | bytes 46084
  949.0 11.4 %copy-start.36 = (f32[1000,768]{1,0:T(8,128)S(1)}, f32[1000,768]{1,0:T(8,128)}, u32[]{:S(2)}) copy-start(f32[1000,768]{1,0:T(8,128)} %param.30) | copy-start | bytes 9216004
  949.0 11.3 %copy-start.37 = (f32[1000,768]{1,0:T(8,128)S(1)}, f32[1000,768]{1,0:T(8,128)}, u32[]{:S(2)}) copy-start(f32[1000,768]{1,0:T(8,128)} %param.32) | copy-start | bytes 9216004
  949.0 11.3 %copy-start.38 = (f32[1000,768]{1,0:T(8,128)S(1)}, f32[1000,768]{1,0:T(8,128)}, u32[]{:S(2)}) copy-start(f32[1000,768]{1,0:T(8,128)} %param.31) | copy-start | bytes 9216004
  949.1 11.9 %copy-start.43 = (f32[1000,768]{1,0:T(8,128)S(1)}, f32[1000,768]{1,0:T(8,128)}, u32[]{:S(2)}) copy-start(f32[1000,768]{1,0:T(8,128)} %get-tuple-element.146) | copy-start | bytes 9216004
  961.0 6.0 copy-start.39
  961.0 6.0 copy-start.40
  961.0 7.4 copy-start.41
  961.0 8.3 copy-start.42
  969.3 4.9 copy-start.1
  (14 other events, 16.0 us)
Sparse Core Ops, SparseCore 0:
  81.8 184.5 all-gather.5
  269.8 90.2 all-gather.7
  548.8 136.1 reduce-scatter.1
  854.7 61.4 all-gather.9
